TPU v7x, 32 devices: a whole 2x2x4 slice. The times are simulated.
32 devices in a mesh: groups: 2 (over y), tok: 16 (over z, x, core).
Axes of the slice: x: 2, y: 2, z: 4, core: 2. Of those that a mesh axis runs over, the one named last changes fastest.
Arguments:
- activations: bfloat16 [2, 20480, 2048], P(None, ('groups', 'tok')), parts along dimension 1, may hold values from -6 to 6
- gradients: bfloat16 [2, 20480, 2048], P(None, ('groups', 'tok')), parts along dimension 1, may hold values from -6 to 6
- query_u: bfloat16 [4, 2048, 1024], P('groups', 'tok'), parts along dimension 0, may hold values from -4 to 4
- query_v: bfloat16 [4, 2048, 1024], P('groups', 'tok'), parts along dimension 0, may hold values from -4 to 4
- block_ids: int32 [4, 16], P('groups'), parts along dimension 0, may hold values from 0 to 31
- counts: int32 [32], P(('groups', 'tok')), parts along dimension 0, may hold values from 1 to 640, 5440 in all
Outputs:
- scores: float32 [20480, 64], P(('groups', 'tok')), parts along dimension 0
There are 2 independent parts, one for each index of `groups`. A program takes and returns all parts, laid end to end along the dimension named above; each array names one. Nothing has to cross between parts.
Inputs may be any that keep to these rules, and one draw needn't show every extreme that they name: The counts of one part sum to (16 + 1) * 320 and the largest equals 640.
All inputs are finite; a program needn't handle non-finite values. No bound on the sum of `counts` on one device may be relied on, other than what follows from the above.
Results may differ from a plain program's by a relative error of at most 0.0003.
Values may be sent and summed in bfloat16 or wider, within the bound.
No kernel may reach another device: no remote copies, remote signals or barrier semaphores. Data moves between devices by JAX's collectives and lax.ppermute only.
A program may use at most 64 MiB of HBM per device.

v0:
```python
import jax
import jax.numpy as jnp
from jax import lax
from jax.sharding import PartitionSpec as P

RANK = 8
QB = 4


def pick_columns(factor, block_ids):
    width = QB * RANK
    chosen = []
    for layer in range(factor.shape[0]):
        slots = factor[layer].reshape(factor.shape[1], -1, width)
        chosen.append(jnp.take(slots, block_ids[layer], axis=1).reshape(factor.shape[1], -1))
    return jnp.stack(chosen)


def rank_grams(factor):
    per = factor.reshape(factor.shape[0], factor.shape[1], -1, RANK)
    return jnp.einsum("lkqr,lkqs->lqrs", per, per, preferred_element_type=jnp.float32)


def per_device(activations, gradients, query_u, query_v, block_ids, counts):
    layers, tok_rows, width = activations.shape
    columns = block_ids.shape[1] * QB * RANK
    queries = columns // RANK
    picked_u = pick_columns(query_u, block_ids)
    picked_v = pick_columns(query_v, block_ids)
    whole_u, whole_v = (
        lax.all_gather(picked_u, "tok", axis=1, tiled=True),
        lax.all_gather(picked_v, "tok", axis=1, tiled=True),
    )
    grad_proj = jnp.einsum("ltk,lkc->ltc", gradients, whole_u, preferred_element_type=jnp.float32)
    act_proj = jnp.einsum("ltk,lkc->ltc", activations, whole_v, preferred_element_type=jnp.float32)
    totals = (grad_proj, act_proj)
    totals = totals + (rank_grams(whole_u), rank_grams(whole_v))
    gram_u = totals[2]
    gram_v = totals[3]
    raw = jnp.sum((totals[0] * totals[1]).reshape(layers, tok_rows, queries, RANK), axis=(0, 3))
    norm_sq = jnp.sum(gram_u * gram_v, axis=(0, 2, 3))
    live = jnp.arange(tok_rows, dtype=jnp.int32) < counts[0]
    scaled = raw / jnp.sqrt(norm_sq + 1e-06)[None, :]
    return jnp.where(live[:, None], scaled, jnp.zeros_like(scaled))


def solution(mesh):
    placed = (
        P(None, ("groups", "tok"), None),
        P(None, ("groups", "tok"), None),
        P("groups", "tok", None),
        P("groups", "tok", None),
        P("groups", None),
        P(("groups", "tok")),
    )
    return jax.shard_map(
        per_device,
        mesh=mesh,
        in_specs=placed,
        out_specs=P(("groups", "tok"), None),
        check_vma=False,
    )
```

profile of v0, /device:TPU:0, one launch (start us, length us, event | category | flops | bytes accessed | tf_op | source)
XLA Modules:
  0.0 146.6 jit_solution(14041610911955827750)
XLA Ops:
  6.5 0.0 all-gather.5.cloned.1.call-start
  6.5 0.8 compare_and_fusion.1
  7.3 1.1 fusion.11
  8.4 0.2 copy.15
  8.6 0.2 copy.16
  8.7 1.1 fusion.10
  9.8 0.2 copy.17
  10.0 0.6 gather_fusion
  10.6 0.6 gather_fusion.2
  11.2 0.2 copy.18
  11.3 0.6 gather_fusion.1
  11.9 0.6 gather_fusion.3
  12.5 0.1 broadcast_select_fusion
  12.6 0.8 pad_maximum_fusion.1
  13.4 0.0 all-gather.5.cloned.1.call-update
  13.4 0.0 all-gather.3.cloned.1.call-start
  13.4 0.7 pad_maximum_fusion
  14.2 0.0 all-gather.3.cloned.1.call-update
  14.9 53.9 %all-gather.5.cloned.1.call-done = bf16[2,2048,512]{1,2,0:T(8,128)(2,1)} async-done(((bf16[2,128,512]{1,2,0:T(8,128)(2,1)}), bf16[2,2048,512]{1,2,0:T(8,128)(2,1)}) %all-gather.5.cloned.1.call-update) | async-done | bytes 4194320 | tf_op jit(solution)/shard_map/all_gather | solution.py:32
  68.8 6.2 %fusion = f32[2,64,8,8]{3,2,1,0:T(8,128)S(1)} fusion(bf16[2,2048,512]{1,2,0:T(8,128)(2,1)} %all-gather.5.cloned.1.call-done), kind=kOutput, calls=%fused_computation.4 | convolution fusion | flops 33554432 | bytes 4227072 | tf_op jit(solution)/shard_map/lkqr,lkqs->lqrs/dot_general | solution.py:21
  74.9 46.7 %all-gather.3.cloned.1.call-done = bf16[2,2048,512]{1,2,0:T(8,128)(2,1)} async-done(((bf16[2,128,512]{1,2,0:T(8,128)(2,1)}), bf16[2,2048,512]{1,2,0:T(8,128)(2,1)}) %all-gather.3.cloned.1.call-update) | async-done | bytes 4194320 | tf_op jit(solution)/shard_map/all_gather | solution.py:31
  121.6 0.0 slice-start
  121.6 6.6 %fusion.7 = f32[64]{0:T(128)S(1)} fusion(f32[2,64,8,8]{3,2,1,0:T(8,128)S(1)} %fusion, bf16[2,2048,512]{1,2,0:T(8,128)(2,1)} %all-gather.3.cloned.1.call-done), kind=kOutput, calls=%fused_computation.11 | convolution fusion | flops 33570752 | bytes 4227328 | tf_op jit(solution)/shard_map/lkqr,lkqs->lqrs/dot_general | solution.py:21
  128.2 0.0 slice-start.1
  128.2 0.0 copy-start
  128.2 7.0 %fusion.12 = f32[2,512,640]{2,1,0:T(8,128)S(1)} fusion(bf16[2,2048,512]{1,2,0:T(8,128)(2,1)} %all-gather.3.cloned.1.call-done, bf16[2,640,2048]{2,1,0:T(8,128)(2,1)} %param.9), kind=kOutput, calls=%fused_computation.29 | convolution fusion | flops 2684354560 | bytes 12058624 | tf_op jit(solution)/shard_map/ltk,lkc->ltc/dot_general | solution.py:34
  135.2 0.0 slice-done
  135.2 0.0 slice-done.1
  135.2 0.0 copy-done
  135.2 3.4 %multiply_reduce_fusion = f32[512,640]{1,0:T(8,128)S(1)} fusion(f32[2,512,640]{2,1,0:T(8,128)S(1)} %fusion.12, bf16[2,2048,512]{1,2,0:T(8,128)(2,1)S(1)} %copy-done, bf16[2,640,2048]{2,1,0:T(8,128)(2,1)S(1)} %bitcast.51), kind=kOutput, calls=%fused_computation.8 | convolution fusion | flops 2685337600 | bytes 13369344 | tf_op jit(solution)/shard_map/ltk,lkc->ltc/dot_general | solution.py:35
  138.7 0.3 bitcast_reduce_fusion
  139.0 0.8 divide_select_fusion
  (5 shorter events, 0.0 us)
Async XLA Ops:
  6.5 62.2 %all-gather.5.cloned.1.call-start = ((), (), s32[]{:S(2)}) async-start(), calls=%async_computation.1 | async-start | bytes 4456448 | tf_op jit(solution)/shard_map/all_gather | solution.py:32
  13.4 108.2 %all-gather.3.cloned.1.call-start = ((), (), s32[]{:S(2)}) async-start(), calls=%async_computation | async-start | bytes 4456448 | tf_op jit(solution)/shard_map/all_gather | solution.py:31
  121.6 13.6 %slice-start = ((s8[5242880]{0:T(1024)(128)(4,1)}), s8[4194304]{0:T(1024)(128)(4,1)S(1)}, s32[]{:S(2)}) async-start(s8[5242880]{0:T(1024)(128)(4,1)} %bitcast.50), calls=%async_computation.2 | async-start | bytes 8388608
  128.2 7.0 %slice-start.1 = ((s8[5242880]{0:T(1024)(128)(4,1)}), s8[1048576]{0:T(1024)(128)(4,1)S(1)}, s32[]{:S(2)}) async-start(s8[5242880]{0:T(1024)(128)(4,1)} %bitcast.50), calls=%async_computation.3 | async-start | bytes 2097152
  128.2 7.0 %copy-start = (bf16[2,2048,512]{1,2,0:T(8,128)(2,1)S(1)}, bf16[2,2048,512]{1,2,0:T(8,128)(2,1)}, u32[]{:S(2)}) copy-start(bf16[2,2048,512]{1,2,0:T(8,128)(2,1)} %all-gather.5.cloned.1.call-done) | copy-start | bytes 12582916
Sparse Core Ops, SparseCore 0:
  13.5 55.2 all-gather.4
  70.9 50.6 all-gather.2
where the time goes:
time: 147 us
  waiting for transfers between devices  101 us (69%)
  matrix products  23.2 us (16%)
  between operations  14.2 us (10%)
  local copies, waits for them, and re-layouts  5.13 us (3%)
  other arithmetic  3.46 us (2%)
    all_gather x1, waiting for transfers between devices, per_device(): lax.all_gather(picked_v, 'tok', axis=1, tiled=True)  53.9 us
    all_gather x1, waiting for transfers between devices, per_device(): lax.all_gather(picked_u, 'tok', axis=1, tiled=True)  46.7 us
    dot_general x2, matrix products, rank_grams(): jnp.einsum('lkqr,lkqs->lqrs', per, per, preferred_element_type=jnp.float32)  12.8 us
    dot_general x1, matrix products, per_device(): jnp.einsum('ltk,lkc->ltc', gradients, whole_u, preferred_element_type=jnp...  6.96 us
    dot_general x1, matrix products, per_device(): jnp.einsum('ltk,lkc->ltc', activations, whole_v, preferred_element_type=j...  3.44 us
  transfers between devices with their start and end apart: 2, of which 2 were waited for; matrix products, arithmetic and copies ran while one was open for 5% of the time, Pallas kernels for 0%

commit v1 on v0

v1 whole, which is shorter than its diff:
```python
import functools

import jax
import jax.numpy as jnp
from jax import lax
from jax.experimental import pallas as pl
from jax.experimental.pallas import tpu as pltpu
from jax.sharding import PartitionSpec as P


RANK = 8
QB = 4
OUTER = 4
LANES = 128
TILE = 256


def pick_columns(factor, block_ids):
    width = QB * RANK
    chosen = []
    for layer in range(factor.shape[0]):
        slots = factor[layer].reshape(factor.shape[1], -1, width)
        chosen.append(jnp.take(slots, block_ids[layer], axis=1).reshape(factor.shape[1], -1))
    return jnp.stack(chosen)


def rank_grams(factor):
    per = factor.reshape(factor.shape[0], factor.shape[1], -1, RANK)
    return jnp.einsum("lkqr,lkqs->lqrs", per, per, preferred_element_type=jnp.float32)


def per_device_plain(activations, gradients, query_u, query_v, block_ids, counts):
    layers, tok_rows, _ = activations.shape
    columns = block_ids.shape[1] * QB * RANK
    queries = columns // RANK
    whole_u = lax.all_gather(pick_columns(query_u, block_ids), "tok", axis=1, tiled=True)
    whole_v = lax.all_gather(pick_columns(query_v, block_ids), "tok", axis=1, tiled=True)
    grad_proj = jnp.einsum("ltk,lkc->ltc", gradients, whole_u, preferred_element_type=jnp.float32)
    act_proj = jnp.einsum("ltk,lkc->ltc", activations, whole_v, preferred_element_type=jnp.float32)
    raw = jnp.sum((grad_proj * act_proj).reshape(layers, tok_rows, queries, RANK), axis=(0, 3))
    norm_sq = jnp.sum(rank_grams(whole_u) * rank_grams(whole_v), axis=(0, 2, 3))
    live = jnp.arange(tok_rows, dtype=jnp.int32) < counts[0]
    scaled = raw / jnp.sqrt(norm_sq + 1e-06)[None, :]
    return jnp.where(live[:, None], scaled, jnp.zeros_like(scaled))


def pick_kernel(layer, ids_ref, u_ref, v_ref, out_ref, held, sems):
    width = QB * RANK
    rows, bank = u_ref.shape[1:]
    columns = out_ref.shape[2]
    copies = [
        pltpu.make_async_copy(ref.at[layer], held.at[pl.ds(s * rows, rows), :], sems.at[s])
        for s, ref in enumerate((u_ref, v_ref))
    ]
    for copy in copies:
        copy.start()
    lane = lax.broadcasted_iota(jnp.int32, (1, columns), 1)
    named = jnp.zeros((1, columns), jnp.int32)
    for block in range(columns // width):
        named = jnp.where(lane // width == block, ids_ref[layer, block], named)
    row = lax.broadcasted_iota(jnp.int32, (width, columns), 0)
    col = lax.broadcasted_iota(jnp.int32, (width, columns), 1) % width
    one = jnp.where(row == col, 1.0, 0.0).astype(jnp.bfloat16)
    chooser = [
        one * jnp.where(named == stored, 1.0, 0.0).astype(jnp.bfloat16) for stored in range(bank // width)
    ]
    chooser = jnp.concatenate(chooser, axis=0)
    for copy in copies:
        copy.wait()
    got = jnp.dot(held[...], chooser, preferred_element_type=jnp.float32).astype(jnp.bfloat16)
    out_ref[0] = got[:rows]
    out_ref[1] = got[rows:]


def pick(layer, query_u, query_v, block_ids):
    _, rows, bank = query_u.shape
    columns = block_ids.shape[1] * QB * RANK
    return pl.pallas_call(
        functools.partial(pick_kernel, layer),
        out_shape=jax.ShapeDtypeStruct((2, rows, columns), jnp.bfloat16),
        in_specs=[pl.BlockSpec(memory_space=pltpu.SMEM)] + [pl.BlockSpec(memory_space=pltpu.HBM)] * 2,
        out_specs=pl.BlockSpec(memory_space=pltpu.VMEM),
        scratch_shapes=[pltpu.VMEM((2 * rows, bank), jnp.bfloat16), pltpu.SemaphoreType.DMA((2,))],
        cost_estimate=pl.CostEstimate(
            flops=4 * rows * bank * columns, bytes_accessed=4 * rows * (bank + columns), transcendentals=0
        ),
    )(block_ids, query_u, query_v)


def split_dot(left, right):
    total = None
    rest = left
    for _ in range(3):
        term = rest.astype(jnp.bfloat16)
        rest = rest - term.astype(jnp.float32)
        part = jnp.dot(term, right, preferred_element_type=jnp.float32)
        total = part if total is None else total + part
    return total


def group_sums(columns):
    row = lax.broadcasted_iota(jnp.int32, (columns, LANES), 0)
    col = lax.broadcasted_iota(jnp.int32, (columns, LANES), 1)
    return jnp.where(row // RANK == col, 1.0, 0.0).astype(jnp.bfloat16)


def stage_kernel(cfg, *refs):
    (outer, inner), groups, last, rows = cfg["shape"], cfg["groups"], cfg["last"], cfg["rows"]
    refs = list(refs)

    def take(n):
        return [refs.pop(0) for _ in range(n)]

    x_refs = take(2)
    counts_ref = take(1)[0] if last else None
    pieces = [[take(2) for _ in g["where"]] for g in groups]
    starts = [take(3) if g["carry"] else None for g in groups]
    outs = take(1) if last else None
    totals = [take(3) for _ in groups]
    x, w, sems = take(3)
    me = lax.axis_index("tok")
    a, b, c = me // (2 * inner), (me // 2) % inner, me % 2
    copies, slot = [], 0
    for g, arrays in zip(groups, pieces):
        for (da, db), pair in zip(g["where"], arrays):
            owner = ((a + outer - da) % outer) * inner + (b + inner - db) % inner
            start = pl.multiple_of(owner * 2 * rows, LANES)
            these = []
            for dc, array in enumerate(pair):
                spot = pl.multiple_of(slot * 2 * rows + ((c + dc) % 2) * rows, LANES)
                these.append((array, w.at[:, pl.ds(spot, rows), :]))
            for s, x_ref in enumerate(x_refs):
                these.append((x_ref.at[g["layer"], :, pl.ds(start, 2 * rows)], x.at[slot, s]))
            these = [pltpu.make_async_copy(*ends, sems.at[4 * slot + i]) for i, ends in enumerate(these)]
            for copy in these:
                copy.start()
            copies.append(these)
            slot += 1
    tiles = w.shape[2] // TILE
    slot = 0
    for g, start, total in zip(groups, starts, totals):
        for first in range(len(g["where"])):
            for copy in copies[slot]:
                copy.wait()
            span = slice(slot * 2 * rows, (slot + 1) * 2 * rows)
            came = start if first == 0 else total
            for s in range(2):
                part = jnp.dot(x[slot, s], w[s, span, :], preferred_element_type=jnp.float32)
                total[s][...] = part if came is None else came[s][...] + part
            for s in range(2):
                for t in range(tiles):
                    one = w[s, span, t * TILE : (t + 1) * TILE]
                    part = lax.dot_general(one, one, (((0,), (0,)), ((), ())), preferred_element_type=jnp.float32)
                    i = s * tiles + t
                    total[2][i] = part if came is None else came[2][i] + part
            slot += 1
    if last:
        columns = w.shape[2]
        row = lax.broadcasted_iota(jnp.int32, (TILE, TILE), 0)
        col = lax.broadcasted_iota(jnp.int32, (TILE, TILE), 1)
        same = row // RANK == col // RANK
        norm = []
        for t in range(tiles):
            both = sum(total[2][t] * total[2][tiles + t] for total in totals)
            norm.append(jnp.sum(jnp.where(same, both, 0.0), axis=0, keepdims=True))
        norm = jnp.broadcast_to(jnp.concatenate(norm, axis=1), (8, columns))
        chooser = group_sums(columns)
        norm = split_dot(norm, chooser)[:1]
        raw = split_dot(sum(total[0][...] * total[1][...] for total in totals), chooser)
        scaled = raw / jnp.sqrt(norm + 1e-06)
        token = lax.broadcasted_iota(jnp.int32, scaled.shape, 0)
        scaled = jnp.where(token < counts_ref[0], scaled, 0.0)
        outs[0][...] = scaled.T[: columns // RANK]


def stage(shape, groups, gradients, activations, counts=None):
    last = counts is not None
    rows, columns = groups[0]["arrays"][0][0].shape[1:]
    tokens = gradients.shape[1]
    slots = sum(len(g["where"]) for g in groups)
    tiles = 2 * (columns // TILE)
    anywhere = pl.BlockSpec(memory_space=pltpu.HBM)
    vmem = pl.BlockSpec(memory_space=pltpu.VMEM)
    args, specs = [gradients, activations], [anywhere, anywhere]
    if last:
        args.append(counts)
        specs.append(pl.BlockSpec(memory_space=pltpu.SMEM))
    for g in groups:
        for pair in g["arrays"]:
            args += pair
            specs += [anywhere] * 2
    aliases = {}
    for n, g in enumerate(groups):
        if g["carry"] is not None:
            if not last:
                aliases.update({len(args) + i: 3 * n + i for i in range(3)})
            args += list(g["carry"])
            specs += [vmem] * 3
    sums = [((tokens, columns), jnp.float32)] * 2 + [((tiles, TILE, TILE), jnp.float32)]
    scratch = []
    if last:
        out_shape = jax.ShapeDtypeStruct((columns // RANK, tokens), jnp.float32)
        out_specs = vmem
        scratch = [pltpu.VMEM(*one) for one in sums] * len(groups)
    else:
        out_shape = tuple(jax.ShapeDtypeStruct(*one) for one in sums) * len(groups)
        out_specs = (vmem,) * len(out_shape)
    cfg = dict(
        shape=shape,
        rows=rows,
        last=last,
        groups=[dict(layer=g["layer"], where=g["where"], carry=g["carry"] is not None) for g in groups],
    )
    flops = 4 * slots * rows * columns * (2 * tokens + tiles * TILE)
    return pl.pallas_call(
        functools.partial(stage_kernel, cfg),
        out_shape=out_shape,
        in_specs=specs,
        out_specs=out_specs,
        scratch_shapes=scratch
        + [
            pltpu.VMEM((slots, 2, tokens, 2 * rows), jnp.bfloat16),
            pltpu.VMEM((2, slots * 2 * rows, columns), jnp.bfloat16),
            pltpu.SemaphoreType.DMA((4 * slots,)),
        ],
        input_output_aliases=aliases,
        compiler_params=pltpu.CompilerParams(vmem_limit_bytes=52 << 20),
        cost_estimate=pl.CostEstimate(
            flops=flops, bytes_accessed=8 * slots * rows * (tokens + columns), transcendentals=0
        ),
    )(*args)


def after(value, *others):
    return lax.optimization_barrier((value,) + others)[0]


def per_device(shape, activations, gradients, query_u, query_v, block_ids, counts):
    outer, inner = shape

    def number(a, b, c):
        return ((a % outer) * inner + b % inner) * 2 + c % 2

    def move(value, da, db, dc):
        steps = [
            (number(a, b, c), number(a + da, b + db, c + dc))
            for a in range(outer)
            for b in range(inner)
            for c in range(2)
        ]
        return lax.ppermute(value, "tok", steps)

    have, pairs = [{}, {}], [{}, {}]
    for layer in range(2):
        have[layer][(0, 0)] = pick(layer, query_u, query_v, block_ids)
    for da in range(outer):
        for layer in range(2):
            h = have[layer]
            if da < outer - 1:
                fed = h[(da, 0)]
                if da:
                    fed = after(fed, h[(da - 1, 1)])
                h[(da + 1, 0)] = move(fed, 1, 0, 0)
            if da == outer - 1 and layer == 1:
                fed = after(h[(0, 1)], h[(da, 0)])
                h[(da, 1)] = move(fed, -1, 0, 0)
            else:
                h[(da, 1)] = move(h[(da, 0)], 0, 1, 0)
    for layer in range(2):
        for key, piece in have[layer].items():
            pairs[layer][key] = [piece, move(piece, 0, 0, 1)]

    def group(layer, keys, carry):
        return dict(layer=layer, where=keys, arrays=[pairs[layer][key] for key in keys], carry=carry)

    parts = [[(0, 0), (0, 1), (1, 0)]] + [[(da, 1), (da + 1, 0)] for da in range(1, outer - 1)]
    carry = [None, None]
    for keys in parts:
        for layer in range(2):
            carry[layer] = stage(shape, [group(layer, keys, carry[layer])], gradients, activations)
    scores = stage(
        shape,
        [group(layer, [(outer - 1, 1)], carry[layer]) for layer in range(2)],
        gradients,
        activations,
        counts=counts,
    )
    return scores.T


def solution(mesh):
    spec = (
        P(None, ("groups", "tok"), None),
        P(None, ("groups", "tok"), None),
        P("groups", "tok", None),
        P("groups", "tok", None),
        P("groups", None),
        P(("groups", "tok")),
    )
    members = mesh.shape["tok"]
    shape = (OUTER, members // (2 * OUTER))
    ring = members == 4 * OUTER

    def body(*args):
        fits = ring and args[2].shape[1] % LANES == 0
        return per_device(shape, *args) if fits else per_device_plain(*args)

    return jax.shard_map(body, mesh=mesh, in_specs=spec, out_specs=P(("groups", "tok"), None), check_vma=False)
```

time: 147 us -> 93.6 us (0.64)
  waiting for transfers between devices: 101 us -> 29.2 us
  Pallas kernels: 0 us -> 46.8 us
  matrix products: 23.2 us -> 0 us
  starting transfers between devices: 0.04 us -> 16.2 us
  between operations: 14.2 us -> 1.01 us
  local copies, waits for them, and re-layouts: 5.13 us -> 0.01 us
  other arithmetic: 3.46 us -> 0 us
    all_gather x2 -> x0, waiting for transfers between devices: 101 us -> none  [the longest x1 53.9 us: per_device(): lax.all_gather(picked_v, 'tok', axis=1, tiled=True)]
    pallas_call x0 -> x9, Pallas kernels: none -> 46.8 us  [the longest x7 41.1 us: stage(): pl.pallas_call(functools.partial(stage_kernel, cfg), out_shape=out_shape,...]
    ppermute x0 -> x30, waiting for transfers between devices: none -> 29.2 us  [move(): return lax.ppermute(value, 'tok', steps)]
    dot_general x4 -> x0, matrix products: 23.2 us -> none  [the longest x2 12.8 us: rank_grams(): jnp.einsum('lkqr,lkqs->lqrs', per, per, preferred_element_type=jnp.float32)]
    ppermute x0 -> x30, starting transfers between devices: none -> 16.2 us  [move(): return lax.ppermute(value, 'tok', steps)]
    gather x4 -> x0, local copies, waits for them, and re-layouts: 2.31 us -> none  [pick_columns(): jnp.take(slots, block_ids[layer], axis=1).reshape(factor.shape[1], -1)]
    slice x2 -> x0, local copies, waits for them, and re-layouts: 2.14 us -> none  [pick_columns(): slots = factor[layer].reshape(factor.shape[1], -1, width)]
    another operation x2 -> x0, other arithmetic: 1.49 us -> none  [pick_columns(): return jnp.stack(chosen)]
  transfers between devices with their start and end apart: 2 -> 30, of which waited for: 2 -> 5; matrix products, arithmetic and copies ran while one was open for 5% -> 0% of each run, Pallas kernels for 0% -> 39%
where the time goes in v1:
time: 93.6 us; the launch traced here: 93.3 us
  Pallas kernels  46.8 us (50%)
  waiting for transfers between devices  29.2 us (31%)
  starting transfers between devices  16.2 us (17%)
  between operations  1.01 us (1%)
    pallas_call x7, Pallas kernels, stage(): pl.pallas_call(functools.partial(stage_kernel, cfg), out_shape=out_shape,...  41.1 us
    ppermute x30, waiting for transfers between devices, move(): return lax.ppermute(value, 'tok', steps)  29.2 us
    ppermute x30, starting transfers between devices, move(): return lax.ppermute(value, 'tok', steps)  16.2 us
    pallas_call x2, Pallas kernels, pick(): pl.pallas_call(functools.partial(pick_kernel, layer), out_shape=jax.Shape...  5.72 us
  transfers between devices with their start and end apart: 30, of which 5 were waited for; matrix products, arithmetic and copies ran while one was open for 0% of the time, Pallas kernels for 39%

profile of v1, /device:TPU:0, one launch (start us, length us, event | category | flops | bytes accessed | tf_op | source)
XLA Modules:
  0.0 93.3 jit_solution(4301354809239842168)
XLA Ops:
  0.0 2.9 %shard_map.65.refs_2_ = bf16[2,128,512]{2,1,0:T(8,128)(2,1)} custom-call(s32[2,16]{1,0:T(2,128)} %ids_ref.3, bf16[2,128,1024]{2,1,0:T(8,128)(2,1)} %u_ref.3, bf16[2,128,1024]{2,1,0:T(8,128)(2,1)} %v_ref.3), custom_call_target="tpu_custom_call" | custom-call | flops 268435456 | bytes 786432 | tf_op jit(solution)/shard_map/pallas_call | solution.py:78
  2.9 3.0 %collective-permute-start.7 = (bf16[2,128,512]{2,1,0:T(8,128)(2,1)}, bf16[2,128,512]{2,1,0:T(8,128)(2,1)S(1)}, u32[]{:S(2)}, u32[]{:S(2)}) collective-permute-start(bf16[2,128,512]{2,1,0:T(8,128)(2,1)} %shard_map.65.refs_2_), channel_id=1, source_target_pairs={{0,2},{1,3},{2,0},{3,1},{4,6},{5,7},{6,4},{7,5},{8,10},{9,11},{10,... | collective-permute-start | bytes 786440 | tf_op jit(solution)/shard_map/ppermute | solution.py:251
  5.9 1.6 %collective-permute-start.8 = (bf16[2,128,512]{2,1,0:T(8,128)(2,1)}, bf16[2,128,512]{2,1,0:T(8,128)(2,1)S(1)}, u32[]{:S(2)}, u32[]{:S(2)}) collective-permute-start(bf16[2,128,512]{2,1,0:T(8,128)(2,1)} %shard_map.65.refs_2_), channel_id=1, source_target_pairs={{0,4},{1,5},{2,6},{3,7},{4,8},{5,9},{6,10},{7,11},{8,12},{9,13},{1... | collective-permute-start | bytes 786440 | tf_op jit(solution)/shard_map/ppermute | solution.py:251
  7.5 0.0 collective-permute-start.27
  7.5 2.9 %shard_map.64.refs_2_ = bf16[2,128,512]{2,1,0:T(8,128)(2,1)} custom-call(s32[2,16]{1,0:T(2,128)} %ids_ref.3, bf16[2,128,1024]{2,1,0:T(8,128)(2,1)} %u_ref.3, bf16[2,128,1024]{2,1,0:T(8,128)(2,1)} %v_ref.3), custom_call_target="tpu_custom_call" | custom-call | flops 268435456 | bytes 786432 | tf_op jit(solution)/shard_map/pallas_call | solution.py:78
  10.4 1.6 %collective-permute-start = (bf16[2,128,512]{2,1,0:T(8,128)(2,1)}, bf16[2,128,512]{2,1,0:T(8,128)(2,1)S(1)}, u32[]{:S(2)}, u32[]{:S(2)}) collective-permute-start(bf16[2,128,512]{2,1,0:T(8,128)(2,1)} %shard_map.64.refs_2_), channel_id=1, source_target_pairs={{0,4},{1,5},{2,6},{3,7},{4,8},{5,9},{6,10},{7,11},{8,12},{9,13},{1... | collective-permute-start | bytes 786440 | tf_op jit(solution)/shard_map/ppermute | solution.py:251
  12.0 0.5 collective-permute-start.1
  12.5 0.0 collective-permute-start.19
  12.5 3.5 %collective-permute-done.8.refs_6_ = bf16[2,128,512]{2,1,0:T(8,128)(2,1)S(1)} collective-permute-done((bf16[2,128,512]{2,1,0:T(8,128)(2,1)}, bf16[2,128,512]{2,1,0:T(8,128)(2,1)S(1)}, u32[]{:S(2)}, u32[]{:S(2)}) %collective-permute-start.8) | collective-permute-done | bytes 262176 | tf_op jit(solution)/shard_map/ppermute | solution.py:251
  16.0 0.5 collective-permute-start.29
  16.5 4.8 %collective-permute-done.refs_6_ = bf16[2,128,512]{2,1,0:T(8,128)(2,1)S(1)} collective-permute-done((bf16[2,128,512]{2,1,0:T(8,128)(2,1)}, bf16[2,128,512]{2,1,0:T(8,128)(2,1)S(1)}, u32[]{:S(2)}, u32[]{:S(2)}) %collective-permute-start) | collective-permute-done | bytes 262176 | tf_op jit(solution)/shard_map/ppermute | solution.py:251
  21.4 0.0 collective-permute-start.9
  21.4 0.5 collective-permute-start.10
  21.9 0.0 collective-permute-done.19.refs_3_
  21.9 0.0 collective-permute-start.21
  21.9 0.0 collective-permute-done.28.refs_5_
  21.9 1.3 %collective-permute-start.2 = (bf16[2,128,512]{2,1,0:T(8,128)(2,1)S(1)}, bf16[2,128,512]{2,1,0:T(8,128)(2,1)S(1)}, u32[]{:S(2)}, u32[]{:S(2)}) collective-permute-start(bf16[2,128,512]{2,1,0:T(8,128)(2,1)S(1)} %collective-permute-done.refs_6_), channel_id=1, source_target_pairs={{0,4},{1,5},{2,6},{3,7},{4,8},{5,9},{6,10},{7,11},{8,12},{9,13},{1... | collective-permute-start | bytes 786440 | tf_op jit(solution)/shard_map/ppermute | solution.py:251
  23.3 0.0 collective-permute-done.29.refs_7_
  23.3 1.5 %collective-permute-start.3 = (bf16[2,128,512]{2,1,0:T(8,128)(2,1)S(1)}, bf16[2,128,512]{2,1,0:T(8,128)(2,1)S(1)}, u32[]{:S(2)}, u32[]{:S(2)}) collective-permute-start(bf16[2,128,512]{2,1,0:T(8,128)(2,1)S(1)} %collective-permute-done.refs_6_), channel_id=1, source_target_pairs={{0,2},{1,3},{2,0},{3,1},{4,6},{5,7},{6,4},{7,5},{8,10},{9,11},{10,... | collective-permute-start | bytes 786440 | tf_op jit(solution)/shard_map/ppermute | solution.py:251
  24.8 7.6 %collective-permute-done.9.refs_4_ = bf16[2,128,512]{2,1,0:T(8,128)(2,1)S(1)} collective-permute-done((bf16[2,128,512]{2,1,0:T(8,128)(2,1)S(1)}, bf16[2,128,512]{2,1,0:T(8,128)(2,1)S(1)}, u32[]{:S(2)}, u32[]{:S(2)}) %collective-permute-start.9) | collective-permute-done | bytes 262176 | tf_op jit(solution)/shard_map/ppermute | solution.py:251
  32.4 0.0 collective-permute-start.20
  32.4 0.0 collective-permute-done.10.refs_2_
  32.4 0.5 collective-permute-start.26
  32.9 0.0 collective-permute-done.21.refs_7_
  32.9 0.1 collective-permute-start.25
  33.0 3.9 %collective-permute-done.2.refs_4_ = bf16[2,128,512]{2,1,0:T(8,128)(2,1)S(1)} collective-permute-done((bf16[2,128,512]{2,1,0:T(8,128)(2,1)S(1)}, bf16[2,128,512]{2,1,0:T(8,128)(2,1)S(1)}, u32[]{:S(2)}, u32[]{:S(2)}) %collective-permute-start.2) | collective-permute-done | bytes 262176 | tf_op jit(solution)/shard_map/ppermute | solution.py:251
  36.9 0.5 collective-permute-start.22
  37.4 0.0 collective-permute-done.20.refs_5_
  37.4 0.0 collective-permute-start.18
  37.4 0.0 collective-permute-done.26.refs_5_
  37.4 0.5 collective-permute-start.17
  37.9 0.0 collective-permute-done.25.refs_3_
  38.6 9.2 %collective-permute-done.11.refs_4_ = bf16[2,128,512]{2,1,0:T(8,128)(2,1)S(1)} collective-permute-done((bf16[2,128,512]{2,1,0:T(8,128)(2,1)S(1)}, bf16[2,128,512]{2,1,0:T(8,128)(2,1)S(1)}, u32[]{:S(2)}, u32[]{:S(2)}) %collective-permute-start.11) | collective-permute-done | bytes 262176 | tf_op jit(solution)/shard_map/ppermute | solution.py:251
  47.9 0.5 collective-permute-start.14
  48.4 4.6 %shard_map.69 = (f32[640,512]{1,0:T(8,128)}, f32[640,512]{1,0:T(8,128)}, f32[4,256,256]{2,1,0:T(8,128)}) custom-call(bf16[2,640,2048]{2,1,0:T(8,128)(2,1)} %refs_0_.13, bf16[2,640,2048]{2,1,0:T(8,128)(2,1)} %refs_1_.13, bf16[2,128,512]{2,1,0:T(8,128)(2,1)S(1)} %copy-done.1, bf16[2,128,512]{2,1,0:T(8,128)(2,1)S(1)} %collective-permute-done.27.refs_3_, ...), custom_call_target="tpu_custom_call" | custom-call | flops 1811939328 | bytes 3538944 | tf_op jit(solution)/shard_map/pallas_call | solution.py:215
  53.0 0.9 collective-permute-start.12
  53.9 0.2 collective-permute-start.23
  54.2 1.2 %collective-permute-start.5 = (bf16[2,128,512]{2,1,0:T(8,128)(2,1)S(1)}, bf16[2,128,512]{2,1,0:T(8,128)(2,1)S(1)}, u32[]{:S(2)}, u32[]{:S(2)}) collective-permute-start(bf16[2,128,512]{2,1,0:T(8,128)(2,1)S(1)} %collective-permute-done.4.refs_4_), channel_id=1, source_target_pairs={{0,2},{1,3},{2,0},{3,1},{4,6},{5,7},{6,4},{7,5},{8,10},{9,11},{10,... | collective-permute-start | bytes 786440 | tf_op jit(solution)/shard_map/ppermute | solution.py:251
  55.3 4.6 %shard_map.66 = (f32[640,512]{1,0:T(8,128)}, f32[640,512]{1,0:T(8,128)}, f32[4,256,256]{2,1,0:T(8,128)}) custom-call(bf16[2,640,2048]{2,1,0:T(8,128)(2,1)} %refs_0_.13, bf16[2,640,2048]{2,1,0:T(8,128)(2,1)} %refs_1_.13, bf16[2,128,512]{2,1,0:T(8,128)(2,1)S(1)} %copy-done, bf16[2,128,512]{2,1,0:T(8,128)(2,1)S(1)} %collective-permute-done.19.refs_3_, ...), custom_call_target="tpu_custom_call" | custom-call | flops 1811939328 | bytes 3538944 | tf_op jit(solution)/shard_map/pallas_call | solution.py:215
  59.9 0.1 collective-permute-start.16
  60.0 0.5 collective-permute-start.15
  60.5 6.0 %shard_map.70 = (f32[640,512]{1,0:T(8,128)}, f32[640,512]{1,0:T(8,128)}, f32[4,256,256]{2,1,0:T(8,128)}) custom-call(bf16[2,640,2048]{2,1,0:T(8,128)(2,1)} %refs_0_.13, bf16[2,640,2048]{2,1,0:T(8,128)(2,1)} %refs_1_.13, bf16[2,128,512]{2,1,0:T(8,128)(2,1)S(1)} %collective-permute-done.10.refs_2_, ...), custom_call_target="tpu_custom_call", output_to_operand_aliasing={{0}: (6, {}), {1}: (7, {}), {2}: (8, {})} | custom-call | flops 1207959552 | bytes 2359296 | tf_op jit(solution)/shard_map/pallas_call | solution.py:215
  66.6 0.2 collective-permute-start.13
  66.7 0.4 collective-permute-start.6
  67.2 6.0 %shard_map.67 = (f32[640,512]{1,0:T(8,128)}, f32[640,512]{1,0:T(8,128)}, f32[4,256,256]{2,1,0:T(8,128)}) custom-call(bf16[2,640,2048]{2,1,0:T(8,128)(2,1)} %refs_0_.13, bf16[2,640,2048]{2,1,0:T(8,128)(2,1)} %refs_1_.13, bf16[2,128,512]{2,1,0:T(8,128)(2,1)S(1)} %collective-permute-done.3.refs_2_, ...), custom_call_target="tpu_custom_call", output_to_operand_aliasing={{0}: (6, {}), {1}: (7, {}), {2}: (8, {})} | custom-call | flops 1207959552 | bytes 2359296 | tf_op jit(solution)/shard_map/pallas_call | solution.py:215
  73.2 6.1 %shard_map.71 = (f32[640,512]{1,0:T(8,128)}, f32[640,512]{1,0:T(8,128)}, f32[4,256,256]{2,1,0:T(8,128)}) custom-call(bf16[2,640,2048]{2,1,0:T(8,128)(2,1)} %refs_0_.13, bf16[2,640,2048]{2,1,0:T(8,128)(2,1)} %refs_1_.13, bf16[2,128,512]{2,1,0:T(8,128)(2,1)S(1)} %collective-permute-done.22.refs_2_, ...), custom_call_target="tpu_custom_call", output_to_operand_aliasing={{0}: (6, {}), {1}: (7, {}), {2}: (8, {})} | custom-call | flops 1207959552 | bytes 2359296 | tf_op jit(solution)/shard_map/pallas_call | solution.py:215
  79.3 6.0 %shard_map.68 = (f32[640,512]{1,0:T(8,128)}, f32[640,512]{1,0:T(8,128)}, f32[4,256,256]{2,1,0:T(8,128)}) custom-call(bf16[2,640,2048]{2,1,0:T(8,128)(2,1)} %refs_0_.13, bf16[2,640,2048]{2,1,0:T(8,128)(2,1)} %refs_1_.13, bf16[2,128,512]{2,1,0:T(8,128)(2,1)S(1)} %collective-permute-done.14.refs_2_, ...), custom_call_target="tpu_custom_call", output_to_operand_aliasing={{0}: (6, {}), {1}: (7, {}), {2}: (8, {})} | custom-call | flops 1207959552 | bytes 2359296 | tf_op jit(solution)/shard_map/pallas_call | solution.py:215
  85.4 7.7 %shard_map.72 = f32[64,640]{1,0:T(8,128)} custom-call(bf16[2,640,2048]{2,1,0:T(8,128)(2,1)} %refs_0_.13, bf16[2,640,2048]{2,1,0:T(8,128)(2,1)} %refs_1_.13, s32[1]{0:T(128)S(6)} %copy.31.refs_2_, bf16[2,128,512]{2,1,0:T(8,128)(2,1)S(1)} %collective-permute-done.5.refs_3_, bf16[2,128,512]{2,1,0:T(8,128)(2,1)S(1)} %collective-permute-done.6.refs_4_, ...), custom_call_target="tpu_custom_call" | custom-call | flops 1207959552 | bytes 2359296 | tf_op jit(solution)/shard_map/pallas_call | solution.py:215
  (25 shorter events, 0.1 us)
Async XLA Ops:
  2.9 45.5 %copy-start.1 = (bf16[2,128,512]{2,1,0:T(8,128)(2,1)S(1)}, bf16[2,128,512]{2,1,0:T(8,128)(2,1)}, u32[]{:S(2)}) copy-start(bf16[2,128,512]{2,1,0:T(8,128)(2,1)} %shard_map.65.refs_2_) | copy-start | bytes 786436
  2.9 9.7 %collective-permute-start.7 = (bf16[2,128,512]{2,1,0:T(8,128)(2,1)}, bf16[2,128,512]{2,1,0:T(8,128)(2,1)S(1)}, u32[]{:S(2)}, u32[]{:S(2)}) collective-permute-start(bf16[2,128,512]{2,1,0:T(8,128)(2,1)} %shard_map.65.refs_2_), channel_id=1, source_target_pairs={{0,2},{1,3},{2,0},{3,1},{4,6},{5,7},{6,4},{7,5},{8,10},{9,11},{10,... | collective-permute-start | bytes 786440 | tf_op jit(solution)/shard_map/ppermute | solution.py:251
  5.9 10.1 %collective-permute-start.8 = (bf16[2,128,512]{2,1,0:T(8,128)(2,1)}, bf16[2,128,512]{2,1,0:T(8,128)(2,1)S(1)}, u32[]{:S(2)}, u32[]{:S(2)}) collective-permute-start(bf16[2,128,512]{2,1,0:T(8,128)(2,1)} %shard_map.65.refs_2_), channel_id=1, source_target_pairs={{0,4},{1,5},{2,6},{3,7},{4,8},{5,9},{6,10},{7,11},{8,12},{9,13},{1... | collective-permute-start | bytes 786440 | tf_op jit(solution)/shard_map/ppermute | solution.py:251
  7.5 8.6 %collective-permute-start.27 = (bf16[2,128,512]{2,1,0:T(8,128)(2,1)}, bf16[2,128,512]{2,1,0:T(8,128)(2,1)S(1)}, u32[]{:S(2)}, u32[]{:S(2)}) collective-permute-start(bf16[2,128,512]{2,1,0:T(8,128)(2,1)} %shard_map.65.refs_2_), channel_id=1, source_target_pairs={{0,1},{1,0},{2,3},{3,2},{4,5},{5,4},{6,7},{7,6},{8,9},{9,8},{10,11... | collective-permute-start | bytes 786440 | tf_op jit(solution)/shard_map/ppermute | solution.py:251
  10.4 11.0 %collective-permute-start = (bf16[2,128,512]{2,1,0:T(8,128)(2,1)}, bf16[2,128,512]{2,1,0:T(8,128)(2,1)S(1)}, u32[]{:S(2)}, u32[]{:S(2)}) collective-permute-start(bf16[2,128,512]{2,1,0:T(8,128)(2,1)} %shard_map.64.refs_2_), channel_id=1, source_target_pairs={{0,4},{1,5},{2,6},{3,7},{4,8},{5,9},{6,10},{7,11},{8,12},{9,13},{1... | collective-permute-start | bytes 786440 | tf_op jit(solution)/shard_map/ppermute | solution.py:251
  12.0 9.4 %collective-permute-start.1 = (bf16[2,128,512]{2,1,0:T(8,128)(2,1)}, bf16[2,128,512]{2,1,0:T(8,128)(2,1)S(1)}, u32[]{:S(2)}, u32[]{:S(2)}) collective-permute-start(bf16[2,128,512]{2,1,0:T(8,128)(2,1)} %shard_map.64.refs_2_), channel_id=1, source_target_pairs={{0,2},{1,3},{2,0},{3,1},{4,6},{5,7},{6,4},{7,5},{8,10},{9,11},{10,... | collective-permute-start | bytes 786440 | tf_op jit(solution)/shard_map/ppermute | solution.py:251
  12.5 9.4 %collective-permute-start.19 = (bf16[2,128,512]{2,1,0:T(8,128)(2,1)}, bf16[2,128,512]{2,1,0:T(8,128)(2,1)S(1)}, u32[]{:S(2)}, u32[]{:S(2)}) collective-permute-start(bf16[2,128,512]{2,1,0:T(8,128)(2,1)} %shard_map.64.refs_2_), channel_id=1, source_target_pairs={{0,1},{1,0},{2,3},{3,2},{4,5},{5,4},{6,7},{7,6},{8,9},{9,8},{10,11... | collective-permute-start | bytes 786440 | tf_op jit(solution)/shard_map/ppermute | solution.py:251
  16.0 5.9 %collective-permute-start.28 = (bf16[2,128,512]{2,1,0:T(8,128)(2,1)S(1)}, bf16[2,128,512]{2,1,0:T(8,128)(2,1)S(1)}, u32[]{:S(2)}, u32[]{:S(2)}) collective-permute-start(bf16[2,128,512]{2,1,0:T(8,128)(2,1)S(1)} %collective-permute-done.7.refs_4_), channel_id=1, source_target_pairs={{0,1},{1,0},{2,3},{3,2},{4,5},{5,4},{6,7},{7,6},{8,9},{9,8},{10,11... | collective-permute-start | bytes 786440 | tf_op jit(solution)/shard_map/ppermute | solution.py:251
  16.0 7.2 %collective-permute-start.29 = (bf16[2,128,512]{2,1,0:T(8,128)(2,1)S(1)}, bf16[2,128,512]{2,1,0:T(8,128)(2,1)S(1)}, u32[]{:S(2)}, u32[]{:S(2)}) collective-permute-start(bf16[2,128,512]{2,1,0:T(8,128)(2,1)S(1)} %collective-permute-done.8.refs_6_), channel_id=1, source_target_pairs={{0,1},{1,0},{2,3},{3,2},{4,5},{5,4},{6,7},{7,6},{8,9},{9,8},{10,11... | collective-permute-start | bytes 786440 | tf_op jit(solution)/shard_map/ppermute | solution.py:251
  21.4 11.0 %collective-permute-start.9 = (bf16[2,128,512]{2,1,0:T(8,128)(2,1)S(1)}, bf16[2,128,512]{2,1,0:T(8,128)(2,1)S(1)}, u32[]{:S(2)}, u32[]{:S(2)}) collective-permute-start(bf16[2,128,512]{2,1,0:T(8,128)(2,1)S(1)} %collective-permute-done.8.refs_6_), channel_id=1, source_target_pairs={{0,4},{1,5},{2,6},{3,7},{4,8},{5,9},{6,10},{7,11},{8,12},{9,13},{1... | collective-permute-start | bytes 786440 | tf_op jit(solution)/shard_map/ppermute | solution.py:251
  21.4 11.0 %collective-permute-start.10 = (bf16[2,128,512]{2,1,0:T(8,128)(2,1)S(1)}, bf16[2,128,512]{2,1,0:T(8,128)(2,1)S(1)}, u32[]{:S(2)}, u32[]{:S(2)}) collective-permute-start(bf16[2,128,512]{2,1,0:T(8,128)(2,1)S(1)} %collective-permute-done.8.refs_6_), channel_id=1, source_target_pairs={{0,2},{1,3},{2,0},{3,1},{4,6},{5,7},{6,4},{7,5},{8,10},{9,11},{10,... | collective-permute-start | bytes 786440 | tf_op jit(solution)/shard_map/ppermute | solution.py:251
  21.9 10.9 %collective-permute-start.21 = (bf16[2,128,512]{2,1,0:T(8,128)(2,1)S(1)}, bf16[2,128,512]{2,1,0:T(8,128)(2,1)S(1)}, u32[]{:S(2)}, u32[]{:S(2)}) collective-permute-start(bf16[2,128,512]{2,1,0:T(8,128)(2,1)S(1)} %collective-permute-done.refs_6_), channel_id=1, source_target_pairs={{0,1},{1,0},{2,3},{3,2},{4,5},{5,4},{6,7},{7,6},{8,9},{9,8},{10,11... | collective-permute-start | bytes 786440 | tf_op jit(solution)/shard_map/ppermute | solution.py:251
  21.9 14.9 %collective-permute-start.2 = (bf16[2,128,512]{2,1,0:T(8,128)(2,1)S(1)}, bf16[2,128,512]{2,1,0:T(8,128)(2,1)S(1)}, u32[]{:S(2)}, u32[]{:S(2)}) collective-permute-start(bf16[2,128,512]{2,1,0:T(8,128)(2,1)S(1)} %collective-permute-done.refs_6_), channel_id=1, source_target_pairs={{0,4},{1,5},{2,6},{3,7},{4,8},{5,9},{6,10},{7,11},{8,12},{9,13},{1... | collective-permute-start | bytes 786440 | tf_op jit(solution)/shard_map/ppermute | solution.py:251
  23.3 13.6 %collective-permute-start.3 = (bf16[2,128,512]{2,1,0:T(8,128)(2,1)S(1)}, bf16[2,128,512]{2,1,0:T(8,128)(2,1)S(1)}, u32[]{:S(2)}, u32[]{:S(2)}) collective-permute-start(bf16[2,128,512]{2,1,0:T(8,128)(2,1)S(1)} %collective-permute-done.refs_6_), channel_id=1, source_target_pairs={{0,2},{1,3},{2,0},{3,1},{4,6},{5,7},{6,4},{7,5},{8,10},{9,11},{10,... | collective-permute-start | bytes 786440 | tf_op jit(solution)/shard_map/ppermute | solution.py:251
  32.4 5.1 %collective-permute-start.20 = (bf16[2,128,512]{2,1,0:T(8,128)(2,1)S(1)}, bf16[2,128,512]{2,1,0:T(8,128)(2,1)S(1)}, u32[]{:S(2)}, u32[]{:S(2)}) collective-permute-start(bf16[2,128,512]{2,1,0:T(8,128)(2,1)S(1)} %collective-permute-done.1.refs_4_), channel_id=1, source_target_pairs={{0,1},{1,0},{2,3},{3,2},{4,5},{5,4},{6,7},{7,6},{8,9},{9,8},{10,11... | collective-permute-start | bytes 786440 | tf_op jit(solution)/shard_map/ppermute | solution.py:251
  32.4 5.1 %collective-permute-start.26 = (bf16[2,128,512]{2,1,0:T(8,128)(2,1)S(1)}, bf16[2,128,512]{2,1,0:T(8,128)(2,1)S(1)}, u32[]{:S(2)}, u32[]{:S(2)}) collective-permute-start(bf16[2,128,512]{2,1,0:T(8,128)(2,1)S(1)} %collective-permute-done.9.refs_4_), channel_id=1, source_target_pairs={{0,1},{1,0},{2,3},{3,2},{4,5},{5,4},{6,7},{7,6},{8,9},{9,8},{10,11... | collective-permute-start | bytes 786440 | tf_op jit(solution)/shard_map/ppermute | solution.py:251
  32.9 5.1 %collective-permute-start.25 = (bf16[2,128,512]{2,1,0:T(8,128)(2,1)S(1)}, bf16[2,128,512]{2,1,0:T(8,128)(2,1)S(1)}, u32[]{:S(2)}, u32[]{:S(2)}) collective-permute-start(bf16[2,128,512]{2,1,0:T(8,128)(2,1)S(1)} %collective-permute-done.10.refs_2_), channel_id=1, source_target_pairs={{0,1},{1,0},{2,3},{3,2},{4,5},{5,4},{6,7},{7,6},{8,9},{9,8},{10,11... | collective-permute-start | bytes 786440 | tf_op jit(solution)/shard_map/ppermute | solution.py:251
  36.9 11.0 %collective-permute-start.11 = (bf16[2,128,512]{2,1,0:T(8,128)(2,1)S(1)}, bf16[2,128,512]{2,1,0:T(8,128)(2,1)S(1)}, u32[]{:S(2)}, u32[]{:S(2)}) collective-permute-start(bf16[2,128,512]{2,1,0:T(8,128)(2,1)S(1)} %collective-permute-done.9.refs_4_), channel_id=1, source_target_pairs={{0,4},{1,5},{2,6},{3,7},{4,8},{5,9},{6,10},{7,11},{8,12},{9,13},{1... | collective-permute-start | bytes 786440 | tf_op jit(solution)/shard_map/ppermute | solution.py:251
  36.9 11.5 %collective-permute-start.22 = (bf16[2,128,512]{2,1,0:T(8,128)(2,1)S(1)}, bf16[2,128,512]{2,1,0:T(8,128)(2,1)S(1)}, u32[]{:S(2)}, u32[]{:S(2)}) collective-permute-start(bf16[2,128,512]{2,1,0:T(8,128)(2,1)S(1)} %collective-permute-done.9.refs_4_), channel_id=1, source_target_pairs={{0,2},{1,3},{2,0},{3,1},{4,6},{5,7},{6,4},{7,5},{8,10},{9,11},{10,... | collective-permute-start | bytes 786440 | tf_op jit(solution)/shard_map/ppermute | solution.py:251
  37.4 15.6 %collective-permute-start.18 = (bf16[2,128,512]{2,1,0:T(8,128)(2,1)S(1)}, bf16[2,128,512]{2,1,0:T(8,128)(2,1)S(1)}, u32[]{:S(2)}, u32[]{:S(2)}) collective-permute-start(bf16[2,128,512]{2,1,0:T(8,128)(2,1)S(1)} %collective-permute-done.2.refs_4_), channel_id=1, source_target_pairs={{0,1},{1,0},{2,3},{3,2},{4,5},{5,4},{6,7},{7,6},{8,9},{9,8},{10,11... | collective-permute-start | bytes 786440 | tf_op jit(solution)/shard_map/ppermute | solution.py:251
  37.4 16.5 %collective-permute-start.17 = (bf16[2,128,512]{2,1,0:T(8,128)(2,1)S(1)}, bf16[2,128,512]{2,1,0:T(8,128)(2,1)S(1)}, u32[]{:S(2)}, u32[]{:S(2)}) collective-permute-start(bf16[2,128,512]{2,1,0:T(8,128)(2,1)S(1)} %collective-permute-done.3.refs_2_), channel_id=1, source_target_pairs={{0,1},{1,0},{2,3},{3,2},{4,5},{5,4},{6,7},{7,6},{8,9},{9,8},{10,11... | collective-permute-start | bytes 786440 | tf_op jit(solution)/shard_map/ppermute | solution.py:251
  37.9 16.2 %collective-permute-start.4 = (bf16[2,128,512]{2,1,0:T(8,128)(2,1)S(1)}, bf16[2,128,512]{2,1,0:T(8,128)(2,1)S(1)}, u32[]{:S(2)}, u32[]{:S(2)}) collective-permute-start(bf16[2,128,512]{2,1,0:T(8,128)(2,1)S(1)} %collective-permute-done.2.refs_4_), channel_id=1, source_target_pairs={{0,4},{1,5},{2,6},{3,7},{4,8},{5,9},{6,10},{7,11},{8,12},{9,13},{1... | collective-permute-start | bytes 786440 | tf_op jit(solution)/shard_map/ppermute | solution.py:251
  38.6 16.7 %copy-start = (bf16[2,128,512]{2,1,0:T(8,128)(2,1)S(1)}, bf16[2,128,512]{2,1,0:T(8,128)(2,1)}, u32[]{:S(2)}) copy-start(bf16[2,128,512]{2,1,0:T(8,128)(2,1)} %shard_map.64.refs_2_) | copy-start | bytes 786436
  47.9 12.1 %collective-permute-start.14 = (bf16[2,128,512]{2,1,0:T(8,128)(2,1)S(1)}, bf16[2,128,512]{2,1,0:T(8,128)(2,1)S(1)}, u32[]{:S(2)}, u32[]{:S(2)}) collective-permute-start(bf16[2,128,512]{2,1,0:T(8,128)(2,1)S(1)} %collective-permute-done.2.refs_4_), channel_id=1, source_target_pairs={{0,2},{1,3},{2,0},{3,1},{4,6},{5,7},{6,4},{7,5},{8,10},{9,11},{10,... | collective-permute-start | bytes 786440 | tf_op jit(solution)/shard_map/ppermute | solution.py:251
  48.4 11.6 %collective-permute-start.24 = (bf16[2,128,512]{2,1,0:T(8,128)(2,1)S(1)}, bf16[2,128,512]{2,1,0:T(8,128)(2,1)S(1)}, u32[]{:S(2)}, u32[]{:S(2)}) collective-permute-start(bf16[2,128,512]{2,1,0:T(8,128)(2,1)S(1)} %collective-permute-done.11.refs_4_), channel_id=1, source_target_pairs={{0,1},{1,0},{2,3},{3,2},{4,5},{5,4},{6,7},{7,6},{8,9},{9,8},{10,11... | collective-permute-start | bytes 786440 | tf_op jit(solution)/shard_map/ppermute | solution.py:251
  53.0 13.5 %collective-permute-start.12 = (bf16[2,128,512]{2,1,0:T(8,128)(2,1)S(1)}, bf16[2,128,512]{2,1,0:T(8,128)(2,1)S(1)}, u32[]{:S(2)}, u32[]{:S(2)}) collective-permute-start(bf16[2,128,512]{2,1,0:T(8,128)(2,1)S(1)} %collective-permute-done.7.refs_4_), channel_id=1, source_target_pairs={{0,12},{1,13},{2,14},{3,15},{4,0},{5,1},{6,2},{7,3},{8,4},{9,5},{1... | collective-permute-start | bytes 786440 | tf_op jit(solution)/shard_map/ppermute | solution.py:251
  53.9 19.3 %collective-permute-start.23 = (bf16[2,128,512]{2,1,0:T(8,128)(2,1)S(1)}, bf16[2,128,512]{2,1,0:T(8,128)(2,1)S(1)}, u32[]{:S(2)}, u32[]{:S(2)}) collective-permute-start(bf16[2,128,512]{2,1,0:T(8,128)(2,1)S(1)} %collective-permute-done.22.refs_2_), channel_id=1, source_target_pairs={{0,1},{1,0},{2,3},{3,2},{4,5},{5,4},{6,7},{7,6},{8,9},{9,8},{10,11... | collective-permute-start | bytes 786440 | tf_op jit(solution)/shard_map/ppermute | solution.py:251
  54.2 12.6 %collective-permute-start.5 = (bf16[2,128,512]{2,1,0:T(8,128)(2,1)S(1)}, bf16[2,128,512]{2,1,0:T(8,128)(2,1)S(1)}, u32[]{:S(2)}, u32[]{:S(2)}) collective-permute-start(bf16[2,128,512]{2,1,0:T(8,128)(2,1)S(1)} %collective-permute-done.4.refs_4_), channel_id=1, source_target_pairs={{0,2},{1,3},{2,0},{3,1},{4,6},{5,7},{6,4},{7,5},{8,10},{9,11},{10,... | collective-permute-start | bytes 786440 | tf_op jit(solution)/shard_map/ppermute | solution.py:251
  59.9 19.3 %collective-permute-start.16 = (bf16[2,128,512]{2,1,0:T(8,128)(2,1)S(1)}, bf16[2,128,512]{2,1,0:T(8,128)(2,1)S(1)}, u32[]{:S(2)}, u32[]{:S(2)}) collective-permute-start(bf16[2,128,512]{2,1,0:T(8,128)(2,1)S(1)} %collective-permute-done.4.refs_4_), channel_id=1, source_target_pairs={{0,1},{1,0},{2,3},{3,2},{4,5},{5,4},{6,7},{7,6},{8,9},{9,8},{10,11... | collective-permute-start | bytes 786440 | tf_op jit(solution)/shard_map/ppermute | solution.py:251
  60.0 19.3 %collective-permute-start.15 = (bf16[2,128,512]{2,1,0:T(8,128)(2,1)S(1)}, bf16[2,128,512]{2,1,0:T(8,128)(2,1)S(1)}, u32[]{:S(2)}, u32[]{:S(2)}) collective-permute-start(bf16[2,128,512]{2,1,0:T(8,128)(2,1)S(1)} %collective-permute-done.14.refs_2_), channel_id=1, source_target_pairs={{0,1},{1,0},{2,3},{3,2},{4,5},{5,4},{6,7},{7,6},{8,9},{9,8},{10,11... | collective-permute-start | bytes 786440 | tf_op jit(solution)/shard_map/ppermute | solution.py:251
  66.6 18.8 %collective-permute-start.13 = (bf16[2,128,512]{2,1,0:T(8,128)(2,1)S(1)}, bf16[2,128,512]{2,1,0:T(8,128)(2,1)S(1)}, u32[]{:S(2)}, u32[]{:S(2)}) collective-permute-start(bf16[2,128,512]{2,1,0:T(8,128)(2,1)S(1)} %collective-permute-done.12.refs_5_), channel_id=1, source_target_pairs={{0,1},{1,0},{2,3},{3,2},{4,5},{5,4},{6,7},{7,6},{8,9},{9,8},{10,11... | collective-permute-start | bytes 786440 | tf_op jit(solution)/shard_map/ppermute | solution.py:251
  66.7 18.6 %collective-permute-start.6 = (bf16[2,128,512]{2,1,0:T(8,128)(2,1)S(1)}, bf16[2,128,512]{2,1,0:T(8,128)(2,1)S(1)}, u32[]{:S(2)}, u32[]{:S(2)}) collective-permute-start(bf16[2,128,512]{2,1,0:T(8,128)(2,1)S(1)} %collective-permute-done.5.refs_3_), channel_id=1, source_target_pairs={{0,1},{1,0},{2,3},{3,2},{4,5},{5,4},{6,7},{7,6},{8,9},{9,8},{10,11... | collective-permute-start | bytes 786440 | tf_op jit(solution)/shard_map/ppermute | solution.py:251

commit v2 on v1

--- a/solution.py
+++ b/solution.py
@@ -60,10 +60,8 @@
         named = jnp.where(lane // width == block, ids_ref[layer, block], named)
     row = lax.broadcasted_iota(jnp.int32, (width, columns), 0)
     col = lax.broadcasted_iota(jnp.int32, (width, columns), 1) % width
-    one = jnp.where(row == col, 1.0, 0.0).astype(jnp.bfloat16)
-    chooser = [
-        one * jnp.where(named == stored, 1.0, 0.0).astype(jnp.bfloat16) for stored in range(bank // width)
-    ]
+    aim = jnp.where(row == col, named, -1)
+    chooser = [jnp.where(aim == stored, 1.0, 0.0).astype(jnp.bfloat16) for stored in range(bank // width)]
     chooser = jnp.concatenate(chooser, axis=0)
     for copy in copies:
         copy.wait()
@@ -87,6 +85,28 @@
     )(block_ids, query_u, query_v)
 
 
+def load_kernel(*refs):
+    half = len(refs) // 2
+    sems = refs[-1]
+    copies = [pltpu.make_async_copy(refs[i], refs[half + i], sems.at[i]) for i in range(half)]
+    for copy in copies:
+        copy.start()
+    for copy in copies:
+        copy.wait()
+
+
+def load(*arrays):
+    return pl.pallas_call(
+        load_kernel,
+        out_shape=tuple(jax.ShapeDtypeStruct(one.shape, one.dtype) for one in arrays),
+        in_specs=[pl.BlockSpec(memory_space=pltpu.HBM)] * len(arrays),
+        out_specs=(pl.BlockSpec(memory_space=pltpu.VMEM),) * len(arrays),
+        scratch_shapes=[pltpu.SemaphoreType.DMA((len(arrays),))],
+        compiler_params=pltpu.CompilerParams(vmem_limit_bytes=51 << 20),
+        name="load",
+    )(*arrays)
+
+
 def split_dot(left, right):
     total = None
     rest = left
@@ -117,7 +137,7 @@
     starts = [take(3) if g["carry"] else None for g in groups]
     outs = take(1) if last else None
     totals = [take(3) for _ in groups]
-    x, w, sems = take(3)
+    w, sems = take(2)
     me = lax.axis_index("tok")
     a, b, c = me // (2 * inner), (me // 2) % inner, me % 2
     copies, slot = [], 0
@@ -129,23 +149,22 @@
             for dc, array in enumerate(pair):
                 spot = pl.multiple_of(slot * 2 * rows + ((c + dc) % 2) * rows, LANES)
                 these.append((array, w.at[:, pl.ds(spot, rows), :]))
-            for s, x_ref in enumerate(x_refs):
-                these.append((x_ref.at[g["layer"], :, pl.ds(start, 2 * rows)], x.at[slot, s]))
-            these = [pltpu.make_async_copy(*ends, sems.at[4 * slot + i]) for i, ends in enumerate(these)]
+            these = [pltpu.make_async_copy(*ends, sems.at[2 * slot + i]) for i, ends in enumerate(these)]
             for copy in these:
                 copy.start()
-            copies.append(these)
+            copies.append((these, pl.ds(start, 2 * rows)))
             slot += 1
     tiles = w.shape[2] // TILE
     slot = 0
     for g, start, total in zip(groups, starts, totals):
         for first in range(len(g["where"])):
-            for copy in copies[slot]:
+            for copy in copies[slot][0]:
                 copy.wait()
             span = slice(slot * 2 * rows, (slot + 1) * 2 * rows)
             came = start if first == 0 else total
             for s in range(2):
-                part = jnp.dot(x[slot, s], w[s, span, :], preferred_element_type=jnp.float32)
+                x = x_refs[s][g["layer"], :, copies[slot][1]]
+                part = jnp.dot(x, w[s, span, :], preferred_element_type=jnp.float32)
                 total[s][...] = part if came is None else came[s][...] + part
             for s in range(2):
                 for t in range(tiles):
@@ -181,7 +200,7 @@
     tiles = 2 * (columns // TILE)
     anywhere = pl.BlockSpec(memory_space=pltpu.HBM)
     vmem = pl.BlockSpec(memory_space=pltpu.VMEM)
-    args, specs = [gradients, activations], [anywhere, anywhere]
+    args, specs = [gradients, activations], [vmem, vmem]
     if last:
         args.append(counts)
         specs.append(pl.BlockSpec(memory_space=pltpu.SMEM))
@@ -219,12 +238,11 @@
         out_specs=out_specs,
         scratch_shapes=scratch
         + [
-            pltpu.VMEM((slots, 2, tokens, 2 * rows), jnp.bfloat16),
             pltpu.VMEM((2, slots * 2 * rows, columns), jnp.bfloat16),
-            pltpu.SemaphoreType.DMA((4 * slots,)),
+            pltpu.SemaphoreType.DMA((2 * slots,)),
         ],
         input_output_aliases=aliases,
-        compiler_params=pltpu.CompilerParams(vmem_limit_bytes=52 << 20),
+        compiler_params=pltpu.CompilerParams(vmem_limit_bytes=(24 if last else 16) << 20),
         cost_estimate=pl.CostEstimate(
             flops=flops, bytes_accessed=8 * slots * rows * (tokens + columns), transcendentals=0
         ),
@@ -270,6 +288,8 @@
         for key, piece in have[layer].items():
             pairs[layer][key] = [piece, move(piece, 0, 0, 1)]
 
+    gradients, activations = load(gradients, activations)
+
     def group(layer, keys, carry):
         return dict(layer=layer, where=keys, arrays=[pairs[layer][key] for key in keys], carry=carry)
 

time: 93.6 us -> 79.5 us (0.85)
  Pallas kernels: 46.8 us -> 28.1 us
  local copies, waits for them, and re-layouts: 0.01 us -> 7.19 us
  waiting for transfers between devices: 29.2 us -> 24.7 us
  starting transfers between devices: 16.2 us -> 18.1 us
    pallas_call x7, Pallas kernels: 41.1 us -> 14.4 us  [stage(): pl.pallas_call(functools.partial(stage_kernel, cfg), out_shape=out_shape,...]
    pallas_call x0 -> x1, Pallas kernels: none -> 8.11 us  [load(): pl.pallas_call(load_kernel, out_shape=tuple((jax.ShapeDtypeStruct(one.sha...]
    unnamed x4 -> x16, local copies, waits for them, and re-layouts: 0.01 us -> 7.19 us
    ppermute x30, waiting for transfers between devices: 29.2 us -> 24.7 us  [move(): return lax.ppermute(value, 'tok', steps)]
    ppermute x30, starting transfers between devices: 16.2 us -> 18.1 us  [move(): return lax.ppermute(value, 'tok', steps)]
  transfers between devices with their start and end apart: 30 -> 30, of which waited for: 5 -> 7; matrix products, arithmetic and copies ran while one was open for 0% -> 0% of each run, Pallas kernels for 39% -> 27%
where the time goes in v2:
time: 79.5 us; the launch traced here: 79.2 us
  Pallas kernels  28.1 us (35%)
  waiting for transfers between devices  24.7 us (31%)
  starting transfers between devices  18.1 us (23%)
  local copies, waits for them, and re-layouts  7.19 us (9%)
  between operations  1.05 us (1%)
    ppermute x30, waiting for transfers between devices, move(): return lax.ppermute(value, 'tok', steps)  24.7 us
    ppermute x30, starting transfers between devices, move(): return lax.ppermute(value, 'tok', steps)  18.1 us
    pallas_call x7, Pallas kernels, stage(): pl.pallas_call(functools.partial(stage_kernel, cfg), out_shape=out_shape,...  14.4 us
    pallas_call x1, Pallas kernels, load(): pl.pallas_call(load_kernel, out_shape=tuple((jax.ShapeDtypeStruct(one.sha...  8.11 us
    unnamed x16, local copies, waits for them, and re-layouts  7.19 us
    pallas_call x2, Pallas kernels, pick(): pl.pallas_call(functools.partial(pick_kernel, layer), out_shape=jax.Shape...  5.68 us
  transfers between devices with their start and end apart: 30, of which 7 were waited for; matrix products, arithmetic and copies ran while one was open for 0% of the time, Pallas kernels for 27%

profile of v2, /device:TPU:0, one launch (start us, length us, event | category | flops | bytes accessed | tf_op | source)
XLA Modules:
  0.0 79.2 jit_solution(11350431072625841885)
XLA Ops:
  0.0 2.8 %shard_map.65.refs_2_ = bf16[2,128,512]{2,1,0:T(8,128)(2,1)} custom-call(s32[2,16]{1,0:T(2,128)} %ids_ref.3, bf16[2,128,1024]{2,1,0:T(8,128)(2,1)} %u_ref.3, bf16[2,128,1024]{2,1,0:T(8,128)(2,1)} %v_ref.3), custom_call_target="tpu_custom_call" | custom-call | flops 268435456 | bytes 786432 | tf_op jit(solution)/shard_map/pallas_call | solution.py:76
  2.8 3.0 %collective-permute-start.7 = (bf16[2,128,512]{2,1,0:T(8,128)(2,1)}, bf16[2,128,512]{2,1,0:T(8,128)(2,1)S(1)}, u32[]{:S(2)}, u32[]{:S(2)}) collective-permute-start(bf16[2,128,512]{2,1,0:T(8,128)(2,1)} %shard_map.65.refs_2_), channel_id=1, source_target_pairs={{0,2},{1,3},{2,0},{3,1},{4,6},{5,7},{6,4},{7,5},{8,10},{9,11},{10,... | collective-permute-start | bytes 786440 | tf_op jit(solution)/shard_map/ppermute | solution.py:269
  5.9 1.6 %collective-permute-start.8 = (bf16[2,128,512]{2,1,0:T(8,128)(2,1)}, bf16[2,128,512]{2,1,0:T(8,128)(2,1)S(1)}, u32[]{:S(2)}, u32[]{:S(2)}) collective-permute-start(bf16[2,128,512]{2,1,0:T(8,128)(2,1)} %shard_map.65.refs_2_), channel_id=1, source_target_pairs={{0,4},{1,5},{2,6},{3,7},{4,8},{5,9},{6,10},{7,11},{8,12},{9,13},{1... | collective-permute-start | bytes 786440 | tf_op jit(solution)/shard_map/ppermute | solution.py:269
  7.5 2.8 %shard_map.64.refs_2_ = bf16[2,128,512]{2,1,0:T(8,128)(2,1)} custom-call(s32[2,16]{1,0:T(2,128)} %ids_ref.3, bf16[2,128,1024]{2,1,0:T(8,128)(2,1)} %u_ref.3, bf16[2,128,1024]{2,1,0:T(8,128)(2,1)} %v_ref.3), custom_call_target="tpu_custom_call" | custom-call | flops 268435456 | bytes 786432 | tf_op jit(solution)/shard_map/pallas_call | solution.py:76
  10.3 1.6 %collective-permute-start = (bf16[2,128,512]{2,1,0:T(8,128)(2,1)}, bf16[2,128,512]{2,1,0:T(8,128)(2,1)S(1)}, u32[]{:S(2)}, u32[]{:S(2)}) collective-permute-start(bf16[2,128,512]{2,1,0:T(8,128)(2,1)} %shard_map.64.refs_2_), channel_id=1, source_target_pairs={{0,4},{1,5},{2,6},{3,7},{4,8},{5,9},{6,10},{7,11},{8,12},{9,13},{1... | collective-permute-start | bytes 786440 | tf_op jit(solution)/shard_map/ppermute | solution.py:269
  11.9 0.5 collective-permute-start.1
  12.5 3.5 %collective-permute-done.8.refs_6_ = bf16[2,128,512]{2,1,0:T(8,128)(2,1)S(1)} collective-permute-done((bf16[2,128,512]{2,1,0:T(8,128)(2,1)}, bf16[2,128,512]{2,1,0:T(8,128)(2,1)S(1)}, u32[]{:S(2)}, u32[]{:S(2)}) %collective-permute-start.8) | collective-permute-done | bytes 262176 | tf_op jit(solution)/shard_map/ppermute | solution.py:269
  16.0 0.5 collective-permute-start.29
  16.5 4.8 %collective-permute-done.refs_6_ = bf16[2,128,512]{2,1,0:T(8,128)(2,1)S(1)} collective-permute-done((bf16[2,128,512]{2,1,0:T(8,128)(2,1)}, bf16[2,128,512]{2,1,0:T(8,128)(2,1)S(1)}, u32[]{:S(2)}, u32[]{:S(2)}) %collective-permute-start) | collective-permute-done | bytes 262176 | tf_op jit(solution)/shard_map/ppermute | solution.py:269
  21.4 0.5 collective-permute-start.10
  21.9 0.0 collective-permute-done.19.refs_3_
  21.9 0.0 collective-permute-start.21
  21.9 1.3 %collective-permute-start.2 = (bf16[2,128,512]{2,1,0:T(8,128)(2,1)S(1)}, bf16[2,128,512]{2,1,0:T(8,128)(2,1)S(1)}, u32[]{:S(2)}, u32[]{:S(2)}) collective-permute-start(bf16[2,128,512]{2,1,0:T(8,128)(2,1)S(1)} %collective-permute-done.refs_6_), channel_id=1, source_target_pairs={{0,4},{1,5},{2,6},{3,7},{4,8},{5,9},{6,10},{7,11},{8,12},{9,13},{1... | collective-permute-start | bytes 786440 | tf_op jit(solution)/shard_map/ppermute | solution.py:269
  23.2 1.5 %collective-permute-start.3 = (bf16[2,128,512]{2,1,0:T(8,128)(2,1)S(1)}, bf16[2,128,512]{2,1,0:T(8,128)(2,1)S(1)}, u32[]{:S(2)}, u32[]{:S(2)}) collective-permute-start(bf16[2,128,512]{2,1,0:T(8,128)(2,1)S(1)} %collective-permute-done.refs_6_), channel_id=1, source_target_pairs={{0,2},{1,3},{2,0},{3,1},{4,6},{5,7},{6,4},{7,5},{8,10},{9,11},{10,... | collective-permute-start | bytes 786440 | tf_op jit(solution)/shard_map/ppermute | solution.py:269
  24.7 7.6 %collective-permute-done.9.refs_4_ = bf16[2,128,512]{2,1,0:T(8,128)(2,1)S(1)} collective-permute-done((bf16[2,128,512]{2,1,0:T(8,128)(2,1)S(1)}, bf16[2,128,512]{2,1,0:T(8,128)(2,1)S(1)}, u32[]{:S(2)}, u32[]{:S(2)}) %collective-permute-start.9) | collective-permute-done | bytes 262176 | tf_op jit(solution)/shard_map/ppermute | solution.py:269
  32.3 0.5 collective-permute-start.26
  32.9 0.1 collective-permute-start.25
  32.9 3.9 %collective-permute-done.2.refs_4_ = bf16[2,128,512]{2,1,0:T(8,128)(2,1)S(1)} collective-permute-done((bf16[2,128,512]{2,1,0:T(8,128)(2,1)S(1)}, bf16[2,128,512]{2,1,0:T(8,128)(2,1)S(1)}, u32[]{:S(2)}, u32[]{:S(2)}) %collective-permute-start.2) | collective-permute-done | bytes 262176 | tf_op jit(solution)/shard_map/ppermute | solution.py:269
  36.8 0.0 collective-permute-start.11
  36.8 0.0 collective-permute-done.3.refs_2_
  36.8 0.5 collective-permute-start.22
  37.4 0.0 collective-permute-done.26.refs_5_
  37.4 0.5 collective-permute-start.17
  38.6 8.1 %load.1 = (bf16[2,640,2048]{2,1,0:T(8,128)(2,1)}, bf16[2,640,2048]{2,1,0:T(8,128)(2,1)}) custom-call(bf16[2,640,2048]{2,1,0:T(8,128)(2,1)} %refs_0_.1, bf16[2,640,2048]{2,1,0:T(8,128)(2,1)} %refs_1_.1), custom_call_target="tpu_custom_call" | custom-call | tf_op jit(solution)/shard_map/load/pallas_call | solution.py:99
  46.7 1.1 %collective-permute-done.11.refs_4_ = bf16[2,128,512]{2,1,0:T(8,128)(2,1)S(1)} collective-permute-done((bf16[2,128,512]{2,1,0:T(8,128)(2,1)S(1)}, bf16[2,128,512]{2,1,0:T(8,128)(2,1)S(1)}, u32[]{:S(2)}, u32[]{:S(2)}) %collective-permute-start.11) | collective-permute-done | bytes 262176 | tf_op jit(solution)/shard_map/ppermute | solution.py:269
  47.8 0.5 collective-permute-start.14
  48.4 2.5 %copy-done = bf16[2,640,2048]{2,1,0:T(8,128)(2,1)S(1)} copy-done((bf16[2,640,2048]{2,1,0:T(8,128)(2,1)S(1)}, bf16[2,640,2048]{2,1,0:T(8,128)(2,1)}, u32[]{:S(2)}) %copy-start) | copy-done | bytes 5242904
  50.8 2.5 %copy-done.1 = bf16[2,640,2048]{2,1,0:T(8,128)(2,1)S(1)} copy-done((bf16[2,640,2048]{2,1,0:T(8,128)(2,1)S(1)}, bf16[2,640,2048]{2,1,0:T(8,128)(2,1)}, u32[]{:S(2)}) %copy-start.1) | copy-done | bytes 5242904
  53.3 2.0 %shard_map.69 = (f32[640,512]{1,0:T(8,128)S(1)}, f32[640,512]{1,0:T(8,128)S(1)}, f32[4,256,256]{2,1,0:T(8,128)S(1)}) custom-call(bf16[2,640,2048]{2,1,0:T(8,128)(2,1)S(1)} %copy-done, bf16[2,640,2048]{2,1,0:T(8,128)(2,1)S(1)} %copy-done.1, bf16[2,128,512]{2,1,0:T(8,128)(2,1)S(1)} %copy-done.3, bf16[2,128,512]{2,1,0:T(8,128)(2,1)S(1)} %collective-permute-done.27.refs_3_, ...), custom_call_target="tpu_custom_call" | custom-call | flops 1811939328 | bytes 3538944 | tf_op jit(solution)/shard_map/pallas_call | solution.py:234
  55.4 4.0 %collective-permute-start.12 = (bf16[2,128,512]{2,1,0:T(8,128)(2,1)S(1)}, bf16[2,128,512]{2,1,0:T(8,128)(2,1)S(1)}, u32[]{:S(2)}, u32[]{:S(2)}) collective-permute-start(bf16[2,128,512]{2,1,0:T(8,128)(2,1)S(1)} %collective-permute-done.7.refs_4_), channel_id=1, source_target_pairs={{0,12},{1,13},{2,14},{3,15},{4,0},{5,1},{6,2},{7,3},{8,4},{9,5},{1... | collective-permute-start | bytes 786440 | tf_op jit(solution)/shard_map/ppermute | solution.py:269
  59.3 0.2 collective-permute-start.23
  59.5 0.0 collective-permute-done.4.refs_4_
  59.5 0.6 collective-permute-start.5
  60.1 2.0 %shard_map.66 = (f32[640,512]{1,0:T(8,128)S(1)}, f32[640,512]{1,0:T(8,128)S(1)}, f32[4,256,256]{2,1,0:T(8,128)S(1)}) custom-call(bf16[2,640,2048]{2,1,0:T(8,128)(2,1)S(1)} %copy-done, bf16[2,640,2048]{2,1,0:T(8,128)(2,1)S(1)} %copy-done.1, bf16[2,128,512]{2,1,0:T(8,128)(2,1)S(1)} %copy-done.2, bf16[2,128,512]{2,1,0:T(8,128)(2,1)S(1)} %collective-permute-done.19.refs_3_, ...), custom_call_target="tpu_custom_call" | custom-call | flops 1811939328 | bytes 3538944 | tf_op jit(solution)/shard_map/pallas_call | solution.py:234
  62.1 0.1 collective-permute-start.16
  62.2 0.5 collective-permute-start.15
  62.7 1.7 %shard_map.70 = (f32[640,512]{1,0:T(8,128)S(1)}, f32[640,512]{1,0:T(8,128)S(1)}, f32[4,256,256]{2,1,0:T(8,128)S(1)}) custom-call(bf16[2,640,2048]{2,1,0:T(8,128)(2,1)S(1)} %copy-done, bf16[2,640,2048]{2,1,0:T(8,128)(2,1)S(1)} %copy-done.1, ...), custom_call_target="tpu_custom_call", output_to_operand_aliasing={{0}: (6, {}), {1}: (7, {}), {2}: (8, {})} | custom-call | flops 1207959552 | bytes 2359296 | tf_op jit(solution)/shard_map/pallas_call | solution.py:234
  64.4 1.2 %collective-permute-done.12.refs_5_ = bf16[2,128,512]{2,1,0:T(8,128)(2,1)S(1)} collective-permute-done((bf16[2,128,512]{2,1,0:T(8,128)(2,1)S(1)}, bf16[2,128,512]{2,1,0:T(8,128)(2,1)S(1)}, u32[]{:S(2)}, u32[]{:S(2)}) %collective-permute-start.12) | collective-permute-done | bytes 262176 | tf_op jit(solution)/shard_map/ppermute | solution.py:269
  65.5 2.5 %collective-permute-done.5.refs_3_ = bf16[2,128,512]{2,1,0:T(8,128)(2,1)S(1)} collective-permute-done((bf16[2,128,512]{2,1,0:T(8,128)(2,1)S(1)}, bf16[2,128,512]{2,1,0:T(8,128)(2,1)S(1)}, u32[]{:S(2)}, u32[]{:S(2)}) %collective-permute-start.5) | collective-permute-done | bytes 262176 | tf_op jit(solution)/shard_map/ppermute | solution.py:269
  68.0 0.0 collective-permute-start.6
  68.0 1.7 %shard_map.67 = (f32[640,512]{1,0:T(8,128)S(1)}, f32[640,512]{1,0:T(8,128)S(1)}, f32[4,256,256]{2,1,0:T(8,128)S(1)}) custom-call(bf16[2,640,2048]{2,1,0:T(8,128)(2,1)S(1)} %copy-done, bf16[2,640,2048]{2,1,0:T(8,128)(2,1)S(1)} %copy-done.1, ...), custom_call_target="tpu_custom_call", output_to_operand_aliasing={{0}: (6, {}), {1}: (7, {}), {2}: (8, {})} | custom-call | flops 1207959552 | bytes 2359296 | tf_op jit(solution)/shard_map/pallas_call | solution.py:234
  69.7 1.7 %shard_map.71 = (f32[640,512]{1,0:T(8,128)S(1)}, f32[640,512]{1,0:T(8,128)S(1)}, f32[4,256,256]{2,1,0:T(8,128)S(1)}) custom-call(bf16[2,640,2048]{2,1,0:T(8,128)(2,1)S(1)} %copy-done, bf16[2,640,2048]{2,1,0:T(8,128)(2,1)S(1)} %copy-done.1, ...), custom_call_target="tpu_custom_call", output_to_operand_aliasing={{0}: (6, {}), {1}: (7, {}), {2}: (8, {})} | custom-call | flops 1207959552 | bytes 2359296 | tf_op jit(solution)/shard_map/pallas_call | solution.py:234
  71.5 1.7 %shard_map.68 = (f32[640,512]{1,0:T(8,128)S(1)}, f32[640,512]{1,0:T(8,128)S(1)}, f32[4,256,256]{2,1,0:T(8,128)S(1)}) custom-call(bf16[2,640,2048]{2,1,0:T(8,128)(2,1)S(1)} %copy-done, bf16[2,640,2048]{2,1,0:T(8,128)(2,1)S(1)} %copy-done.1, ...), custom_call_target="tpu_custom_call", output_to_operand_aliasing={{0}: (6, {}), {1}: (7, {}), {2}: (8, {})} | custom-call | flops 1207959552 | bytes 2359296 | tf_op jit(solution)/shard_map/pallas_call | solution.py:234
  73.2 0.4 slice-done
  73.7 1.3 %slice-done.2 = s8[4194304]{0:T(1024)(128)(4,1)S(1)} async-done(((s8[5242880]{0:T(1024)(128)(4,1)}), s8[4194304]{0:T(1024)(128)(4,1)S(1)}, s32[]{:S(2)}) %slice-start.2) | async-done | bytes 4194328
  74.9 0.2 slice-done.1
  75.1 0.3 slice-done.3
  75.5 3.6 %shard_map.72 = f32[64,640]{1,0:T(8,128)} custom-call(bf16[2,640,2048]{2,1,0:T(8,128)(2,1)S(1)} %bitcast.2, bf16[2,640,2048]{2,1,0:T(8,128)(2,1)S(1)} %bitcast.4, s32[1]{0:T(128)S(6)} %copy.31.refs_2_, bf16[2,128,512]{2,1,0:T(8,128)(2,1)S(1)} %collective-permute-done.5.refs_3_, bf16[2,128,512]{2,1,0:T(8,128)(2,1)S(1)} %collective-permute-done.6.refs_4_, ...), custom_call_target="tpu_custom_call" | custom-call | flops 1207959552 | bytes 2359296 | tf_op jit(solution)/shard_map/pallas_call | solution.py:234
  (40 shorter events, 0.1 us)
Async XLA Ops:
  2.8 9.6 %collective-permute-start.7 = (bf16[2,128,512]{2,1,0:T(8,128)(2,1)}, bf16[2,128,512]{2,1,0:T(8,128)(2,1)S(1)}, u32[]{:S(2)}, u32[]{:S(2)}) collective-permute-start(bf16[2,128,512]{2,1,0:T(8,128)(2,1)} %shard_map.65.refs_2_), channel_id=1, source_target_pairs={{0,2},{1,3},{2,0},{3,1},{4,6},{5,7},{6,4},{7,5},{8,10},{9,11},{10,... | collective-permute-start | bytes 786440 | tf_op jit(solution)/shard_map/ppermute | solution.py:269
  5.9 10.1 %collective-permute-start.8 = (bf16[2,128,512]{2,1,0:T(8,128)(2,1)}, bf16[2,128,512]{2,1,0:T(8,128)(2,1)S(1)}, u32[]{:S(2)}, u32[]{:S(2)}) collective-permute-start(bf16[2,128,512]{2,1,0:T(8,128)(2,1)} %shard_map.65.refs_2_), channel_id=1, source_target_pairs={{0,4},{1,5},{2,6},{3,7},{4,8},{5,9},{6,10},{7,11},{8,12},{9,13},{1... | collective-permute-start | bytes 786440 | tf_op jit(solution)/shard_map/ppermute | solution.py:269
  7.5 8.6 %collective-permute-start.27 = (bf16[2,128,512]{2,1,0:T(8,128)(2,1)}, bf16[2,128,512]{2,1,0:T(8,128)(2,1)S(1)}, u32[]{:S(2)}, u32[]{:S(2)}) collective-permute-start(bf16[2,128,512]{2,1,0:T(8,128)(2,1)} %shard_map.65.refs_2_), channel_id=1, source_target_pairs={{0,1},{1,0},{2,3},{3,2},{4,5},{5,4},{6,7},{7,6},{8,9},{9,8},{10,11... | collective-permute-start | bytes 786440 | tf_op jit(solution)/shard_map/ppermute | solution.py:269
  10.3 11.1 %collective-permute-start = (bf16[2,128,512]{2,1,0:T(8,128)(2,1)}, bf16[2,128,512]{2,1,0:T(8,128)(2,1)S(1)}, u32[]{:S(2)}, u32[]{:S(2)}) collective-permute-start(bf16[2,128,512]{2,1,0:T(8,128)(2,1)} %shard_map.64.refs_2_), channel_id=1, source_target_pairs={{0,4},{1,5},{2,6},{3,7},{4,8},{5,9},{6,10},{7,11},{8,12},{9,13},{1... | collective-permute-start | bytes 786440 | tf_op jit(solution)/shard_map/ppermute | solution.py:269
  11.9 9.4 %collective-permute-start.1 = (bf16[2,128,512]{2,1,0:T(8,128)(2,1)}, bf16[2,128,512]{2,1,0:T(8,128)(2,1)S(1)}, u32[]{:S(2)}, u32[]{:S(2)}) collective-permute-start(bf16[2,128,512]{2,1,0:T(8,128)(2,1)} %shard_map.64.refs_2_), channel_id=1, source_target_pairs={{0,2},{1,3},{2,0},{3,1},{4,6},{5,7},{6,4},{7,5},{8,10},{9,11},{10,... | collective-permute-start | bytes 786440 | tf_op jit(solution)/shard_map/ppermute | solution.py:269
  12.5 9.4 %collective-permute-start.19 = (bf16[2,128,512]{2,1,0:T(8,128)(2,1)}, bf16[2,128,512]{2,1,0:T(8,128)(2,1)S(1)}, u32[]{:S(2)}, u32[]{:S(2)}) collective-permute-start(bf16[2,128,512]{2,1,0:T(8,128)(2,1)} %shard_map.64.refs_2_), channel_id=1, source_target_pairs={{0,1},{1,0},{2,3},{3,2},{4,5},{5,4},{6,7},{7,6},{8,9},{9,8},{10,11... | collective-permute-start | bytes 786440 | tf_op jit(solution)/shard_map/ppermute | solution.py:269
  16.0 5.9 %collective-permute-start.28 = (bf16[2,128,512]{2,1,0:T(8,128)(2,1)S(1)}, bf16[2,128,512]{2,1,0:T(8,128)(2,1)S(1)}, u32[]{:S(2)}, u32[]{:S(2)}) collective-permute-start(bf16[2,128,512]{2,1,0:T(8,128)(2,1)S(1)} %collective-permute-done.7.refs_4_), channel_id=1, source_target_pairs={{0,1},{1,0},{2,3},{3,2},{4,5},{5,4},{6,7},{7,6},{8,9},{9,8},{10,11... | collective-permute-start | bytes 786440 | tf_op jit(solution)/shard_map/ppermute | solution.py:269
  16.0 7.2 %collective-permute-start.29 = (bf16[2,128,512]{2,1,0:T(8,128)(2,1)S(1)}, bf16[2,128,512]{2,1,0:T(8,128)(2,1)S(1)}, u32[]{:S(2)}, u32[]{:S(2)}) collective-permute-start(bf16[2,128,512]{2,1,0:T(8,128)(2,1)S(1)} %collective-permute-done.8.refs_6_), channel_id=1, source_target_pairs={{0,1},{1,0},{2,3},{3,2},{4,5},{5,4},{6,7},{7,6},{8,9},{9,8},{10,11... | collective-permute-start | bytes 786440 | tf_op jit(solution)/shard_map/ppermute | solution.py:269
  21.4 11.0 %collective-permute-start.9 = (bf16[2,128,512]{2,1,0:T(8,128)(2,1)S(1)}, bf16[2,128,512]{2,1,0:T(8,128)(2,1)S(1)}, u32[]{:S(2)}, u32[]{:S(2)}) collective-permute-start(bf16[2,128,512]{2,1,0:T(8,128)(2,1)S(1)} %collective-permute-done.8.refs_6_), channel_id=1, source_target_pairs={{0,4},{1,5},{2,6},{3,7},{4,8},{5,9},{6,10},{7,11},{8,12},{9,13},{1... | collective-permute-start | bytes 786440 | tf_op jit(solution)/shard_map/ppermute | solution.py:269
  21.4 11.0 %collective-permute-start.10 = (bf16[2,128,512]{2,1,0:T(8,128)(2,1)S(1)}, bf16[2,128,512]{2,1,0:T(8,128)(2,1)S(1)}, u32[]{:S(2)}, u32[]{:S(2)}) collective-permute-start(bf16[2,128,512]{2,1,0:T(8,128)(2,1)S(1)} %collective-permute-done.8.refs_6_), channel_id=1, source_target_pairs={{0,2},{1,3},{2,0},{3,1},{4,6},{5,7},{6,4},{7,5},{8,10},{9,11},{10,... | collective-permute-start | bytes 786440 | tf_op jit(solution)/shard_map/ppermute | solution.py:269
  21.9 10.9 %collective-permute-start.21 = (bf16[2,128,512]{2,1,0:T(8,128)(2,1)S(1)}, bf16[2,128,512]{2,1,0:T(8,128)(2,1)S(1)}, u32[]{:S(2)}, u32[]{:S(2)}) collective-permute-start(bf16[2,128,512]{2,1,0:T(8,128)(2,1)S(1)} %collective-permute-done.refs_6_), channel_id=1, source_target_pairs={{0,1},{1,0},{2,3},{3,2},{4,5},{5,4},{6,7},{7,6},{8,9},{9,8},{10,11... | collective-permute-start | bytes 786440 | tf_op jit(solution)/shard_map/ppermute | solution.py:269
  21.9 14.9 %collective-permute-start.2 = (bf16[2,128,512]{2,1,0:T(8,128)(2,1)S(1)}, bf16[2,128,512]{2,1,0:T(8,128)(2,1)S(1)}, u32[]{:S(2)}, u32[]{:S(2)}) collective-permute-start(bf16[2,128,512]{2,1,0:T(8,128)(2,1)S(1)} %collective-permute-done.refs_6_), channel_id=1, source_target_pairs={{0,4},{1,5},{2,6},{3,7},{4,8},{5,9},{6,10},{7,11},{8,12},{9,13},{1... | collective-permute-start | bytes 786440 | tf_op jit(solution)/shard_map/ppermute | solution.py:269
  23.2 13.6 %collective-permute-start.3 = (bf16[2,128,512]{2,1,0:T(8,128)(2,1)S(1)}, bf16[2,128,512]{2,1,0:T(8,128)(2,1)S(1)}, u32[]{:S(2)}, u32[]{:S(2)}) collective-permute-start(bf16[2,128,512]{2,1,0:T(8,128)(2,1)S(1)} %collective-permute-done.refs_6_), channel_id=1, source_target_pairs={{0,2},{1,3},{2,0},{3,1},{4,6},{5,7},{6,4},{7,5},{8,10},{9,11},{10,... | collective-permute-start | bytes 786440 | tf_op jit(solution)/shard_map/ppermute | solution.py:269
  32.3 5.0 %collective-permute-start.20 = (bf16[2,128,512]{2,1,0:T(8,128)(2,1)S(1)}, bf16[2,128,512]{2,1,0:T(8,128)(2,1)S(1)}, u32[]{:S(2)}, u32[]{:S(2)}) collective-permute-start(bf16[2,128,512]{2,1,0:T(8,128)(2,1)S(1)} %collective-permute-done.1.refs_4_), channel_id=1, source_target_pairs={{0,1},{1,0},{2,3},{3,2},{4,5},{5,4},{6,7},{7,6},{8,9},{9,8},{10,11... | collective-permute-start | bytes 786440 | tf_op jit(solution)/shard_map/ppermute | solution.py:269
  32.3 5.0 %collective-permute-start.26 = (bf16[2,128,512]{2,1,0:T(8,128)(2,1)S(1)}, bf16[2,128,512]{2,1,0:T(8,128)(2,1)S(1)}, u32[]{:S(2)}, u32[]{:S(2)}) collective-permute-start(bf16[2,128,512]{2,1,0:T(8,128)(2,1)S(1)} %collective-permute-done.9.refs_4_), channel_id=1, source_target_pairs={{0,1},{1,0},{2,3},{3,2},{4,5},{5,4},{6,7},{7,6},{8,9},{9,8},{10,11... | collective-permute-start | bytes 786440 | tf_op jit(solution)/shard_map/ppermute | solution.py:269
  32.9 5.0 %collective-permute-start.25 = (bf16[2,128,512]{2,1,0:T(8,128)(2,1)S(1)}, bf16[2,128,512]{2,1,0:T(8,128)(2,1)S(1)}, u32[]{:S(2)}, u32[]{:S(2)}) collective-permute-start(bf16[2,128,512]{2,1,0:T(8,128)(2,1)S(1)} %collective-permute-done.10.refs_2_), channel_id=1, source_target_pairs={{0,1},{1,0},{2,3},{3,2},{4,5},{5,4},{6,7},{7,6},{8,9},{9,8},{10,11... | collective-permute-start | bytes 786440 | tf_op jit(solution)/shard_map/ppermute | solution.py:269
  36.8 11.0 %collective-permute-start.11 = (bf16[2,128,512]{2,1,0:T(8,128)(2,1)S(1)}, bf16[2,128,512]{2,1,0:T(8,128)(2,1)S(1)}, u32[]{:S(2)}, u32[]{:S(2)}) collective-permute-start(bf16[2,128,512]{2,1,0:T(8,128)(2,1)S(1)} %collective-permute-done.9.refs_4_), channel_id=1, source_target_pairs={{0,4},{1,5},{2,6},{3,7},{4,8},{5,9},{6,10},{7,11},{8,12},{9,13},{1... | collective-permute-start | bytes 786440 | tf_op jit(solution)/shard_map/ppermute | solution.py:269
  36.8 11.5 %collective-permute-start.22 = (bf16[2,128,512]{2,1,0:T(8,128)(2,1)S(1)}, bf16[2,128,512]{2,1,0:T(8,128)(2,1)S(1)}, u32[]{:S(2)}, u32[]{:S(2)}) collective-permute-start(bf16[2,128,512]{2,1,0:T(8,128)(2,1)S(1)} %collective-permute-done.9.refs_4_), channel_id=1, source_target_pairs={{0,2},{1,3},{2,0},{3,1},{4,6},{5,7},{6,4},{7,5},{8,10},{9,11},{10,... | collective-permute-start | bytes 786440 | tf_op jit(solution)/shard_map/ppermute | solution.py:269
  37.4 18.0 %collective-permute-start.18 = (bf16[2,128,512]{2,1,0:T(8,128)(2,1)S(1)}, bf16[2,128,512]{2,1,0:T(8,128)(2,1)S(1)}, u32[]{:S(2)}, u32[]{:S(2)}) collective-permute-start(bf16[2,128,512]{2,1,0:T(8,128)(2,1)S(1)} %collective-permute-done.2.refs_4_), channel_id=1, source_target_pairs={{0,1},{1,0},{2,3},{3,2},{4,5},{5,4},{6,7},{7,6},{8,9},{9,8},{10,11... | collective-permute-start | bytes 786440 | tf_op jit(solution)/shard_map/ppermute | solution.py:269
  37.4 21.9 %collective-permute-start.17 = (bf16[2,128,512]{2,1,0:T(8,128)(2,1)S(1)}, bf16[2,128,512]{2,1,0:T(8,128)(2,1)S(1)}, u32[]{:S(2)}, u32[]{:S(2)}) collective-permute-start(bf16[2,128,512]{2,1,0:T(8,128)(2,1)S(1)} %collective-permute-done.3.refs_2_), channel_id=1, source_target_pairs={{0,1},{1,0},{2,3},{3,2},{4,5},{5,4},{6,7},{7,6},{8,9},{9,8},{10,11... | collective-permute-start | bytes 786440 | tf_op jit(solution)/shard_map/ppermute | solution.py:269
  37.9 21.6 %collective-permute-start.4 = (bf16[2,128,512]{2,1,0:T(8,128)(2,1)S(1)}, bf16[2,128,512]{2,1,0:T(8,128)(2,1)S(1)}, u32[]{:S(2)}, u32[]{:S(2)}) collective-permute-start(bf16[2,128,512]{2,1,0:T(8,128)(2,1)S(1)} %collective-permute-done.2.refs_4_), channel_id=1, source_target_pairs={{0,4},{1,5},{2,6},{3,7},{4,8},{5,9},{6,10},{7,11},{8,12},{9,13},{1... | collective-permute-start | bytes 786440 | tf_op jit(solution)/shard_map/ppermute | solution.py:269
  38.6 9.8 %copy-start.3 = (bf16[2,128,512]{2,1,0:T(8,128)(2,1)S(1)}, bf16[2,128,512]{2,1,0:T(8,128)(2,1)}, u32[]{:S(2)}) copy-start(bf16[2,128,512]{2,1,0:T(8,128)(2,1)} %shard_map.65.refs_2_) | copy-start | bytes 786436
  47.8 14.3 %collective-permute-start.14 = (bf16[2,128,512]{2,1,0:T(8,128)(2,1)S(1)}, bf16[2,128,512]{2,1,0:T(8,128)(2,1)S(1)}, u32[]{:S(2)}, u32[]{:S(2)}) collective-permute-start(bf16[2,128,512]{2,1,0:T(8,128)(2,1)S(1)} %collective-permute-done.2.refs_4_), channel_id=1, source_target_pairs={{0,2},{1,3},{2,0},{3,1},{4,6},{5,7},{6,4},{7,5},{8,10},{9,11},{10,... | collective-permute-start | bytes 786440 | tf_op jit(solution)/shard_map/ppermute | solution.py:269
  48.3 13.9 %collective-permute-start.24 = (bf16[2,128,512]{2,1,0:T(8,128)(2,1)S(1)}, bf16[2,128,512]{2,1,0:T(8,128)(2,1)S(1)}, u32[]{:S(2)}, u32[]{:S(2)}) collective-permute-start(bf16[2,128,512]{2,1,0:T(8,128)(2,1)S(1)} %collective-permute-done.11.refs_4_), channel_id=1, source_target_pairs={{0,1},{1,0},{2,3},{3,2},{4,5},{5,4},{6,7},{7,6},{8,9},{9,8},{10,11... | collective-permute-start | bytes 786440 | tf_op jit(solution)/shard_map/ppermute | solution.py:269
  48.4 2.5 %copy-start = (bf16[2,640,2048]{2,1,0:T(8,128)(2,1)S(1)}, bf16[2,640,2048]{2,1,0:T(8,128)(2,1)}, u32[]{:S(2)}) copy-start(bf16[2,640,2048]{2,1,0:T(8,128)(2,1)} %get-tuple-element.30.refs_0_) | copy-start | bytes 15728644
  50.8 2.5 %copy-start.1 = (bf16[2,640,2048]{2,1,0:T(8,128)(2,1)S(1)}, bf16[2,640,2048]{2,1,0:T(8,128)(2,1)}, u32[]{:S(2)}) copy-start(bf16[2,640,2048]{2,1,0:T(8,128)(2,1)} %get-tuple-element.31.refs_1_) | copy-start | bytes 15728644
  53.3 6.8 %copy-start.2 = (bf16[2,128,512]{2,1,0:T(8,128)(2,1)S(1)}, bf16[2,128,512]{2,1,0:T(8,128)(2,1)}, u32[]{:S(2)}) copy-start(bf16[2,128,512]{2,1,0:T(8,128)(2,1)} %shard_map.64.refs_2_) | copy-start | bytes 786436
  55.4 10.2 %collective-permute-start.12 = (bf16[2,128,512]{2,1,0:T(8,128)(2,1)S(1)}, bf16[2,128,512]{2,1,0:T(8,128)(2,1)S(1)}, u32[]{:S(2)}, u32[]{:S(2)}) collective-permute-start(bf16[2,128,512]{2,1,0:T(8,128)(2,1)S(1)} %collective-permute-done.7.refs_4_), channel_id=1, source_target_pairs={{0,12},{1,13},{2,14},{3,15},{4,0},{5,1},{6,2},{7,3},{8,4},{9,5},{1... | collective-permute-start | bytes 786440 | tf_op jit(solution)/shard_map/ppermute | solution.py:269
  59.3 10.4 %collective-permute-start.23 = (bf16[2,128,512]{2,1,0:T(8,128)(2,1)S(1)}, bf16[2,128,512]{2,1,0:T(8,128)(2,1)S(1)}, u32[]{:S(2)}, u32[]{:S(2)}) collective-permute-start(bf16[2,128,512]{2,1,0:T(8,128)(2,1)S(1)} %collective-permute-done.22.refs_2_), channel_id=1, source_target_pairs={{0,1},{1,0},{2,3},{3,2},{4,5},{5,4},{6,7},{7,6},{8,9},{9,8},{10,11... | collective-permute-start | bytes 786440 | tf_op jit(solution)/shard_map/ppermute | solution.py:269
  59.5 8.5 %collective-permute-start.5 = (bf16[2,128,512]{2,1,0:T(8,128)(2,1)S(1)}, bf16[2,128,512]{2,1,0:T(8,128)(2,1)S(1)}, u32[]{:S(2)}, u32[]{:S(2)}) collective-permute-start(bf16[2,128,512]{2,1,0:T(8,128)(2,1)S(1)} %collective-permute-done.4.refs_4_), channel_id=1, source_target_pairs={{0,2},{1,3},{2,0},{3,1},{4,6},{5,7},{6,4},{7,5},{8,10},{9,11},{10,... | collective-permute-start | bytes 786440 | tf_op jit(solution)/shard_map/ppermute | solution.py:269
  62.1 9.3 %collective-permute-start.16 = (bf16[2,128,512]{2,1,0:T(8,128)(2,1)S(1)}, bf16[2,128,512]{2,1,0:T(8,128)(2,1)S(1)}, u32[]{:S(2)}, u32[]{:S(2)}) collective-permute-start(bf16[2,128,512]{2,1,0:T(8,128)(2,1)S(1)} %collective-permute-done.4.refs_4_), channel_id=1, source_target_pairs={{0,1},{1,0},{2,3},{3,2},{4,5},{5,4},{6,7},{7,6},{8,9},{9,8},{10,11... | collective-permute-start | bytes 786440 | tf_op jit(solution)/shard_map/ppermute | solution.py:269
  62.2 9.2 %collective-permute-start.15 = (bf16[2,128,512]{2,1,0:T(8,128)(2,1)S(1)}, bf16[2,128,512]{2,1,0:T(8,128)(2,1)S(1)}, u32[]{:S(2)}, u32[]{:S(2)}) collective-permute-start(bf16[2,128,512]{2,1,0:T(8,128)(2,1)S(1)} %collective-permute-done.14.refs_2_), channel_id=1, source_target_pairs={{0,1},{1,0},{2,3},{3,2},{4,5},{5,4},{6,7},{7,6},{8,9},{9,8},{10,11... | collective-permute-start | bytes 786440 | tf_op jit(solution)/shard_map/ppermute | solution.py:269
  65.5 7.7 %collective-permute-start.13 = (bf16[2,128,512]{2,1,0:T(8,128)(2,1)S(1)}, bf16[2,128,512]{2,1,0:T(8,128)(2,1)S(1)}, u32[]{:S(2)}, u32[]{:S(2)}) collective-permute-start(bf16[2,128,512]{2,1,0:T(8,128)(2,1)S(1)} %collective-permute-done.12.refs_5_), channel_id=1, source_target_pairs={{0,1},{1,0},{2,3},{3,2},{4,5},{5,4},{6,7},{7,6},{8,9},{9,8},{10,11... | collective-permute-start | bytes 786440 | tf_op jit(solution)/shard_map/ppermute | solution.py:269
  68.0 5.2 %collective-permute-start.6 = (bf16[2,128,512]{2,1,0:T(8,128)(2,1)S(1)}, bf16[2,128,512]{2,1,0:T(8,128)(2,1)S(1)}, u32[]{:S(2)}, u32[]{:S(2)}) collective-permute-start(bf16[2,128,512]{2,1,0:T(8,128)(2,1)S(1)} %collective-permute-done.5.refs_3_), channel_id=1, source_target_pairs={{0,1},{1,0},{2,3},{3,2},{4,5},{5,4},{6,7},{7,6},{8,9},{9,8},{10,11... | collective-permute-start | bytes 786440 | tf_op jit(solution)/shard_map/ppermute | solution.py:269
  71.5 2.2 %slice-start = ((s8[5242880]{0:T(1024)(128)(4,1)}), s8[4194304]{0:T(1024)(128)(4,1)S(1)}, s32[]{:S(2)}) async-start(s8[5242880]{0:T(1024)(128)(4,1)} %bitcast.1), calls=%async_computation | async-start | bytes 8388608
  71.5 3.5 %slice-start.2 = ((s8[5242880]{0:T(1024)(128)(4,1)}), s8[4194304]{0:T(1024)(128)(4,1)S(1)}, s32[]{:S(2)}) async-start(s8[5242880]{0:T(1024)(128)(4,1)} %bitcast.3), calls=%async_computation.2 | async-start | bytes 8388608
  71.5 3.7 %slice-start.1 = ((s8[5242880]{0:T(1024)(128)(4,1)}), s8[1048576]{0:T(1024)(128)(4,1)S(1)}, s32[]{:S(2)}) async-start(s8[5242880]{0:T(1024)(128)(4,1)} %bitcast.1), calls=%async_computation.1 | async-start | bytes 2097152
  71.5 4.0 %slice-start.3 = ((s8[5242880]{0:T(1024)(128)(4,1)}), s8[1048576]{0:T(1024)(128)(4,1)S(1)}, s32[]{:S(2)}) async-start(s8[5242880]{0:T(1024)(128)(4,1)} %bitcast.3), calls=%async_computation.3 | async-start | bytes 2097152

commit v3 on v2

--- a/solution.py
+++ b/solution.py
@@ -44,43 +44,56 @@
     return jnp.where(live[:, None], scaled, jnp.zeros_like(scaled))
 
 
-def pick_kernel(layer, ids_ref, u_ref, v_ref, out_ref, held, sems):
+def pick_kernel(layer, ids_hbm, u_ref, v_ref, out_ref, ids_ref, held, made, sems):
     width = QB * RANK
-    rows, bank = u_ref.shape[1:]
+    rows = u_ref.shape[1]
     columns = out_ref.shape[2]
+    per = LANES // width
+    named = pltpu.make_async_copy(ids_hbm, ids_ref, sems.at[4])
+    named.start()
     copies = [
-        pltpu.make_async_copy(ref.at[layer], held.at[pl.ds(s * rows, rows), :], sems.at[s])
-        for s, ref in enumerate((u_ref, v_ref))
+        pltpu.make_async_copy(ref.at[layer], held.at[s], sems.at[s]) for s, ref in enumerate((u_ref, v_ref))
     ]
     for copy in copies:
         copy.start()
-    lane = lax.broadcasted_iota(jnp.int32, (1, columns), 1)
-    named = jnp.zeros((1, columns), jnp.int32)
-    for block in range(columns // width):
-        named = jnp.where(lane // width == block, ids_ref[layer, block], named)
-    row = lax.broadcasted_iota(jnp.int32, (width, columns), 0)
-    col = lax.broadcasted_iota(jnp.int32, (width, columns), 1) % width
-    aim = jnp.where(row == col, named, -1)
-    chooser = [jnp.where(aim == stored, 1.0, 0.0).astype(jnp.bfloat16) for stored in range(bank // width)]
-    chooser = jnp.concatenate(chooser, axis=0)
-    for copy in copies:
-        copy.wait()
-    got = jnp.dot(held[...], chooser, preferred_element_type=jnp.float32).astype(jnp.bfloat16)
-    out_ref[0] = got[:rows]
-    out_ref[1] = got[rows:]
+    named.wait()
+    lane = lax.broadcasted_iota(jnp.int32, (rows, LANES), 1) // width
+    outs = []
+    for s in range(2):
+        copies[s].wait()
+        for chunk in range(columns // LANES):
+            total = None
+            for k in range(per):
+                stored = ids_ref[layer, chunk * per + k]
+                start = pl.multiple_of((stored // per) * LANES, LANES)
+                part = held[s, :, pl.ds(start, LANES)].astype(jnp.float32)
+                part = pltpu.roll(part, lax.rem(k - stored % per + per, per) * width, 1)
+                total = part if total is None else jnp.where(lane == k, part, total)
+            made[s, :, chunk * LANES : (chunk + 1) * LANES] = total.astype(jnp.bfloat16)
+        out = pltpu.make_async_copy(made.at[s], out_ref.at[s], sems.at[2 + s])
+        out.start()
+        outs.append(out)
+    for out in outs:
+        out.wait()
 
 
 def pick(layer, query_u, query_v, block_ids):
     _, rows, bank = query_u.shape
     columns = block_ids.shape[1] * QB * RANK
+    anywhere = pl.BlockSpec(memory_space=pltpu.HBM)
     return pl.pallas_call(
         functools.partial(pick_kernel, layer),
         out_shape=jax.ShapeDtypeStruct((2, rows, columns), jnp.bfloat16),
-        in_specs=[pl.BlockSpec(memory_space=pltpu.SMEM)] + [pl.BlockSpec(memory_space=pltpu.HBM)] * 2,
-        out_specs=pl.BlockSpec(memory_space=pltpu.VMEM),
-        scratch_shapes=[pltpu.VMEM((2 * rows, bank), jnp.bfloat16), pltpu.SemaphoreType.DMA((2,))],
+        in_specs=[anywhere] * 3,
+        out_specs=anywhere,
+        scratch_shapes=[
+            pltpu.SMEM(block_ids.shape, jnp.int32),
+            pltpu.VMEM((2, rows, bank), jnp.bfloat16),
+            pltpu.VMEM((2, rows, columns), jnp.bfloat16),
+            pltpu.SemaphoreType.DMA((5,)),
+        ],
         cost_estimate=pl.CostEstimate(
-            flops=4 * rows * bank * columns, bytes_accessed=4 * rows * (bank + columns), transcendentals=0
+            flops=4 * rows * columns, bytes_accessed=4 * rows * (bank + columns), transcendentals=0
         ),
     )(block_ids, query_u, query_v)
 
@@ -102,7 +115,7 @@
         in_specs=[pl.BlockSpec(memory_space=pltpu.HBM)] * len(arrays),
         out_specs=(pl.BlockSpec(memory_space=pltpu.VMEM),) * len(arrays),
         scratch_shapes=[pltpu.SemaphoreType.DMA((len(arrays),))],
-        compiler_params=pltpu.CompilerParams(vmem_limit_bytes=51 << 20),
+        compiler_params=pltpu.CompilerParams(vmem_limit_bytes=42 << 20),
         name="load",
     )(*arrays)
 
@@ -132,10 +145,11 @@
         return [refs.pop(0) for _ in range(n)]
 
     x_refs = take(2)
-    counts_ref = take(1)[0] if last else None
+    counts_hbm = take(1)[0] if last else None
     pieces = [[take(2) for _ in g["where"]] for g in groups]
     starts = [take(3) if g["carry"] else None for g in groups]
     outs = take(1) if last else None
+    product, counts_ref = take(2) if last else (None, None)
     totals = [take(3) for _ in groups]
     w, sems = take(2)
     me = lax.axis_index("tok")
@@ -154,6 +168,9 @@
                 copy.start()
             copies.append((these, pl.ds(start, 2 * rows)))
             slot += 1
+    if last:
+        live = pltpu.make_async_copy(counts_hbm, counts_ref, sems.at[2 * slot])
+        live.start()
     tiles = w.shape[2] // TILE
     slot = 0
     for g, start, total in zip(groups, starts, totals):
@@ -165,7 +182,13 @@
             for s in range(2):
                 x = x_refs[s][g["layer"], :, copies[slot][1]]
                 part = jnp.dot(x, w[s, span, :], preferred_element_type=jnp.float32)
-                total[s][...] = part if came is None else came[s][...] + part
+                if came is not None:
+                    part = came[s][...] + part
+                if last and s == 1:
+                    part = total[0][...] * part
+                    product[...] = part if g is groups[0] else product[...] + part
+                else:
+                    total[s][...] = part
             for s in range(2):
                 for t in range(tiles):
                     one = w[s, span, t * TILE : (t + 1) * TILE]
@@ -185,8 +208,9 @@
         norm = jnp.broadcast_to(jnp.concatenate(norm, axis=1), (8, columns))
         chooser = group_sums(columns)
         norm = split_dot(norm, chooser)[:1]
-        raw = split_dot(sum(total[0][...] * total[1][...] for total in totals), chooser)
+        raw = split_dot(product[...], chooser)
         scaled = raw / jnp.sqrt(norm + 1e-06)
+        live.wait()
         token = lax.broadcasted_iota(jnp.int32, scaled.shape, 0)
         scaled = jnp.where(token < counts_ref[0], scaled, 0.0)
         outs[0][...] = scaled.T[: columns // RANK]
@@ -203,7 +227,7 @@
     args, specs = [gradients, activations], [vmem, vmem]
     if last:
         args.append(counts)
-        specs.append(pl.BlockSpec(memory_space=pltpu.SMEM))
+        specs.append(anywhere)
     for g in groups:
         for pair in g["arrays"]:
             args += pair
@@ -220,7 +244,7 @@
     if last:
         out_shape = jax.ShapeDtypeStruct((columns // RANK, tokens), jnp.float32)
         out_specs = vmem
-        scratch = [pltpu.VMEM(*one) for one in sums] * len(groups)
+        scratch = [pltpu.VMEM(*sums[0]), pltpu.SMEM(counts.shape, jnp.int32)] + [pltpu.VMEM(*one) for one in sums] * len(groups)
     else:
         out_shape = tuple(jax.ShapeDtypeStruct(*one) for one in sums) * len(groups)
         out_specs = (vmem,) * len(out_shape)
@@ -239,7 +263,7 @@
         scratch_shapes=scratch
         + [
             pltpu.VMEM((2, slots * 2 * rows, columns), jnp.bfloat16),
-            pltpu.SemaphoreType.DMA((2 * slots,)),
+            pltpu.SemaphoreType.DMA((2 * slots + 1,)),
         ],
         input_output_aliases=aliases,
         compiler_params=pltpu.CompilerParams(vmem_limit_bytes=(24 if last else 16) << 20),

time: 79.5 us -> 67.2 us (0.85)
  local copies, waits for them, and re-layouts: 7.19 us -> 0.01 us
  Pallas kernels: 28.1 us -> 22.9 us
  waiting for transfers between devices: 24.7 us -> 27.6 us
  starting transfers between devices: 18.1 us -> 15.5 us
    unnamed x16 -> x4, local copies, waits for them, and re-layouts: 7.19 us -> 0.01 us
    pallas_call x1, Pallas kernels: 8.11 us -> 4.11 us  [load(): pl.pallas_call(load_kernel, out_shape=tuple((jax.ShapeDtypeStruct(one.sha...]
    ppermute x30, waiting for transfers between devices: 24.7 us -> 27.6 us  [move(): return lax.ppermute(value, 'tok', steps)]
    ppermute x30, starting transfers between devices: 18.1 us -> 15.5 us  [move(): return lax.ppermute(value, 'tok', steps)]
    pallas_call x2, Pallas kernels: 5.68 us -> 4.18 us  [pick(): pl.pallas_call(functools.partial(pick_kernel, layer), out_shape=jax.Shape...]
  transfers between devices with their start and end apart: 30 -> 30, of which waited for: 7 -> 9; matrix products, arithmetic and copies ran while one was open for 0% -> 0% of each run, Pallas kernels for 27% -> 25%
where the time goes in v3:
time: 67.2 us; the launch traced here: 67.1 us
  waiting for transfers between devices  27.6 us (41%)
  Pallas kernels  22.9 us (34%)
  starting transfers between devices  15.5 us (23%)
  between operations  1.02 us (2%)
    ppermute x30, waiting for transfers between devices, move(): return lax.ppermute(value, 'tok', steps)  27.6 us
    ppermute x30, starting transfers between devices, move(): return lax.ppermute(value, 'tok', steps)  15.5 us
    pallas_call x7, Pallas kernels, stage(): pl.pallas_call(functools.partial(stage_kernel, cfg), out_shape=out_shape,...  14.6 us
    pallas_call x2, Pallas kernels, pick(): pl.pallas_call(functools.partial(pick_kernel, layer), out_shape=jax.Shape...  4.18 us
    pallas_call x1, Pallas kernels, load(): pl.pallas_call(load_kernel, out_shape=tuple((jax.ShapeDtypeStruct(one.sha...  4.11 us
  transfers between devices with their start and end apart: 30, of which 9 were waited for; matrix products, arithmetic and copies ran while one was open for 0% of the time, Pallas kernels for 25%

profile of v3, /device:TPU:0, one launch (start us, length us, event | category | flops | bytes accessed | tf_op | source)
XLA Modules:
  0.0 67.1 jit_solution(9533198035319495111)
XLA Ops:
  0.0 2.1 %shard_map.65.refs_2_ = bf16[2,128,512]{2,1,0:T(8,128)(2,1)} custom-call(s32[2,16]{1,0:T(2,128)} %ids_hbm.3, bf16[2,128,1024]{2,1,0:T(8,128)(2,1)} %u_ref.3, bf16[2,128,1024]{2,1,0:T(8,128)(2,1)} %v_ref.3), custom_call_target="tpu_custom_call" | custom-call | flops 262144 | bytes 786432 | tf_op jit(solution)/shard_map/pallas_call | solution.py:84
  2.1 3.0 %collective-permute-start.7 = (bf16[2,128,512]{2,1,0:T(8,128)(2,1)}, bf16[2,128,512]{2,1,0:T(8,128)(2,1)S(1)}, u32[]{:S(2)}, u32[]{:S(2)}) collective-permute-start(bf16[2,128,512]{2,1,0:T(8,128)(2,1)} %shard_map.65.refs_2_), channel_id=1, source_target_pairs={{0,2},{1,3},{2,0},{3,1},{4,6},{5,7},{6,4},{7,5},{8,10},{9,11},{10,... | collective-permute-start | bytes 786440 | tf_op jit(solution)/shard_map/ppermute | solution.py:293
  5.1 1.6 %collective-permute-start.8 = (bf16[2,128,512]{2,1,0:T(8,128)(2,1)}, bf16[2,128,512]{2,1,0:T(8,128)(2,1)S(1)}, u32[]{:S(2)}, u32[]{:S(2)}) collective-permute-start(bf16[2,128,512]{2,1,0:T(8,128)(2,1)} %shard_map.65.refs_2_), channel_id=1, source_target_pairs={{0,4},{1,5},{2,6},{3,7},{4,8},{5,9},{6,10},{7,11},{8,12},{9,13},{1... | collective-permute-start | bytes 786440 | tf_op jit(solution)/shard_map/ppermute | solution.py:293
  6.7 0.0 collective-permute-start.27
  6.7 2.1 %shard_map.64.refs_2_ = bf16[2,128,512]{2,1,0:T(8,128)(2,1)} custom-call(s32[2,16]{1,0:T(2,128)} %ids_hbm.3, bf16[2,128,1024]{2,1,0:T(8,128)(2,1)} %u_ref.3, bf16[2,128,1024]{2,1,0:T(8,128)(2,1)} %v_ref.3), custom_call_target="tpu_custom_call" | custom-call | flops 262144 | bytes 786432 | tf_op jit(solution)/shard_map/pallas_call | solution.py:84
  8.8 1.6 %collective-permute-start = (bf16[2,128,512]{2,1,0:T(8,128)(2,1)}, bf16[2,128,512]{2,1,0:T(8,128)(2,1)S(1)}, u32[]{:S(2)}, u32[]{:S(2)}) collective-permute-start(bf16[2,128,512]{2,1,0:T(8,128)(2,1)} %shard_map.64.refs_2_), channel_id=1, source_target_pairs={{0,4},{1,5},{2,6},{3,7},{4,8},{5,9},{6,10},{7,11},{8,12},{9,13},{1... | collective-permute-start | bytes 786440 | tf_op jit(solution)/shard_map/ppermute | solution.py:293
  10.4 0.5 collective-permute-start.1
  11.0 0.7 %collective-permute-done.7.refs_4_ = bf16[2,128,512]{2,1,0:T(8,128)(2,1)S(1)} collective-permute-done((bf16[2,128,512]{2,1,0:T(8,128)(2,1)}, bf16[2,128,512]{2,1,0:T(8,128)(2,1)S(1)}, u32[]{:S(2)}, u32[]{:S(2)}) %collective-permute-start.7) | collective-permute-done | bytes 262176 | tf_op jit(solution)/shard_map/ppermute | solution.py:293
  11.6 4.4 %collective-permute-done.8.refs_6_ = bf16[2,128,512]{2,1,0:T(8,128)(2,1)S(1)} collective-permute-done((bf16[2,128,512]{2,1,0:T(8,128)(2,1)}, bf16[2,128,512]{2,1,0:T(8,128)(2,1)S(1)}, u32[]{:S(2)}, u32[]{:S(2)}) %collective-permute-start.8) | collective-permute-done | bytes 262176 | tf_op jit(solution)/shard_map/ppermute | solution.py:293
  16.0 0.0 collective-permute-start.28
  16.0 0.0 collective-permute-done.27.refs_3_
  16.0 0.5 collective-permute-start.29
  16.5 4.1 %collective-permute-done.refs_6_ = bf16[2,128,512]{2,1,0:T(8,128)(2,1)S(1)} collective-permute-done((bf16[2,128,512]{2,1,0:T(8,128)(2,1)}, bf16[2,128,512]{2,1,0:T(8,128)(2,1)S(1)}, u32[]{:S(2)}, u32[]{:S(2)}) %collective-permute-start) | collective-permute-done | bytes 262176 | tf_op jit(solution)/shard_map/ppermute | solution.py:293
  20.6 0.0 collective-permute-done.1.refs_4_
  20.6 0.5 collective-permute-start.10
  21.2 0.0 collective-permute-done.19.refs_3_
  21.2 0.0 collective-permute-start.21
  21.2 0.0 collective-permute-done.28.refs_5_
  21.2 1.3 %collective-permute-start.2 = (bf16[2,128,512]{2,1,0:T(8,128)(2,1)S(1)}, bf16[2,128,512]{2,1,0:T(8,128)(2,1)S(1)}, u32[]{:S(2)}, u32[]{:S(2)}) collective-permute-start(bf16[2,128,512]{2,1,0:T(8,128)(2,1)S(1)} %collective-permute-done.refs_6_), channel_id=1, source_target_pairs={{0,4},{1,5},{2,6},{3,7},{4,8},{5,9},{6,10},{7,11},{8,12},{9,13},{1... | collective-permute-start | bytes 786440 | tf_op jit(solution)/shard_map/ppermute | solution.py:293
  22.5 0.0 collective-permute-done.29.refs_7_
  22.5 1.5 %collective-permute-start.3 = (bf16[2,128,512]{2,1,0:T(8,128)(2,1)S(1)}, bf16[2,128,512]{2,1,0:T(8,128)(2,1)S(1)}, u32[]{:S(2)}, u32[]{:S(2)}) collective-permute-start(bf16[2,128,512]{2,1,0:T(8,128)(2,1)S(1)} %collective-permute-done.refs_6_), channel_id=1, source_target_pairs={{0,2},{1,3},{2,0},{3,1},{4,6},{5,7},{6,4},{7,5},{8,10},{9,11},{10,... | collective-permute-start | bytes 786440 | tf_op jit(solution)/shard_map/ppermute | solution.py:293
  24.0 7.6 %collective-permute-done.9.refs_4_ = bf16[2,128,512]{2,1,0:T(8,128)(2,1)S(1)} collective-permute-done((bf16[2,128,512]{2,1,0:T(8,128)(2,1)S(1)}, bf16[2,128,512]{2,1,0:T(8,128)(2,1)S(1)}, u32[]{:S(2)}, u32[]{:S(2)}) %collective-permute-start.9) | collective-permute-done | bytes 262176 | tf_op jit(solution)/shard_map/ppermute | solution.py:293
  31.6 0.0 collective-permute-start.20
  31.6 0.0 collective-permute-done.10.refs_2_
  31.6 0.5 collective-permute-start.26
  32.1 0.0 collective-permute-done.21.refs_7_
  32.1 0.1 collective-permute-start.25
  32.2 3.1 %collective-permute-done.2.refs_4_ = bf16[2,128,512]{2,1,0:T(8,128)(2,1)S(1)} collective-permute-done((bf16[2,128,512]{2,1,0:T(8,128)(2,1)S(1)}, bf16[2,128,512]{2,1,0:T(8,128)(2,1)S(1)}, u32[]{:S(2)}, u32[]{:S(2)}) %collective-permute-start.2) | collective-permute-done | bytes 262176 | tf_op jit(solution)/shard_map/ppermute | solution.py:293
  35.3 0.0 collective-permute-start.11
  35.3 0.5 collective-permute-start.22
  35.9 0.5 collective-permute-start.17
  37.1 4.1 %load.1 = (bf16[2,640,2048]{2,1,0:T(8,128)(2,1)S(1)}, bf16[2,640,2048]{2,1,0:T(8,128)(2,1)S(1)}) custom-call(bf16[2,640,2048]{2,1,0:T(8,128)(2,1)} %refs_0_.1, bf16[2,640,2048]{2,1,0:T(8,128)(2,1)} %refs_1_.1), custom_call_target="tpu_custom_call" | custom-call | tf_op jit(solution)/shard_map/load/pallas_call | solution.py:112
  41.2 4.8 %collective-permute-done.11.refs_4_ = bf16[2,128,512]{2,1,0:T(8,128)(2,1)S(1)} collective-permute-done((bf16[2,128,512]{2,1,0:T(8,128)(2,1)S(1)}, bf16[2,128,512]{2,1,0:T(8,128)(2,1)S(1)}, u32[]{:S(2)}, u32[]{:S(2)}) %collective-permute-start.11) | collective-permute-done | bytes 262176 | tf_op jit(solution)/shard_map/ppermute | solution.py:293
  46.0 2.1 %shard_map.69 = (f32[640,512]{1,0:T(8,128)S(1)}, f32[640,512]{1,0:T(8,128)S(1)}, f32[4,256,256]{2,1,0:T(8,128)S(1)}) custom-call(bf16[2,640,2048]{2,1,0:T(8,128)(2,1)S(1)} %get-tuple-element.30.refs_0_, bf16[2,640,2048]{2,1,0:T(8,128)(2,1)S(1)} %get-tuple-element.31.refs_1_, bf16[2,128,512]{2,1,0:T(8,128)(2,1)S(1)} %copy-done.1, ...), custom_call_target="tpu_custom_call" | custom-call | flops 1811939328 | bytes 3538944 | tf_op jit(solution)/shard_map/pallas_call | solution.py:258
  48.1 0.8 %collective-permute-start.12 = (bf16[2,128,512]{2,1,0:T(8,128)(2,1)S(1)}, bf16[2,128,512]{2,1,0:T(8,128)(2,1)S(1)}, u32[]{:S(2)}, u32[]{:S(2)}) collective-permute-start(bf16[2,128,512]{2,1,0:T(8,128)(2,1)S(1)} %collective-permute-done.7.refs_4_), channel_id=1, source_target_pairs={{0,12},{1,13},{2,14},{3,15},{4,0},{5,1},{6,2},{7,3},{8,4},{9,5},{1... | collective-permute-start | bytes 786440 | tf_op jit(solution)/shard_map/ppermute | solution.py:293
  48.9 0.2 collective-permute-start.23
  49.1 0.1 collective-permute-done.4.refs_4_
  49.2 1.7 %collective-permute-start.5 = (bf16[2,128,512]{2,1,0:T(8,128)(2,1)S(1)}, bf16[2,128,512]{2,1,0:T(8,128)(2,1)S(1)}, u32[]{:S(2)}, u32[]{:S(2)}) collective-permute-start(bf16[2,128,512]{2,1,0:T(8,128)(2,1)S(1)} %collective-permute-done.4.refs_4_), channel_id=1, source_target_pairs={{0,2},{1,3},{2,0},{3,1},{4,6},{5,7},{6,4},{7,5},{8,10},{9,11},{10,... | collective-permute-start | bytes 786440 | tf_op jit(solution)/shard_map/ppermute | solution.py:293
  50.9 2.0 %shard_map.66 = (f32[640,512]{1,0:T(8,128)S(1)}, f32[640,512]{1,0:T(8,128)S(1)}, f32[4,256,256]{2,1,0:T(8,128)S(1)}) custom-call(bf16[2,640,2048]{2,1,0:T(8,128)(2,1)S(1)} %get-tuple-element.30.refs_0_, bf16[2,640,2048]{2,1,0:T(8,128)(2,1)S(1)} %get-tuple-element.31.refs_1_, bf16[2,128,512]{2,1,0:T(8,128)(2,1)S(1)} %copy-done, ...), custom_call_target="tpu_custom_call" | custom-call | flops 1811939328 | bytes 3538944 | tf_op jit(solution)/shard_map/pallas_call | solution.py:258
  53.0 0.1 collective-permute-start.16
  53.0 0.5 collective-permute-start.15
  53.5 1.7 %shard_map.70 = (f32[640,512]{1,0:T(8,128)S(1)}, f32[640,512]{1,0:T(8,128)S(1)}, f32[4,256,256]{2,1,0:T(8,128)S(1)}) custom-call(bf16[2,640,2048]{2,1,0:T(8,128)(2,1)S(1)} %get-tuple-element.30.refs_0_, bf16[2,640,2048]{2,1,0:T(8,128)(2,1)S(1)} %get-tuple-element.31.refs_1_, ...), custom_call_target="tpu_custom_call", output_to_operand_aliasing={{0}: (6, {}), {1}: (7, {}), {2}: (8, {})} | custom-call | flops 1207959552 | bytes 2359296 | tf_op jit(solution)/shard_map/pallas_call | solution.py:258
  55.2 1.8 %collective-permute-done.12.refs_5_ = bf16[2,128,512]{2,1,0:T(8,128)(2,1)S(1)} collective-permute-done((bf16[2,128,512]{2,1,0:T(8,128)(2,1)S(1)}, bf16[2,128,512]{2,1,0:T(8,128)(2,1)S(1)}, u32[]{:S(2)}, u32[]{:S(2)}) %collective-permute-start.12) | collective-permute-done | bytes 262176 | tf_op jit(solution)/shard_map/ppermute | solution.py:293
  57.0 1.0 %collective-permute-done.5.refs_3_ = bf16[2,128,512]{2,1,0:T(8,128)(2,1)S(1)} collective-permute-done((bf16[2,128,512]{2,1,0:T(8,128)(2,1)S(1)}, bf16[2,128,512]{2,1,0:T(8,128)(2,1)S(1)}, u32[]{:S(2)}, u32[]{:S(2)}) %collective-permute-start.5) | collective-permute-done | bytes 262176 | tf_op jit(solution)/shard_map/ppermute | solution.py:293
  58.0 1.7 %shard_map.67 = (f32[640,512]{1,0:T(8,128)S(1)}, f32[640,512]{1,0:T(8,128)S(1)}, f32[4,256,256]{2,1,0:T(8,128)S(1)}) custom-call(bf16[2,640,2048]{2,1,0:T(8,128)(2,1)S(1)} %get-tuple-element.30.refs_0_, bf16[2,640,2048]{2,1,0:T(8,128)(2,1)S(1)} %get-tuple-element.31.refs_1_, ...), custom_call_target="tpu_custom_call", output_to_operand_aliasing={{0}: (6, {}), {1}: (7, {}), {2}: (8, {})} | custom-call | flops 1207959552 | bytes 2359296 | tf_op jit(solution)/shard_map/pallas_call | solution.py:258
  59.7 1.7 %shard_map.71 = (f32[640,512]{1,0:T(8,128)S(1)}, f32[640,512]{1,0:T(8,128)S(1)}, f32[4,256,256]{2,1,0:T(8,128)S(1)}) custom-call(bf16[2,640,2048]{2,1,0:T(8,128)(2,1)S(1)} %get-tuple-element.30.refs_0_, bf16[2,640,2048]{2,1,0:T(8,128)(2,1)S(1)} %get-tuple-element.31.refs_1_, ...), custom_call_target="tpu_custom_call", output_to_operand_aliasing={{0}: (6, {}), {1}: (7, {}), {2}: (8, {})} | custom-call | flops 1207959552 | bytes 2359296 | tf_op jit(solution)/shard_map/pallas_call | solution.py:258
  61.4 1.7 %shard_map.68 = (f32[640,512]{1,0:T(8,128)S(1)}, f32[640,512]{1,0:T(8,128)S(1)}, f32[4,256,256]{2,1,0:T(8,128)S(1)}) custom-call(bf16[2,640,2048]{2,1,0:T(8,128)(2,1)S(1)} %get-tuple-element.30.refs_0_, bf16[2,640,2048]{2,1,0:T(8,128)(2,1)S(1)} %get-tuple-element.31.refs_1_, ...), custom_call_target="tpu_custom_call", output_to_operand_aliasing={{0}: (6, {}), {1}: (7, {}), {2}: (8, {})} | custom-call | flops 1207959552 | bytes 2359296 | tf_op jit(solution)/shard_map/pallas_call | solution.py:258
  63.2 3.7 %shard_map.72 = f32[64,640]{1,0:T(8,128)} custom-call(bf16[2,640,2048]{2,1,0:T(8,128)(2,1)S(1)} %get-tuple-element.30.refs_0_, bf16[2,640,2048]{2,1,0:T(8,128)(2,1)S(1)} %get-tuple-element.31.refs_1_, s32[1]{0:T(128)S(6)} %copy.31.refs_2_, bf16[2,128,512]{2,1,0:T(8,128)(2,1)S(1)} %collective-permute-done.5.refs_3_, ...), custom_call_target="tpu_custom_call" | custom-call | flops 1207959552 | bytes 2359296 | tf_op jit(solution)/shard_map/pallas_call | solution.py:258
  (26 shorter events, 0.1 us)
Async XLA Ops:
  2.1 9.5 %collective-permute-start.7 = (bf16[2,128,512]{2,1,0:T(8,128)(2,1)}, bf16[2,128,512]{2,1,0:T(8,128)(2,1)S(1)}, u32[]{:S(2)}, u32[]{:S(2)}) collective-permute-start(bf16[2,128,512]{2,1,0:T(8,128)(2,1)} %shard_map.65.refs_2_), channel_id=1, source_target_pairs={{0,2},{1,3},{2,0},{3,1},{4,6},{5,7},{6,4},{7,5},{8,10},{9,11},{10,... | collective-permute-start | bytes 786440 | tf_op jit(solution)/shard_map/ppermute | solution.py:293
  5.1 10.9 %collective-permute-start.8 = (bf16[2,128,512]{2,1,0:T(8,128)(2,1)}, bf16[2,128,512]{2,1,0:T(8,128)(2,1)S(1)}, u32[]{:S(2)}, u32[]{:S(2)}) collective-permute-start(bf16[2,128,512]{2,1,0:T(8,128)(2,1)} %shard_map.65.refs_2_), channel_id=1, source_target_pairs={{0,4},{1,5},{2,6},{3,7},{4,8},{5,9},{6,10},{7,11},{8,12},{9,13},{1... | collective-permute-start | bytes 786440 | tf_op jit(solution)/shard_map/ppermute | solution.py:293
  6.7 9.3 %collective-permute-start.27 = (bf16[2,128,512]{2,1,0:T(8,128)(2,1)}, bf16[2,128,512]{2,1,0:T(8,128)(2,1)S(1)}, u32[]{:S(2)}, u32[]{:S(2)}) collective-permute-start(bf16[2,128,512]{2,1,0:T(8,128)(2,1)} %shard_map.65.refs_2_), channel_id=1, source_target_pairs={{0,1},{1,0},{2,3},{3,2},{4,5},{5,4},{6,7},{7,6},{8,9},{9,8},{10,11... | collective-permute-start | bytes 786440 | tf_op jit(solution)/shard_map/ppermute | solution.py:293
  8.8 11.8 %collective-permute-start = (bf16[2,128,512]{2,1,0:T(8,128)(2,1)}, bf16[2,128,512]{2,1,0:T(8,128)(2,1)S(1)}, u32[]{:S(2)}, u32[]{:S(2)}) collective-permute-start(bf16[2,128,512]{2,1,0:T(8,128)(2,1)} %shard_map.64.refs_2_), channel_id=1, source_target_pairs={{0,4},{1,5},{2,6},{3,7},{4,8},{5,9},{6,10},{7,11},{8,12},{9,13},{1... | collective-permute-start | bytes 786440 | tf_op jit(solution)/shard_map/ppermute | solution.py:293
  10.4 10.2 %collective-permute-start.1 = (bf16[2,128,512]{2,1,0:T(8,128)(2,1)}, bf16[2,128,512]{2,1,0:T(8,128)(2,1)S(1)}, u32[]{:S(2)}, u32[]{:S(2)}) collective-permute-start(bf16[2,128,512]{2,1,0:T(8,128)(2,1)} %shard_map.64.refs_2_), channel_id=1, source_target_pairs={{0,2},{1,3},{2,0},{3,1},{4,6},{5,7},{6,4},{7,5},{8,10},{9,11},{10,... | collective-permute-start | bytes 786440 | tf_op jit(solution)/shard_map/ppermute | solution.py:293
  11.6 9.5 %collective-permute-start.19 = (bf16[2,128,512]{2,1,0:T(8,128)(2,1)}, bf16[2,128,512]{2,1,0:T(8,128)(2,1)S(1)}, u32[]{:S(2)}, u32[]{:S(2)}) collective-permute-start(bf16[2,128,512]{2,1,0:T(8,128)(2,1)} %shard_map.64.refs_2_), channel_id=1, source_target_pairs={{0,1},{1,0},{2,3},{3,2},{4,5},{5,4},{6,7},{7,6},{8,9},{9,8},{10,11... | collective-permute-start | bytes 786440 | tf_op jit(solution)/shard_map/ppermute | solution.py:293
  16.0 5.1 %collective-permute-start.28 = (bf16[2,128,512]{2,1,0:T(8,128)(2,1)S(1)}, bf16[2,128,512]{2,1,0:T(8,128)(2,1)S(1)}, u32[]{:S(2)}, u32[]{:S(2)}) collective-permute-start(bf16[2,128,512]{2,1,0:T(8,128)(2,1)S(1)} %collective-permute-done.7.refs_4_), channel_id=1, source_target_pairs={{0,1},{1,0},{2,3},{3,2},{4,5},{5,4},{6,7},{7,6},{8,9},{9,8},{10,11... | collective-permute-start | bytes 786440 | tf_op jit(solution)/shard_map/ppermute | solution.py:293
  16.0 6.5 %collective-permute-start.29 = (bf16[2,128,512]{2,1,0:T(8,128)(2,1)S(1)}, bf16[2,128,512]{2,1,0:T(8,128)(2,1)S(1)}, u32[]{:S(2)}, u32[]{:S(2)}) collective-permute-start(bf16[2,128,512]{2,1,0:T(8,128)(2,1)S(1)} %collective-permute-done.8.refs_6_), channel_id=1, source_target_pairs={{0,1},{1,0},{2,3},{3,2},{4,5},{5,4},{6,7},{7,6},{8,9},{9,8},{10,11... | collective-permute-start | bytes 786440 | tf_op jit(solution)/shard_map/ppermute | solution.py:293
  20.6 11.0 %collective-permute-start.9 = (bf16[2,128,512]{2,1,0:T(8,128)(2,1)S(1)}, bf16[2,128,512]{2,1,0:T(8,128)(2,1)S(1)}, u32[]{:S(2)}, u32[]{:S(2)}) collective-permute-start(bf16[2,128,512]{2,1,0:T(8,128)(2,1)S(1)} %collective-permute-done.8.refs_6_), channel_id=1, source_target_pairs={{0,4},{1,5},{2,6},{3,7},{4,8},{5,9},{6,10},{7,11},{8,12},{9,13},{1... | collective-permute-start | bytes 786440 | tf_op jit(solution)/shard_map/ppermute | solution.py:293
  20.6 11.0 %collective-permute-start.10 = (bf16[2,128,512]{2,1,0:T(8,128)(2,1)S(1)}, bf16[2,128,512]{2,1,0:T(8,128)(2,1)S(1)}, u32[]{:S(2)}, u32[]{:S(2)}) collective-permute-start(bf16[2,128,512]{2,1,0:T(8,128)(2,1)S(1)} %collective-permute-done.8.refs_6_), channel_id=1, source_target_pairs={{0,2},{1,3},{2,0},{3,1},{4,6},{5,7},{6,4},{7,5},{8,10},{9,11},{10,... | collective-permute-start | bytes 786440 | tf_op jit(solution)/shard_map/ppermute | solution.py:293
  21.2 10.9 %collective-permute-start.21 = (bf16[2,128,512]{2,1,0:T(8,128)(2,1)S(1)}, bf16[2,128,512]{2,1,0:T(8,128)(2,1)S(1)}, u32[]{:S(2)}, u32[]{:S(2)}) collective-permute-start(bf16[2,128,512]{2,1,0:T(8,128)(2,1)S(1)} %collective-permute-done.refs_6_), channel_id=1, source_target_pairs={{0,1},{1,0},{2,3},{3,2},{4,5},{5,4},{6,7},{7,6},{8,9},{9,8},{10,11... | collective-permute-start | bytes 786440 | tf_op jit(solution)/shard_map/ppermute | solution.py:293
  21.2 14.2 %collective-permute-start.2 = (bf16[2,128,512]{2,1,0:T(8,128)(2,1)S(1)}, bf16[2,128,512]{2,1,0:T(8,128)(2,1)S(1)}, u32[]{:S(2)}, u32[]{:S(2)}) collective-permute-start(bf16[2,128,512]{2,1,0:T(8,128)(2,1)S(1)} %collective-permute-done.refs_6_), channel_id=1, source_target_pairs={{0,4},{1,5},{2,6},{3,7},{4,8},{5,9},{6,10},{7,11},{8,12},{9,13},{1... | collective-permute-start | bytes 786440 | tf_op jit(solution)/shard_map/ppermute | solution.py:293
  22.5 12.8 %collective-permute-start.3 = (bf16[2,128,512]{2,1,0:T(8,128)(2,1)S(1)}, bf16[2,128,512]{2,1,0:T(8,128)(2,1)S(1)}, u32[]{:S(2)}, u32[]{:S(2)}) collective-permute-start(bf16[2,128,512]{2,1,0:T(8,128)(2,1)S(1)} %collective-permute-done.refs_6_), channel_id=1, source_target_pairs={{0,2},{1,3},{2,0},{3,1},{4,6},{5,7},{6,4},{7,5},{8,10},{9,11},{10,... | collective-permute-start | bytes 786440 | tf_op jit(solution)/shard_map/ppermute | solution.py:293
  31.6 4.3 %collective-permute-start.20 = (bf16[2,128,512]{2,1,0:T(8,128)(2,1)S(1)}, bf16[2,128,512]{2,1,0:T(8,128)(2,1)S(1)}, u32[]{:S(2)}, u32[]{:S(2)}) collective-permute-start(bf16[2,128,512]{2,1,0:T(8,128)(2,1)S(1)} %collective-permute-done.1.refs_4_), channel_id=1, source_target_pairs={{0,1},{1,0},{2,3},{3,2},{4,5},{5,4},{6,7},{7,6},{8,9},{9,8},{10,11... | collective-permute-start | bytes 786440 | tf_op jit(solution)/shard_map/ppermute | solution.py:293
  31.6 4.3 %collective-permute-start.26 = (bf16[2,128,512]{2,1,0:T(8,128)(2,1)S(1)}, bf16[2,128,512]{2,1,0:T(8,128)(2,1)S(1)}, u32[]{:S(2)}, u32[]{:S(2)}) collective-permute-start(bf16[2,128,512]{2,1,0:T(8,128)(2,1)S(1)} %collective-permute-done.9.refs_4_), channel_id=1, source_target_pairs={{0,1},{1,0},{2,3},{3,2},{4,5},{5,4},{6,7},{7,6},{8,9},{9,8},{10,11... | collective-permute-start | bytes 786440 | tf_op jit(solution)/shard_map/ppermute | solution.py:293
  32.1 4.3 %collective-permute-start.25 = (bf16[2,128,512]{2,1,0:T(8,128)(2,1)S(1)}, bf16[2,128,512]{2,1,0:T(8,128)(2,1)S(1)}, u32[]{:S(2)}, u32[]{:S(2)}) collective-permute-start(bf16[2,128,512]{2,1,0:T(8,128)(2,1)S(1)} %collective-permute-done.10.refs_2_), channel_id=1, source_target_pairs={{0,1},{1,0},{2,3},{3,2},{4,5},{5,4},{6,7},{7,6},{8,9},{9,8},{10,11... | collective-permute-start | bytes 786440 | tf_op jit(solution)/shard_map/ppermute | solution.py:293
  35.3 10.7 %collective-permute-start.11 = (bf16[2,128,512]{2,1,0:T(8,128)(2,1)S(1)}, bf16[2,128,512]{2,1,0:T(8,128)(2,1)S(1)}, u32[]{:S(2)}, u32[]{:S(2)}) collective-permute-start(bf16[2,128,512]{2,1,0:T(8,128)(2,1)S(1)} %collective-permute-done.9.refs_4_), channel_id=1, source_target_pairs={{0,4},{1,5},{2,6},{3,7},{4,8},{5,9},{6,10},{7,11},{8,12},{9,13},{1... | collective-permute-start | bytes 786440 | tf_op jit(solution)/shard_map/ppermute | solution.py:293
  35.3 10.7 %collective-permute-start.22 = (bf16[2,128,512]{2,1,0:T(8,128)(2,1)S(1)}, bf16[2,128,512]{2,1,0:T(8,128)(2,1)S(1)}, u32[]{:S(2)}, u32[]{:S(2)}) collective-permute-start(bf16[2,128,512]{2,1,0:T(8,128)(2,1)S(1)} %collective-permute-done.9.refs_4_), channel_id=1, source_target_pairs={{0,2},{1,3},{2,0},{3,1},{4,6},{5,7},{6,4},{7,5},{8,10},{9,11},{10,... | collective-permute-start | bytes 786440 | tf_op jit(solution)/shard_map/ppermute | solution.py:293
  35.9 12.2 %collective-permute-start.18 = (bf16[2,128,512]{2,1,0:T(8,128)(2,1)S(1)}, bf16[2,128,512]{2,1,0:T(8,128)(2,1)S(1)}, u32[]{:S(2)}, u32[]{:S(2)}) collective-permute-start(bf16[2,128,512]{2,1,0:T(8,128)(2,1)S(1)} %collective-permute-done.2.refs_4_), channel_id=1, source_target_pairs={{0,1},{1,0},{2,3},{3,2},{4,5},{5,4},{6,7},{7,6},{8,9},{9,8},{10,11... | collective-permute-start | bytes 786440 | tf_op jit(solution)/shard_map/ppermute | solution.py:293
  35.9 13.0 %collective-permute-start.17 = (bf16[2,128,512]{2,1,0:T(8,128)(2,1)S(1)}, bf16[2,128,512]{2,1,0:T(8,128)(2,1)S(1)}, u32[]{:S(2)}, u32[]{:S(2)}) collective-permute-start(bf16[2,128,512]{2,1,0:T(8,128)(2,1)S(1)} %collective-permute-done.3.refs_2_), channel_id=1, source_target_pairs={{0,1},{1,0},{2,3},{3,2},{4,5},{5,4},{6,7},{7,6},{8,9},{9,8},{10,11... | collective-permute-start | bytes 786440 | tf_op jit(solution)/shard_map/ppermute | solution.py:293
  36.4 12.8 %collective-permute-start.4 = (bf16[2,128,512]{2,1,0:T(8,128)(2,1)S(1)}, bf16[2,128,512]{2,1,0:T(8,128)(2,1)S(1)}, u32[]{:S(2)}, u32[]{:S(2)}) collective-permute-start(bf16[2,128,512]{2,1,0:T(8,128)(2,1)S(1)} %collective-permute-done.2.refs_4_), channel_id=1, source_target_pairs={{0,4},{1,5},{2,6},{3,7},{4,8},{5,9},{6,10},{7,11},{8,12},{9,13},{1... | collective-permute-start | bytes 786440 | tf_op jit(solution)/shard_map/ppermute | solution.py:293
  37.0 9.0 %copy-start.1 = (bf16[2,128,512]{2,1,0:T(8,128)(2,1)S(1)}, bf16[2,128,512]{2,1,0:T(8,128)(2,1)}, u32[]{:S(2)}) copy-start(bf16[2,128,512]{2,1,0:T(8,128)(2,1)} %shard_map.65.refs_2_) | copy-start | bytes 786436
  46.0 7.0 %collective-permute-start.14 = (bf16[2,128,512]{2,1,0:T(8,128)(2,1)S(1)}, bf16[2,128,512]{2,1,0:T(8,128)(2,1)S(1)}, u32[]{:S(2)}, u32[]{:S(2)}) collective-permute-start(bf16[2,128,512]{2,1,0:T(8,128)(2,1)S(1)} %collective-permute-done.2.refs_4_), channel_id=1, source_target_pairs={{0,2},{1,3},{2,0},{3,1},{4,6},{5,7},{6,4},{7,5},{8,10},{9,11},{10,... | collective-permute-start | bytes 786440 | tf_op jit(solution)/shard_map/ppermute | solution.py:293
  46.0 7.0 %collective-permute-start.24 = (bf16[2,128,512]{2,1,0:T(8,128)(2,1)S(1)}, bf16[2,128,512]{2,1,0:T(8,128)(2,1)S(1)}, u32[]{:S(2)}, u32[]{:S(2)}) collective-permute-start(bf16[2,128,512]{2,1,0:T(8,128)(2,1)S(1)} %collective-permute-done.11.refs_4_), channel_id=1, source_target_pairs={{0,1},{1,0},{2,3},{3,2},{4,5},{5,4},{6,7},{7,6},{8,9},{9,8},{10,11... | collective-permute-start | bytes 786440 | tf_op jit(solution)/shard_map/ppermute | solution.py:293
  46.0 4.9 %copy-start = (bf16[2,128,512]{2,1,0:T(8,128)(2,1)S(1)}, bf16[2,128,512]{2,1,0:T(8,128)(2,1)}, u32[]{:S(2)}) copy-start(bf16[2,128,512]{2,1,0:T(8,128)(2,1)} %shard_map.64.refs_2_) | copy-start | bytes 786436
  48.1 8.9 %collective-permute-start.12 = (bf16[2,128,512]{2,1,0:T(8,128)(2,1)S(1)}, bf16[2,128,512]{2,1,0:T(8,128)(2,1)S(1)}, u32[]{:S(2)}, u32[]{:S(2)}) collective-permute-start(bf16[2,128,512]{2,1,0:T(8,128)(2,1)S(1)} %collective-permute-done.7.refs_4_), channel_id=1, source_target_pairs={{0,12},{1,13},{2,14},{3,15},{4,0},{5,1},{6,2},{7,3},{8,4},{9,5},{1... | collective-permute-start | bytes 786440 | tf_op jit(solution)/shard_map/ppermute | solution.py:293
  48.9 10.8 %collective-permute-start.23 = (bf16[2,128,512]{2,1,0:T(8,128)(2,1)S(1)}, bf16[2,128,512]{2,1,0:T(8,128)(2,1)S(1)}, u32[]{:S(2)}, u32[]{:S(2)}) collective-permute-start(bf16[2,128,512]{2,1,0:T(8,128)(2,1)S(1)} %collective-permute-done.22.refs_2_), channel_id=1, source_target_pairs={{0,1},{1,0},{2,3},{3,2},{4,5},{5,4},{6,7},{7,6},{8,9},{9,8},{10,11... | collective-permute-start | bytes 786440 | tf_op jit(solution)/shard_map/ppermute | solution.py:293
  49.2 8.8 %collective-permute-start.5 = (bf16[2,128,512]{2,1,0:T(8,128)(2,1)S(1)}, bf16[2,128,512]{2,1,0:T(8,128)(2,1)S(1)}, u32[]{:S(2)}, u32[]{:S(2)}) collective-permute-start(bf16[2,128,512]{2,1,0:T(8,128)(2,1)S(1)} %collective-permute-done.4.refs_4_), channel_id=1, source_target_pairs={{0,2},{1,3},{2,0},{3,1},{4,6},{5,7},{6,4},{7,5},{8,10},{9,11},{10,... | collective-permute-start | bytes 786440 | tf_op jit(solution)/shard_map/ppermute | solution.py:293
  53.0 8.4 %collective-permute-start.16 = (bf16[2,128,512]{2,1,0:T(8,128)(2,1)S(1)}, bf16[2,128,512]{2,1,0:T(8,128)(2,1)S(1)}, u32[]{:S(2)}, u32[]{:S(2)}) collective-permute-start(bf16[2,128,512]{2,1,0:T(8,128)(2,1)S(1)} %collective-permute-done.4.refs_4_), channel_id=1, source_target_pairs={{0,1},{1,0},{2,3},{3,2},{4,5},{5,4},{6,7},{7,6},{8,9},{9,8},{10,11... | collective-permute-start | bytes 786440 | tf_op jit(solution)/shard_map/ppermute | solution.py:293
  53.0 8.4 %collective-permute-start.15 = (bf16[2,128,512]{2,1,0:T(8,128)(2,1)S(1)}, bf16[2,128,512]{2,1,0:T(8,128)(2,1)S(1)}, u32[]{:S(2)}, u32[]{:S(2)}) collective-permute-start(bf16[2,128,512]{2,1,0:T(8,128)(2,1)S(1)} %collective-permute-done.14.refs_2_), channel_id=1, source_target_pairs={{0,1},{1,0},{2,3},{3,2},{4,5},{5,4},{6,7},{7,6},{8,9},{9,8},{10,11... | collective-permute-start | bytes 786440 | tf_op jit(solution)/shard_map/ppermute | solution.py:293
  57.0 6.1 %collective-permute-start.13 = (bf16[2,128,512]{2,1,0:T(8,128)(2,1)S(1)}, bf16[2,128,512]{2,1,0:T(8,128)(2,1)S(1)}, u32[]{:S(2)}, u32[]{:S(2)}) collective-permute-start(bf16[2,128,512]{2,1,0:T(8,128)(2,1)S(1)} %collective-permute-done.12.refs_5_), channel_id=1, source_target_pairs={{0,1},{1,0},{2,3},{3,2},{4,5},{5,4},{6,7},{7,6},{8,9},{9,8},{10,11... | collective-permute-start | bytes 786440 | tf_op jit(solution)/shard_map/ppermute | solution.py:293
  58.0 5.2 %collective-permute-start.6 = (bf16[2,128,512]{2,1,0:T(8,128)(2,1)S(1)}, bf16[2,128,512]{2,1,0:T(8,128)(2,1)S(1)}, u32[]{:S(2)}, u32[]{:S(2)}) collective-permute-start(bf16[2,128,512]{2,1,0:T(8,128)(2,1)S(1)} %collective-permute-done.5.refs_3_), channel_id=1, source_target_pairs={{0,1},{1,0},{2,3},{3,2},{4,5},{5,4},{6,7},{7,6},{8,9},{9,8},{10,11... | collective-permute-start | bytes 786440 | tf_op jit(solution)/shard_map/ppermute | solution.py:293

commit v4 on v3

--- a/solution.py
+++ b/solution.py
@@ -98,26 +98,31 @@
     )(block_ids, query_u, query_v)
 
 
-def load_kernel(*refs):
-    half = len(refs) // 2
+def load_kernel(counts_ref, *refs):
+    half = (len(refs) - 1) // 2
     sems = refs[-1]
-    copies = [pltpu.make_async_copy(refs[i], refs[half + i], sems.at[i]) for i in range(half)]
+    live_ref = refs[half]
+    copies = [pltpu.make_async_copy(refs[i], refs[half + 1 + i], sems.at[i]) for i in range(half)]
     for copy in copies:
         copy.start()
+    live_ref[...] = jnp.full(live_ref.shape, counts_ref[0], jnp.int32)
     for copy in copies:
         copy.wait()
 
 
-def load(*arrays):
+def load(counts, *arrays):
+    outs = [jax.ShapeDtypeStruct((8, LANES), jnp.int32)]
+    outs += [jax.ShapeDtypeStruct(one.shape, one.dtype) for one in arrays]
     return pl.pallas_call(
         load_kernel,
-        out_shape=tuple(jax.ShapeDtypeStruct(one.shape, one.dtype) for one in arrays),
-        in_specs=[pl.BlockSpec(memory_space=pltpu.HBM)] * len(arrays),
-        out_specs=(pl.BlockSpec(memory_space=pltpu.VMEM),) * len(arrays),
+        out_shape=tuple(outs),
+        in_specs=[pl.BlockSpec(memory_space=pltpu.SMEM)]
+        + [pl.BlockSpec(memory_space=pltpu.HBM)] * len(arrays),
+        out_specs=(pl.BlockSpec(memory_space=pltpu.VMEM),) * len(outs),
         scratch_shapes=[pltpu.SemaphoreType.DMA((len(arrays),))],
         compiler_params=pltpu.CompilerParams(vmem_limit_bytes=42 << 20),
         name="load",
-    )(*arrays)
+    )(counts, *arrays)
 
 
 def split_dot(left, right):
@@ -145,11 +150,11 @@
         return [refs.pop(0) for _ in range(n)]
 
     x_refs = take(2)
-    counts_hbm = take(1)[0] if last else None
+    live_ref = take(1)[0] if last else None
     pieces = [[take(2) for _ in g["where"]] for g in groups]
     starts = [take(3) if g["carry"] else None for g in groups]
     outs = take(1) if last else None
-    product, counts_ref = take(2) if last else (None, None)
+    product = take(1)[0] if last else None
     totals = [take(3) for _ in groups]
     w, sems = take(2)
     me = lax.axis_index("tok")
@@ -168,9 +173,6 @@
                 copy.start()
             copies.append((these, pl.ds(start, 2 * rows)))
             slot += 1
-    if last:
-        live = pltpu.make_async_copy(counts_hbm, counts_ref, sems.at[2 * slot])
-        live.start()
     tiles = w.shape[2] // TILE
     slot = 0
     for g, start, total in zip(groups, starts, totals):
@@ -210,14 +212,13 @@
         norm = split_dot(norm, chooser)[:1]
         raw = split_dot(product[...], chooser)
         scaled = raw / jnp.sqrt(norm + 1e-06)
-        live.wait()
         token = lax.broadcasted_iota(jnp.int32, scaled.shape, 0)
-        scaled = jnp.where(token < counts_ref[0], scaled, 0.0)
+        scaled = jnp.where(token < live_ref[:1], scaled, 0.0)
         outs[0][...] = scaled.T[: columns // RANK]
 
 
-def stage(shape, groups, gradients, activations, counts=None):
-    last = counts is not None
+def stage(shape, groups, gradients, activations, live=None):
+    last = live is not None
     rows, columns = groups[0]["arrays"][0][0].shape[1:]
     tokens = gradients.shape[1]
     slots = sum(len(g["where"]) for g in groups)
@@ -226,8 +227,8 @@
     vmem = pl.BlockSpec(memory_space=pltpu.VMEM)
     args, specs = [gradients, activations], [vmem, vmem]
     if last:
-        args.append(counts)
-        specs.append(anywhere)
+        args.append(live)
+        specs.append(vmem)
     for g in groups:
         for pair in g["arrays"]:
             args += pair
@@ -244,7 +245,7 @@
     if last:
         out_shape = jax.ShapeDtypeStruct((columns // RANK, tokens), jnp.float32)
         out_specs = vmem
-        scratch = [pltpu.VMEM(*sums[0]), pltpu.SMEM(counts.shape, jnp.int32)] + [pltpu.VMEM(*one) for one in sums] * len(groups)
+        scratch = [pltpu.VMEM(*sums[0])] + [pltpu.VMEM(*one) for one in sums] * len(groups)
     else:
         out_shape = tuple(jax.ShapeDtypeStruct(*one) for one in sums) * len(groups)
         out_specs = (vmem,) * len(out_shape)
@@ -263,7 +264,7 @@
         scratch_shapes=scratch
         + [
             pltpu.VMEM((2, slots * 2 * rows, columns), jnp.bfloat16),
-            pltpu.SemaphoreType.DMA((2 * slots + 1,)),
+            pltpu.SemaphoreType.DMA((2 * slots,)),
         ],
         input_output_aliases=aliases,
         compiler_params=pltpu.CompilerParams(vmem_limit_bytes=(24 if last else 16) << 20),
@@ -304,7 +305,7 @@
                     fed = after(fed, h[(da - 1, 1)])
                 h[(da + 1, 0)] = move(fed, 1, 0, 0)
             if da == outer - 1 and layer == 1:
-                fed = after(h[(0, 1)], h[(da, 0)])
+                fed = after(h[(0, 1)], have[0][(da, 0)])
                 h[(da, 1)] = move(fed, -1, 0, 0)
             else:
                 h[(da, 1)] = move(h[(da, 0)], 0, 1, 0)
@@ -312,7 +313,7 @@
         for key, piece in have[layer].items():
             pairs[layer][key] = [piece, move(piece, 0, 0, 1)]
 
-    gradients, activations = load(gradients, activations)
+    live, gradients, activations = load(counts, gradients, activations)
 
     def group(layer, keys, carry):
         return dict(layer=layer, where=keys, arrays=[pairs[layer][key] for key in keys], carry=carry)
@@ -323,11 +324,7 @@
         for layer in range(2):
             carry[layer] = stage(shape, [group(layer, keys, carry[layer])], gradients, activations)
     scores = stage(
-        shape,
-        [group(layer, [(outer - 1, 1)], carry[layer]) for layer in range(2)],
-        gradients,
-        activations,
-        counts=counts,
+        shape, [group(layer, [(outer - 1, 1)], carry[layer]) for layer in range(2)], gradients, activations, live=live
     )
     return scores.T
 

time: 67.2 us -> 72.2 us (1.074)
  waiting for transfers between devices: 27.6 us -> 32.8 us
    ppermute x30, waiting for transfers between devices: 27.6 us -> 32.8 us  [move(): return lax.ppermute(value, 'tok', steps)]
  transfers between devices with their start and end apart: 30 -> 30, of which waited for: 9 -> 11; matrix products, arithmetic and copies ran while one was open for 0% -> 0% of each run, Pallas kernels for 25% -> 24%
where the time goes in v4:
time: 72.2 us; the launch traced here: 72 us
  waiting for transfers between devices  32.8 us (45%)
  Pallas kernels  23 us (32%)
  starting transfers between devices  15.2 us (21%)
  between operations  0.99 us (1%)
    ppermute x30, waiting for transfers between devices, move(): return lax.ppermute(value, 'tok', steps)  32.8 us
    ppermute x30, starting transfers between devices, move(): return lax.ppermute(value, 'tok', steps)  15.2 us
    pallas_call x7, Pallas kernels, stage(): pl.pallas_call(functools.partial(stage_kernel, cfg), out_shape=out_shape,...  14.8 us
    pallas_call x2, Pallas kernels, pick(): pl.pallas_call(functools.partial(pick_kernel, layer), out_shape=jax.Shape...  4.18 us
    pallas_call x1, Pallas kernels, load(): pl.pallas_call(load_kernel, out_shape=tuple(outs), in_specs=[pl.BlockSpec...  4.08 us
  transfers between devices with their start and end apart: 30, of which 11 were waited for; matrix products, arithmetic and copies ran while one was open for 0% of the time, Pallas kernels for 24%

profile of v4, /device:TPU:0, one launch (start us, length us, event | category | flops | bytes accessed | tf_op | source)
XLA Modules:
  0.0 72.0 jit_solution(9605265116857743200)
XLA Ops:
  0.0 2.1 %shard_map.65.refs_2_ = bf16[2,128,512]{2,1,0:T(8,128)(2,1)} custom-call(s32[2,16]{1,0:T(2,128)} %ids_hbm.3, bf16[2,128,1024]{2,1,0:T(8,128)(2,1)} %u_ref.3, bf16[2,128,1024]{2,1,0:T(8,128)(2,1)} %v_ref.3), custom_call_target="tpu_custom_call" | custom-call | flops 262144 | bytes 786432 | tf_op jit(solution)/shard_map/pallas_call | solution.py:84
  2.1 3.0 %collective-permute-start.7 = (bf16[2,128,512]{2,1,0:T(8,128)(2,1)}, bf16[2,128,512]{2,1,0:T(8,128)(2,1)S(1)}, u32[]{:S(2)}, u32[]{:S(2)}) collective-permute-start(bf16[2,128,512]{2,1,0:T(8,128)(2,1)} %shard_map.65.refs_2_), channel_id=1, source_target_pairs={{0,2},{1,3},{2,0},{3,1},{4,6},{5,7},{6,4},{7,5},{8,10},{9,11},{10,... | collective-permute-start | bytes 786440 | tf_op jit(solution)/shard_map/ppermute | solution.py:294
  5.1 1.6 %collective-permute-start.18 = (bf16[2,128,512]{2,1,0:T(8,128)(2,1)}, bf16[2,128,512]{2,1,0:T(8,128)(2,1)S(1)}, u32[]{:S(2)}, u32[]{:S(2)}) collective-permute-start(bf16[2,128,512]{2,1,0:T(8,128)(2,1)} %shard_map.65.refs_2_), channel_id=1, source_target_pairs={{0,4},{1,5},{2,6},{3,7},{4,8},{5,9},{6,10},{7,11},{8,12},{9,13},{1... | collective-permute-start | bytes 786440 | tf_op jit(solution)/shard_map/ppermute | solution.py:294
  6.7 2.1 %shard_map.64.refs_2_ = bf16[2,128,512]{2,1,0:T(8,128)(2,1)} custom-call(s32[2,16]{1,0:T(2,128)} %ids_hbm.3, bf16[2,128,1024]{2,1,0:T(8,128)(2,1)} %u_ref.3, bf16[2,128,1024]{2,1,0:T(8,128)(2,1)} %v_ref.3), custom_call_target="tpu_custom_call" | custom-call | flops 262144 | bytes 786432 | tf_op jit(solution)/shard_map/pallas_call | solution.py:84
  8.8 1.6 %collective-permute-start = (bf16[2,128,512]{2,1,0:T(8,128)(2,1)}, bf16[2,128,512]{2,1,0:T(8,128)(2,1)S(1)}, u32[]{:S(2)}, u32[]{:S(2)}) collective-permute-start(bf16[2,128,512]{2,1,0:T(8,128)(2,1)} %shard_map.64.refs_2_), channel_id=1, source_target_pairs={{0,4},{1,5},{2,6},{3,7},{4,8},{5,9},{6,10},{7,11},{8,12},{9,13},{1... | collective-permute-start | bytes 786440 | tf_op jit(solution)/shard_map/ppermute | solution.py:294
  10.4 0.5 collective-permute-start.1
  11.0 0.0 collective-permute-start.27
  11.0 0.7 collective-permute-done.7.refs_4_
  11.7 4.7 %collective-permute-done.18.refs_6_ = bf16[2,128,512]{2,1,0:T(8,128)(2,1)S(1)} collective-permute-done((bf16[2,128,512]{2,1,0:T(8,128)(2,1)}, bf16[2,128,512]{2,1,0:T(8,128)(2,1)S(1)}, u32[]{:S(2)}, u32[]{:S(2)}) %collective-permute-start.18) | collective-permute-done | bytes 262176 | tf_op jit(solution)/shard_map/ppermute | solution.py:294
  16.3 4.3 %collective-permute-done.refs_6_ = bf16[2,128,512]{2,1,0:T(8,128)(2,1)S(1)} collective-permute-done((bf16[2,128,512]{2,1,0:T(8,128)(2,1)}, bf16[2,128,512]{2,1,0:T(8,128)(2,1)S(1)}, u32[]{:S(2)}, u32[]{:S(2)}) %collective-permute-start) | collective-permute-done | bytes 262176 | tf_op jit(solution)/shard_map/ppermute | solution.py:294
  20.6 0.0 collective-permute-done.1.refs_4_
  20.6 0.5 collective-permute-start.22
  21.2 0.0 collective-permute-done.27.refs_3_
  21.2 1.3 %collective-permute-start.2 = (bf16[2,128,512]{2,1,0:T(8,128)(2,1)S(1)}, bf16[2,128,512]{2,1,0:T(8,128)(2,1)S(1)}, u32[]{:S(2)}, u32[]{:S(2)}) collective-permute-start(bf16[2,128,512]{2,1,0:T(8,128)(2,1)S(1)} %collective-permute-done.refs_6_), channel_id=1, source_target_pairs={{0,4},{1,5},{2,6},{3,7},{4,8},{5,9},{6,10},{7,11},{8,12},{9,13},{1... | collective-permute-start | bytes 786440 | tf_op jit(solution)/shard_map/ppermute | solution.py:294
  22.4 1.5 %collective-permute-start.3 = (bf16[2,128,512]{2,1,0:T(8,128)(2,1)S(1)}, bf16[2,128,512]{2,1,0:T(8,128)(2,1)S(1)}, u32[]{:S(2)}, u32[]{:S(2)}) collective-permute-start(bf16[2,128,512]{2,1,0:T(8,128)(2,1)S(1)} %collective-permute-done.refs_6_), channel_id=1, source_target_pairs={{0,2},{1,3},{2,0},{3,1},{4,6},{5,7},{6,4},{7,5},{8,10},{9,11},{10,... | collective-permute-start | bytes 786440 | tf_op jit(solution)/shard_map/ppermute | solution.py:294
  23.9 7.7 %collective-permute-done.19.refs_4_ = bf16[2,128,512]{2,1,0:T(8,128)(2,1)S(1)} collective-permute-done((bf16[2,128,512]{2,1,0:T(8,128)(2,1)S(1)}, bf16[2,128,512]{2,1,0:T(8,128)(2,1)S(1)}, u32[]{:S(2)}, u32[]{:S(2)}) %collective-permute-start.19) | collective-permute-done | bytes 262176 | tf_op jit(solution)/shard_map/ppermute | solution.py:294
  31.6 0.5 collective-permute-start.16
  32.1 2.9 %collective-permute-done.2.refs_4_ = bf16[2,128,512]{2,1,0:T(8,128)(2,1)S(1)} collective-permute-done((bf16[2,128,512]{2,1,0:T(8,128)(2,1)S(1)}, bf16[2,128,512]{2,1,0:T(8,128)(2,1)S(1)}, u32[]{:S(2)}, u32[]{:S(2)}) %collective-permute-start.2) | collective-permute-done | bytes 262176 | tf_op jit(solution)/shard_map/ppermute | solution.py:294
  35.1 0.5 collective-permute-start.25
  35.6 0.0 collective-permute-done.17.refs_7_
  35.6 0.2 collective-permute-start.4
  35.7 0.7 collective-permute-start.20
  36.4 0.1 collective-permute-done.26.refs_5_
  36.6 0.1 collective-permute-start.14
  36.7 0.2 collective-permute-done.25.refs_3_
  37.0 0.1 collective-permute-start.13
  37.7 4.1 %load.1 = (s32[8,128]{1,0:T(8,128)S(1)}, bf16[2,640,2048]{2,1,0:T(8,128)(2,1)S(1)}, bf16[2,640,2048]{2,1,0:T(8,128)(2,1)S(1)}) custom-call(s32[1]{0:T(128)S(6)} %copy.31.counts_ref, bf16[2,640,2048]{2,1,0:T(8,128)(2,1)} %refs_0_.1, bf16[2,640,2048]{2,1,0:T(8,128)(2,1)} %refs_1_.1), custom_call_target="tpu_custom_call" | custom-call | tf_op jit(solution)/shard_map/load/pallas_call | solution.py:116
  41.8 4.7 %collective-permute-done.23.refs_4_ = bf16[2,128,512]{2,1,0:T(8,128)(2,1)S(1)} collective-permute-done((bf16[2,128,512]{2,1,0:T(8,128)(2,1)S(1)}, bf16[2,128,512]{2,1,0:T(8,128)(2,1)S(1)}, u32[]{:S(2)}, u32[]{:S(2)}) %collective-permute-start.23) | collective-permute-done | bytes 262176 | tf_op jit(solution)/shard_map/ppermute | solution.py:294
  46.5 0.7 %collective-permute-start.10 = (bf16[2,128,512]{2,1,0:T(8,128)(2,1)S(1)}, bf16[2,128,512]{2,1,0:T(8,128)(2,1)S(1)}, u32[]{:S(2)}, u32[]{:S(2)}) collective-permute-start(bf16[2,128,512]{2,1,0:T(8,128)(2,1)S(1)} %collective-permute-done.2.refs_4_), channel_id=1, source_target_pairs={{0,2},{1,3},{2,0},{3,1},{4,6},{5,7},{6,4},{7,5},{8,10},{9,11},{10,... | collective-permute-start | bytes 786440 | tf_op jit(solution)/shard_map/ppermute | solution.py:294
  47.3 4.0 %collective-permute-done.4.refs_4_ = bf16[2,128,512]{2,1,0:T(8,128)(2,1)S(1)} collective-permute-done((bf16[2,128,512]{2,1,0:T(8,128)(2,1)S(1)}, bf16[2,128,512]{2,1,0:T(8,128)(2,1)S(1)}, u32[]{:S(2)}, u32[]{:S(2)}) %collective-permute-start.4) | collective-permute-done | bytes 262176 | tf_op jit(solution)/shard_map/ppermute | solution.py:294
  51.2 0.0 collective-permute-start.24
  51.3 2.1 %shard_map.69 = (f32[640,512]{1,0:T(8,128)S(1)}, f32[640,512]{1,0:T(8,128)S(1)}, f32[4,256,256]{2,1,0:T(8,128)S(1)}) custom-call(bf16[2,640,2048]{2,1,0:T(8,128)(2,1)S(1)} %get-tuple-element.31.refs_0_, bf16[2,640,2048]{2,1,0:T(8,128)(2,1)S(1)} %get-tuple-element.32.refs_1_, bf16[2,128,512]{2,1,0:T(8,128)(2,1)S(1)} %copy-done.1, ...), custom_call_target="tpu_custom_call" | custom-call | flops 1811939328 | bytes 3538944 | tf_op jit(solution)/shard_map/pallas_call | solution.py:259
  53.4 0.0 collective-permute-done.20.refs_2_
  53.4 0.2 collective-permute-start.8
  53.6 0.0 collective-permute-done.14.refs_5_
  53.6 0.8 %collective-permute-start.5 = (bf16[2,128,512]{2,1,0:T(8,128)(2,1)S(1)}, bf16[2,128,512]{2,1,0:T(8,128)(2,1)S(1)}, u32[]{:S(2)}, u32[]{:S(2)}) collective-permute-start(bf16[2,128,512]{2,1,0:T(8,128)(2,1)S(1)} %collective-permute-done.4.refs_4_), channel_id=1, source_target_pairs={{0,2},{1,3},{2,0},{3,1},{4,6},{5,7},{6,4},{7,5},{8,10},{9,11},{10,... | collective-permute-start | bytes 786440 | tf_op jit(solution)/shard_map/ppermute | solution.py:294
  54.4 0.2 collective-permute-start.21
  54.6 2.1 %shard_map.66 = (f32[640,512]{1,0:T(8,128)S(1)}, f32[640,512]{1,0:T(8,128)S(1)}, f32[4,256,256]{2,1,0:T(8,128)S(1)}) custom-call(bf16[2,640,2048]{2,1,0:T(8,128)(2,1)S(1)} %get-tuple-element.31.refs_0_, bf16[2,640,2048]{2,1,0:T(8,128)(2,1)S(1)} %get-tuple-element.32.refs_1_, bf16[2,128,512]{2,1,0:T(8,128)(2,1)S(1)} %copy-done, ...), custom_call_target="tpu_custom_call" | custom-call | flops 1811939328 | bytes 3538944 | tf_op jit(solution)/shard_map/pallas_call | solution.py:259
  56.7 0.3 collective-permute-start.12
  57.0 0.2 collective-permute-start.11
  57.3 1.7 %shard_map.70 = (f32[640,512]{1,0:T(8,128)S(1)}, f32[640,512]{1,0:T(8,128)S(1)}, f32[4,256,256]{2,1,0:T(8,128)S(1)}) custom-call(bf16[2,640,2048]{2,1,0:T(8,128)(2,1)S(1)} %get-tuple-element.31.refs_0_, bf16[2,640,2048]{2,1,0:T(8,128)(2,1)S(1)} %get-tuple-element.32.refs_1_, ...), custom_call_target="tpu_custom_call", output_to_operand_aliasing={{0}: (6, {}), {1}: (7, {}), {2}: (8, {})} | custom-call | flops 1207959552 | bytes 2359296 | tf_op jit(solution)/shard_map/pallas_call | solution.py:259
  59.0 3.3 %collective-permute-done.8.refs_5_ = bf16[2,128,512]{2,1,0:T(8,128)(2,1)S(1)} collective-permute-done((bf16[2,128,512]{2,1,0:T(8,128)(2,1)S(1)}, bf16[2,128,512]{2,1,0:T(8,128)(2,1)S(1)}, u32[]{:S(2)}, u32[]{:S(2)}) %collective-permute-start.8) | collective-permute-done | bytes 262176 | tf_op jit(solution)/shard_map/ppermute | solution.py:294
  62.3 0.1 collective-permute-done.5.refs_3_
  62.4 0.4 collective-permute-start.6
  62.8 1.7 %shard_map.67 = (f32[640,512]{1,0:T(8,128)S(1)}, f32[640,512]{1,0:T(8,128)S(1)}, f32[4,256,256]{2,1,0:T(8,128)S(1)}) custom-call(bf16[2,640,2048]{2,1,0:T(8,128)(2,1)S(1)} %get-tuple-element.31.refs_0_, bf16[2,640,2048]{2,1,0:T(8,128)(2,1)S(1)} %get-tuple-element.32.refs_1_, ...), custom_call_target="tpu_custom_call", output_to_operand_aliasing={{0}: (6, {}), {1}: (7, {}), {2}: (8, {})} | custom-call | flops 1207959552 | bytes 2359296 | tf_op jit(solution)/shard_map/pallas_call | solution.py:259
  64.5 1.8 %shard_map.71 = (f32[640,512]{1,0:T(8,128)S(1)}, f32[640,512]{1,0:T(8,128)S(1)}, f32[4,256,256]{2,1,0:T(8,128)S(1)}) custom-call(bf16[2,640,2048]{2,1,0:T(8,128)(2,1)S(1)} %get-tuple-element.31.refs_0_, bf16[2,640,2048]{2,1,0:T(8,128)(2,1)S(1)} %get-tuple-element.32.refs_1_, ...), custom_call_target="tpu_custom_call", output_to_operand_aliasing={{0}: (6, {}), {1}: (7, {}), {2}: (8, {})} | custom-call | flops 1207959552 | bytes 2359296 | tf_op jit(solution)/shard_map/pallas_call | solution.py:259
  66.3 1.7 %shard_map.68 = (f32[640,512]{1,0:T(8,128)S(1)}, f32[640,512]{1,0:T(8,128)S(1)}, f32[4,256,256]{2,1,0:T(8,128)S(1)}) custom-call(bf16[2,640,2048]{2,1,0:T(8,128)(2,1)S(1)} %get-tuple-element.31.refs_0_, bf16[2,640,2048]{2,1,0:T(8,128)(2,1)S(1)} %get-tuple-element.32.refs_1_, ...), custom_call_target="tpu_custom_call", output_to_operand_aliasing={{0}: (6, {}), {1}: (7, {}), {2}: (8, {})} | custom-call | flops 1207959552 | bytes 2359296 | tf_op jit(solution)/shard_map/pallas_call | solution.py:259
  68.1 3.7 %shard_map.72 = f32[64,640]{1,0:T(8,128)} custom-call(bf16[2,640,2048]{2,1,0:T(8,128)(2,1)S(1)} %get-tuple-element.31.refs_0_, bf16[2,640,2048]{2,1,0:T(8,128)(2,1)S(1)} %get-tuple-element.32.refs_1_, s32[8,128]{1,0:T(8,128)S(1)} %get-tuple-element.33.refs_2_, bf16[2,128,512]{2,1,0:T(8,128)(2,1)S(1)} %collective-permute-done.5.refs_3_, ...), custom_call_target="tpu_custom_call" | custom-call | flops 1207959552 | bytes 2359296 | tf_op jit(solution)/shard_map/pallas_call | solution.py:259
  (26 shorter events, 0.1 us)
Async XLA Ops:
  2.1 8.9 %copy-start.1 = (bf16[2,128,512]{2,1,0:T(8,128)(2,1)S(1)}, bf16[2,128,512]{2,1,0:T(8,128)(2,1)}, u32[]{:S(2)}) copy-start(bf16[2,128,512]{2,1,0:T(8,128)(2,1)} %shard_map.65.refs_2_) | copy-start | bytes 786436
  2.1 9.5 %collective-permute-start.7 = (bf16[2,128,512]{2,1,0:T(8,128)(2,1)}, bf16[2,128,512]{2,1,0:T(8,128)(2,1)S(1)}, u32[]{:S(2)}, u32[]{:S(2)}) collective-permute-start(bf16[2,128,512]{2,1,0:T(8,128)(2,1)} %shard_map.65.refs_2_), channel_id=1, source_target_pairs={{0,2},{1,3},{2,0},{3,1},{4,6},{5,7},{6,4},{7,5},{8,10},{9,11},{10,... | collective-permute-start | bytes 786440 | tf_op jit(solution)/shard_map/ppermute | solution.py:294
  5.1 11.2 %collective-permute-start.18 = (bf16[2,128,512]{2,1,0:T(8,128)(2,1)}, bf16[2,128,512]{2,1,0:T(8,128)(2,1)S(1)}, u32[]{:S(2)}, u32[]{:S(2)}) collective-permute-start(bf16[2,128,512]{2,1,0:T(8,128)(2,1)} %shard_map.65.refs_2_), channel_id=1, source_target_pairs={{0,4},{1,5},{2,6},{3,7},{4,8},{5,9},{6,10},{7,11},{8,12},{9,13},{1... | collective-permute-start | bytes 786440 | tf_op jit(solution)/shard_map/ppermute | solution.py:294
  8.8 11.8 %collective-permute-start = (bf16[2,128,512]{2,1,0:T(8,128)(2,1)}, bf16[2,128,512]{2,1,0:T(8,128)(2,1)S(1)}, u32[]{:S(2)}, u32[]{:S(2)}) collective-permute-start(bf16[2,128,512]{2,1,0:T(8,128)(2,1)} %shard_map.64.refs_2_), channel_id=1, source_target_pairs={{0,4},{1,5},{2,6},{3,7},{4,8},{5,9},{6,10},{7,11},{8,12},{9,13},{1... | collective-permute-start | bytes 786440 | tf_op jit(solution)/shard_map/ppermute | solution.py:294
  10.4 10.2 %collective-permute-start.1 = (bf16[2,128,512]{2,1,0:T(8,128)(2,1)}, bf16[2,128,512]{2,1,0:T(8,128)(2,1)S(1)}, u32[]{:S(2)}, u32[]{:S(2)}) collective-permute-start(bf16[2,128,512]{2,1,0:T(8,128)(2,1)} %shard_map.64.refs_2_), channel_id=1, source_target_pairs={{0,2},{1,3},{2,0},{3,1},{4,6},{5,7},{6,4},{7,5},{8,10},{9,11},{10,... | collective-permute-start | bytes 786440 | tf_op jit(solution)/shard_map/ppermute | solution.py:294
  11.0 10.2 %collective-permute-start.27 = (bf16[2,128,512]{2,1,0:T(8,128)(2,1)S(1)}, bf16[2,128,512]{2,1,0:T(8,128)(2,1)S(1)}, u32[]{:S(2)}, u32[]{:S(2)}) collective-permute-start(bf16[2,128,512]{2,1,0:T(8,128)(2,1)S(1)} %copy-done.1), channel_id=1, source_target_pairs={{0,1},{1,0},{2,3},{3,2},{4,5},{5,4},{6,7},{7,6},{8,9},{9,8},{10,11... | collective-permute-start | bytes 786440 | tf_op jit(solution)/shard_map/ppermute | solution.py:294
  11.7 10.8 %collective-permute-start.15 = (bf16[2,128,512]{2,1,0:T(8,128)(2,1)}, bf16[2,128,512]{2,1,0:T(8,128)(2,1)S(1)}, u32[]{:S(2)}, u32[]{:S(2)}) collective-permute-start(bf16[2,128,512]{2,1,0:T(8,128)(2,1)} %shard_map.64.refs_2_), channel_id=1, source_target_pairs={{0,1},{1,0},{2,3},{3,2},{4,5},{5,4},{6,7},{7,6},{8,9},{9,8},{10,11... | collective-permute-start | bytes 786440 | tf_op jit(solution)/shard_map/ppermute | solution.py:294
  16.3 7.6 %collective-permute-start.28 = (bf16[2,128,512]{2,1,0:T(8,128)(2,1)S(1)}, bf16[2,128,512]{2,1,0:T(8,128)(2,1)S(1)}, u32[]{:S(2)}, u32[]{:S(2)}) collective-permute-start(bf16[2,128,512]{2,1,0:T(8,128)(2,1)S(1)} %collective-permute-done.7.refs_4_), channel_id=1, source_target_pairs={{0,1},{1,0},{2,3},{3,2},{4,5},{5,4},{6,7},{7,6},{8,9},{9,8},{10,11... | collective-permute-start | bytes 786440 | tf_op jit(solution)/shard_map/ppermute | solution.py:294
  20.6 11.0 %collective-permute-start.19 = (bf16[2,128,512]{2,1,0:T(8,128)(2,1)S(1)}, bf16[2,128,512]{2,1,0:T(8,128)(2,1)S(1)}, u32[]{:S(2)}, u32[]{:S(2)}) collective-permute-start(bf16[2,128,512]{2,1,0:T(8,128)(2,1)S(1)} %collective-permute-done.18.refs_6_), channel_id=1, source_target_pairs={{0,4},{1,5},{2,6},{3,7},{4,8},{5,9},{6,10},{7,11},{8,12},{9,13},{1... | collective-permute-start | bytes 786440 | tf_op jit(solution)/shard_map/ppermute | solution.py:294
  20.6 11.0 %collective-permute-start.22 = (bf16[2,128,512]{2,1,0:T(8,128)(2,1)S(1)}, bf16[2,128,512]{2,1,0:T(8,128)(2,1)S(1)}, u32[]{:S(2)}, u32[]{:S(2)}) collective-permute-start(bf16[2,128,512]{2,1,0:T(8,128)(2,1)S(1)} %collective-permute-done.18.refs_6_), channel_id=1, source_target_pairs={{0,2},{1,3},{2,0},{3,1},{4,6},{5,7},{6,4},{7,5},{8,10},{9,11},{10,... | collective-permute-start | bytes 786440 | tf_op jit(solution)/shard_map/ppermute | solution.py:294
  21.2 13.9 %collective-permute-start.2 = (bf16[2,128,512]{2,1,0:T(8,128)(2,1)S(1)}, bf16[2,128,512]{2,1,0:T(8,128)(2,1)S(1)}, u32[]{:S(2)}, u32[]{:S(2)}) collective-permute-start(bf16[2,128,512]{2,1,0:T(8,128)(2,1)S(1)} %collective-permute-done.refs_6_), channel_id=1, source_target_pairs={{0,4},{1,5},{2,6},{3,7},{4,8},{5,9},{6,10},{7,11},{8,12},{9,13},{1... | collective-permute-start | bytes 786440 | tf_op jit(solution)/shard_map/ppermute | solution.py:294
  22.4 12.6 %collective-permute-start.3 = (bf16[2,128,512]{2,1,0:T(8,128)(2,1)S(1)}, bf16[2,128,512]{2,1,0:T(8,128)(2,1)S(1)}, u32[]{:S(2)}, u32[]{:S(2)}) collective-permute-start(bf16[2,128,512]{2,1,0:T(8,128)(2,1)S(1)} %collective-permute-done.refs_6_), channel_id=1, source_target_pairs={{0,2},{1,3},{2,0},{3,1},{4,6},{5,7},{6,4},{7,5},{8,10},{9,11},{10,... | collective-permute-start | bytes 786440 | tf_op jit(solution)/shard_map/ppermute | solution.py:294
  23.9 11.6 %collective-permute-start.29 = (bf16[2,128,512]{2,1,0:T(8,128)(2,1)S(1)}, bf16[2,128,512]{2,1,0:T(8,128)(2,1)S(1)}, u32[]{:S(2)}, u32[]{:S(2)}) collective-permute-start(bf16[2,128,512]{2,1,0:T(8,128)(2,1)S(1)} %collective-permute-done.18.refs_6_), channel_id=1, source_target_pairs={{0,1},{1,0},{2,3},{3,2},{4,5},{5,4},{6,7},{7,6},{8,9},{9,8},{10,11... | collective-permute-start | bytes 786440 | tf_op jit(solution)/shard_map/ppermute | solution.py:294
  31.6 4.0 %collective-permute-start.17 = (bf16[2,128,512]{2,1,0:T(8,128)(2,1)S(1)}, bf16[2,128,512]{2,1,0:T(8,128)(2,1)S(1)}, u32[]{:S(2)}, u32[]{:S(2)}) collective-permute-start(bf16[2,128,512]{2,1,0:T(8,128)(2,1)S(1)} %collective-permute-done.refs_6_), channel_id=1, source_target_pairs={{0,1},{1,0},{2,3},{3,2},{4,5},{5,4},{6,7},{7,6},{8,9},{9,8},{10,11... | collective-permute-start | bytes 786440 | tf_op jit(solution)/shard_map/ppermute | solution.py:294
  31.6 4.1 %collective-permute-start.16 = (bf16[2,128,512]{2,1,0:T(8,128)(2,1)S(1)}, bf16[2,128,512]{2,1,0:T(8,128)(2,1)S(1)}, u32[]{:S(2)}, u32[]{:S(2)}) collective-permute-start(bf16[2,128,512]{2,1,0:T(8,128)(2,1)S(1)} %collective-permute-done.1.refs_4_), channel_id=1, source_target_pairs={{0,1},{1,0},{2,3},{3,2},{4,5},{5,4},{6,7},{7,6},{8,9},{9,8},{10,11... | collective-permute-start | bytes 786440 | tf_op jit(solution)/shard_map/ppermute | solution.py:294
  35.0 1.5 %collective-permute-start.26 = (bf16[2,128,512]{2,1,0:T(8,128)(2,1)S(1)}, bf16[2,128,512]{2,1,0:T(8,128)(2,1)S(1)}, u32[]{:S(2)}, u32[]{:S(2)}) collective-permute-start(bf16[2,128,512]{2,1,0:T(8,128)(2,1)S(1)} %collective-permute-done.19.refs_4_), channel_id=1, source_target_pairs={{0,1},{1,0},{2,3},{3,2},{4,5},{5,4},{6,7},{7,6},{8,9},{9,8},{10,11... | collective-permute-start | bytes 786440 | tf_op jit(solution)/shard_map/ppermute | solution.py:294
  35.1 1.9 %collective-permute-start.25 = (bf16[2,128,512]{2,1,0:T(8,128)(2,1)S(1)}, bf16[2,128,512]{2,1,0:T(8,128)(2,1)S(1)}, u32[]{:S(2)}, u32[]{:S(2)}) collective-permute-start(bf16[2,128,512]{2,1,0:T(8,128)(2,1)S(1)} %collective-permute-done.22.refs_2_), channel_id=1, source_target_pairs={{0,1},{1,0},{2,3},{3,2},{4,5},{5,4},{6,7},{7,6},{8,9},{9,8},{10,11... | collective-permute-start | bytes 786440 | tf_op jit(solution)/shard_map/ppermute | solution.py:294
  35.6 11.0 %collective-permute-start.23 = (bf16[2,128,512]{2,1,0:T(8,128)(2,1)S(1)}, bf16[2,128,512]{2,1,0:T(8,128)(2,1)S(1)}, u32[]{:S(2)}, u32[]{:S(2)}) collective-permute-start(bf16[2,128,512]{2,1,0:T(8,128)(2,1)S(1)} %collective-permute-done.19.refs_4_), channel_id=1, source_target_pairs={{0,4},{1,5},{2,6},{3,7},{4,8},{5,9},{6,10},{7,11},{8,12},{9,13},{1... | collective-permute-start | bytes 786440 | tf_op jit(solution)/shard_map/ppermute | solution.py:294
  35.6 15.7 %collective-permute-start.4 = (bf16[2,128,512]{2,1,0:T(8,128)(2,1)S(1)}, bf16[2,128,512]{2,1,0:T(8,128)(2,1)S(1)}, u32[]{:S(2)}, u32[]{:S(2)}) collective-permute-start(bf16[2,128,512]{2,1,0:T(8,128)(2,1)S(1)} %collective-permute-done.2.refs_4_), channel_id=1, source_target_pairs={{0,4},{1,5},{2,6},{3,7},{4,8},{5,9},{6,10},{7,11},{8,12},{9,13},{1... | collective-permute-start | bytes 786440 | tf_op jit(solution)/shard_map/ppermute | solution.py:294
  35.7 17.6 %collective-permute-start.20 = (bf16[2,128,512]{2,1,0:T(8,128)(2,1)S(1)}, bf16[2,128,512]{2,1,0:T(8,128)(2,1)S(1)}, u32[]{:S(2)}, u32[]{:S(2)}) collective-permute-start(bf16[2,128,512]{2,1,0:T(8,128)(2,1)S(1)} %collective-permute-done.19.refs_4_), channel_id=1, source_target_pairs={{0,2},{1,3},{2,0},{3,1},{4,6},{5,7},{6,4},{7,5},{8,10},{9,11},{10,... | collective-permute-start | bytes 786440 | tf_op jit(solution)/shard_map/ppermute | solution.py:294
  36.6 17.0 %collective-permute-start.14 = (bf16[2,128,512]{2,1,0:T(8,128)(2,1)S(1)}, bf16[2,128,512]{2,1,0:T(8,128)(2,1)S(1)}, u32[]{:S(2)}, u32[]{:S(2)}) collective-permute-start(bf16[2,128,512]{2,1,0:T(8,128)(2,1)S(1)} %collective-permute-done.2.refs_4_), channel_id=1, source_target_pairs={{0,1},{1,0},{2,3},{3,2},{4,5},{5,4},{6,7},{7,6},{8,9},{9,8},{10,11... | collective-permute-start | bytes 786440 | tf_op jit(solution)/shard_map/ppermute | solution.py:294
  37.0 17.4 %collective-permute-start.13 = (bf16[2,128,512]{2,1,0:T(8,128)(2,1)S(1)}, bf16[2,128,512]{2,1,0:T(8,128)(2,1)S(1)}, u32[]{:S(2)}, u32[]{:S(2)}) collective-permute-start(bf16[2,128,512]{2,1,0:T(8,128)(2,1)S(1)} %collective-permute-done.3.refs_2_), channel_id=1, source_target_pairs={{0,1},{1,0},{2,3},{3,2},{4,5},{5,4},{6,7},{7,6},{8,9},{9,8},{10,11... | collective-permute-start | bytes 786440 | tf_op jit(solution)/shard_map/ppermute | solution.py:294
  46.5 10.1 %collective-permute-start.10 = (bf16[2,128,512]{2,1,0:T(8,128)(2,1)S(1)}, bf16[2,128,512]{2,1,0:T(8,128)(2,1)S(1)}, u32[]{:S(2)}, u32[]{:S(2)}) collective-permute-start(bf16[2,128,512]{2,1,0:T(8,128)(2,1)S(1)} %collective-permute-done.2.refs_4_), channel_id=1, source_target_pairs={{0,2},{1,3},{2,0},{3,1},{4,6},{5,7},{6,4},{7,5},{8,10},{9,11},{10,... | collective-permute-start | bytes 786440 | tf_op jit(solution)/shard_map/ppermute | solution.py:294
  51.2 5.8 %collective-permute-start.24 = (bf16[2,128,512]{2,1,0:T(8,128)(2,1)S(1)}, bf16[2,128,512]{2,1,0:T(8,128)(2,1)S(1)}, u32[]{:S(2)}, u32[]{:S(2)}) collective-permute-start(bf16[2,128,512]{2,1,0:T(8,128)(2,1)S(1)} %collective-permute-done.23.refs_4_), channel_id=1, source_target_pairs={{0,1},{1,0},{2,3},{3,2},{4,5},{5,4},{6,7},{7,6},{8,9},{9,8},{10,11... | collective-permute-start | bytes 786440 | tf_op jit(solution)/shard_map/ppermute | solution.py:294
  51.3 3.4 %copy-start = (bf16[2,128,512]{2,1,0:T(8,128)(2,1)S(1)}, bf16[2,128,512]{2,1,0:T(8,128)(2,1)}, u32[]{:S(2)}) copy-start(bf16[2,128,512]{2,1,0:T(8,128)(2,1)} %shard_map.64.refs_2_) | copy-start | bytes 786436
  53.4 8.9 %collective-permute-start.8 = (bf16[2,128,512]{2,1,0:T(8,128)(2,1)S(1)}, bf16[2,128,512]{2,1,0:T(8,128)(2,1)S(1)}, u32[]{:S(2)}, u32[]{:S(2)}) collective-permute-start(bf16[2,128,512]{2,1,0:T(8,128)(2,1)S(1)} %collective-permute-done.7.refs_4_), channel_id=1, source_target_pairs={{0,12},{1,13},{2,14},{3,15},{4,0},{5,1},{6,2},{7,3},{8,4},{9,5},{1... | collective-permute-start | bytes 786440 | tf_op jit(solution)/shard_map/ppermute | solution.py:294
  53.6 8.8 %collective-permute-start.5 = (bf16[2,128,512]{2,1,0:T(8,128)(2,1)S(1)}, bf16[2,128,512]{2,1,0:T(8,128)(2,1)S(1)}, u32[]{:S(2)}, u32[]{:S(2)}) collective-permute-start(bf16[2,128,512]{2,1,0:T(8,128)(2,1)S(1)} %collective-permute-done.4.refs_4_), channel_id=1, source_target_pairs={{0,2},{1,3},{2,0},{3,1},{4,6},{5,7},{6,4},{7,5},{8,10},{9,11},{10,... | collective-permute-start | bytes 786440 | tf_op jit(solution)/shard_map/ppermute | solution.py:294
  54.4 10.1 %collective-permute-start.21 = (bf16[2,128,512]{2,1,0:T(8,128)(2,1)S(1)}, bf16[2,128,512]{2,1,0:T(8,128)(2,1)S(1)}, u32[]{:S(2)}, u32[]{:S(2)}) collective-permute-start(bf16[2,128,512]{2,1,0:T(8,128)(2,1)S(1)} %collective-permute-done.20.refs_2_), channel_id=1, source_target_pairs={{0,1},{1,0},{2,3},{3,2},{4,5},{5,4},{6,7},{7,6},{8,9},{9,8},{10,11... | collective-permute-start | bytes 786440 | tf_op jit(solution)/shard_map/ppermute | solution.py:294
  56.7 9.6 %collective-permute-start.12 = (bf16[2,128,512]{2,1,0:T(8,128)(2,1)S(1)}, bf16[2,128,512]{2,1,0:T(8,128)(2,1)S(1)}, u32[]{:S(2)}, u32[]{:S(2)}) collective-permute-start(bf16[2,128,512]{2,1,0:T(8,128)(2,1)S(1)} %collective-permute-done.4.refs_4_), channel_id=1, source_target_pairs={{0,1},{1,0},{2,3},{3,2},{4,5},{5,4},{6,7},{7,6},{8,9},{9,8},{10,11... | collective-permute-start | bytes 786440 | tf_op jit(solution)/shard_map/ppermute | solution.py:294
  57.0 9.3 %collective-permute-start.11 = (bf16[2,128,512]{2,1,0:T(8,128)(2,1)S(1)}, bf16[2,128,512]{2,1,0:T(8,128)(2,1)S(1)}, u32[]{:S(2)}, u32[]{:S(2)}) collective-permute-start(bf16[2,128,512]{2,1,0:T(8,128)(2,1)S(1)} %collective-permute-done.10.refs_2_), channel_id=1, source_target_pairs={{0,1},{1,0},{2,3},{3,2},{4,5},{5,4},{6,7},{7,6},{8,9},{9,8},{10,11... | collective-permute-start | bytes 786440 | tf_op jit(solution)/shard_map/ppermute | solution.py:294
  62.3 5.8 %collective-permute-start.9 = (bf16[2,128,512]{2,1,0:T(8,128)(2,1)S(1)}, bf16[2,128,512]{2,1,0:T(8,128)(2,1)S(1)}, u32[]{:S(2)}, u32[]{:S(2)}) collective-permute-start(bf16[2,128,512]{2,1,0:T(8,128)(2,1)S(1)} %collective-permute-done.8.refs_5_), channel_id=1, source_target_pairs={{0,1},{1,0},{2,3},{3,2},{4,5},{5,4},{6,7},{7,6},{8,9},{9,8},{10,11... | collective-permute-start | bytes 786440 | tf_op jit(solution)/shard_map/ppermute | solution.py:294
  62.4 5.7 %collective-permute-start.6 = (bf16[2,128,512]{2,1,0:T(8,128)(2,1)S(1)}, bf16[2,128,512]{2,1,0:T(8,128)(2,1)S(1)}, u32[]{:S(2)}, u32[]{:S(2)}) collective-permute-start(bf16[2,128,512]{2,1,0:T(8,128)(2,1)S(1)} %collective-permute-done.5.refs_3_), channel_id=1, source_target_pairs={{0,1},{1,0},{2,3},{3,2},{4,5},{5,4},{6,7},{7,6},{8,9},{9,8},{10,11... | collective-permute-start | bytes 786440 | tf_op jit(solution)/shard_map/ppermute | solution.py:294

commit v5 on v4

--- a/solution.py
+++ b/solution.py
@@ -13,6 +13,7 @@
 OUTER = 4
 LANES = 128
 TILE = 256
+LOAD_GRANTS = (46 << 20, 45 << 20)
 
 
 def pick_columns(factor, block_ids):
@@ -98,31 +99,33 @@
     )(block_ids, query_u, query_v)
 
 
-def load_kernel(counts_ref, *refs):
-    half = (len(refs) - 1) // 2
-    sems = refs[-1]
-    live_ref = refs[half]
-    copies = [pltpu.make_async_copy(refs[i], refs[half + 1 + i], sems.at[i]) for i in range(half)]
+def load_kernel(layer, *refs):
+    half = (len(refs) - 2) // 2 if layer == 0 else (len(refs) - 1) // 2
+    refs, sems = list(refs[:-1]), refs[-1]
+    if layer == 0:
+        counts_ref, live_ref = refs.pop(0), refs.pop(half)
+    copies = [pltpu.make_async_copy(refs[i].at[layer], refs[half + i], sems.at[i]) for i in range(half)]
     for copy in copies:
         copy.start()
-    live_ref[...] = jnp.full(live_ref.shape, counts_ref[0], jnp.int32)
+    if layer == 0:
+        live_ref[...] = jnp.full(live_ref.shape, counts_ref[0], jnp.int32)
     for copy in copies:
         copy.wait()
 
 
-def load(counts, *arrays):
-    outs = [jax.ShapeDtypeStruct((8, LANES), jnp.int32)]
-    outs += [jax.ShapeDtypeStruct(one.shape, one.dtype) for one in arrays]
+def load(layer, counts, *arrays):
+    outs = [jax.ShapeDtypeStruct((8, LANES), jnp.int32)] if layer == 0 else []
+    outs += [jax.ShapeDtypeStruct(one.shape[1:], one.dtype) for one in arrays]
+    specs = [pl.BlockSpec(memory_space=pltpu.SMEM)] if layer == 0 else []
+    args = ([counts] if layer == 0 else []) + list(arrays)
     return pl.pallas_call(
-        load_kernel,
+        functools.partial(load_kernel, layer),
         out_shape=tuple(outs),
-        in_specs=[pl.BlockSpec(memory_space=pltpu.SMEM)]
-        + [pl.BlockSpec(memory_space=pltpu.HBM)] * len(arrays),
+        in_specs=specs + [pl.BlockSpec(memory_space=pltpu.HBM)] * len(arrays),
         out_specs=(pl.BlockSpec(memory_space=pltpu.VMEM),) * len(outs),
         scratch_shapes=[pltpu.SemaphoreType.DMA((len(arrays),))],
-        compiler_params=pltpu.CompilerParams(vmem_limit_bytes=42 << 20),
-        name="load",
-    )(counts, *arrays)
+        compiler_params=pltpu.CompilerParams(vmem_limit_bytes=LOAD_GRANTS[layer]),
+    )(*args)
 
 
 def split_dot(left, right):
@@ -149,12 +152,12 @@
     def take(n):
         return [refs.pop(0) for _ in range(n)]
 
-    x_refs = take(2)
+    x_refs = [take(2) for _ in groups]
     live_ref = take(1)[0] if last else None
     pieces = [[take(2) for _ in g["where"]] for g in groups]
     starts = [take(3) if g["carry"] else None for g in groups]
     outs = take(1) if last else None
-    product = take(1)[0] if last else None
+    product, made = take(2) if last else (None, None)
     totals = [take(3) for _ in groups]
     w, sems = take(2)
     me = lax.axis_index("tok")
@@ -165,24 +168,25 @@
             owner = ((a + outer - da) % outer) * inner + (b + inner - db) % inner
             start = pl.multiple_of(owner * 2 * rows, LANES)
             these = []
-            for dc, array in enumerate(pair):
-                spot = pl.multiple_of(slot * 2 * rows + ((c + dc) % 2) * rows, LANES)
-                these.append((array, w.at[:, pl.ds(spot, rows), :]))
-            these = [pltpu.make_async_copy(*ends, sems.at[2 * slot + i]) for i, ends in enumerate(these)]
+            for s in range(2):
+                for dc, array in enumerate(pair):
+                    spot = pl.multiple_of(slot * 2 * rows + ((c + dc) % 2) * rows, LANES)
+                    these.append((array.at[s], w.at[s, pl.ds(spot, rows), :]))
+            these = [pltpu.make_async_copy(*ends, sems.at[4 * slot + i]) for i, ends in enumerate(these)]
             for copy in these:
                 copy.start()
             copies.append((these, pl.ds(start, 2 * rows)))
             slot += 1
     tiles = w.shape[2] // TILE
     slot = 0
-    for g, start, total in zip(groups, starts, totals):
+    for n, (g, start, total) in enumerate(zip(groups, starts, totals)):
         for first in range(len(g["where"])):
-            for copy in copies[slot][0]:
-                copy.wait()
             span = slice(slot * 2 * rows, (slot + 1) * 2 * rows)
             came = start if first == 0 else total
             for s in range(2):
-                x = x_refs[s][g["layer"], :, copies[slot][1]]
+                for copy in copies[slot][0][2 * s : 2 * s + 2]:
+                    copy.wait()
+                x = x_refs[n][s][:, copies[slot][1]]
                 part = jnp.dot(x, w[s, span, :], preferred_element_type=jnp.float32)
                 if came is not None:
                     part = came[s][...] + part
@@ -209,23 +213,35 @@
             norm.append(jnp.sum(jnp.where(same, both, 0.0), axis=0, keepdims=True))
         norm = jnp.broadcast_to(jnp.concatenate(norm, axis=1), (8, columns))
         chooser = group_sums(columns)
-        norm = split_dot(norm, chooser)[:1]
-        raw = split_dot(product[...], chooser)
-        scaled = raw / jnp.sqrt(norm + 1e-06)
-        token = lax.broadcasted_iota(jnp.int32, scaled.shape, 0)
-        scaled = jnp.where(token < live_ref[:1], scaled, 0.0)
-        outs[0][...] = scaled.T[: columns // RANK]
-
-
-def stage(shape, groups, gradients, activations, live=None):
+        scale = 1.0 / jnp.sqrt(split_dot(norm, chooser)[:1] + 1e-06)
+        tokens = product.shape[0]
+        cut = tokens // (2 * LANES) * LANES
+        outs_now = []
+        for i, (low, high) in enumerate(((0, cut), (cut, tokens))):
+            scaled = split_dot(product[low:high], chooser) * scale
+            token = low + lax.broadcasted_iota(jnp.int32, scaled.shape, 0)
+            scaled = jnp.where(token < live_ref[:1], scaled, 0.0)
+            made[:, low:high] = scaled.T[: columns // RANK]
+            span = pl.ds(low, high - low)
+            out = pltpu.make_async_copy(made.at[:, span], outs[0].at[:, span], sems.at[4 * slot + i])
+            out.start()
+            outs_now.append(out)
+        for out in outs_now:
+            out.wait()
+
+
+def stage(shape, groups, live=None):
     last = live is not None
     rows, columns = groups[0]["arrays"][0][0].shape[1:]
-    tokens = gradients.shape[1]
+    tokens = groups[0]["tokens"][0].shape[0]
     slots = sum(len(g["where"]) for g in groups)
     tiles = 2 * (columns // TILE)
     anywhere = pl.BlockSpec(memory_space=pltpu.HBM)
     vmem = pl.BlockSpec(memory_space=pltpu.VMEM)
-    args, specs = [gradients, activations], [vmem, vmem]
+    args, specs = [], []
+    for g in groups:
+        args += g["tokens"]
+        specs += [vmem] * 2
     if last:
         args.append(live)
         specs.append(vmem)
@@ -244,8 +260,8 @@
     scratch = []
     if last:
         out_shape = jax.ShapeDtypeStruct((columns // RANK, tokens), jnp.float32)
-        out_specs = vmem
-        scratch = [pltpu.VMEM(*sums[0])] + [pltpu.VMEM(*one) for one in sums] * len(groups)
+        out_specs = anywhere
+        scratch = [pltpu.VMEM(*sums[0]), pltpu.VMEM((columns // RANK, tokens), jnp.float32)] + [pltpu.VMEM(*one) for one in sums] * len(groups)
     else:
         out_shape = tuple(jax.ShapeDtypeStruct(*one) for one in sums) * len(groups)
         out_specs = (vmem,) * len(out_shape)
@@ -264,7 +280,7 @@
         scratch_shapes=scratch
         + [
             pltpu.VMEM((2, slots * 2 * rows, columns), jnp.bfloat16),
-            pltpu.SemaphoreType.DMA((2 * slots,)),
+            pltpu.SemaphoreType.DMA((4 * slots + 2,)),
         ],
         input_output_aliases=aliases,
         compiler_params=pltpu.CompilerParams(vmem_limit_bytes=(24 if last else 16) << 20),
@@ -313,19 +329,19 @@
         for key, piece in have[layer].items():
             pairs[layer][key] = [piece, move(piece, 0, 0, 1)]
 
-    live, gradients, activations = load(counts, gradients, activations)
+    live, *first = load(0, counts, gradients, activations)
+    tokens = [first, load(1, counts, gradients, activations)]
 
     def group(layer, keys, carry):
-        return dict(layer=layer, where=keys, arrays=[pairs[layer][key] for key in keys], carry=carry)
+        return dict(layer=layer, where=keys, arrays=[pairs[layer][key] for key in keys], carry=carry, tokens=tokens[layer])
 
     parts = [[(0, 0), (0, 1), (1, 0)]] + [[(da, 1), (da + 1, 0)] for da in range(1, outer - 1)]
     carry = [None, None]
     for keys in parts:
         for layer in range(2):
-            carry[layer] = stage(shape, [group(layer, keys, carry[layer])], gradients, activations)
-    scores = stage(
-        shape, [group(layer, [(outer - 1, 1)], carry[layer]) for layer in range(2)], gradients, activations, live=live
-    )
+            carry[layer] = stage(
+                shape, [group(layer, keys, carry[layer])])
+    scores = stage(shape, [group(layer, [(outer - 1, 1)], carry[layer]) for layer in range(2)], live=live)
     return scores.T
 
 

time: 72.2 us -> 81.7 us (1.13)
  Pallas kernels: 23 us -> 36.9 us
  waiting for transfers between devices: 32.8 us -> 28.3 us
    pallas_call x7, Pallas kernels: 14.8 us -> 27.6 us  [stage(): pl.pallas_call(functools.partial(stage_kernel, cfg), out_shape=out_shape,...]
    ppermute x30, waiting for transfers between devices: 32.8 us -> 28.3 us  [move(): return lax.ppermute(value, 'tok', steps)]
    pallas_call x1 -> x2, Pallas kernels: 4.08 us -> 5.1 us  [load(): pl.pallas_call(functools.partial(load_kernel, layer), out_shape=tuple(out...]
  transfers between devices with their start and end apart: 30 -> 30, of which waited for: 11 -> 9; matrix products, arithmetic and copies ran while one was open for 0% -> 0% of each run, Pallas kernels for 24% -> 36%
where the time goes in v5:
time: 81.7 us; the launch traced here: 81.6 us
  Pallas kernels  36.9 us (45%)
  waiting for transfers between devices  28.3 us (35%)
  starting transfers between devices  15.3 us (19%)
  between operations  1.01 us (1%)
    ppermute x30, waiting for transfers between devices, move(): return lax.ppermute(value, 'tok', steps)  28.3 us
    pallas_call x7, Pallas kernels, stage(): pl.pallas_call(functools.partial(stage_kernel, cfg), out_shape=out_shape,...  27.6 us
    ppermute x30, starting transfers between devices, move(): return lax.ppermute(value, 'tok', steps)  15.3 us
    pallas_call x2, Pallas kernels, load(): pl.pallas_call(functools.partial(load_kernel, layer), out_shape=tuple(out...  5.1 us
    pallas_call x2, Pallas kernels, pick(): pl.pallas_call(functools.partial(pick_kernel, layer), out_shape=jax.Shape...  4.18 us
  transfers between devices with their start and end apart: 30, of which 9 were waited for; matrix products, arithmetic and copies ran while one was open for 0% of the time, Pallas kernels for 36%

profile of v5, /device:TPU:0, one launch (start us, length us, event | category | flops | bytes accessed | tf_op | source)
XLA Modules:
  0.0 81.6 jit_solution(10732635856517869167)
XLA Ops:
  0.0 2.1 %shard_map.67.refs_2_ = bf16[2,128,512]{2,1,0:T(8,128)(2,1)} custom-call(s32[2,16]{1,0:T(2,128)} %ids_hbm.3, bf16[2,128,1024]{2,1,0:T(8,128)(2,1)} %u_ref.3, bf16[2,128,1024]{2,1,0:T(8,128)(2,1)} %v_ref.3), custom_call_target="tpu_custom_call" | custom-call | flops 262144 | bytes 786432 | tf_op jit(solution)/shard_map/pallas_call | solution.py:85
  2.1 3.0 %collective-permute-start.7 = (bf16[2,128,512]{2,1,0:T(8,128)(2,1)}, bf16[2,128,512]{2,1,0:T(8,128)(2,1)S(1)}, u32[]{:S(2)}, u32[]{:S(2)}) collective-permute-start(bf16[2,128,512]{2,1,0:T(8,128)(2,1)} %shard_map.67.refs_2_), channel_id=1, source_target_pairs={{0,2},{1,3},{2,0},{3,1},{4,6},{5,7},{6,4},{7,5},{8,10},{9,11},{10,... | collective-permute-start | bytes 786440 | tf_op jit(solution)/shard_map/ppermute | solution.py:310
  5.1 1.6 %collective-permute-start.18 = (bf16[2,128,512]{2,1,0:T(8,128)(2,1)}, bf16[2,128,512]{2,1,0:T(8,128)(2,1)S(1)}, u32[]{:S(2)}, u32[]{:S(2)}) collective-permute-start(bf16[2,128,512]{2,1,0:T(8,128)(2,1)} %shard_map.67.refs_2_), channel_id=1, source_target_pairs={{0,4},{1,5},{2,6},{3,7},{4,8},{5,9},{6,10},{7,11},{8,12},{9,13},{1... | collective-permute-start | bytes 786440 | tf_op jit(solution)/shard_map/ppermute | solution.py:310
  6.7 2.1 %shard_map.66.refs_2_ = bf16[2,128,512]{2,1,0:T(8,128)(2,1)} custom-call(s32[2,16]{1,0:T(2,128)} %ids_hbm.3, bf16[2,128,1024]{2,1,0:T(8,128)(2,1)} %u_ref.3, bf16[2,128,1024]{2,1,0:T(8,128)(2,1)} %v_ref.3), custom_call_target="tpu_custom_call" | custom-call | flops 262144 | bytes 786432 | tf_op jit(solution)/shard_map/pallas_call | solution.py:85
  8.8 1.6 %collective-permute-start = (bf16[2,128,512]{2,1,0:T(8,128)(2,1)}, bf16[2,128,512]{2,1,0:T(8,128)(2,1)S(1)}, u32[]{:S(2)}, u32[]{:S(2)}) collective-permute-start(bf16[2,128,512]{2,1,0:T(8,128)(2,1)} %shard_map.66.refs_2_), channel_id=1, source_target_pairs={{0,4},{1,5},{2,6},{3,7},{4,8},{5,9},{6,10},{7,11},{8,12},{9,13},{1... | collective-permute-start | bytes 786440 | tf_op jit(solution)/shard_map/ppermute | solution.py:310
  10.4 0.5 collective-permute-start.1
  11.0 0.7 collective-permute-done.7.refs_4_
  11.7 0.0 collective-permute-start.15
  11.7 4.7 %collective-permute-done.18.refs_6_ = bf16[2,128,512]{2,1,0:T(8,128)(2,1)S(1)} collective-permute-done((bf16[2,128,512]{2,1,0:T(8,128)(2,1)}, bf16[2,128,512]{2,1,0:T(8,128)(2,1)S(1)}, u32[]{:S(2)}, u32[]{:S(2)}) %collective-permute-start.18) | collective-permute-done | bytes 262176 | tf_op jit(solution)/shard_map/ppermute | solution.py:310
  16.3 0.0 collective-permute-start.28
  16.3 4.3 %collective-permute-done.refs_6_ = bf16[2,128,512]{2,1,0:T(8,128)(2,1)S(1)} collective-permute-done((bf16[2,128,512]{2,1,0:T(8,128)(2,1)}, bf16[2,128,512]{2,1,0:T(8,128)(2,1)S(1)}, u32[]{:S(2)}, u32[]{:S(2)}) %collective-permute-start) | collective-permute-done | bytes 262176 | tf_op jit(solution)/shard_map/ppermute | solution.py:310
  20.6 0.0 collective-permute-start.19
  20.6 0.5 collective-permute-start.22
  21.2 1.3 %collective-permute-start.2 = (bf16[2,128,512]{2,1,0:T(8,128)(2,1)S(1)}, bf16[2,128,512]{2,1,0:T(8,128)(2,1)S(1)}, u32[]{:S(2)}, u32[]{:S(2)}) collective-permute-start(bf16[2,128,512]{2,1,0:T(8,128)(2,1)S(1)} %collective-permute-done.refs_6_), channel_id=1, source_target_pairs={{0,4},{1,5},{2,6},{3,7},{4,8},{5,9},{6,10},{7,11},{8,12},{9,13},{1... | collective-permute-start | bytes 786440 | tf_op jit(solution)/shard_map/ppermute | solution.py:310
  22.4 0.0 collective-permute-done.15.refs_3_
  22.4 1.5 %collective-permute-start.3 = (bf16[2,128,512]{2,1,0:T(8,128)(2,1)S(1)}, bf16[2,128,512]{2,1,0:T(8,128)(2,1)S(1)}, u32[]{:S(2)}, u32[]{:S(2)}) collective-permute-start(bf16[2,128,512]{2,1,0:T(8,128)(2,1)S(1)} %collective-permute-done.refs_6_), channel_id=1, source_target_pairs={{0,2},{1,3},{2,0},{3,1},{4,6},{5,7},{6,4},{7,5},{8,10},{9,11},{10,... | collective-permute-start | bytes 786440 | tf_op jit(solution)/shard_map/ppermute | solution.py:310
  23.9 0.0 collective-permute-done.28.refs_5_
  23.9 0.0 collective-permute-start.29
  23.9 7.7 %collective-permute-done.19.refs_4_ = bf16[2,128,512]{2,1,0:T(8,128)(2,1)S(1)} collective-permute-done((bf16[2,128,512]{2,1,0:T(8,128)(2,1)S(1)}, bf16[2,128,512]{2,1,0:T(8,128)(2,1)S(1)}, u32[]{:S(2)}, u32[]{:S(2)}) %collective-permute-start.19) | collective-permute-done | bytes 262176 | tf_op jit(solution)/shard_map/ppermute | solution.py:310
  31.6 0.0 collective-permute-start.17
  31.6 0.5 collective-permute-start.16
  32.1 2.9 %collective-permute-done.2.refs_4_ = bf16[2,128,512]{2,1,0:T(8,128)(2,1)S(1)} collective-permute-done((bf16[2,128,512]{2,1,0:T(8,128)(2,1)S(1)}, bf16[2,128,512]{2,1,0:T(8,128)(2,1)S(1)}, u32[]{:S(2)}, u32[]{:S(2)}) %collective-permute-start.2) | collective-permute-done | bytes 262176 | tf_op jit(solution)/shard_map/ppermute | solution.py:310
  35.0 0.5 collective-permute-start.25
  35.6 0.2 collective-permute-start.4
  35.7 0.7 collective-permute-start.20
  36.4 0.1 collective-permute-done.26.refs_5_
  36.6 0.1 collective-permute-start.14
  36.7 0.2 collective-permute-done.25.refs_3_
  37.0 0.1 collective-permute-start.13
  37.7 2.6 %shard_map.65 = (bf16[640,2048]{1,0:T(8,128)(2,1)S(1)}, bf16[640,2048]{1,0:T(8,128)(2,1)S(1)}) custom-call(bf16[2,640,2048]{2,1,0:T(8,128)(2,1)} %refs_0_.2, bf16[2,640,2048]{2,1,0:T(8,128)(2,1)} %refs_1_.3), custom_call_target="tpu_custom_call" | custom-call | tf_op jit(solution)/shard_map/pallas_call | solution.py:121
  40.3 2.6 %shard_map.64 = (s32[8,128]{1,0:T(8,128)S(1)}, bf16[640,2048]{1,0:T(8,128)(2,1)S(1)}, bf16[640,2048]{1,0:T(8,128)(2,1)S(1)}) custom-call(s32[1]{0:T(128)S(6)} %copy.31.refs_0_, bf16[2,640,2048]{2,1,0:T(8,128)(2,1)} %refs_0_.2, bf16[2,640,2048]{2,1,0:T(8,128)(2,1)} %refs_1_.3), custom_call_target="tpu_custom_call" | custom-call | tf_op jit(solution)/shard_map/pallas_call | solution.py:121
  42.9 3.7 %collective-permute-done.23.refs_4_ = bf16[2,128,512]{2,1,0:T(8,128)(2,1)S(1)} collective-permute-done((bf16[2,128,512]{2,1,0:T(8,128)(2,1)S(1)}, bf16[2,128,512]{2,1,0:T(8,128)(2,1)S(1)}, u32[]{:S(2)}, u32[]{:S(2)}) %collective-permute-start.23) | collective-permute-done | bytes 262176 | tf_op jit(solution)/shard_map/ppermute | solution.py:310
  46.5 0.7 collective-permute-start.10
  47.3 4.0 %collective-permute-done.4.refs_4_ = bf16[2,128,512]{2,1,0:T(8,128)(2,1)S(1)} collective-permute-done((bf16[2,128,512]{2,1,0:T(8,128)(2,1)S(1)}, bf16[2,128,512]{2,1,0:T(8,128)(2,1)S(1)}, u32[]{:S(2)}, u32[]{:S(2)}) %collective-permute-start.4) | collective-permute-done | bytes 262176 | tf_op jit(solution)/shard_map/ppermute | solution.py:310
  51.3 4.5 %shard_map.71 = (f32[640,512]{1,0:T(8,128)S(1)}, f32[640,512]{1,0:T(8,128)S(1)}, f32[4,256,256]{2,1,0:T(8,128)S(1)}) custom-call(bf16[640,2048]{1,0:T(8,128)(2,1)S(1)} %get-tuple-element.35.refs_0_.refs_2_, bf16[640,2048]{1,0:T(8,128)(2,1)S(1)} %get-tuple-element.36.refs_1_.refs_3_, bf16[2,128,512]{2,1,0:T(8,128)(2,1)S(1)} %copy-done.1, ...), custom_call_target="tpu_custom_call" | custom-call | flops 1811939328 | bytes 3538944 | tf_op jit(solution)/shard_map/pallas_call | solution.py:275
  55.8 0.2 collective-permute-start.8
  56.0 0.8 collective-permute-start.5
  56.8 0.2 collective-permute-start.21
  57.0 4.5 %shard_map.68 = (f32[640,512]{1,0:T(8,128)S(1)}, f32[640,512]{1,0:T(8,128)S(1)}, f32[4,256,256]{2,1,0:T(8,128)S(1)}) custom-call(bf16[640,2048]{1,0:T(8,128)(2,1)S(1)} %get-tuple-element.33.refs_0_, bf16[640,2048]{1,0:T(8,128)(2,1)S(1)} %get-tuple-element.34.refs_1_, bf16[2,128,512]{2,1,0:T(8,128)(2,1)S(1)} %copy-done, ...), custom_call_target="tpu_custom_call" | custom-call | flops 1811939328 | bytes 3538944 | tf_op jit(solution)/shard_map/pallas_call | solution.py:275
  61.6 0.4 collective-permute-start.12
  61.9 0.2 collective-permute-start.11
  62.1 3.3 %shard_map.72 = (f32[640,512]{1,0:T(8,128)S(1)}, f32[640,512]{1,0:T(8,128)S(1)}, f32[4,256,256]{2,1,0:T(8,128)S(1)}) custom-call(bf16[640,2048]{1,0:T(8,128)(2,1)S(1)} %get-tuple-element.35.refs_0_.refs_2_, bf16[640,2048]{1,0:T(8,128)(2,1)S(1)} %get-tuple-element.36.refs_1_.refs_3_, ...), custom_call_target="tpu_custom_call", output_to_operand_aliasing={{0}: (6, {}), {1}: (7, {}), {2}: (8, {})} | custom-call | flops 1207959552 | bytes 2359296 | tf_op jit(solution)/shard_map/pallas_call | solution.py:275
  65.4 0.4 collective-permute-start.9
  65.8 0.2 collective-permute-start.6
  66.0 3.3 %shard_map.69 = (f32[640,512]{1,0:T(8,128)S(1)}, f32[640,512]{1,0:T(8,128)S(1)}, f32[4,256,256]{2,1,0:T(8,128)S(1)}) custom-call(bf16[640,2048]{1,0:T(8,128)(2,1)S(1)} %get-tuple-element.33.refs_0_, bf16[640,2048]{1,0:T(8,128)(2,1)S(1)} %get-tuple-element.34.refs_1_, ...), custom_call_target="tpu_custom_call", output_to_operand_aliasing={{0}: (6, {}), {1}: (7, {}), {2}: (8, {})} | custom-call | flops 1207959552 | bytes 2359296 | tf_op jit(solution)/shard_map/pallas_call | solution.py:275
  69.3 3.3 %shard_map.73 = (f32[640,512]{1,0:T(8,128)S(1)}, f32[640,512]{1,0:T(8,128)S(1)}, f32[4,256,256]{2,1,0:T(8,128)S(1)}) custom-call(bf16[640,2048]{1,0:T(8,128)(2,1)S(1)} %get-tuple-element.35.refs_0_.refs_2_, bf16[640,2048]{1,0:T(8,128)(2,1)S(1)} %get-tuple-element.36.refs_1_.refs_3_, ...), custom_call_target="tpu_custom_call", output_to_operand_aliasing={{0}: (6, {}), {1}: (7, {}), {2}: (8, {})} | custom-call | flops 1207959552 | bytes 2359296 | tf_op jit(solution)/shard_map/pallas_call | solution.py:275
  72.7 3.4 %shard_map.70 = (f32[640,512]{1,0:T(8,128)S(1)}, f32[640,512]{1,0:T(8,128)S(1)}, f32[4,256,256]{2,1,0:T(8,128)S(1)}) custom-call(bf16[640,2048]{1,0:T(8,128)(2,1)S(1)} %get-tuple-element.33.refs_0_, bf16[640,2048]{1,0:T(8,128)(2,1)S(1)} %get-tuple-element.34.refs_1_, ...), custom_call_target="tpu_custom_call", output_to_operand_aliasing={{0}: (6, {}), {1}: (7, {}), {2}: (8, {})} | custom-call | flops 1207959552 | bytes 2359296 | tf_op jit(solution)/shard_map/pallas_call | solution.py:275
  76.1 5.4 %shard_map.74 = f32[64,640]{1,0:T(8,128)} custom-call(bf16[640,2048]{1,0:T(8,128)(2,1)S(1)} %get-tuple-element.33.refs_0_, bf16[640,2048]{1,0:T(8,128)(2,1)S(1)} %get-tuple-element.34.refs_1_, bf16[640,2048]{1,0:T(8,128)(2,1)S(1)} %get-tuple-element.35.refs_0_.refs_2_, bf16[640,2048]{1,0:T(8,128)(2,1)S(1)} %get-tuple-element.36.refs_1_.refs_3_, ...), custom_call_target="tpu_custom_call" | custom-call | flops 1207959552 | bytes 2359296 | tf_op jit(solution)/shard_map/pallas_call | solution.py:275
  (27 shorter events, 0.1 us)
Async XLA Ops:
  2.1 8.9 %copy-start.1 = (bf16[2,128,512]{2,1,0:T(8,128)(2,1)S(1)}, bf16[2,128,512]{2,1,0:T(8,128)(2,1)}, u32[]{:S(2)}) copy-start(bf16[2,128,512]{2,1,0:T(8,128)(2,1)} %shard_map.67.refs_2_) | copy-start | bytes 786436
  2.1 9.5 %collective-permute-start.7 = (bf16[2,128,512]{2,1,0:T(8,128)(2,1)}, bf16[2,128,512]{2,1,0:T(8,128)(2,1)S(1)}, u32[]{:S(2)}, u32[]{:S(2)}) collective-permute-start(bf16[2,128,512]{2,1,0:T(8,128)(2,1)} %shard_map.67.refs_2_), channel_id=1, source_target_pairs={{0,2},{1,3},{2,0},{3,1},{4,6},{5,7},{6,4},{7,5},{8,10},{9,11},{10,... | collective-permute-start | bytes 786440 | tf_op jit(solution)/shard_map/ppermute | solution.py:310
  5.1 11.2 %collective-permute-start.18 = (bf16[2,128,512]{2,1,0:T(8,128)(2,1)}, bf16[2,128,512]{2,1,0:T(8,128)(2,1)S(1)}, u32[]{:S(2)}, u32[]{:S(2)}) collective-permute-start(bf16[2,128,512]{2,1,0:T(8,128)(2,1)} %shard_map.67.refs_2_), channel_id=1, source_target_pairs={{0,4},{1,5},{2,6},{3,7},{4,8},{5,9},{6,10},{7,11},{8,12},{9,13},{1... | collective-permute-start | bytes 786440 | tf_op jit(solution)/shard_map/ppermute | solution.py:310
  8.8 11.8 %collective-permute-start = (bf16[2,128,512]{2,1,0:T(8,128)(2,1)}, bf16[2,128,512]{2,1,0:T(8,128)(2,1)S(1)}, u32[]{:S(2)}, u32[]{:S(2)}) collective-permute-start(bf16[2,128,512]{2,1,0:T(8,128)(2,1)} %shard_map.66.refs_2_), channel_id=1, source_target_pairs={{0,4},{1,5},{2,6},{3,7},{4,8},{5,9},{6,10},{7,11},{8,12},{9,13},{1... | collective-permute-start | bytes 786440 | tf_op jit(solution)/shard_map/ppermute | solution.py:310
  10.4 10.2 %collective-permute-start.1 = (bf16[2,128,512]{2,1,0:T(8,128)(2,1)}, bf16[2,128,512]{2,1,0:T(8,128)(2,1)S(1)}, u32[]{:S(2)}, u32[]{:S(2)}) collective-permute-start(bf16[2,128,512]{2,1,0:T(8,128)(2,1)} %shard_map.66.refs_2_), channel_id=1, source_target_pairs={{0,2},{1,3},{2,0},{3,1},{4,6},{5,7},{6,4},{7,5},{8,10},{9,11},{10,... | collective-permute-start | bytes 786440 | tf_op jit(solution)/shard_map/ppermute | solution.py:310
  11.0 10.2 %collective-permute-start.27 = (bf16[2,128,512]{2,1,0:T(8,128)(2,1)S(1)}, bf16[2,128,512]{2,1,0:T(8,128)(2,1)S(1)}, u32[]{:S(2)}, u32[]{:S(2)}) collective-permute-start(bf16[2,128,512]{2,1,0:T(8,128)(2,1)S(1)} %copy-done.1), channel_id=1, source_target_pairs={{0,1},{1,0},{2,3},{3,2},{4,5},{5,4},{6,7},{7,6},{8,9},{9,8},{10,11... | collective-permute-start | bytes 786440 | tf_op jit(solution)/shard_map/ppermute | solution.py:310
  11.7 10.8 %collective-permute-start.15 = (bf16[2,128,512]{2,1,0:T(8,128)(2,1)}, bf16[2,128,512]{2,1,0:T(8,128)(2,1)S(1)}, u32[]{:S(2)}, u32[]{:S(2)}) collective-permute-start(bf16[2,128,512]{2,1,0:T(8,128)(2,1)} %shard_map.66.refs_2_), channel_id=1, source_target_pairs={{0,1},{1,0},{2,3},{3,2},{4,5},{5,4},{6,7},{7,6},{8,9},{9,8},{10,11... | collective-permute-start | bytes 786440 | tf_op jit(solution)/shard_map/ppermute | solution.py:310
  16.3 7.6 %collective-permute-start.28 = (bf16[2,128,512]{2,1,0:T(8,128)(2,1)S(1)}, bf16[2,128,512]{2,1,0:T(8,128)(2,1)S(1)}, u32[]{:S(2)}, u32[]{:S(2)}) collective-permute-start(bf16[2,128,512]{2,1,0:T(8,128)(2,1)S(1)} %collective-permute-done.7.refs_4_), channel_id=1, source_target_pairs={{0,1},{1,0},{2,3},{3,2},{4,5},{5,4},{6,7},{7,6},{8,9},{9,8},{10,11... | collective-permute-start | bytes 786440 | tf_op jit(solution)/shard_map/ppermute | solution.py:310
  20.6 11.0 %collective-permute-start.19 = (bf16[2,128,512]{2,1,0:T(8,128)(2,1)S(1)}, bf16[2,128,512]{2,1,0:T(8,128)(2,1)S(1)}, u32[]{:S(2)}, u32[]{:S(2)}) collective-permute-start(bf16[2,128,512]{2,1,0:T(8,128)(2,1)S(1)} %collective-permute-done.18.refs_6_), channel_id=1, source_target_pairs={{0,4},{1,5},{2,6},{3,7},{4,8},{5,9},{6,10},{7,11},{8,12},{9,13},{1... | collective-permute-start | bytes 786440 | tf_op jit(solution)/shard_map/ppermute | solution.py:310
  20.6 11.0 %collective-permute-start.22 = (bf16[2,128,512]{2,1,0:T(8,128)(2,1)S(1)}, bf16[2,128,512]{2,1,0:T(8,128)(2,1)S(1)}, u32[]{:S(2)}, u32[]{:S(2)}) collective-permute-start(bf16[2,128,512]{2,1,0:T(8,128)(2,1)S(1)} %collective-permute-done.18.refs_6_), channel_id=1, source_target_pairs={{0,2},{1,3},{2,0},{3,1},{4,6},{5,7},{6,4},{7,5},{8,10},{9,11},{10,... | collective-permute-start | bytes 786440 | tf_op jit(solution)/shard_map/ppermute | solution.py:310
  21.2 13.9 %collective-permute-start.2 = (bf16[2,128,512]{2,1,0:T(8,128)(2,1)S(1)}, bf16[2,128,512]{2,1,0:T(8,128)(2,1)S(1)}, u32[]{:S(2)}, u32[]{:S(2)}) collective-permute-start(bf16[2,128,512]{2,1,0:T(8,128)(2,1)S(1)} %collective-permute-done.refs_6_), channel_id=1, source_target_pairs={{0,4},{1,5},{2,6},{3,7},{4,8},{5,9},{6,10},{7,11},{8,12},{9,13},{1... | collective-permute-start | bytes 786440 | tf_op jit(solution)/shard_map/ppermute | solution.py:310
  22.4 12.6 %collective-permute-start.3 = (bf16[2,128,512]{2,1,0:T(8,128)(2,1)S(1)}, bf16[2,128,512]{2,1,0:T(8,128)(2,1)S(1)}, u32[]{:S(2)}, u32[]{:S(2)}) collective-permute-start(bf16[2,128,512]{2,1,0:T(8,128)(2,1)S(1)} %collective-permute-done.refs_6_), channel_id=1, source_target_pairs={{0,2},{1,3},{2,0},{3,1},{4,6},{5,7},{6,4},{7,5},{8,10},{9,11},{10,... | collective-permute-start | bytes 786440 | tf_op jit(solution)/shard_map/ppermute | solution.py:310
  23.9 11.6 %collective-permute-start.29 = (bf16[2,128,512]{2,1,0:T(8,128)(2,1)S(1)}, bf16[2,128,512]{2,1,0:T(8,128)(2,1)S(1)}, u32[]{:S(2)}, u32[]{:S(2)}) collective-permute-start(bf16[2,128,512]{2,1,0:T(8,128)(2,1)S(1)} %collective-permute-done.18.refs_6_), channel_id=1, source_target_pairs={{0,1},{1,0},{2,3},{3,2},{4,5},{5,4},{6,7},{7,6},{8,9},{9,8},{10,11... | collective-permute-start | bytes 786440 | tf_op jit(solution)/shard_map/ppermute | solution.py:310
  31.6 4.0 %collective-permute-start.17 = (bf16[2,128,512]{2,1,0:T(8,128)(2,1)S(1)}, bf16[2,128,512]{2,1,0:T(8,128)(2,1)S(1)}, u32[]{:S(2)}, u32[]{:S(2)}) collective-permute-start(bf16[2,128,512]{2,1,0:T(8,128)(2,1)S(1)} %collective-permute-done.refs_6_), channel_id=1, source_target_pairs={{0,1},{1,0},{2,3},{3,2},{4,5},{5,4},{6,7},{7,6},{8,9},{9,8},{10,11... | collective-permute-start | bytes 786440 | tf_op jit(solution)/shard_map/ppermute | solution.py:310
  31.6 4.1 %collective-permute-start.16 = (bf16[2,128,512]{2,1,0:T(8,128)(2,1)S(1)}, bf16[2,128,512]{2,1,0:T(8,128)(2,1)S(1)}, u32[]{:S(2)}, u32[]{:S(2)}) collective-permute-start(bf16[2,128,512]{2,1,0:T(8,128)(2,1)S(1)} %collective-permute-done.1.refs_4_), channel_id=1, source_target_pairs={{0,1},{1,0},{2,3},{3,2},{4,5},{5,4},{6,7},{7,6},{8,9},{9,8},{10,11... | collective-permute-start | bytes 786440 | tf_op jit(solution)/shard_map/ppermute | solution.py:310
  35.0 1.5 %collective-permute-start.26 = (bf16[2,128,512]{2,1,0:T(8,128)(2,1)S(1)}, bf16[2,128,512]{2,1,0:T(8,128)(2,1)S(1)}, u32[]{:S(2)}, u32[]{:S(2)}) collective-permute-start(bf16[2,128,512]{2,1,0:T(8,128)(2,1)S(1)} %collective-permute-done.19.refs_4_), channel_id=1, source_target_pairs={{0,1},{1,0},{2,3},{3,2},{4,5},{5,4},{6,7},{7,6},{8,9},{9,8},{10,11... | collective-permute-start | bytes 786440 | tf_op jit(solution)/shard_map/ppermute | solution.py:310
  35.0 1.9 %collective-permute-start.25 = (bf16[2,128,512]{2,1,0:T(8,128)(2,1)S(1)}, bf16[2,128,512]{2,1,0:T(8,128)(2,1)S(1)}, u32[]{:S(2)}, u32[]{:S(2)}) collective-permute-start(bf16[2,128,512]{2,1,0:T(8,128)(2,1)S(1)} %collective-permute-done.22.refs_2_), channel_id=1, source_target_pairs={{0,1},{1,0},{2,3},{3,2},{4,5},{5,4},{6,7},{7,6},{8,9},{9,8},{10,11... | collective-permute-start | bytes 786440 | tf_op jit(solution)/shard_map/ppermute | solution.py:310
  35.6 11.0 %collective-permute-start.23 = (bf16[2,128,512]{2,1,0:T(8,128)(2,1)S(1)}, bf16[2,128,512]{2,1,0:T(8,128)(2,1)S(1)}, u32[]{:S(2)}, u32[]{:S(2)}) collective-permute-start(bf16[2,128,512]{2,1,0:T(8,128)(2,1)S(1)} %collective-permute-done.19.refs_4_), channel_id=1, source_target_pairs={{0,4},{1,5},{2,6},{3,7},{4,8},{5,9},{6,10},{7,11},{8,12},{9,13},{1... | collective-permute-start | bytes 786440 | tf_op jit(solution)/shard_map/ppermute | solution.py:310
  35.6 15.7 %collective-permute-start.4 = (bf16[2,128,512]{2,1,0:T(8,128)(2,1)S(1)}, bf16[2,128,512]{2,1,0:T(8,128)(2,1)S(1)}, u32[]{:S(2)}, u32[]{:S(2)}) collective-permute-start(bf16[2,128,512]{2,1,0:T(8,128)(2,1)S(1)} %collective-permute-done.2.refs_4_), channel_id=1, source_target_pairs={{0,4},{1,5},{2,6},{3,7},{4,8},{5,9},{6,10},{7,11},{8,12},{9,13},{1... | collective-permute-start | bytes 786440 | tf_op jit(solution)/shard_map/ppermute | solution.py:310
  35.7 20.1 %collective-permute-start.20 = (bf16[2,128,512]{2,1,0:T(8,128)(2,1)S(1)}, bf16[2,128,512]{2,1,0:T(8,128)(2,1)S(1)}, u32[]{:S(2)}, u32[]{:S(2)}) collective-permute-start(bf16[2,128,512]{2,1,0:T(8,128)(2,1)S(1)} %collective-permute-done.19.refs_4_), channel_id=1, source_target_pairs={{0,2},{1,3},{2,0},{3,1},{4,6},{5,7},{6,4},{7,5},{8,10},{9,11},{10,... | collective-permute-start | bytes 786440 | tf_op jit(solution)/shard_map/ppermute | solution.py:310
  36.6 19.5 %collective-permute-start.14 = (bf16[2,128,512]{2,1,0:T(8,128)(2,1)S(1)}, bf16[2,128,512]{2,1,0:T(8,128)(2,1)S(1)}, u32[]{:S(2)}, u32[]{:S(2)}) collective-permute-start(bf16[2,128,512]{2,1,0:T(8,128)(2,1)S(1)} %collective-permute-done.2.refs_4_), channel_id=1, source_target_pairs={{0,1},{1,0},{2,3},{3,2},{4,5},{5,4},{6,7},{7,6},{8,9},{9,8},{10,11... | collective-permute-start | bytes 786440 | tf_op jit(solution)/shard_map/ppermute | solution.py:310
  37.0 19.9 %collective-permute-start.13 = (bf16[2,128,512]{2,1,0:T(8,128)(2,1)S(1)}, bf16[2,128,512]{2,1,0:T(8,128)(2,1)S(1)}, u32[]{:S(2)}, u32[]{:S(2)}) collective-permute-start(bf16[2,128,512]{2,1,0:T(8,128)(2,1)S(1)} %collective-permute-done.3.refs_2_), channel_id=1, source_target_pairs={{0,1},{1,0},{2,3},{3,2},{4,5},{5,4},{6,7},{7,6},{8,9},{9,8},{10,11... | collective-permute-start | bytes 786440 | tf_op jit(solution)/shard_map/ppermute | solution.py:310
  46.5 15.0 %collective-permute-start.10 = (bf16[2,128,512]{2,1,0:T(8,128)(2,1)S(1)}, bf16[2,128,512]{2,1,0:T(8,128)(2,1)S(1)}, u32[]{:S(2)}, u32[]{:S(2)}) collective-permute-start(bf16[2,128,512]{2,1,0:T(8,128)(2,1)S(1)} %collective-permute-done.2.refs_4_), channel_id=1, source_target_pairs={{0,2},{1,3},{2,0},{3,1},{4,6},{5,7},{6,4},{7,5},{8,10},{9,11},{10,... | collective-permute-start | bytes 786440 | tf_op jit(solution)/shard_map/ppermute | solution.py:310
  51.2 10.7 %collective-permute-start.24 = (bf16[2,128,512]{2,1,0:T(8,128)(2,1)S(1)}, bf16[2,128,512]{2,1,0:T(8,128)(2,1)S(1)}, u32[]{:S(2)}, u32[]{:S(2)}) collective-permute-start(bf16[2,128,512]{2,1,0:T(8,128)(2,1)S(1)} %collective-permute-done.23.refs_4_), channel_id=1, source_target_pairs={{0,1},{1,0},{2,3},{3,2},{4,5},{5,4},{6,7},{7,6},{8,9},{9,8},{10,11... | collective-permute-start | bytes 786440 | tf_op jit(solution)/shard_map/ppermute | solution.py:310
  51.2 5.8 %copy-start = (bf16[2,128,512]{2,1,0:T(8,128)(2,1)S(1)}, bf16[2,128,512]{2,1,0:T(8,128)(2,1)}, u32[]{:S(2)}) copy-start(bf16[2,128,512]{2,1,0:T(8,128)(2,1)} %shard_map.66.refs_2_) | copy-start | bytes 786436
  55.8 9.6 %collective-permute-start.8 = (bf16[2,128,512]{2,1,0:T(8,128)(2,1)S(1)}, bf16[2,128,512]{2,1,0:T(8,128)(2,1)S(1)}, u32[]{:S(2)}, u32[]{:S(2)}) collective-permute-start(bf16[2,128,512]{2,1,0:T(8,128)(2,1)S(1)} %collective-permute-done.7.refs_4_), channel_id=1, source_target_pairs={{0,12},{1,13},{2,14},{3,15},{4,0},{5,1},{6,2},{7,3},{8,4},{9,5},{1... | collective-permute-start | bytes 786440 | tf_op jit(solution)/shard_map/ppermute | solution.py:310
  56.0 9.8 %collective-permute-start.5 = (bf16[2,128,512]{2,1,0:T(8,128)(2,1)S(1)}, bf16[2,128,512]{2,1,0:T(8,128)(2,1)S(1)}, u32[]{:S(2)}, u32[]{:S(2)}) collective-permute-start(bf16[2,128,512]{2,1,0:T(8,128)(2,1)S(1)} %collective-permute-done.4.refs_4_), channel_id=1, source_target_pairs={{0,2},{1,3},{2,0},{3,1},{4,6},{5,7},{6,4},{7,5},{8,10},{9,11},{10,... | collective-permute-start | bytes 786440 | tf_op jit(solution)/shard_map/ppermute | solution.py:310
  56.8 12.5 %collective-permute-start.21 = (bf16[2,128,512]{2,1,0:T(8,128)(2,1)S(1)}, bf16[2,128,512]{2,1,0:T(8,128)(2,1)S(1)}, u32[]{:S(2)}, u32[]{:S(2)}) collective-permute-start(bf16[2,128,512]{2,1,0:T(8,128)(2,1)S(1)} %collective-permute-done.20.refs_2_), channel_id=1, source_target_pairs={{0,1},{1,0},{2,3},{3,2},{4,5},{5,4},{6,7},{7,6},{8,9},{9,8},{10,11... | collective-permute-start | bytes 786440 | tf_op jit(solution)/shard_map/ppermute | solution.py:310
  61.6 11.1 %collective-permute-start.12 = (bf16[2,128,512]{2,1,0:T(8,128)(2,1)S(1)}, bf16[2,128,512]{2,1,0:T(8,128)(2,1)S(1)}, u32[]{:S(2)}, u32[]{:S(2)}) collective-permute-start(bf16[2,128,512]{2,1,0:T(8,128)(2,1)S(1)} %collective-permute-done.4.refs_4_), channel_id=1, source_target_pairs={{0,1},{1,0},{2,3},{3,2},{4,5},{5,4},{6,7},{7,6},{8,9},{9,8},{10,11... | collective-permute-start | bytes 786440 | tf_op jit(solution)/shard_map/ppermute | solution.py:310
  61.9 10.7 %collective-permute-start.11 = (bf16[2,128,512]{2,1,0:T(8,128)(2,1)S(1)}, bf16[2,128,512]{2,1,0:T(8,128)(2,1)S(1)}, u32[]{:S(2)}, u32[]{:S(2)}) collective-permute-start(bf16[2,128,512]{2,1,0:T(8,128)(2,1)S(1)} %collective-permute-done.10.refs_2_), channel_id=1, source_target_pairs={{0,1},{1,0},{2,3},{3,2},{4,5},{5,4},{6,7},{7,6},{8,9},{9,8},{10,11... | collective-permute-start | bytes 786440 | tf_op jit(solution)/shard_map/ppermute | solution.py:310
  65.4 10.6 %collective-permute-start.9 = (bf16[2,128,512]{2,1,0:T(8,128)(2,1)S(1)}, bf16[2,128,512]{2,1,0:T(8,128)(2,1)S(1)}, u32[]{:S(2)}, u32[]{:S(2)}) collective-permute-start(bf16[2,128,512]{2,1,0:T(8,128)(2,1)S(1)} %collective-permute-done.8.refs_7_), channel_id=1, source_target_pairs={{0,1},{1,0},{2,3},{3,2},{4,5},{5,4},{6,7},{7,6},{8,9},{9,8},{10,11... | collective-permute-start | bytes 786440 | tf_op jit(solution)/shard_map/ppermute | solution.py:310
  65.8 10.2 %collective-permute-start.6 = (bf16[2,128,512]{2,1,0:T(8,128)(2,1)S(1)}, bf16[2,128,512]{2,1,0:T(8,128)(2,1)S(1)}, u32[]{:S(2)}, u32[]{:S(2)}) collective-permute-start(bf16[2,128,512]{2,1,0:T(8,128)(2,1)S(1)} %collective-permute-done.5.refs_5_), channel_id=1, source_target_pairs={{0,1},{1,0},{2,3},{3,2},{4,5},{5,4},{6,7},{7,6},{8,9},{9,8},{10,11... | collective-permute-start | bytes 786440 | tf_op jit(solution)/shard_map/ppermute | solution.py:310

commit v6 on v5

--- a/solution.py
+++ b/solution.py
@@ -157,25 +157,20 @@
     pieces = [[take(2) for _ in g["where"]] for g in groups]
     starts = [take(3) if g["carry"] else None for g in groups]
     outs = take(1) if last else None
-    product, made = take(2) if last else (None, None)
+    product = take(1)[0] if last else None
     totals = [take(3) for _ in groups]
-    w, sems = take(2)
+    w = take(1)[0]
     me = lax.axis_index("tok")
     a, b, c = me // (2 * inner), (me // 2) % inner, me % 2
-    copies, slot = [], 0
+    spans, slot = [], 0
     for g, arrays in zip(groups, pieces):
         for (da, db), pair in zip(g["where"], arrays):
             owner = ((a + outer - da) % outer) * inner + (b + inner - db) % inner
             start = pl.multiple_of(owner * 2 * rows, LANES)
-            these = []
-            for s in range(2):
-                for dc, array in enumerate(pair):
-                    spot = pl.multiple_of(slot * 2 * rows + ((c + dc) % 2) * rows, LANES)
-                    these.append((array.at[s], w.at[s, pl.ds(spot, rows), :]))
-            these = [pltpu.make_async_copy(*ends, sems.at[4 * slot + i]) for i, ends in enumerate(these)]
-            for copy in these:
-                copy.start()
-            copies.append((these, pl.ds(start, 2 * rows)))
+            for dc, array in enumerate(pair):
+                spot = pl.multiple_of(slot * 2 * rows + ((c + dc) % 2) * rows, LANES)
+                w[:, pl.ds(spot, rows), :] = array[...]
+            spans.append(pl.ds(start, 2 * rows))
             slot += 1
     tiles = w.shape[2] // TILE
     slot = 0
@@ -184,9 +179,7 @@
             span = slice(slot * 2 * rows, (slot + 1) * 2 * rows)
             came = start if first == 0 else total
             for s in range(2):
-                for copy in copies[slot][0][2 * s : 2 * s + 2]:
-                    copy.wait()
-                x = x_refs[n][s][:, copies[slot][1]]
+                x = x_refs[n][s][:, spans[slot]]
                 part = jnp.dot(x, w[s, span, :], preferred_element_type=jnp.float32)
                 if came is not None:
                     part = came[s][...] + part
@@ -214,20 +207,10 @@
         norm = jnp.broadcast_to(jnp.concatenate(norm, axis=1), (8, columns))
         chooser = group_sums(columns)
         scale = 1.0 / jnp.sqrt(split_dot(norm, chooser)[:1] + 1e-06)
-        tokens = product.shape[0]
-        cut = tokens // (2 * LANES) * LANES
-        outs_now = []
-        for i, (low, high) in enumerate(((0, cut), (cut, tokens))):
-            scaled = split_dot(product[low:high], chooser) * scale
-            token = low + lax.broadcasted_iota(jnp.int32, scaled.shape, 0)
-            scaled = jnp.where(token < live_ref[:1], scaled, 0.0)
-            made[:, low:high] = scaled.T[: columns // RANK]
-            span = pl.ds(low, high - low)
-            out = pltpu.make_async_copy(made.at[:, span], outs[0].at[:, span], sems.at[4 * slot + i])
-            out.start()
-            outs_now.append(out)
-        for out in outs_now:
-            out.wait()
+        scaled = split_dot(product[...], chooser) * scale
+        token = lax.broadcasted_iota(jnp.int32, scaled.shape, 0)
+        scaled = jnp.where(token < live_ref[:1], scaled, 0.0)
+        outs[0][...] = scaled.T[: columns // RANK]
 
 
 def stage(shape, groups, live=None):
@@ -236,7 +219,6 @@
     tokens = groups[0]["tokens"][0].shape[0]
     slots = sum(len(g["where"]) for g in groups)
     tiles = 2 * (columns // TILE)
-    anywhere = pl.BlockSpec(memory_space=pltpu.HBM)
     vmem = pl.BlockSpec(memory_space=pltpu.VMEM)
     args, specs = [], []
     for g in groups:
@@ -248,7 +230,7 @@
     for g in groups:
         for pair in g["arrays"]:
             args += pair
-            specs += [anywhere] * 2
+            specs += [vmem] * 2
     aliases = {}
     for n, g in enumerate(groups):
         if g["carry"] is not None:
@@ -260,8 +242,8 @@
     scratch = []
     if last:
         out_shape = jax.ShapeDtypeStruct((columns // RANK, tokens), jnp.float32)
-        out_specs = anywhere
-        scratch = [pltpu.VMEM(*sums[0]), pltpu.VMEM((columns // RANK, tokens), jnp.float32)] + [pltpu.VMEM(*one) for one in sums] * len(groups)
+        out_specs = vmem
+        scratch = [pltpu.VMEM(*sums[0])] + [pltpu.VMEM(*one) for one in sums] * len(groups)
     else:
         out_shape = tuple(jax.ShapeDtypeStruct(*one) for one in sums) * len(groups)
         out_specs = (vmem,) * len(out_shape)
@@ -277,11 +259,7 @@
         out_shape=out_shape,
         in_specs=specs,
         out_specs=out_specs,
-        scratch_shapes=scratch
-        + [
-            pltpu.VMEM((2, slots * 2 * rows, columns), jnp.bfloat16),
-            pltpu.SemaphoreType.DMA((4 * slots + 2,)),
-        ],
+        scratch_shapes=scratch + [pltpu.VMEM((2, slots * 2 * rows, columns), jnp.bfloat16)],
         input_output_aliases=aliases,
         compiler_params=pltpu.CompilerParams(vmem_limit_bytes=(24 if last else 16) << 20),
         cost_estimate=pl.CostEstimate(

time: 81.7 us -> 70.6 us (0.86)
  Pallas kernels: 36.9 us -> 22.1 us
  waiting for transfers between devices: 28.3 us -> 32.3 us
    pallas_call x7, Pallas kernels: 27.6 us -> 12.8 us  [stage(): pl.pallas_call(functools.partial(stage_kernel, cfg), out_shape=out_shape,...]
    ppermute x30, waiting for transfers between devices: 28.3 us -> 32.3 us  [move(): return lax.ppermute(value, 'tok', steps)]
  transfers between devices with their start and end apart: 30 -> 30, of which waited for: 9 -> 11; matrix products, arithmetic and copies ran while one was open for 0% -> 0% of each run, Pallas kernels for 36% -> 23%
where the time goes in v6:
time: 70.6 us; the launch traced here: 70.4 us
  waiting for transfers between devices  32.3 us (46%)
  Pallas kernels  22.1 us (31%)
  starting transfers between devices  15.2 us (22%)
  between operations  0.84 us (1%)
    ppermute x30, waiting for transfers between devices, move(): return lax.ppermute(value, 'tok', steps)  32.3 us
    ppermute x30, starting transfers between devices, move(): return lax.ppermute(value, 'tok', steps)  15.2 us
    pallas_call x7, Pallas kernels, stage(): pl.pallas_call(functools.partial(stage_kernel, cfg), out_shape=out_shape,...  12.8 us
    pallas_call x2, Pallas kernels, load(): pl.pallas_call(functools.partial(load_kernel, layer), out_shape=tuple(out...  5.1 us
    pallas_call x2, Pallas kernels, pick(): pl.pallas_call(functools.partial(pick_kernel, layer), out_shape=jax.Shape...  4.18 us
  transfers between devices with their start and end apart: 30, of which 11 were waited for; matrix products, arithmetic and copies ran while one was open for 0% of the time, Pallas kernels for 23%

profile of v6, /device:TPU:0, one launch (start us, length us, event | category | flops | bytes accessed | tf_op | source)
XLA Modules:
  0.0 70.4 jit_solution(11990064712309173183)
XLA Ops:
  0.0 2.1 %shard_map.67.refs_2_ = bf16[2,128,512]{2,1,0:T(8,128)(2,1)} custom-call(s32[2,16]{1,0:T(2,128)} %ids_hbm.3, bf16[2,128,1024]{2,1,0:T(8,128)(2,1)} %u_ref.3, bf16[2,128,1024]{2,1,0:T(8,128)(2,1)} %v_ref.3), custom_call_target="tpu_custom_call" | custom-call | flops 262144 | bytes 786432 | tf_op jit(solution)/shard_map/pallas_call | solution.py:85
  2.1 3.0 %collective-permute-start.7 = (bf16[2,128,512]{2,1,0:T(8,128)(2,1)}, bf16[2,128,512]{2,1,0:T(8,128)(2,1)S(1)}, u32[]{:S(2)}, u32[]{:S(2)}) collective-permute-start(bf16[2,128,512]{2,1,0:T(8,128)(2,1)} %shard_map.67.refs_2_), channel_id=1, source_target_pairs={{0,2},{1,3},{2,0},{3,1},{4,6},{5,7},{6,4},{7,5},{8,10},{9,11},{10,... | collective-permute-start | bytes 786440 | tf_op jit(solution)/shard_map/ppermute | solution.py:288
  5.1 1.6 %collective-permute-start.18 = (bf16[2,128,512]{2,1,0:T(8,128)(2,1)}, bf16[2,128,512]{2,1,0:T(8,128)(2,1)S(1)}, u32[]{:S(2)}, u32[]{:S(2)}) collective-permute-start(bf16[2,128,512]{2,1,0:T(8,128)(2,1)} %shard_map.67.refs_2_), channel_id=1, source_target_pairs={{0,4},{1,5},{2,6},{3,7},{4,8},{5,9},{6,10},{7,11},{8,12},{9,13},{1... | collective-permute-start | bytes 786440 | tf_op jit(solution)/shard_map/ppermute | solution.py:288
  6.7 2.1 %shard_map.66.refs_2_ = bf16[2,128,512]{2,1,0:T(8,128)(2,1)} custom-call(s32[2,16]{1,0:T(2,128)} %ids_hbm.3, bf16[2,128,1024]{2,1,0:T(8,128)(2,1)} %u_ref.3, bf16[2,128,1024]{2,1,0:T(8,128)(2,1)} %v_ref.3), custom_call_target="tpu_custom_call" | custom-call | flops 262144 | bytes 786432 | tf_op jit(solution)/shard_map/pallas_call | solution.py:85
  8.8 1.6 %collective-permute-start = (bf16[2,128,512]{2,1,0:T(8,128)(2,1)}, bf16[2,128,512]{2,1,0:T(8,128)(2,1)S(1)}, u32[]{:S(2)}, u32[]{:S(2)}) collective-permute-start(bf16[2,128,512]{2,1,0:T(8,128)(2,1)} %shard_map.66.refs_2_), channel_id=1, source_target_pairs={{0,4},{1,5},{2,6},{3,7},{4,8},{5,9},{6,10},{7,11},{8,12},{9,13},{1... | collective-permute-start | bytes 786440 | tf_op jit(solution)/shard_map/ppermute | solution.py:288
  10.4 0.5 collective-permute-start.1
  11.0 0.7 collective-permute-done.7.refs_4_
  11.7 0.0 collective-permute-start.15
  11.7 4.7 %collective-permute-done.18.refs_6_ = bf16[2,128,512]{2,1,0:T(8,128)(2,1)S(1)} collective-permute-done((bf16[2,128,512]{2,1,0:T(8,128)(2,1)}, bf16[2,128,512]{2,1,0:T(8,128)(2,1)S(1)}, u32[]{:S(2)}, u32[]{:S(2)}) %collective-permute-start.18) | collective-permute-done | bytes 262176 | tf_op jit(solution)/shard_map/ppermute | solution.py:288
  16.3 0.0 collective-permute-start.28
  16.3 4.3 %collective-permute-done.refs_6_ = bf16[2,128,512]{2,1,0:T(8,128)(2,1)S(1)} collective-permute-done((bf16[2,128,512]{2,1,0:T(8,128)(2,1)}, bf16[2,128,512]{2,1,0:T(8,128)(2,1)S(1)}, u32[]{:S(2)}, u32[]{:S(2)}) %collective-permute-start) | collective-permute-done | bytes 262176 | tf_op jit(solution)/shard_map/ppermute | solution.py:288
  20.6 0.0 collective-permute-start.19
  20.6 0.5 collective-permute-start.22
  21.2 1.3 %collective-permute-start.2 = (bf16[2,128,512]{2,1,0:T(8,128)(2,1)S(1)}, bf16[2,128,512]{2,1,0:T(8,128)(2,1)S(1)}, u32[]{:S(2)}, u32[]{:S(2)}) collective-permute-start(bf16[2,128,512]{2,1,0:T(8,128)(2,1)S(1)} %collective-permute-done.refs_6_), channel_id=1, source_target_pairs={{0,4},{1,5},{2,6},{3,7},{4,8},{5,9},{6,10},{7,11},{8,12},{9,13},{1... | collective-permute-start | bytes 786440 | tf_op jit(solution)/shard_map/ppermute | solution.py:288
  22.4 0.0 collective-permute-done.15.refs_3_
  22.4 1.5 %collective-permute-start.3 = (bf16[2,128,512]{2,1,0:T(8,128)(2,1)S(1)}, bf16[2,128,512]{2,1,0:T(8,128)(2,1)S(1)}, u32[]{:S(2)}, u32[]{:S(2)}) collective-permute-start(bf16[2,128,512]{2,1,0:T(8,128)(2,1)S(1)} %collective-permute-done.refs_6_), channel_id=1, source_target_pairs={{0,2},{1,3},{2,0},{3,1},{4,6},{5,7},{6,4},{7,5},{8,10},{9,11},{10,... | collective-permute-start | bytes 786440 | tf_op jit(solution)/shard_map/ppermute | solution.py:288
  23.9 0.0 collective-permute-done.28.refs_5_
  23.9 0.0 collective-permute-start.29
  23.9 7.7 %collective-permute-done.19.refs_4_ = bf16[2,128,512]{2,1,0:T(8,128)(2,1)S(1)} collective-permute-done((bf16[2,128,512]{2,1,0:T(8,128)(2,1)S(1)}, bf16[2,128,512]{2,1,0:T(8,128)(2,1)S(1)}, u32[]{:S(2)}, u32[]{:S(2)}) %collective-permute-start.19) | collective-permute-done | bytes 262176 | tf_op jit(solution)/shard_map/ppermute | solution.py:288
  31.6 0.5 collective-permute-start.16
  32.1 2.9 %collective-permute-done.2.refs_4_ = bf16[2,128,512]{2,1,0:T(8,128)(2,1)S(1)} collective-permute-done((bf16[2,128,512]{2,1,0:T(8,128)(2,1)S(1)}, bf16[2,128,512]{2,1,0:T(8,128)(2,1)S(1)}, u32[]{:S(2)}, u32[]{:S(2)}) %collective-permute-start.2) | collective-permute-done | bytes 262176 | tf_op jit(solution)/shard_map/ppermute | solution.py:288
  35.0 0.5 collective-permute-start.25
  35.6 0.2 collective-permute-start.4
  35.7 0.7 collective-permute-start.20
  36.4 0.1 collective-permute-done.26.refs_5_
  36.6 0.1 collective-permute-start.14
  36.7 0.2 collective-permute-done.25.refs_3_
  37.0 0.1 collective-permute-start.13
  37.7 2.6 %shard_map.65 = (bf16[640,2048]{1,0:T(8,128)(2,1)S(1)}, bf16[640,2048]{1,0:T(8,128)(2,1)S(1)}) custom-call(bf16[2,640,2048]{2,1,0:T(8,128)(2,1)} %refs_0_.2, bf16[2,640,2048]{2,1,0:T(8,128)(2,1)} %refs_1_.3), custom_call_target="tpu_custom_call" | custom-call | tf_op jit(solution)/shard_map/pallas_call | solution.py:121
  40.3 2.6 %shard_map.64 = (s32[8,128]{1,0:T(8,128)S(1)}, bf16[640,2048]{1,0:T(8,128)(2,1)S(1)}, bf16[640,2048]{1,0:T(8,128)(2,1)S(1)}) custom-call(s32[1]{0:T(128)S(6)} %copy.31.refs_0_, bf16[2,640,2048]{2,1,0:T(8,128)(2,1)} %refs_0_.2, bf16[2,640,2048]{2,1,0:T(8,128)(2,1)} %refs_1_.3), custom_call_target="tpu_custom_call" | custom-call | tf_op jit(solution)/shard_map/pallas_call | solution.py:121
  42.9 3.7 %collective-permute-done.23.refs_4_ = bf16[2,128,512]{2,1,0:T(8,128)(2,1)S(1)} collective-permute-done((bf16[2,128,512]{2,1,0:T(8,128)(2,1)S(1)}, bf16[2,128,512]{2,1,0:T(8,128)(2,1)S(1)}, u32[]{:S(2)}, u32[]{:S(2)}) %collective-permute-start.23) | collective-permute-done | bytes 262176 | tf_op jit(solution)/shard_map/ppermute | solution.py:288
  46.5 0.7 %collective-permute-start.10 = (bf16[2,128,512]{2,1,0:T(8,128)(2,1)S(1)}, bf16[2,128,512]{2,1,0:T(8,128)(2,1)S(1)}, u32[]{:S(2)}, u32[]{:S(2)}) collective-permute-start(bf16[2,128,512]{2,1,0:T(8,128)(2,1)S(1)} %collective-permute-done.2.refs_4_), channel_id=1, source_target_pairs={{0,2},{1,3},{2,0},{3,1},{4,6},{5,7},{6,4},{7,5},{8,10},{9,11},{10,... | collective-permute-start | bytes 786440 | tf_op jit(solution)/shard_map/ppermute | solution.py:288
  47.3 4.0 %collective-permute-done.4.refs_4_ = bf16[2,128,512]{2,1,0:T(8,128)(2,1)S(1)} collective-permute-done((bf16[2,128,512]{2,1,0:T(8,128)(2,1)S(1)}, bf16[2,128,512]{2,1,0:T(8,128)(2,1)S(1)}, u32[]{:S(2)}, u32[]{:S(2)}) %collective-permute-start.4) | collective-permute-done | bytes 262176 | tf_op jit(solution)/shard_map/ppermute | solution.py:288
  51.3 1.8 %shard_map.71 = (f32[640,512]{1,0:T(8,128)S(1)}, f32[640,512]{1,0:T(8,128)S(1)}, f32[4,256,256]{2,1,0:T(8,128)S(1)}) custom-call(bf16[640,2048]{1,0:T(8,128)(2,1)S(1)} %get-tuple-element.35.refs_0_.refs_2_, bf16[640,2048]{1,0:T(8,128)(2,1)S(1)} %get-tuple-element.36.refs_1_.refs_3_, bf16[2,128,512]{2,1,0:T(8,128)(2,1)S(1)} %copy-done.1, ...), custom_call_target="tpu_custom_call" | custom-call | flops 1811939328 | bytes 3538944 | tf_op jit(solution)/shard_map/pallas_call | solution.py:257
  53.1 0.2 collective-permute-start.8
  53.3 0.8 %collective-permute-start.5 = (bf16[2,128,512]{2,1,0:T(8,128)(2,1)S(1)}, bf16[2,128,512]{2,1,0:T(8,128)(2,1)S(1)}, u32[]{:S(2)}, u32[]{:S(2)}) collective-permute-start(bf16[2,128,512]{2,1,0:T(8,128)(2,1)S(1)} %collective-permute-done.4.refs_4_), channel_id=1, source_target_pairs={{0,2},{1,3},{2,0},{3,1},{4,6},{5,7},{6,4},{7,5},{8,10},{9,11},{10,... | collective-permute-start | bytes 786440 | tf_op jit(solution)/shard_map/ppermute | solution.py:288
  54.1 0.2 collective-permute-start.21
  54.3 1.8 %shard_map.68 = (f32[640,512]{1,0:T(8,128)S(1)}, f32[640,512]{1,0:T(8,128)S(1)}, f32[4,256,256]{2,1,0:T(8,128)S(1)}) custom-call(bf16[640,2048]{1,0:T(8,128)(2,1)S(1)} %get-tuple-element.33.refs_0_, bf16[640,2048]{1,0:T(8,128)(2,1)S(1)} %get-tuple-element.34.refs_1_, bf16[2,128,512]{2,1,0:T(8,128)(2,1)S(1)} %copy-done, ...), custom_call_target="tpu_custom_call" | custom-call | flops 1811939328 | bytes 3538944 | tf_op jit(solution)/shard_map/pallas_call | solution.py:257
  56.1 0.3 collective-permute-start.12
  56.5 0.2 collective-permute-start.11
  56.7 1.4 %shard_map.72 = (f32[640,512]{1,0:T(8,128)S(1)}, f32[640,512]{1,0:T(8,128)S(1)}, f32[4,256,256]{2,1,0:T(8,128)S(1)}) custom-call(bf16[640,2048]{1,0:T(8,128)(2,1)S(1)} %get-tuple-element.35.refs_0_.refs_2_, bf16[640,2048]{1,0:T(8,128)(2,1)S(1)} %get-tuple-element.36.refs_1_.refs_3_, ...), custom_call_target="tpu_custom_call", output_to_operand_aliasing={{0}: (6, {}), {1}: (7, {}), {2}: (8, {})} | custom-call | flops 1207959552 | bytes 2359296 | tf_op jit(solution)/shard_map/pallas_call | solution.py:257
  58.1 3.9 %collective-permute-done.8.refs_7_ = bf16[2,128,512]{2,1,0:T(8,128)(2,1)S(1)} collective-permute-done((bf16[2,128,512]{2,1,0:T(8,128)(2,1)S(1)}, bf16[2,128,512]{2,1,0:T(8,128)(2,1)S(1)}, u32[]{:S(2)}, u32[]{:S(2)}) %collective-permute-start.8) | collective-permute-done | bytes 262176 | tf_op jit(solution)/shard_map/ppermute | solution.py:288
  62.0 0.1 collective-permute-done.5.refs_5_
  62.1 0.4 collective-permute-start.6
  62.5 1.4 %shard_map.69 = (f32[640,512]{1,0:T(8,128)S(1)}, f32[640,512]{1,0:T(8,128)S(1)}, f32[4,256,256]{2,1,0:T(8,128)S(1)}) custom-call(bf16[640,2048]{1,0:T(8,128)(2,1)S(1)} %get-tuple-element.33.refs_0_, bf16[640,2048]{1,0:T(8,128)(2,1)S(1)} %get-tuple-element.34.refs_1_, ...), custom_call_target="tpu_custom_call", output_to_operand_aliasing={{0}: (6, {}), {1}: (7, {}), {2}: (8, {})} | custom-call | flops 1207959552 | bytes 2359296 | tf_op jit(solution)/shard_map/pallas_call | solution.py:257
  64.0 1.4 %shard_map.73 = (f32[640,512]{1,0:T(8,128)S(1)}, f32[640,512]{1,0:T(8,128)S(1)}, f32[4,256,256]{2,1,0:T(8,128)S(1)}) custom-call(bf16[640,2048]{1,0:T(8,128)(2,1)S(1)} %get-tuple-element.35.refs_0_.refs_2_, bf16[640,2048]{1,0:T(8,128)(2,1)S(1)} %get-tuple-element.36.refs_1_.refs_3_, ...), custom_call_target="tpu_custom_call", output_to_operand_aliasing={{0}: (6, {}), {1}: (7, {}), {2}: (8, {})} | custom-call | flops 1207959552 | bytes 2359296 | tf_op jit(solution)/shard_map/pallas_call | solution.py:257
  65.4 1.4 %shard_map.70 = (f32[640,512]{1,0:T(8,128)S(1)}, f32[640,512]{1,0:T(8,128)S(1)}, f32[4,256,256]{2,1,0:T(8,128)S(1)}) custom-call(bf16[640,2048]{1,0:T(8,128)(2,1)S(1)} %get-tuple-element.33.refs_0_, bf16[640,2048]{1,0:T(8,128)(2,1)S(1)} %get-tuple-element.34.refs_1_, ...), custom_call_target="tpu_custom_call", output_to_operand_aliasing={{0}: (6, {}), {1}: (7, {}), {2}: (8, {})} | custom-call | flops 1207959552 | bytes 2359296 | tf_op jit(solution)/shard_map/pallas_call | solution.py:257
  66.9 3.5 %shard_map.74 = f32[64,640]{1,0:T(8,128)} custom-call(bf16[640,2048]{1,0:T(8,128)(2,1)S(1)} %get-tuple-element.33.refs_0_, bf16[640,2048]{1,0:T(8,128)(2,1)S(1)} %get-tuple-element.34.refs_1_, bf16[640,2048]{1,0:T(8,128)(2,1)S(1)} %get-tuple-element.35.refs_0_.refs_2_, bf16[640,2048]{1,0:T(8,128)(2,1)S(1)} %get-tuple-element.36.refs_1_.refs_3_, ...), custom_call_target="tpu_custom_call" | custom-call | flops 1207959552 | bytes 2359296 | tf_op jit(solution)/shard_map/pallas_call | solution.py:257
  (27 shorter events, 0.1 us)
Async XLA Ops:
  2.1 8.9 %copy-start.1 = (bf16[2,128,512]{2,1,0:T(8,128)(2,1)S(1)}, bf16[2,128,512]{2,1,0:T(8,128)(2,1)}, u32[]{:S(2)}) copy-start(bf16[2,128,512]{2,1,0:T(8,128)(2,1)} %shard_map.67.refs_2_) | copy-start | bytes 786436
  2.1 9.5 %collective-permute-start.7 = (bf16[2,128,512]{2,1,0:T(8,128)(2,1)}, bf16[2,128,512]{2,1,0:T(8,128)(2,1)S(1)}, u32[]{:S(2)}, u32[]{:S(2)}) collective-permute-start(bf16[2,128,512]{2,1,0:T(8,128)(2,1)} %shard_map.67.refs_2_), channel_id=1, source_target_pairs={{0,2},{1,3},{2,0},{3,1},{4,6},{5,7},{6,4},{7,5},{8,10},{9,11},{10,... | collective-permute-start | bytes 786440 | tf_op jit(solution)/shard_map/ppermute | solution.py:288
  5.1 11.2 %collective-permute-start.18 = (bf16[2,128,512]{2,1,0:T(8,128)(2,1)}, bf16[2,128,512]{2,1,0:T(8,128)(2,1)S(1)}, u32[]{:S(2)}, u32[]{:S(2)}) collective-permute-start(bf16[2,128,512]{2,1,0:T(8,128)(2,1)} %shard_map.67.refs_2_), channel_id=1, source_target_pairs={{0,4},{1,5},{2,6},{3,7},{4,8},{5,9},{6,10},{7,11},{8,12},{9,13},{1... | collective-permute-start | bytes 786440 | tf_op jit(solution)/shard_map/ppermute | solution.py:288
  8.8 11.8 %collective-permute-start = (bf16[2,128,512]{2,1,0:T(8,128)(2,1)}, bf16[2,128,512]{2,1,0:T(8,128)(2,1)S(1)}, u32[]{:S(2)}, u32[]{:S(2)}) collective-permute-start(bf16[2,128,512]{2,1,0:T(8,128)(2,1)} %shard_map.66.refs_2_), channel_id=1, source_target_pairs={{0,4},{1,5},{2,6},{3,7},{4,8},{5,9},{6,10},{7,11},{8,12},{9,13},{1... | collective-permute-start | bytes 786440 | tf_op jit(solution)/shard_map/ppermute | solution.py:288
  10.4 10.2 %collective-permute-start.1 = (bf16[2,128,512]{2,1,0:T(8,128)(2,1)}, bf16[2,128,512]{2,1,0:T(8,128)(2,1)S(1)}, u32[]{:S(2)}, u32[]{:S(2)}) collective-permute-start(bf16[2,128,512]{2,1,0:T(8,128)(2,1)} %shard_map.66.refs_2_), channel_id=1, source_target_pairs={{0,2},{1,3},{2,0},{3,1},{4,6},{5,7},{6,4},{7,5},{8,10},{9,11},{10,... | collective-permute-start | bytes 786440 | tf_op jit(solution)/shard_map/ppermute | solution.py:288
  11.0 10.2 %collective-permute-start.27 = (bf16[2,128,512]{2,1,0:T(8,128)(2,1)S(1)}, bf16[2,128,512]{2,1,0:T(8,128)(2,1)S(1)}, u32[]{:S(2)}, u32[]{:S(2)}) collective-permute-start(bf16[2,128,512]{2,1,0:T(8,128)(2,1)S(1)} %copy-done.1), channel_id=1, source_target_pairs={{0,1},{1,0},{2,3},{3,2},{4,5},{5,4},{6,7},{7,6},{8,9},{9,8},{10,11... | collective-permute-start | bytes 786440 | tf_op jit(solution)/shard_map/ppermute | solution.py:288
  11.7 10.8 %collective-permute-start.15 = (bf16[2,128,512]{2,1,0:T(8,128)(2,1)}, bf16[2,128,512]{2,1,0:T(8,128)(2,1)S(1)}, u32[]{:S(2)}, u32[]{:S(2)}) collective-permute-start(bf16[2,128,512]{2,1,0:T(8,128)(2,1)} %shard_map.66.refs_2_), channel_id=1, source_target_pairs={{0,1},{1,0},{2,3},{3,2},{4,5},{5,4},{6,7},{7,6},{8,9},{9,8},{10,11... | collective-permute-start | bytes 786440 | tf_op jit(solution)/shard_map/ppermute | solution.py:288
  16.3 7.6 %collective-permute-start.28 = (bf16[2,128,512]{2,1,0:T(8,128)(2,1)S(1)}, bf16[2,128,512]{2,1,0:T(8,128)(2,1)S(1)}, u32[]{:S(2)}, u32[]{:S(2)}) collective-permute-start(bf16[2,128,512]{2,1,0:T(8,128)(2,1)S(1)} %collective-permute-done.7.refs_4_), channel_id=1, source_target_pairs={{0,1},{1,0},{2,3},{3,2},{4,5},{5,4},{6,7},{7,6},{8,9},{9,8},{10,11... | collective-permute-start | bytes 786440 | tf_op jit(solution)/shard_map/ppermute | solution.py:288
  20.6 11.0 %collective-permute-start.19 = (bf16[2,128,512]{2,1,0:T(8,128)(2,1)S(1)}, bf16[2,128,512]{2,1,0:T(8,128)(2,1)S(1)}, u32[]{:S(2)}, u32[]{:S(2)}) collective-permute-start(bf16[2,128,512]{2,1,0:T(8,128)(2,1)S(1)} %collective-permute-done.18.refs_6_), channel_id=1, source_target_pairs={{0,4},{1,5},{2,6},{3,7},{4,8},{5,9},{6,10},{7,11},{8,12},{9,13},{1... | collective-permute-start | bytes 786440 | tf_op jit(solution)/shard_map/ppermute | solution.py:288
  20.6 11.0 %collective-permute-start.22 = (bf16[2,128,512]{2,1,0:T(8,128)(2,1)S(1)}, bf16[2,128,512]{2,1,0:T(8,128)(2,1)S(1)}, u32[]{:S(2)}, u32[]{:S(2)}) collective-permute-start(bf16[2,128,512]{2,1,0:T(8,128)(2,1)S(1)} %collective-permute-done.18.refs_6_), channel_id=1, source_target_pairs={{0,2},{1,3},{2,0},{3,1},{4,6},{5,7},{6,4},{7,5},{8,10},{9,11},{10,... | collective-permute-start | bytes 786440 | tf_op jit(solution)/shard_map/ppermute | solution.py:288
  21.2 13.9 %collective-permute-start.2 = (bf16[2,128,512]{2,1,0:T(8,128)(2,1)S(1)}, bf16[2,128,512]{2,1,0:T(8,128)(2,1)S(1)}, u32[]{:S(2)}, u32[]{:S(2)}) collective-permute-start(bf16[2,128,512]{2,1,0:T(8,128)(2,1)S(1)} %collective-permute-done.refs_6_), channel_id=1, source_target_pairs={{0,4},{1,5},{2,6},{3,7},{4,8},{5,9},{6,10},{7,11},{8,12},{9,13},{1... | collective-permute-start | bytes 786440 | tf_op jit(solution)/shard_map/ppermute | solution.py:288
  22.4 12.6 %collective-permute-start.3 = (bf16[2,128,512]{2,1,0:T(8,128)(2,1)S(1)}, bf16[2,128,512]{2,1,0:T(8,128)(2,1)S(1)}, u32[]{:S(2)}, u32[]{:S(2)}) collective-permute-start(bf16[2,128,512]{2,1,0:T(8,128)(2,1)S(1)} %collective-permute-done.refs_6_), channel_id=1, source_target_pairs={{0,2},{1,3},{2,0},{3,1},{4,6},{5,7},{6,4},{7,5},{8,10},{9,11},{10,... | collective-permute-start | bytes 786440 | tf_op jit(solution)/shard_map/ppermute | solution.py:288
  23.9 11.6 %collective-permute-start.29 = (bf16[2,128,512]{2,1,0:T(8,128)(2,1)S(1)}, bf16[2,128,512]{2,1,0:T(8,128)(2,1)S(1)}, u32[]{:S(2)}, u32[]{:S(2)}) collective-permute-start(bf16[2,128,512]{2,1,0:T(8,128)(2,1)S(1)} %collective-permute-done.18.refs_6_), channel_id=1, source_target_pairs={{0,1},{1,0},{2,3},{3,2},{4,5},{5,4},{6,7},{7,6},{8,9},{9,8},{10,11... | collective-permute-start | bytes 786440 | tf_op jit(solution)/shard_map/ppermute | solution.py:288
  31.6 4.0 %collective-permute-start.17 = (bf16[2,128,512]{2,1,0:T(8,128)(2,1)S(1)}, bf16[2,128,512]{2,1,0:T(8,128)(2,1)S(1)}, u32[]{:S(2)}, u32[]{:S(2)}) collective-permute-start(bf16[2,128,512]{2,1,0:T(8,128)(2,1)S(1)} %collective-permute-done.refs_6_), channel_id=1, source_target_pairs={{0,1},{1,0},{2,3},{3,2},{4,5},{5,4},{6,7},{7,6},{8,9},{9,8},{10,11... | collective-permute-start | bytes 786440 | tf_op jit(solution)/shard_map/ppermute | solution.py:288
  31.6 4.1 %collective-permute-start.16 = (bf16[2,128,512]{2,1,0:T(8,128)(2,1)S(1)}, bf16[2,128,512]{2,1,0:T(8,128)(2,1)S(1)}, u32[]{:S(2)}, u32[]{:S(2)}) collective-permute-start(bf16[2,128,512]{2,1,0:T(8,128)(2,1)S(1)} %collective-permute-done.1.refs_4_), channel_id=1, source_target_pairs={{0,1},{1,0},{2,3},{3,2},{4,5},{5,4},{6,7},{7,6},{8,9},{9,8},{10,11... | collective-permute-start | bytes 786440 | tf_op jit(solution)/shard_map/ppermute | solution.py:288
  35.0 1.5 %collective-permute-start.26 = (bf16[2,128,512]{2,1,0:T(8,128)(2,1)S(1)}, bf16[2,128,512]{2,1,0:T(8,128)(2,1)S(1)}, u32[]{:S(2)}, u32[]{:S(2)}) collective-permute-start(bf16[2,128,512]{2,1,0:T(8,128)(2,1)S(1)} %collective-permute-done.19.refs_4_), channel_id=1, source_target_pairs={{0,1},{1,0},{2,3},{3,2},{4,5},{5,4},{6,7},{7,6},{8,9},{9,8},{10,11... | collective-permute-start | bytes 786440 | tf_op jit(solution)/shard_map/ppermute | solution.py:288
  35.0 1.9 %collective-permute-start.25 = (bf16[2,128,512]{2,1,0:T(8,128)(2,1)S(1)}, bf16[2,128,512]{2,1,0:T(8,128)(2,1)S(1)}, u32[]{:S(2)}, u32[]{:S(2)}) collective-permute-start(bf16[2,128,512]{2,1,0:T(8,128)(2,1)S(1)} %collective-permute-done.22.refs_2_), channel_id=1, source_target_pairs={{0,1},{1,0},{2,3},{3,2},{4,5},{5,4},{6,7},{7,6},{8,9},{9,8},{10,11... | collective-permute-start | bytes 786440 | tf_op jit(solution)/shard_map/ppermute | solution.py:288
  35.6 11.0 %collective-permute-start.23 = (bf16[2,128,512]{2,1,0:T(8,128)(2,1)S(1)}, bf16[2,128,512]{2,1,0:T(8,128)(2,1)S(1)}, u32[]{:S(2)}, u32[]{:S(2)}) collective-permute-start(bf16[2,128,512]{2,1,0:T(8,128)(2,1)S(1)} %collective-permute-done.19.refs_4_), channel_id=1, source_target_pairs={{0,4},{1,5},{2,6},{3,7},{4,8},{5,9},{6,10},{7,11},{8,12},{9,13},{1... | collective-permute-start | bytes 786440 | tf_op jit(solution)/shard_map/ppermute | solution.py:288
  35.6 15.7 %collective-permute-start.4 = (bf16[2,128,512]{2,1,0:T(8,128)(2,1)S(1)}, bf16[2,128,512]{2,1,0:T(8,128)(2,1)S(1)}, u32[]{:S(2)}, u32[]{:S(2)}) collective-permute-start(bf16[2,128,512]{2,1,0:T(8,128)(2,1)S(1)} %collective-permute-done.2.refs_4_), channel_id=1, source_target_pairs={{0,4},{1,5},{2,6},{3,7},{4,8},{5,9},{6,10},{7,11},{8,12},{9,13},{1... | collective-permute-start | bytes 786440 | tf_op jit(solution)/shard_map/ppermute | solution.py:288
  35.7 17.3 %collective-permute-start.20 = (bf16[2,128,512]{2,1,0:T(8,128)(2,1)S(1)}, bf16[2,128,512]{2,1,0:T(8,128)(2,1)S(1)}, u32[]{:S(2)}, u32[]{:S(2)}) collective-permute-start(bf16[2,128,512]{2,1,0:T(8,128)(2,1)S(1)} %collective-permute-done.19.refs_4_), channel_id=1, source_target_pairs={{0,2},{1,3},{2,0},{3,1},{4,6},{5,7},{6,4},{7,5},{8,10},{9,11},{10,... | collective-permute-start | bytes 786440 | tf_op jit(solution)/shard_map/ppermute | solution.py:288
  36.6 16.7 %collective-permute-start.14 = (bf16[2,128,512]{2,1,0:T(8,128)(2,1)S(1)}, bf16[2,128,512]{2,1,0:T(8,128)(2,1)S(1)}, u32[]{:S(2)}, u32[]{:S(2)}) collective-permute-start(bf16[2,128,512]{2,1,0:T(8,128)(2,1)S(1)} %collective-permute-done.2.refs_4_), channel_id=1, source_target_pairs={{0,1},{1,0},{2,3},{3,2},{4,5},{5,4},{6,7},{7,6},{8,9},{9,8},{10,11... | collective-permute-start | bytes 786440 | tf_op jit(solution)/shard_map/ppermute | solution.py:288
  37.0 17.1 %collective-permute-start.13 = (bf16[2,128,512]{2,1,0:T(8,128)(2,1)S(1)}, bf16[2,128,512]{2,1,0:T(8,128)(2,1)S(1)}, u32[]{:S(2)}, u32[]{:S(2)}) collective-permute-start(bf16[2,128,512]{2,1,0:T(8,128)(2,1)S(1)} %collective-permute-done.3.refs_2_), channel_id=1, source_target_pairs={{0,1},{1,0},{2,3},{3,2},{4,5},{5,4},{6,7},{7,6},{8,9},{9,8},{10,11... | collective-permute-start | bytes 786440 | tf_op jit(solution)/shard_map/ppermute | solution.py:288
  46.5 9.6 %collective-permute-start.10 = (bf16[2,128,512]{2,1,0:T(8,128)(2,1)S(1)}, bf16[2,128,512]{2,1,0:T(8,128)(2,1)S(1)}, u32[]{:S(2)}, u32[]{:S(2)}) collective-permute-start(bf16[2,128,512]{2,1,0:T(8,128)(2,1)S(1)} %collective-permute-done.2.refs_4_), channel_id=1, source_target_pairs={{0,2},{1,3},{2,0},{3,1},{4,6},{5,7},{6,4},{7,5},{8,10},{9,11},{10,... | collective-permute-start | bytes 786440 | tf_op jit(solution)/shard_map/ppermute | solution.py:288
  51.2 5.2 %collective-permute-start.24 = (bf16[2,128,512]{2,1,0:T(8,128)(2,1)S(1)}, bf16[2,128,512]{2,1,0:T(8,128)(2,1)S(1)}, u32[]{:S(2)}, u32[]{:S(2)}) collective-permute-start(bf16[2,128,512]{2,1,0:T(8,128)(2,1)S(1)} %collective-permute-done.23.refs_4_), channel_id=1, source_target_pairs={{0,1},{1,0},{2,3},{3,2},{4,5},{5,4},{6,7},{7,6},{8,9},{9,8},{10,11... | collective-permute-start | bytes 786440 | tf_op jit(solution)/shard_map/ppermute | solution.py:288
  51.2 3.1 %copy-start = (bf16[2,128,512]{2,1,0:T(8,128)(2,1)S(1)}, bf16[2,128,512]{2,1,0:T(8,128)(2,1)}, u32[]{:S(2)}) copy-start(bf16[2,128,512]{2,1,0:T(8,128)(2,1)} %shard_map.66.refs_2_) | copy-start | bytes 786436
  53.1 8.9 %collective-permute-start.8 = (bf16[2,128,512]{2,1,0:T(8,128)(2,1)S(1)}, bf16[2,128,512]{2,1,0:T(8,128)(2,1)S(1)}, u32[]{:S(2)}, u32[]{:S(2)}) collective-permute-start(bf16[2,128,512]{2,1,0:T(8,128)(2,1)S(1)} %collective-permute-done.7.refs_4_), channel_id=1, source_target_pairs={{0,12},{1,13},{2,14},{3,15},{4,0},{5,1},{6,2},{7,3},{8,4},{9,5},{1... | collective-permute-start | bytes 786440 | tf_op jit(solution)/shard_map/ppermute | solution.py:288
  53.3 8.8 %collective-permute-start.5 = (bf16[2,128,512]{2,1,0:T(8,128)(2,1)S(1)}, bf16[2,128,512]{2,1,0:T(8,128)(2,1)S(1)}, u32[]{:S(2)}, u32[]{:S(2)}) collective-permute-start(bf16[2,128,512]{2,1,0:T(8,128)(2,1)S(1)} %collective-permute-done.4.refs_4_), channel_id=1, source_target_pairs={{0,2},{1,3},{2,0},{3,1},{4,6},{5,7},{6,4},{7,5},{8,10},{9,11},{10,... | collective-permute-start | bytes 786440 | tf_op jit(solution)/shard_map/ppermute | solution.py:288
  54.1 9.9 %collective-permute-start.21 = (bf16[2,128,512]{2,1,0:T(8,128)(2,1)S(1)}, bf16[2,128,512]{2,1,0:T(8,128)(2,1)S(1)}, u32[]{:S(2)}, u32[]{:S(2)}) collective-permute-start(bf16[2,128,512]{2,1,0:T(8,128)(2,1)S(1)} %collective-permute-done.20.refs_2_), channel_id=1, source_target_pairs={{0,1},{1,0},{2,3},{3,2},{4,5},{5,4},{6,7},{7,6},{8,9},{9,8},{10,11... | collective-permute-start | bytes 786440 | tf_op jit(solution)/shard_map/ppermute | solution.py:288
  56.1 9.3 %collective-permute-start.12 = (bf16[2,128,512]{2,1,0:T(8,128)(2,1)S(1)}, bf16[2,128,512]{2,1,0:T(8,128)(2,1)S(1)}, u32[]{:S(2)}, u32[]{:S(2)}) collective-permute-start(bf16[2,128,512]{2,1,0:T(8,128)(2,1)S(1)} %collective-permute-done.4.refs_4_), channel_id=1, source_target_pairs={{0,1},{1,0},{2,3},{3,2},{4,5},{5,4},{6,7},{7,6},{8,9},{9,8},{10,11... | collective-permute-start | bytes 786440 | tf_op jit(solution)/shard_map/ppermute | solution.py:288
  56.5 9.0 %collective-permute-start.11 = (bf16[2,128,512]{2,1,0:T(8,128)(2,1)S(1)}, bf16[2,128,512]{2,1,0:T(8,128)(2,1)S(1)}, u32[]{:S(2)}, u32[]{:S(2)}) collective-permute-start(bf16[2,128,512]{2,1,0:T(8,128)(2,1)S(1)} %collective-permute-done.10.refs_2_), channel_id=1, source_target_pairs={{0,1},{1,0},{2,3},{3,2},{4,5},{5,4},{6,7},{7,6},{8,9},{9,8},{10,11... | collective-permute-start | bytes 786440 | tf_op jit(solution)/shard_map/ppermute | solution.py:288
  62.0 4.9 %collective-permute-start.9 = (bf16[2,128,512]{2,1,0:T(8,128)(2,1)S(1)}, bf16[2,128,512]{2,1,0:T(8,128)(2,1)S(1)}, u32[]{:S(2)}, u32[]{:S(2)}) collective-permute-start(bf16[2,128,512]{2,1,0:T(8,128)(2,1)S(1)} %collective-permute-done.8.refs_7_), channel_id=1, source_target_pairs={{0,1},{1,0},{2,3},{3,2},{4,5},{5,4},{6,7},{7,6},{8,9},{9,8},{10,11... | collective-permute-start | bytes 786440 | tf_op jit(solution)/shard_map/ppermute | solution.py:288
  62.1 4.8 %collective-permute-start.6 = (bf16[2,128,512]{2,1,0:T(8,128)(2,1)S(1)}, bf16[2,128,512]{2,1,0:T(8,128)(2,1)S(1)}, u32[]{:S(2)}, u32[]{:S(2)}) collective-permute-start(bf16[2,128,512]{2,1,0:T(8,128)(2,1)S(1)} %collective-permute-done.5.refs_5_), channel_id=1, source_target_pairs={{0,1},{1,0},{2,3},{3,2},{4,5},{5,4},{6,7},{7,6},{8,9},{9,8},{10,11... | collective-permute-start | bytes 786440 | tf_op jit(solution)/shard_map/ppermute | solution.py:288

commit v7 on v6

--- a/solution.py
+++ b/solution.py
@@ -13,6 +13,7 @@
 OUTER = 4
 LANES = 128
 TILE = 256
+TERMS = 2
 LOAD_GRANTS = (46 << 20, 45 << 20)
 
 
@@ -131,7 +132,7 @@
 def split_dot(left, right):
     total = None
     rest = left
-    for _ in range(3):
+    for _ in range(TERMS):
         term = rest.astype(jnp.bfloat16)
         rest = rest - term.astype(jnp.float32)
         part = jnp.dot(term, right, preferred_element_type=jnp.float32)
@@ -207,10 +208,18 @@
         norm = jnp.broadcast_to(jnp.concatenate(norm, axis=1), (8, columns))
         chooser = group_sums(columns)
         scale = 1.0 / jnp.sqrt(split_dot(norm, chooser)[:1] + 1e-06)
-        scaled = split_dot(product[...], chooser) * scale
-        token = lax.broadcasted_iota(jnp.int32, scaled.shape, 0)
-        scaled = jnp.where(token < live_ref[:1], scaled, 0.0)
-        outs[0][...] = scaled.T[: columns // RANK]
+        tokens = product.shape[0]
+        for low in range(0, tokens, LANES):
+            span = slice(low, low + LANES)
+            rest, terms = product[span], []
+            for _ in range(TERMS):
+                terms.append(rest.astype(jnp.bfloat16))
+                rest = rest - terms[-1].astype(jnp.float32)
+            raw = jnp.dot(jnp.concatenate(terms, axis=0), chooser, preferred_element_type=jnp.float32)
+            raw = sum(raw[i * LANES : (i + 1) * LANES] for i in range(TERMS))
+            token = low + lax.broadcasted_iota(jnp.int32, raw.shape, 0)
+            scaled = jnp.where(token < live_ref[:1], raw * scale, 0.0)
+            outs[0][:, span] = scaled.T[: columns // RANK]
 
 
 def stage(shape, groups, live=None):

time: 70.6 us -> 70.1 us (level)
  transfers between devices with their start and end apart: 30 -> 30, of which waited for: 11 -> 11; matrix products, arithmetic and copies ran while one was open for 0% -> 0% of each run, Pallas kernels for 23% -> 24%
where the time goes in v7:
time: 70.1 us; the launch traced here: 69.9 us
  waiting for transfers between devices  32.3 us (46%)
  Pallas kernels  21.6 us (31%)
  starting transfers between devices  15.2 us (22%)
  between operations  0.84 us (1%)
    ppermute x30, waiting for transfers between devices, move(): return lax.ppermute(value, 'tok', steps)  32.3 us
    ppermute x30, starting transfers between devices, move(): return lax.ppermute(value, 'tok', steps)  15.2 us
    pallas_call x7, Pallas kernels, stage(): pl.pallas_call(functools.partial(stage_kernel, cfg), out_shape=out_shape,...  12.3 us
    pallas_call x2, Pallas kernels, load(): pl.pallas_call(functools.partial(load_kernel, layer), out_shape=tuple(out...  5.1 us
    pallas_call x2, Pallas kernels, pick(): pl.pallas_call(functools.partial(pick_kernel, layer), out_shape=jax.Shape...  4.18 us
  transfers between devices with their start and end apart: 30, of which 11 were waited for; matrix products, arithmetic and copies ran while one was open for 0% of the time, Pallas kernels for 24%

profile of v7, /device:TPU:0, one launch (start us, length us, event | category | flops | bytes accessed | tf_op | source)
XLA Modules:
  0.0 69.9 jit_solution(868543929926112782)
XLA Ops:
  0.0 2.1 %shard_map.67.refs_2_ = bf16[2,128,512]{2,1,0:T(8,128)(2,1)} custom-call(s32[2,16]{1,0:T(2,128)} %ids_hbm.3, bf16[2,128,1024]{2,1,0:T(8,128)(2,1)} %u_ref.3, bf16[2,128,1024]{2,1,0:T(8,128)(2,1)} %v_ref.3), custom_call_target="tpu_custom_call" | custom-call | flops 262144 | bytes 786432 | tf_op jit(solution)/shard_map/pallas_call | solution.py:86
  2.1 3.0 %collective-permute-start.7 = (bf16[2,128,512]{2,1,0:T(8,128)(2,1)}, bf16[2,128,512]{2,1,0:T(8,128)(2,1)S(1)}, u32[]{:S(2)}, u32[]{:S(2)}) collective-permute-start(bf16[2,128,512]{2,1,0:T(8,128)(2,1)} %shard_map.67.refs_2_), channel_id=1, source_target_pairs={{0,2},{1,3},{2,0},{3,1},{4,6},{5,7},{6,4},{7,5},{8,10},{9,11},{10,... | collective-permute-start | bytes 786440 | tf_op jit(solution)/shard_map/ppermute | solution.py:297
  5.1 1.6 %collective-permute-start.18 = (bf16[2,128,512]{2,1,0:T(8,128)(2,1)}, bf16[2,128,512]{2,1,0:T(8,128)(2,1)S(1)}, u32[]{:S(2)}, u32[]{:S(2)}) collective-permute-start(bf16[2,128,512]{2,1,0:T(8,128)(2,1)} %shard_map.67.refs_2_), channel_id=1, source_target_pairs={{0,4},{1,5},{2,6},{3,7},{4,8},{5,9},{6,10},{7,11},{8,12},{9,13},{1... | collective-permute-start | bytes 786440 | tf_op jit(solution)/shard_map/ppermute | solution.py:297
  6.7 2.1 %shard_map.66.refs_2_ = bf16[2,128,512]{2,1,0:T(8,128)(2,1)} custom-call(s32[2,16]{1,0:T(2,128)} %ids_hbm.3, bf16[2,128,1024]{2,1,0:T(8,128)(2,1)} %u_ref.3, bf16[2,128,1024]{2,1,0:T(8,128)(2,1)} %v_ref.3), custom_call_target="tpu_custom_call" | custom-call | flops 262144 | bytes 786432 | tf_op jit(solution)/shard_map/pallas_call | solution.py:86
  8.8 1.6 %collective-permute-start = (bf16[2,128,512]{2,1,0:T(8,128)(2,1)}, bf16[2,128,512]{2,1,0:T(8,128)(2,1)S(1)}, u32[]{:S(2)}, u32[]{:S(2)}) collective-permute-start(bf16[2,128,512]{2,1,0:T(8,128)(2,1)} %shard_map.66.refs_2_), channel_id=1, source_target_pairs={{0,4},{1,5},{2,6},{3,7},{4,8},{5,9},{6,10},{7,11},{8,12},{9,13},{1... | collective-permute-start | bytes 786440 | tf_op jit(solution)/shard_map/ppermute | solution.py:297
  10.4 0.5 collective-permute-start.1
  11.0 0.7 collective-permute-done.7.refs_4_
  11.7 0.0 collective-permute-start.15
  11.7 4.7 %collective-permute-done.18.refs_6_ = bf16[2,128,512]{2,1,0:T(8,128)(2,1)S(1)} collective-permute-done((bf16[2,128,512]{2,1,0:T(8,128)(2,1)}, bf16[2,128,512]{2,1,0:T(8,128)(2,1)S(1)}, u32[]{:S(2)}, u32[]{:S(2)}) %collective-permute-start.18) | collective-permute-done | bytes 262176 | tf_op jit(solution)/shard_map/ppermute | solution.py:297
  16.3 0.0 collective-permute-start.28
  16.3 4.3 %collective-permute-done.refs_6_ = bf16[2,128,512]{2,1,0:T(8,128)(2,1)S(1)} collective-permute-done((bf16[2,128,512]{2,1,0:T(8,128)(2,1)}, bf16[2,128,512]{2,1,0:T(8,128)(2,1)S(1)}, u32[]{:S(2)}, u32[]{:S(2)}) %collective-permute-start) | collective-permute-done | bytes 262176 | tf_op jit(solution)/shard_map/ppermute | solution.py:297
  20.6 0.0 collective-permute-start.19
  20.6 0.5 collective-permute-start.22
  21.2 1.3 %collective-permute-start.2 = (bf16[2,128,512]{2,1,0:T(8,128)(2,1)S(1)}, bf16[2,128,512]{2,1,0:T(8,128)(2,1)S(1)}, u32[]{:S(2)}, u32[]{:S(2)}) collective-permute-start(bf16[2,128,512]{2,1,0:T(8,128)(2,1)S(1)} %collective-permute-done.refs_6_), channel_id=1, source_target_pairs={{0,4},{1,5},{2,6},{3,7},{4,8},{5,9},{6,10},{7,11},{8,12},{9,13},{1... | collective-permute-start | bytes 786440 | tf_op jit(solution)/shard_map/ppermute | solution.py:297
  22.4 0.0 collective-permute-done.15.refs_3_
  22.4 1.5 %collective-permute-start.3 = (bf16[2,128,512]{2,1,0:T(8,128)(2,1)S(1)}, bf16[2,128,512]{2,1,0:T(8,128)(2,1)S(1)}, u32[]{:S(2)}, u32[]{:S(2)}) collective-permute-start(bf16[2,128,512]{2,1,0:T(8,128)(2,1)S(1)} %collective-permute-done.refs_6_), channel_id=1, source_target_pairs={{0,2},{1,3},{2,0},{3,1},{4,6},{5,7},{6,4},{7,5},{8,10},{9,11},{10,... | collective-permute-start | bytes 786440 | tf_op jit(solution)/shard_map/ppermute | solution.py:297
  23.9 0.0 collective-permute-done.28.refs_5_
  23.9 0.0 collective-permute-start.29
  23.9 7.7 %collective-permute-done.19.refs_4_ = bf16[2,128,512]{2,1,0:T(8,128)(2,1)S(1)} collective-permute-done((bf16[2,128,512]{2,1,0:T(8,128)(2,1)S(1)}, bf16[2,128,512]{2,1,0:T(8,128)(2,1)S(1)}, u32[]{:S(2)}, u32[]{:S(2)}) %collective-permute-start.19) | collective-permute-done | bytes 262176 | tf_op jit(solution)/shard_map/ppermute | solution.py:297
  31.6 0.5 collective-permute-start.16
  32.1 2.9 %collective-permute-done.2.refs_4_ = bf16[2,128,512]{2,1,0:T(8,128)(2,1)S(1)} collective-permute-done((bf16[2,128,512]{2,1,0:T(8,128)(2,1)S(1)}, bf16[2,128,512]{2,1,0:T(8,128)(2,1)S(1)}, u32[]{:S(2)}, u32[]{:S(2)}) %collective-permute-start.2) | collective-permute-done | bytes 262176 | tf_op jit(solution)/shard_map/ppermute | solution.py:297
  35.0 0.5 collective-permute-start.25
  35.6 0.2 collective-permute-start.4
  35.7 0.7 %collective-permute-start.20 = (bf16[2,128,512]{2,1,0:T(8,128)(2,1)S(1)}, bf16[2,128,512]{2,1,0:T(8,128)(2,1)S(1)}, u32[]{:S(2)}, u32[]{:S(2)}) collective-permute-start(bf16[2,128,512]{2,1,0:T(8,128)(2,1)S(1)} %collective-permute-done.19.refs_4_), channel_id=1, source_target_pairs={{0,2},{1,3},{2,0},{3,1},{4,6},{5,7},{6,4},{7,5},{8,10},{9,11},{10,... | collective-permute-start | bytes 786440 | tf_op jit(solution)/shard_map/ppermute | solution.py:297
  36.4 0.1 collective-permute-done.26.refs_5_
  36.6 0.1 collective-permute-start.14
  36.7 0.2 collective-permute-done.25.refs_3_
  37.0 0.1 collective-permute-start.13
  37.7 2.6 %shard_map.65 = (bf16[640,2048]{1,0:T(8,128)(2,1)S(1)}, bf16[640,2048]{1,0:T(8,128)(2,1)S(1)}) custom-call(bf16[2,640,2048]{2,1,0:T(8,128)(2,1)} %refs_0_.2, bf16[2,640,2048]{2,1,0:T(8,128)(2,1)} %refs_1_.3), custom_call_target="tpu_custom_call" | custom-call | tf_op jit(solution)/shard_map/pallas_call | solution.py:122
  40.3 2.6 %shard_map.64 = (s32[8,128]{1,0:T(8,128)S(1)}, bf16[640,2048]{1,0:T(8,128)(2,1)S(1)}, bf16[640,2048]{1,0:T(8,128)(2,1)S(1)}) custom-call(s32[1]{0:T(128)S(6)} %copy.31.refs_0_, bf16[2,640,2048]{2,1,0:T(8,128)(2,1)} %refs_0_.2, bf16[2,640,2048]{2,1,0:T(8,128)(2,1)} %refs_1_.3), custom_call_target="tpu_custom_call" | custom-call | tf_op jit(solution)/shard_map/pallas_call | solution.py:122
  42.9 3.7 %collective-permute-done.23.refs_4_ = bf16[2,128,512]{2,1,0:T(8,128)(2,1)S(1)} collective-permute-done((bf16[2,128,512]{2,1,0:T(8,128)(2,1)S(1)}, bf16[2,128,512]{2,1,0:T(8,128)(2,1)S(1)}, u32[]{:S(2)}, u32[]{:S(2)}) %collective-permute-start.23) | collective-permute-done | bytes 262176 | tf_op jit(solution)/shard_map/ppermute | solution.py:297
  46.5 0.7 %collective-permute-start.10 = (bf16[2,128,512]{2,1,0:T(8,128)(2,1)S(1)}, bf16[2,128,512]{2,1,0:T(8,128)(2,1)S(1)}, u32[]{:S(2)}, u32[]{:S(2)}) collective-permute-start(bf16[2,128,512]{2,1,0:T(8,128)(2,1)S(1)} %collective-permute-done.2.refs_4_), channel_id=1, source_target_pairs={{0,2},{1,3},{2,0},{3,1},{4,6},{5,7},{6,4},{7,5},{8,10},{9,11},{10,... | collective-permute-start | bytes 786440 | tf_op jit(solution)/shard_map/ppermute | solution.py:297
  47.3 4.0 %collective-permute-done.4.refs_4_ = bf16[2,128,512]{2,1,0:T(8,128)(2,1)S(1)} collective-permute-done((bf16[2,128,512]{2,1,0:T(8,128)(2,1)S(1)}, bf16[2,128,512]{2,1,0:T(8,128)(2,1)S(1)}, u32[]{:S(2)}, u32[]{:S(2)}) %collective-permute-start.4) | collective-permute-done | bytes 262176 | tf_op jit(solution)/shard_map/ppermute | solution.py:297
  51.3 1.8 %shard_map.71 = (f32[640,512]{1,0:T(8,128)S(1)}, f32[640,512]{1,0:T(8,128)S(1)}, f32[4,256,256]{2,1,0:T(8,128)S(1)}) custom-call(bf16[640,2048]{1,0:T(8,128)(2,1)S(1)} %get-tuple-element.35.refs_0_.refs_2_, bf16[640,2048]{1,0:T(8,128)(2,1)S(1)} %get-tuple-element.36.refs_1_.refs_3_, bf16[2,128,512]{2,1,0:T(8,128)(2,1)S(1)} %copy-done.1, ...), custom_call_target="tpu_custom_call" | custom-call | flops 1811939328 | bytes 3538944 | tf_op jit(solution)/shard_map/pallas_call | solution.py:266
  53.1 0.2 collective-permute-start.8
  53.3 0.8 %collective-permute-start.5 = (bf16[2,128,512]{2,1,0:T(8,128)(2,1)S(1)}, bf16[2,128,512]{2,1,0:T(8,128)(2,1)S(1)}, u32[]{:S(2)}, u32[]{:S(2)}) collective-permute-start(bf16[2,128,512]{2,1,0:T(8,128)(2,1)S(1)} %collective-permute-done.4.refs_4_), channel_id=1, source_target_pairs={{0,2},{1,3},{2,0},{3,1},{4,6},{5,7},{6,4},{7,5},{8,10},{9,11},{10,... | collective-permute-start | bytes 786440 | tf_op jit(solution)/shard_map/ppermute | solution.py:297
  54.1 0.2 collective-permute-start.21
  54.3 1.8 %shard_map.68 = (f32[640,512]{1,0:T(8,128)S(1)}, f32[640,512]{1,0:T(8,128)S(1)}, f32[4,256,256]{2,1,0:T(8,128)S(1)}) custom-call(bf16[640,2048]{1,0:T(8,128)(2,1)S(1)} %get-tuple-element.33.refs_0_, bf16[640,2048]{1,0:T(8,128)(2,1)S(1)} %get-tuple-element.34.refs_1_, bf16[2,128,512]{2,1,0:T(8,128)(2,1)S(1)} %copy-done, ...), custom_call_target="tpu_custom_call" | custom-call | flops 1811939328 | bytes 3538944 | tf_op jit(solution)/shard_map/pallas_call | solution.py:266
  56.1 0.3 collective-permute-start.12
  56.5 0.2 collective-permute-start.11
  56.7 1.4 %shard_map.72 = (f32[640,512]{1,0:T(8,128)S(1)}, f32[640,512]{1,0:T(8,128)S(1)}, f32[4,256,256]{2,1,0:T(8,128)S(1)}) custom-call(bf16[640,2048]{1,0:T(8,128)(2,1)S(1)} %get-tuple-element.35.refs_0_.refs_2_, bf16[640,2048]{1,0:T(8,128)(2,1)S(1)} %get-tuple-element.36.refs_1_.refs_3_, ...), custom_call_target="tpu_custom_call", output_to_operand_aliasing={{0}: (6, {}), {1}: (7, {}), {2}: (8, {})} | custom-call | flops 1207959552 | bytes 2359296 | tf_op jit(solution)/shard_map/pallas_call | solution.py:266
  58.1 3.9 %collective-permute-done.8.refs_7_ = bf16[2,128,512]{2,1,0:T(8,128)(2,1)S(1)} collective-permute-done((bf16[2,128,512]{2,1,0:T(8,128)(2,1)S(1)}, bf16[2,128,512]{2,1,0:T(8,128)(2,1)S(1)}, u32[]{:S(2)}, u32[]{:S(2)}) %collective-permute-start.8) | collective-permute-done | bytes 262176 | tf_op jit(solution)/shard_map/ppermute | solution.py:297
  62.0 0.1 collective-permute-done.5.refs_5_
  62.1 0.4 collective-permute-start.6
  62.5 1.4 %shard_map.69 = (f32[640,512]{1,0:T(8,128)S(1)}, f32[640,512]{1,0:T(8,128)S(1)}, f32[4,256,256]{2,1,0:T(8,128)S(1)}) custom-call(bf16[640,2048]{1,0:T(8,128)(2,1)S(1)} %get-tuple-element.33.refs_0_, bf16[640,2048]{1,0:T(8,128)(2,1)S(1)} %get-tuple-element.34.refs_1_, ...), custom_call_target="tpu_custom_call", output_to_operand_aliasing={{0}: (6, {}), {1}: (7, {}), {2}: (8, {})} | custom-call | flops 1207959552 | bytes 2359296 | tf_op jit(solution)/shard_map/pallas_call | solution.py:266
  64.0 1.4 %shard_map.73 = (f32[640,512]{1,0:T(8,128)S(1)}, f32[640,512]{1,0:T(8,128)S(1)}, f32[4,256,256]{2,1,0:T(8,128)S(1)}) custom-call(bf16[640,2048]{1,0:T(8,128)(2,1)S(1)} %get-tuple-element.35.refs_0_.refs_2_, bf16[640,2048]{1,0:T(8,128)(2,1)S(1)} %get-tuple-element.36.refs_1_.refs_3_, ...), custom_call_target="tpu_custom_call", output_to_operand_aliasing={{0}: (6, {}), {1}: (7, {}), {2}: (8, {})} | custom-call | flops 1207959552 | bytes 2359296 | tf_op jit(solution)/shard_map/pallas_call | solution.py:266
  65.4 1.4 %shard_map.70 = (f32[640,512]{1,0:T(8,128)S(1)}, f32[640,512]{1,0:T(8,128)S(1)}, f32[4,256,256]{2,1,0:T(8,128)S(1)}) custom-call(bf16[640,2048]{1,0:T(8,128)(2,1)S(1)} %get-tuple-element.33.refs_0_, bf16[640,2048]{1,0:T(8,128)(2,1)S(1)} %get-tuple-element.34.refs_1_, ...), custom_call_target="tpu_custom_call", output_to_operand_aliasing={{0}: (6, {}), {1}: (7, {}), {2}: (8, {})} | custom-call | flops 1207959552 | bytes 2359296 | tf_op jit(solution)/shard_map/pallas_call | solution.py:266
  66.9 3.0 %shard_map.74 = f32[64,640]{1,0:T(8,128)} custom-call(bf16[640,2048]{1,0:T(8,128)(2,1)S(1)} %get-tuple-element.33.refs_0_, bf16[640,2048]{1,0:T(8,128)(2,1)S(1)} %get-tuple-element.34.refs_1_, bf16[640,2048]{1,0:T(8,128)(2,1)S(1)} %get-tuple-element.35.refs_0_.refs_2_, bf16[640,2048]{1,0:T(8,128)(2,1)S(1)} %get-tuple-element.36.refs_1_.refs_3_, ...), custom_call_target="tpu_custom_call" | custom-call | flops 1207959552 | bytes 2359296 | tf_op jit(solution)/shard_map/pallas_call | solution.py:266
  (27 shorter events, 0.1 us)
Async XLA Ops:
  2.1 8.9 %copy-start.1 = (bf16[2,128,512]{2,1,0:T(8,128)(2,1)S(1)}, bf16[2,128,512]{2,1,0:T(8,128)(2,1)}, u32[]{:S(2)}) copy-start(bf16[2,128,512]{2,1,0:T(8,128)(2,1)} %shard_map.67.refs_2_) | copy-start | bytes 786436
  2.1 9.5 %collective-permute-start.7 = (bf16[2,128,512]{2,1,0:T(8,128)(2,1)}, bf16[2,128,512]{2,1,0:T(8,128)(2,1)S(1)}, u32[]{:S(2)}, u32[]{:S(2)}) collective-permute-start(bf16[2,128,512]{2,1,0:T(8,128)(2,1)} %shard_map.67.refs_2_), channel_id=1, source_target_pairs={{0,2},{1,3},{2,0},{3,1},{4,6},{5,7},{6,4},{7,5},{8,10},{9,11},{10,... | collective-permute-start | bytes 786440 | tf_op jit(solution)/shard_map/ppermute | solution.py:297
  5.1 11.2 %collective-permute-start.18 = (bf16[2,128,512]{2,1,0:T(8,128)(2,1)}, bf16[2,128,512]{2,1,0:T(8,128)(2,1)S(1)}, u32[]{:S(2)}, u32[]{:S(2)}) collective-permute-start(bf16[2,128,512]{2,1,0:T(8,128)(2,1)} %shard_map.67.refs_2_), channel_id=1, source_target_pairs={{0,4},{1,5},{2,6},{3,7},{4,8},{5,9},{6,10},{7,11},{8,12},{9,13},{1... | collective-permute-start | bytes 786440 | tf_op jit(solution)/shard_map/ppermute | solution.py:297
  8.8 11.8 %collective-permute-start = (bf16[2,128,512]{2,1,0:T(8,128)(2,1)}, bf16[2,128,512]{2,1,0:T(8,128)(2,1)S(1)}, u32[]{:S(2)}, u32[]{:S(2)}) collective-permute-start(bf16[2,128,512]{2,1,0:T(8,128)(2,1)} %shard_map.66.refs_2_), channel_id=1, source_target_pairs={{0,4},{1,5},{2,6},{3,7},{4,8},{5,9},{6,10},{7,11},{8,12},{9,13},{1... | collective-permute-start | bytes 786440 | tf_op jit(solution)/shard_map/ppermute | solution.py:297
  10.4 10.2 %collective-permute-start.1 = (bf16[2,128,512]{2,1,0:T(8,128)(2,1)}, bf16[2,128,512]{2,1,0:T(8,128)(2,1)S(1)}, u32[]{:S(2)}, u32[]{:S(2)}) collective-permute-start(bf16[2,128,512]{2,1,0:T(8,128)(2,1)} %shard_map.66.refs_2_), channel_id=1, source_target_pairs={{0,2},{1,3},{2,0},{3,1},{4,6},{5,7},{6,4},{7,5},{8,10},{9,11},{10,... | collective-permute-start | bytes 786440 | tf_op jit(solution)/shard_map/ppermute | solution.py:297
  11.0 10.2 %collective-permute-start.27 = (bf16[2,128,512]{2,1,0:T(8,128)(2,1)S(1)}, bf16[2,128,512]{2,1,0:T(8,128)(2,1)S(1)}, u32[]{:S(2)}, u32[]{:S(2)}) collective-permute-start(bf16[2,128,512]{2,1,0:T(8,128)(2,1)S(1)} %copy-done.1), channel_id=1, source_target_pairs={{0,1},{1,0},{2,3},{3,2},{4,5},{5,4},{6,7},{7,6},{8,9},{9,8},{10,11... | collective-permute-start | bytes 786440 | tf_op jit(solution)/shard_map/ppermute | solution.py:297
  11.7 10.8 %collective-permute-start.15 = (bf16[2,128,512]{2,1,0:T(8,128)(2,1)}, bf16[2,128,512]{2,1,0:T(8,128)(2,1)S(1)}, u32[]{:S(2)}, u32[]{:S(2)}) collective-permute-start(bf16[2,128,512]{2,1,0:T(8,128)(2,1)} %shard_map.66.refs_2_), channel_id=1, source_target_pairs={{0,1},{1,0},{2,3},{3,2},{4,5},{5,4},{6,7},{7,6},{8,9},{9,8},{10,11... | collective-permute-start | bytes 786440 | tf_op jit(solution)/shard_map/ppermute | solution.py:297
  16.3 7.6 %collective-permute-start.28 = (bf16[2,128,512]{2,1,0:T(8,128)(2,1)S(1)}, bf16[2,128,512]{2,1,0:T(8,128)(2,1)S(1)}, u32[]{:S(2)}, u32[]{:S(2)}) collective-permute-start(bf16[2,128,512]{2,1,0:T(8,128)(2,1)S(1)} %collective-permute-done.7.refs_4_), channel_id=1, source_target_pairs={{0,1},{1,0},{2,3},{3,2},{4,5},{5,4},{6,7},{7,6},{8,9},{9,8},{10,11... | collective-permute-start | bytes 786440 | tf_op jit(solution)/shard_map/ppermute | solution.py:297
  20.6 11.0 %collective-permute-start.19 = (bf16[2,128,512]{2,1,0:T(8,128)(2,1)S(1)}, bf16[2,128,512]{2,1,0:T(8,128)(2,1)S(1)}, u32[]{:S(2)}, u32[]{:S(2)}) collective-permute-start(bf16[2,128,512]{2,1,0:T(8,128)(2,1)S(1)} %collective-permute-done.18.refs_6_), channel_id=1, source_target_pairs={{0,4},{1,5},{2,6},{3,7},{4,8},{5,9},{6,10},{7,11},{8,12},{9,13},{1... | collective-permute-start | bytes 786440 | tf_op jit(solution)/shard_map/ppermute | solution.py:297
  20.6 11.0 %collective-permute-start.22 = (bf16[2,128,512]{2,1,0:T(8,128)(2,1)S(1)}, bf16[2,128,512]{2,1,0:T(8,128)(2,1)S(1)}, u32[]{:S(2)}, u32[]{:S(2)}) collective-permute-start(bf16[2,128,512]{2,1,0:T(8,128)(2,1)S(1)} %collective-permute-done.18.refs_6_), channel_id=1, source_target_pairs={{0,2},{1,3},{2,0},{3,1},{4,6},{5,7},{6,4},{7,5},{8,10},{9,11},{10,... | collective-permute-start | bytes 786440 | tf_op jit(solution)/shard_map/ppermute | solution.py:297
  21.2 13.9 %collective-permute-start.2 = (bf16[2,128,512]{2,1,0:T(8,128)(2,1)S(1)}, bf16[2,128,512]{2,1,0:T(8,128)(2,1)S(1)}, u32[]{:S(2)}, u32[]{:S(2)}) collective-permute-start(bf16[2,128,512]{2,1,0:T(8,128)(2,1)S(1)} %collective-permute-done.refs_6_), channel_id=1, source_target_pairs={{0,4},{1,5},{2,6},{3,7},{4,8},{5,9},{6,10},{7,11},{8,12},{9,13},{1... | collective-permute-start | bytes 786440 | tf_op jit(solution)/shard_map/ppermute | solution.py:297
  22.4 12.6 %collective-permute-start.3 = (bf16[2,128,512]{2,1,0:T(8,128)(2,1)S(1)}, bf16[2,128,512]{2,1,0:T(8,128)(2,1)S(1)}, u32[]{:S(2)}, u32[]{:S(2)}) collective-permute-start(bf16[2,128,512]{2,1,0:T(8,128)(2,1)S(1)} %collective-permute-done.refs_6_), channel_id=1, source_target_pairs={{0,2},{1,3},{2,0},{3,1},{4,6},{5,7},{6,4},{7,5},{8,10},{9,11},{10,... | collective-permute-start | bytes 786440 | tf_op jit(solution)/shard_map/ppermute | solution.py:297
  23.9 11.6 %collective-permute-start.29 = (bf16[2,128,512]{2,1,0:T(8,128)(2,1)S(1)}, bf16[2,128,512]{2,1,0:T(8,128)(2,1)S(1)}, u32[]{:S(2)}, u32[]{:S(2)}) collective-permute-start(bf16[2,128,512]{2,1,0:T(8,128)(2,1)S(1)} %collective-permute-done.18.refs_6_), channel_id=1, source_target_pairs={{0,1},{1,0},{2,3},{3,2},{4,5},{5,4},{6,7},{7,6},{8,9},{9,8},{10,11... | collective-permute-start | bytes 786440 | tf_op jit(solution)/shard_map/ppermute | solution.py:297
  31.6 4.0 %collective-permute-start.17 = (bf16[2,128,512]{2,1,0:T(8,128)(2,1)S(1)}, bf16[2,128,512]{2,1,0:T(8,128)(2,1)S(1)}, u32[]{:S(2)}, u32[]{:S(2)}) collective-permute-start(bf16[2,128,512]{2,1,0:T(8,128)(2,1)S(1)} %collective-permute-done.refs_6_), channel_id=1, source_target_pairs={{0,1},{1,0},{2,3},{3,2},{4,5},{5,4},{6,7},{7,6},{8,9},{9,8},{10,11... | collective-permute-start | bytes 786440 | tf_op jit(solution)/shard_map/ppermute | solution.py:297
  31.6 4.1 %collective-permute-start.16 = (bf16[2,128,512]{2,1,0:T(8,128)(2,1)S(1)}, bf16[2,128,512]{2,1,0:T(8,128)(2,1)S(1)}, u32[]{:S(2)}, u32[]{:S(2)}) collective-permute-start(bf16[2,128,512]{2,1,0:T(8,128)(2,1)S(1)} %collective-permute-done.1.refs_4_), channel_id=1, source_target_pairs={{0,1},{1,0},{2,3},{3,2},{4,5},{5,4},{6,7},{7,6},{8,9},{9,8},{10,11... | collective-permute-start | bytes 786440 | tf_op jit(solution)/shard_map/ppermute | solution.py:297
  35.0 1.5 %collective-permute-start.26 = (bf16[2,128,512]{2,1,0:T(8,128)(2,1)S(1)}, bf16[2,128,512]{2,1,0:T(8,128)(2,1)S(1)}, u32[]{:S(2)}, u32[]{:S(2)}) collective-permute-start(bf16[2,128,512]{2,1,0:T(8,128)(2,1)S(1)} %collective-permute-done.19.refs_4_), channel_id=1, source_target_pairs={{0,1},{1,0},{2,3},{3,2},{4,5},{5,4},{6,7},{7,6},{8,9},{9,8},{10,11... | collective-permute-start | bytes 786440 | tf_op jit(solution)/shard_map/ppermute | solution.py:297
  35.0 1.9 %collective-permute-start.25 = (bf16[2,128,512]{2,1,0:T(8,128)(2,1)S(1)}, bf16[2,128,512]{2,1,0:T(8,128)(2,1)S(1)}, u32[]{:S(2)}, u32[]{:S(2)}) collective-permute-start(bf16[2,128,512]{2,1,0:T(8,128)(2,1)S(1)} %collective-permute-done.22.refs_2_), channel_id=1, source_target_pairs={{0,1},{1,0},{2,3},{3,2},{4,5},{5,4},{6,7},{7,6},{8,9},{9,8},{10,11... | collective-permute-start | bytes 786440 | tf_op jit(solution)/shard_map/ppermute | solution.py:297
  35.6 11.0 %collective-permute-start.23 = (bf16[2,128,512]{2,1,0:T(8,128)(2,1)S(1)}, bf16[2,128,512]{2,1,0:T(8,128)(2,1)S(1)}, u32[]{:S(2)}, u32[]{:S(2)}) collective-permute-start(bf16[2,128,512]{2,1,0:T(8,128)(2,1)S(1)} %collective-permute-done.19.refs_4_), channel_id=1, source_target_pairs={{0,4},{1,5},{2,6},{3,7},{4,8},{5,9},{6,10},{7,11},{8,12},{9,13},{1... | collective-permute-start | bytes 786440 | tf_op jit(solution)/shard_map/ppermute | solution.py:297
  35.6 15.7 %collective-permute-start.4 = (bf16[2,128,512]{2,1,0:T(8,128)(2,1)S(1)}, bf16[2,128,512]{2,1,0:T(8,128)(2,1)S(1)}, u32[]{:S(2)}, u32[]{:S(2)}) collective-permute-start(bf16[2,128,512]{2,1,0:T(8,128)(2,1)S(1)} %collective-permute-done.2.refs_4_), channel_id=1, source_target_pairs={{0,4},{1,5},{2,6},{3,7},{4,8},{5,9},{6,10},{7,11},{8,12},{9,13},{1... | collective-permute-start | bytes 786440 | tf_op jit(solution)/shard_map/ppermute | solution.py:297
  35.7 17.3 %collective-permute-start.20 = (bf16[2,128,512]{2,1,0:T(8,128)(2,1)S(1)}, bf16[2,128,512]{2,1,0:T(8,128)(2,1)S(1)}, u32[]{:S(2)}, u32[]{:S(2)}) collective-permute-start(bf16[2,128,512]{2,1,0:T(8,128)(2,1)S(1)} %collective-permute-done.19.refs_4_), channel_id=1, source_target_pairs={{0,2},{1,3},{2,0},{3,1},{4,6},{5,7},{6,4},{7,5},{8,10},{9,11},{10,... | collective-permute-start | bytes 786440 | tf_op jit(solution)/shard_map/ppermute | solution.py:297
  36.6 16.7 %collective-permute-start.14 = (bf16[2,128,512]{2,1,0:T(8,128)(2,1)S(1)}, bf16[2,128,512]{2,1,0:T(8,128)(2,1)S(1)}, u32[]{:S(2)}, u32[]{:S(2)}) collective-permute-start(bf16[2,128,512]{2,1,0:T(8,128)(2,1)S(1)} %collective-permute-done.2.refs_4_), channel_id=1, source_target_pairs={{0,1},{1,0},{2,3},{3,2},{4,5},{5,4},{6,7},{7,6},{8,9},{9,8},{10,11... | collective-permute-start | bytes 786440 | tf_op jit(solution)/shard_map/ppermute | solution.py:297
  37.0 17.1 %collective-permute-start.13 = (bf16[2,128,512]{2,1,0:T(8,128)(2,1)S(1)}, bf16[2,128,512]{2,1,0:T(8,128)(2,1)S(1)}, u32[]{:S(2)}, u32[]{:S(2)}) collective-permute-start(bf16[2,128,512]{2,1,0:T(8,128)(2,1)S(1)} %collective-permute-done.3.refs_2_), channel_id=1, source_target_pairs={{0,1},{1,0},{2,3},{3,2},{4,5},{5,4},{6,7},{7,6},{8,9},{9,8},{10,11... | collective-permute-start | bytes 786440 | tf_op jit(solution)/shard_map/ppermute | solution.py:297
  46.5 9.6 %collective-permute-start.10 = (bf16[2,128,512]{2,1,0:T(8,128)(2,1)S(1)}, bf16[2,128,512]{2,1,0:T(8,128)(2,1)S(1)}, u32[]{:S(2)}, u32[]{:S(2)}) collective-permute-start(bf16[2,128,512]{2,1,0:T(8,128)(2,1)S(1)} %collective-permute-done.2.refs_4_), channel_id=1, source_target_pairs={{0,2},{1,3},{2,0},{3,1},{4,6},{5,7},{6,4},{7,5},{8,10},{9,11},{10,... | collective-permute-start | bytes 786440 | tf_op jit(solution)/shard_map/ppermute | solution.py:297
  51.2 5.2 %collective-permute-start.24 = (bf16[2,128,512]{2,1,0:T(8,128)(2,1)S(1)}, bf16[2,128,512]{2,1,0:T(8,128)(2,1)S(1)}, u32[]{:S(2)}, u32[]{:S(2)}) collective-permute-start(bf16[2,128,512]{2,1,0:T(8,128)(2,1)S(1)} %collective-permute-done.23.refs_4_), channel_id=1, source_target_pairs={{0,1},{1,0},{2,3},{3,2},{4,5},{5,4},{6,7},{7,6},{8,9},{9,8},{10,11... | collective-permute-start | bytes 786440 | tf_op jit(solution)/shard_map/ppermute | solution.py:297
  51.2 3.1 %copy-start = (bf16[2,128,512]{2,1,0:T(8,128)(2,1)S(1)}, bf16[2,128,512]{2,1,0:T(8,128)(2,1)}, u32[]{:S(2)}) copy-start(bf16[2,128,512]{2,1,0:T(8,128)(2,1)} %shard_map.66.refs_2_) | copy-start | bytes 786436
  53.1 8.9 %collective-permute-start.8 = (bf16[2,128,512]{2,1,0:T(8,128)(2,1)S(1)}, bf16[2,128,512]{2,1,0:T(8,128)(2,1)S(1)}, u32[]{:S(2)}, u32[]{:S(2)}) collective-permute-start(bf16[2,128,512]{2,1,0:T(8,128)(2,1)S(1)} %collective-permute-done.7.refs_4_), channel_id=1, source_target_pairs={{0,12},{1,13},{2,14},{3,15},{4,0},{5,1},{6,2},{7,3},{8,4},{9,5},{1... | collective-permute-start | bytes 786440 | tf_op jit(solution)/shard_map/ppermute | solution.py:297
  53.3 8.8 %collective-permute-start.5 = (bf16[2,128,512]{2,1,0:T(8,128)(2,1)S(1)}, bf16[2,128,512]{2,1,0:T(8,128)(2,1)S(1)}, u32[]{:S(2)}, u32[]{:S(2)}) collective-permute-start(bf16[2,128,512]{2,1,0:T(8,128)(2,1)S(1)} %collective-permute-done.4.refs_4_), channel_id=1, source_target_pairs={{0,2},{1,3},{2,0},{3,1},{4,6},{5,7},{6,4},{7,5},{8,10},{9,11},{10,... | collective-permute-start | bytes 786440 | tf_op jit(solution)/shard_map/ppermute | solution.py:297
  54.1 9.9 %collective-permute-start.21 = (bf16[2,128,512]{2,1,0:T(8,128)(2,1)S(1)}, bf16[2,128,512]{2,1,0:T(8,128)(2,1)S(1)}, u32[]{:S(2)}, u32[]{:S(2)}) collective-permute-start(bf16[2,128,512]{2,1,0:T(8,128)(2,1)S(1)} %collective-permute-done.20.refs_2_), channel_id=1, source_target_pairs={{0,1},{1,0},{2,3},{3,2},{4,5},{5,4},{6,7},{7,6},{8,9},{9,8},{10,11... | collective-permute-start | bytes 786440 | tf_op jit(solution)/shard_map/ppermute | solution.py:297
  56.1 9.3 %collective-permute-start.12 = (bf16[2,128,512]{2,1,0:T(8,128)(2,1)S(1)}, bf16[2,128,512]{2,1,0:T(8,128)(2,1)S(1)}, u32[]{:S(2)}, u32[]{:S(2)}) collective-permute-start(bf16[2,128,512]{2,1,0:T(8,128)(2,1)S(1)} %collective-permute-done.4.refs_4_), channel_id=1, source_target_pairs={{0,1},{1,0},{2,3},{3,2},{4,5},{5,4},{6,7},{7,6},{8,9},{9,8},{10,11... | collective-permute-start | bytes 786440 | tf_op jit(solution)/shard_map/ppermute | solution.py:297
  56.5 9.0 %collective-permute-start.11 = (bf16[2,128,512]{2,1,0:T(8,128)(2,1)S(1)}, bf16[2,128,512]{2,1,0:T(8,128)(2,1)S(1)}, u32[]{:S(2)}, u32[]{:S(2)}) collective-permute-start(bf16[2,128,512]{2,1,0:T(8,128)(2,1)S(1)} %collective-permute-done.10.refs_2_), channel_id=1, source_target_pairs={{0,1},{1,0},{2,3},{3,2},{4,5},{5,4},{6,7},{7,6},{8,9},{9,8},{10,11... | collective-permute-start | bytes 786440 | tf_op jit(solution)/shard_map/ppermute | solution.py:297
  62.0 4.9 %collective-permute-start.9 = (bf16[2,128,512]{2,1,0:T(8,128)(2,1)S(1)}, bf16[2,128,512]{2,1,0:T(8,128)(2,1)S(1)}, u32[]{:S(2)}, u32[]{:S(2)}) collective-permute-start(bf16[2,128,512]{2,1,0:T(8,128)(2,1)S(1)} %collective-permute-done.8.refs_7_), channel_id=1, source_target_pairs={{0,1},{1,0},{2,3},{3,2},{4,5},{5,4},{6,7},{7,6},{8,9},{9,8},{10,11... | collective-permute-start | bytes 786440 | tf_op jit(solution)/shard_map/ppermute | solution.py:297
  62.1 4.8 %collective-permute-start.6 = (bf16[2,128,512]{2,1,0:T(8,128)(2,1)S(1)}, bf16[2,128,512]{2,1,0:T(8,128)(2,1)S(1)}, u32[]{:S(2)}, u32[]{:S(2)}) collective-permute-start(bf16[2,128,512]{2,1,0:T(8,128)(2,1)S(1)} %collective-permute-done.5.refs_5_), channel_id=1, source_target_pairs={{0,1},{1,0},{2,3},{3,2},{4,5},{5,4},{6,7},{7,6},{8,9},{9,8},{10,11... | collective-permute-start | bytes 786440 | tf_op jit(solution)/shard_map/ppermute | solution.py:297

commit v8 on v7

--- a/solution.py
+++ b/solution.py
@@ -14,7 +14,7 @@
 LANES = 128
 TILE = 256
 TERMS = 2
-LOAD_GRANTS = (46 << 20, 45 << 20)
+GRANT = 24 << 20
 
 
 def pick_columns(factor, block_ids):
@@ -46,7 +46,7 @@
     return jnp.where(live[:, None], scaled, jnp.zeros_like(scaled))
 
 
-def pick_kernel(layer, ids_hbm, u_ref, v_ref, out_ref, ids_ref, held, made, sems):
+def pick_kernel(layer, ids_hbm, u_ref, v_ref, out_ref, ids_ref, held, sems):
     width = QB * RANK
     rows = u_ref.shape[1]
     columns = out_ref.shape[2]
@@ -60,7 +60,6 @@
         copy.start()
     named.wait()
     lane = lax.broadcasted_iota(jnp.int32, (rows, LANES), 1) // width
-    outs = []
     for s in range(2):
         copies[s].wait()
         for chunk in range(columns // LANES):
@@ -71,12 +70,11 @@
                 part = held[s, :, pl.ds(start, LANES)].astype(jnp.float32)
                 part = pltpu.roll(part, lax.rem(k - stored % per + per, per) * width, 1)
                 total = part if total is None else jnp.where(lane == k, part, total)
-            made[s, :, chunk * LANES : (chunk + 1) * LANES] = total.astype(jnp.bfloat16)
-        out = pltpu.make_async_copy(made.at[s], out_ref.at[s], sems.at[2 + s])
-        out.start()
-        outs.append(out)
-    for out in outs:
-        out.wait()
+            out_ref[s, :, chunk * LANES : (chunk + 1) * LANES] = total.astype(jnp.bfloat16)
+
+
+def in_hbm(*arrays):
+    return [pltpu.with_memory_space_constraint(one, pltpu.HBM) for one in arrays]
 
 
 def pick(layer, query_u, query_v, block_ids):
@@ -87,17 +85,17 @@
         functools.partial(pick_kernel, layer),
         out_shape=jax.ShapeDtypeStruct((2, rows, columns), jnp.bfloat16),
         in_specs=[anywhere] * 3,
-        out_specs=anywhere,
+        out_specs=pl.BlockSpec(memory_space=pltpu.VMEM),
         scratch_shapes=[
             pltpu.SMEM(block_ids.shape, jnp.int32),
             pltpu.VMEM((2, rows, bank), jnp.bfloat16),
-            pltpu.VMEM((2, rows, columns), jnp.bfloat16),
             pltpu.SemaphoreType.DMA((5,)),
         ],
+        compiler_params=pltpu.CompilerParams(vmem_limit_bytes=GRANT),
         cost_estimate=pl.CostEstimate(
             flops=4 * rows * columns, bytes_accessed=4 * rows * (bank + columns), transcendentals=0
         ),
-    )(block_ids, query_u, query_v)
+    )(*in_hbm(block_ids, query_u, query_v))
 
 
 def load_kernel(layer, *refs):
@@ -118,14 +116,14 @@
     outs = [jax.ShapeDtypeStruct((8, LANES), jnp.int32)] if layer == 0 else []
     outs += [jax.ShapeDtypeStruct(one.shape[1:], one.dtype) for one in arrays]
     specs = [pl.BlockSpec(memory_space=pltpu.SMEM)] if layer == 0 else []
-    args = ([counts] if layer == 0 else []) + list(arrays)
+    args = ([counts] if layer == 0 else []) + in_hbm(*arrays)
     return pl.pallas_call(
         functools.partial(load_kernel, layer),
         out_shape=tuple(outs),
         in_specs=specs + [pl.BlockSpec(memory_space=pltpu.HBM)] * len(arrays),
         out_specs=(pl.BlockSpec(memory_space=pltpu.VMEM),) * len(outs),
         scratch_shapes=[pltpu.SemaphoreType.DMA((len(arrays),))],
-        compiler_params=pltpu.CompilerParams(vmem_limit_bytes=LOAD_GRANTS[layer]),
+        compiler_params=pltpu.CompilerParams(vmem_limit_bytes=GRANT),
     )(*args)
 
 
@@ -270,7 +268,7 @@
         out_specs=out_specs,
         scratch_shapes=scratch + [pltpu.VMEM((2, slots * 2 * rows, columns), jnp.bfloat16)],
         input_output_aliases=aliases,
-        compiler_params=pltpu.CompilerParams(vmem_limit_bytes=(24 if last else 16) << 20),
+        compiler_params=pltpu.CompilerParams(vmem_limit_bytes=GRANT),
         cost_estimate=pl.CostEstimate(
             flops=flops, bytes_accessed=8 * slots * rows * (tokens + columns), transcendentals=0
         ),
@@ -304,8 +302,6 @@
             h = have[layer]
             if da < outer - 1:
                 fed = h[(da, 0)]
-                if da:
-                    fed = after(fed, h[(da - 1, 1)])
                 h[(da + 1, 0)] = move(fed, 1, 0, 0)
             if da == outer - 1 and layer == 1:
                 fed = after(h[(0, 1)], have[0][(da, 0)])

time: 70.1 us -> 68.1 us (0.971)
  waiting for transfers between devices: 32.3 us -> 25.9 us
  starting transfers between devices: 15.2 us -> 21 us
  Pallas kernels: 21.6 us -> 20.2 us
    ppermute x30, waiting for transfers between devices: 32.3 us -> 25.9 us  [move(): return lax.ppermute(value, 'tok', steps)]
    ppermute x30, starting transfers between devices: 15.2 us -> 21 us  [move(): return lax.ppermute(value, 'tok', steps)]
    pallas_call x2, Pallas kernels: 4.18 us -> 2.88 us  [pick(): pl.pallas_call(functools.partial(pick_kernel, layer), out_shape=jax.Shape...]
  transfers between devices with their start and end apart: 30 -> 30, of which waited for: 11 -> 8; matrix products, arithmetic and copies ran while one was open for 0% -> 0% of each run, Pallas kernels for 24% -> 23%
where the time goes in v8:
time: 68.1 us; the launch traced here: 67.9 us
  waiting for transfers between devices  25.9 us (38%)
  starting transfers between devices  21 us (31%)
  Pallas kernels  20.2 us (30%)
  between operations  0.83 us (1%)
    ppermute x30, waiting for transfers between devices, move(): return lax.ppermute(value, 'tok', steps)  25.9 us
    ppermute x30, starting transfers between devices, move(): return lax.ppermute(value, 'tok', steps)  21 us
    pallas_call x7, Pallas kernels, stage(): pl.pallas_call(functools.partial(stage_kernel, cfg), out_shape=out_shape,...  12.2 us
    pallas_call x2, Pallas kernels, load(): pl.pallas_call(functools.partial(load_kernel, layer), out_shape=tuple(out...  5.1 us
    pallas_call x2, Pallas kernels, pick(): pl.pallas_call(functools.partial(pick_kernel, layer), out_shape=jax.Shape...  2.88 us
  transfers between devices with their start and end apart: 30, of which 8 were waited for; matrix products, arithmetic and copies ran while one was open for 0% of the time, Pallas kernels for 23%

profile of v8, /device:TPU:0, one launch (start us, length us, event | category | flops | bytes accessed | tf_op | source)
XLA Modules:
  0.0 67.9 jit_solution(13830383065386996887)
XLA Ops:
  0.0 1.4 %shard_map.67.refs_2_ = bf16[2,128,512]{2,1,0:T(8,128)(2,1)S(1)} custom-call(s32[2,16]{1,0:T(2,128)} %ids_hbm.3, bf16[2,128,1024]{2,1,0:T(8,128)(2,1)} %u_ref.3, bf16[2,128,1024]{2,1,0:T(8,128)(2,1)} %v_ref.3), custom_call_target="tpu_custom_call" | custom-call | flops 262144 | bytes 786432 | tf_op jit(solution)/shard_map/pallas_call | solution.py:84
  1.4 3.1 %collective-permute-start.18 = (bf16[2,128,512]{2,1,0:T(8,128)(2,1)S(1)}, bf16[2,128,512]{2,1,0:T(8,128)(2,1)S(1)}, u32[]{:S(2)}, u32[]{:S(2)}) collective-permute-start(bf16[2,128,512]{2,1,0:T(8,128)(2,1)S(1)} %shard_map.67.refs_2_), channel_id=1, source_target_pairs={{0,4},{1,5},{2,6},{3,7},{4,8},{5,9},{6,10},{7,11},{8,12},{9,13},{1... | collective-permute-start | bytes 786440 | tf_op jit(solution)/shard_map/ppermute | solution.py:295
  4.6 1.5 %collective-permute-start.5 = (bf16[2,128,512]{2,1,0:T(8,128)(2,1)S(1)}, bf16[2,128,512]{2,1,0:T(8,128)(2,1)S(1)}, u32[]{:S(2)}, u32[]{:S(2)}) collective-permute-start(bf16[2,128,512]{2,1,0:T(8,128)(2,1)S(1)} %shard_map.67.refs_2_), channel_id=1, source_target_pairs={{0,2},{1,3},{2,0},{3,1},{4,6},{5,7},{6,4},{7,5},{8,10},{9,11},{10,... | collective-permute-start | bytes 786440 | tf_op jit(solution)/shard_map/ppermute | solution.py:295
  6.0 0.0 collective-permute-start.27
  6.0 1.4 %shard_map.66.refs_2_ = bf16[2,128,512]{2,1,0:T(8,128)(2,1)S(1)} custom-call(s32[2,16]{1,0:T(2,128)} %ids_hbm.3, bf16[2,128,1024]{2,1,0:T(8,128)(2,1)} %u_ref.3, bf16[2,128,1024]{2,1,0:T(8,128)(2,1)} %v_ref.3), custom_call_target="tpu_custom_call" | custom-call | flops 262144 | bytes 786432 | tf_op jit(solution)/shard_map/pallas_call | solution.py:84
  7.5 1.6 %collective-permute-start = (bf16[2,128,512]{2,1,0:T(8,128)(2,1)S(1)}, bf16[2,128,512]{2,1,0:T(8,128)(2,1)S(1)}, u32[]{:S(2)}, u32[]{:S(2)}) collective-permute-start(bf16[2,128,512]{2,1,0:T(8,128)(2,1)S(1)} %shard_map.66.refs_2_), channel_id=1, source_target_pairs={{0,4},{1,5},{2,6},{3,7},{4,8},{5,9},{6,10},{7,11},{8,12},{9,13},{1... | collective-permute-start | bytes 786440 | tf_op jit(solution)/shard_map/ppermute | solution.py:295
  9.1 0.5 collective-permute-start.15
  9.7 3.7 %collective-permute-done.18.refs_6_ = bf16[2,128,512]{2,1,0:T(8,128)(2,1)S(1)} collective-permute-done((bf16[2,128,512]{2,1,0:T(8,128)(2,1)S(1)}, bf16[2,128,512]{2,1,0:T(8,128)(2,1)S(1)}, u32[]{:S(2)}, u32[]{:S(2)}) %collective-permute-start.18) | collective-permute-done | bytes 262176 | tf_op jit(solution)/shard_map/ppermute | solution.py:295
  13.3 0.0 collective-permute-start.14
  13.3 0.0 collective-permute-done.5.refs_4_
  13.3 0.5 collective-permute-start.29
  13.8 0.1 collective-permute-start.28
  13.9 4.6 %collective-permute-done.refs_6_ = bf16[2,128,512]{2,1,0:T(8,128)(2,1)S(1)} collective-permute-done((bf16[2,128,512]{2,1,0:T(8,128)(2,1)S(1)}, bf16[2,128,512]{2,1,0:T(8,128)(2,1)S(1)}, u32[]{:S(2)}, u32[]{:S(2)}) %collective-permute-start) | collective-permute-done | bytes 262176 | tf_op jit(solution)/shard_map/ppermute | solution.py:295
  18.5 0.0 collective-permute-done.15.refs_4_
  18.5 1.5 %collective-permute-start.24 = (bf16[2,128,512]{2,1,0:T(8,128)(2,1)S(1)}, bf16[2,128,512]{2,1,0:T(8,128)(2,1)S(1)}, u32[]{:S(2)}, u32[]{:S(2)}) collective-permute-start(bf16[2,128,512]{2,1,0:T(8,128)(2,1)S(1)} %collective-permute-done.18.refs_6_), channel_id=1, source_target_pairs={{0,2},{1,3},{2,0},{3,1},{4,6},{5,7},{6,4},{7,5},{8,10},{9,11},{10,... | collective-permute-start | bytes 786440 | tf_op jit(solution)/shard_map/ppermute | solution.py:295
  20.0 0.0 collective-permute-done.14.refs_3_
  20.0 0.0 collective-permute-start.17
  20.0 0.0 collective-permute-done.29.refs_7_
  20.0 0.5 collective-permute-start.16
  20.5 0.0 collective-permute-done.28.refs_5_
  20.5 1.3 %collective-permute-start.1 = (bf16[2,128,512]{2,1,0:T(8,128)(2,1)S(1)}, bf16[2,128,512]{2,1,0:T(8,128)(2,1)S(1)}, u32[]{:S(2)}, u32[]{:S(2)}) collective-permute-start(bf16[2,128,512]{2,1,0:T(8,128)(2,1)S(1)} %collective-permute-done.refs_6_), channel_id=1, source_target_pairs={{0,4},{1,5},{2,6},{3,7},{4,8},{5,9},{6,10},{7,11},{8,12},{9,13},{1... | collective-permute-start | bytes 786440 | tf_op jit(solution)/shard_map/ppermute | solution.py:295
  21.8 7.7 %collective-permute-done.19.refs_4_ = bf16[2,128,512]{2,1,0:T(8,128)(2,1)S(1)} collective-permute-done((bf16[2,128,512]{2,1,0:T(8,128)(2,1)S(1)}, bf16[2,128,512]{2,1,0:T(8,128)(2,1)S(1)}, u32[]{:S(2)}, u32[]{:S(2)}) %collective-permute-start.19) | collective-permute-done | bytes 262176 | tf_op jit(solution)/shard_map/ppermute | solution.py:295
  29.5 1.5 %collective-permute-start.11 = (bf16[2,128,512]{2,1,0:T(8,128)(2,1)S(1)}, bf16[2,128,512]{2,1,0:T(8,128)(2,1)S(1)}, u32[]{:S(2)}, u32[]{:S(2)}) collective-permute-start(bf16[2,128,512]{2,1,0:T(8,128)(2,1)S(1)} %collective-permute-done.refs_6_), channel_id=1, source_target_pairs={{0,2},{1,3},{2,0},{3,1},{4,6},{5,7},{6,4},{7,5},{8,10},{9,11},{10,... | collective-permute-start | bytes 786440 | tf_op jit(solution)/shard_map/ppermute | solution.py:295
  31.0 0.0 collective-permute-done.17.refs_7_
  31.0 0.5 collective-permute-start.25
  31.5 0.5 collective-permute-start.20
  32.0 1.8 %collective-permute-done.1.refs_4_ = bf16[2,128,512]{2,1,0:T(8,128)(2,1)S(1)} collective-permute-done((bf16[2,128,512]{2,1,0:T(8,128)(2,1)S(1)}, bf16[2,128,512]{2,1,0:T(8,128)(2,1)S(1)}, u32[]{:S(2)}, u32[]{:S(2)}) %collective-permute-start.1) | collective-permute-done | bytes 262176 | tf_op jit(solution)/shard_map/ppermute | solution.py:295
  33.8 3.7 %collective-permute-done.11.refs_2_ = bf16[2,128,512]{2,1,0:T(8,128)(2,1)S(1)} collective-permute-done((bf16[2,128,512]{2,1,0:T(8,128)(2,1)S(1)}, bf16[2,128,512]{2,1,0:T(8,128)(2,1)S(1)}, u32[]{:S(2)}, u32[]{:S(2)}) %collective-permute-start.11) | collective-permute-done | bytes 262176 | tf_op jit(solution)/shard_map/ppermute | solution.py:295
  37.5 0.0 collective-permute-start.22
  37.6 0.5 collective-permute-start.12
  38.7 2.6 %shard_map.65 = (bf16[640,2048]{1,0:T(8,128)(2,1)S(1)}, bf16[640,2048]{1,0:T(8,128)(2,1)S(1)}) custom-call(bf16[2,640,2048]{2,1,0:T(8,128)(2,1)} %refs_0_.2, bf16[2,640,2048]{2,1,0:T(8,128)(2,1)} %refs_1_.3), custom_call_target="tpu_custom_call" | custom-call | tf_op jit(solution)/shard_map/pallas_call | solution.py:120
  41.3 2.6 %shard_map.64 = (s32[8,128]{1,0:T(8,128)S(1)}, bf16[640,2048]{1,0:T(8,128)(2,1)S(1)}, bf16[640,2048]{1,0:T(8,128)(2,1)S(1)}) custom-call(s32[1]{0:T(128)S(6)} %copy.31.refs_0_, bf16[2,640,2048]{2,1,0:T(8,128)(2,1)} %refs_0_.2, bf16[2,640,2048]{2,1,0:T(8,128)(2,1)} %refs_1_.3), custom_call_target="tpu_custom_call" | custom-call | tf_op jit(solution)/shard_map/pallas_call | solution.py:120
  43.9 2.5 %collective-permute-start.8 = (bf16[2,128,512]{2,1,0:T(8,128)(2,1)S(1)}, bf16[2,128,512]{2,1,0:T(8,128)(2,1)S(1)}, u32[]{:S(2)}, u32[]{:S(2)}) collective-permute-start(bf16[2,128,512]{2,1,0:T(8,128)(2,1)S(1)} %collective-permute-done.1.refs_4_), channel_id=1, source_target_pairs={{0,2},{1,3},{2,0},{3,1},{4,6},{5,7},{6,4},{7,5},{8,10},{9,11},{10,... | collective-permute-start | bytes 786440 | tf_op jit(solution)/shard_map/ppermute | solution.py:295
  46.4 1.8 %shard_map.71 = (f32[640,512]{1,0:T(8,128)S(1)}, f32[640,512]{1,0:T(8,128)S(1)}, f32[4,256,256]{2,1,0:T(8,128)S(1)}) custom-call(bf16[640,2048]{1,0:T(8,128)(2,1)S(1)} %get-tuple-element.31.refs_0_.refs_2_, bf16[640,2048]{1,0:T(8,128)(2,1)S(1)} %get-tuple-element.32.refs_1_.refs_3_, bf16[2,128,512]{2,1,0:T(8,128)(2,1)S(1)} %shard_map.67.refs_2_, ...), custom_call_target="tpu_custom_call" | custom-call | flops 1811939328 | bytes 3538944 | tf_op jit(solution)/shard_map/pallas_call | solution.py:264
  48.2 0.1 collective-permute-done.22.refs_4_
  48.3 3.9 %collective-permute-start.6 = (bf16[2,128,512]{2,1,0:T(8,128)(2,1)S(1)}, bf16[2,128,512]{2,1,0:T(8,128)(2,1)S(1)}, u32[]{:S(2)}, u32[]{:S(2)}) collective-permute-start(bf16[2,128,512]{2,1,0:T(8,128)(2,1)S(1)} %collective-permute-done.5.refs_4_), channel_id=1, source_target_pairs={{0,12},{1,13},{2,14},{3,15},{4,0},{5,1},{6,2},{7,3},{8,4},{9,5},{1... | collective-permute-start | bytes 786440 | tf_op jit(solution)/shard_map/ppermute | solution.py:295
  52.2 0.2 collective-permute-start.3
  52.4 0.2 collective-permute-start.23
  52.5 1.8 %shard_map.68 = (f32[640,512]{1,0:T(8,128)S(1)}, f32[640,512]{1,0:T(8,128)S(1)}, f32[4,256,256]{2,1,0:T(8,128)S(1)}) custom-call(bf16[640,2048]{1,0:T(8,128)(2,1)S(1)} %get-tuple-element.29.refs_0_, bf16[640,2048]{1,0:T(8,128)(2,1)S(1)} %get-tuple-element.30.refs_1_, bf16[2,128,512]{2,1,0:T(8,128)(2,1)S(1)} %shard_map.66.refs_2_, ...), custom_call_target="tpu_custom_call" | custom-call | flops 1811939328 | bytes 3538944 | tf_op jit(solution)/shard_map/pallas_call | solution.py:264
  54.3 0.4 collective-permute-start.10
  54.7 0.2 collective-permute-start.9
  54.9 1.4 %shard_map.72 = (f32[640,512]{1,0:T(8,128)S(1)}, f32[640,512]{1,0:T(8,128)S(1)}, f32[4,256,256]{2,1,0:T(8,128)S(1)}) custom-call(bf16[640,2048]{1,0:T(8,128)(2,1)S(1)} %get-tuple-element.31.refs_0_.refs_2_, bf16[640,2048]{1,0:T(8,128)(2,1)S(1)} %get-tuple-element.32.refs_1_.refs_3_, ...), custom_call_target="tpu_custom_call", output_to_operand_aliasing={{0}: (6, {}), {1}: (7, {}), {2}: (8, {})} | custom-call | flops 1207959552 | bytes 2359296 | tf_op jit(solution)/shard_map/pallas_call | solution.py:264
  56.3 2.1 %collective-permute-done.6.refs_7_ = bf16[2,128,512]{2,1,0:T(8,128)(2,1)S(1)} collective-permute-done((bf16[2,128,512]{2,1,0:T(8,128)(2,1)S(1)}, bf16[2,128,512]{2,1,0:T(8,128)(2,1)S(1)}, u32[]{:S(2)}, u32[]{:S(2)}) %collective-permute-start.6) | collective-permute-done | bytes 262176 | tf_op jit(solution)/shard_map/ppermute | solution.py:295
  58.5 2.2 %collective-permute-done.3.refs_5_ = bf16[2,128,512]{2,1,0:T(8,128)(2,1)S(1)} collective-permute-done((bf16[2,128,512]{2,1,0:T(8,128)(2,1)S(1)}, bf16[2,128,512]{2,1,0:T(8,128)(2,1)S(1)}, u32[]{:S(2)}, u32[]{:S(2)}) %collective-permute-start.3) | collective-permute-done | bytes 262176 | tf_op jit(solution)/shard_map/ppermute | solution.py:295
  60.7 1.4 %shard_map.69 = (f32[640,512]{1,0:T(8,128)S(1)}, f32[640,512]{1,0:T(8,128)S(1)}, f32[4,256,256]{2,1,0:T(8,128)S(1)}) custom-call(bf16[640,2048]{1,0:T(8,128)(2,1)S(1)} %get-tuple-element.29.refs_0_, bf16[640,2048]{1,0:T(8,128)(2,1)S(1)} %get-tuple-element.30.refs_1_, ...), custom_call_target="tpu_custom_call", output_to_operand_aliasing={{0}: (6, {}), {1}: (7, {}), {2}: (8, {})} | custom-call | flops 1207959552 | bytes 2359296 | tf_op jit(solution)/shard_map/pallas_call | solution.py:264
  62.1 1.4 %shard_map.73 = (f32[640,512]{1,0:T(8,128)S(1)}, f32[640,512]{1,0:T(8,128)S(1)}, f32[4,256,256]{2,1,0:T(8,128)S(1)}) custom-call(bf16[640,2048]{1,0:T(8,128)(2,1)S(1)} %get-tuple-element.31.refs_0_.refs_2_, bf16[640,2048]{1,0:T(8,128)(2,1)S(1)} %get-tuple-element.32.refs_1_.refs_3_, ...), custom_call_target="tpu_custom_call", output_to_operand_aliasing={{0}: (6, {}), {1}: (7, {}), {2}: (8, {})} | custom-call | flops 1207959552 | bytes 2359296 | tf_op jit(solution)/shard_map/pallas_call | solution.py:264
  63.5 1.4 %shard_map.70 = (f32[640,512]{1,0:T(8,128)S(1)}, f32[640,512]{1,0:T(8,128)S(1)}, f32[4,256,256]{2,1,0:T(8,128)S(1)}) custom-call(bf16[640,2048]{1,0:T(8,128)(2,1)S(1)} %get-tuple-element.29.refs_0_, bf16[640,2048]{1,0:T(8,128)(2,1)S(1)} %get-tuple-element.30.refs_1_, ...), custom_call_target="tpu_custom_call", output_to_operand_aliasing={{0}: (6, {}), {1}: (7, {}), {2}: (8, {})} | custom-call | flops 1207959552 | bytes 2359296 | tf_op jit(solution)/shard_map/pallas_call | solution.py:264
  65.0 2.9 %shard_map.74 = f32[64,640]{1,0:T(8,128)} custom-call(bf16[640,2048]{1,0:T(8,128)(2,1)S(1)} %get-tuple-element.29.refs_0_, bf16[640,2048]{1,0:T(8,128)(2,1)S(1)} %get-tuple-element.30.refs_1_, bf16[640,2048]{1,0:T(8,128)(2,1)S(1)} %get-tuple-element.31.refs_0_.refs_2_, bf16[640,2048]{1,0:T(8,128)(2,1)S(1)} %get-tuple-element.32.refs_1_.refs_3_, ...), custom_call_target="tpu_custom_call" | custom-call | flops 1207959552 | bytes 2359296 | tf_op jit(solution)/shard_map/pallas_call | solution.py:264
  (23 shorter events, 0.1 us)
Async XLA Ops:
  1.4 11.9 %collective-permute-start.18 = (bf16[2,128,512]{2,1,0:T(8,128)(2,1)S(1)}, bf16[2,128,512]{2,1,0:T(8,128)(2,1)S(1)}, u32[]{:S(2)}, u32[]{:S(2)}) collective-permute-start(bf16[2,128,512]{2,1,0:T(8,128)(2,1)S(1)} %shard_map.67.refs_2_), channel_id=1, source_target_pairs={{0,4},{1,5},{2,6},{3,7},{4,8},{5,9},{6,10},{7,11},{8,12},{9,13},{1... | collective-permute-start | bytes 786440 | tf_op jit(solution)/shard_map/ppermute | solution.py:295
  4.6 8.8 %collective-permute-start.5 = (bf16[2,128,512]{2,1,0:T(8,128)(2,1)S(1)}, bf16[2,128,512]{2,1,0:T(8,128)(2,1)S(1)}, u32[]{:S(2)}, u32[]{:S(2)}) collective-permute-start(bf16[2,128,512]{2,1,0:T(8,128)(2,1)S(1)} %shard_map.67.refs_2_), channel_id=1, source_target_pairs={{0,2},{1,3},{2,0},{3,1},{4,6},{5,7},{6,4},{7,5},{8,10},{9,11},{10,... | collective-permute-start | bytes 786440 | tf_op jit(solution)/shard_map/ppermute | solution.py:295
  6.0 7.8 %collective-permute-start.27 = (bf16[2,128,512]{2,1,0:T(8,128)(2,1)S(1)}, bf16[2,128,512]{2,1,0:T(8,128)(2,1)S(1)}, u32[]{:S(2)}, u32[]{:S(2)}) collective-permute-start(bf16[2,128,512]{2,1,0:T(8,128)(2,1)S(1)} %shard_map.67.refs_2_), channel_id=1, source_target_pairs={{0,1},{1,0},{2,3},{3,2},{4,5},{5,4},{6,7},{7,6},{8,9},{9,8},{10,11... | collective-permute-start | bytes 786440 | tf_op jit(solution)/shard_map/ppermute | solution.py:295
  7.5 11.0 %collective-permute-start = (bf16[2,128,512]{2,1,0:T(8,128)(2,1)S(1)}, bf16[2,128,512]{2,1,0:T(8,128)(2,1)S(1)}, u32[]{:S(2)}, u32[]{:S(2)}) collective-permute-start(bf16[2,128,512]{2,1,0:T(8,128)(2,1)S(1)} %shard_map.66.refs_2_), channel_id=1, source_target_pairs={{0,4},{1,5},{2,6},{3,7},{4,8},{5,9},{6,10},{7,11},{8,12},{9,13},{1... | collective-permute-start | bytes 786440 | tf_op jit(solution)/shard_map/ppermute | solution.py:295
  9.1 9.4 %collective-permute-start.15 = (bf16[2,128,512]{2,1,0:T(8,128)(2,1)S(1)}, bf16[2,128,512]{2,1,0:T(8,128)(2,1)S(1)}, u32[]{:S(2)}, u32[]{:S(2)}) collective-permute-start(bf16[2,128,512]{2,1,0:T(8,128)(2,1)S(1)} %shard_map.66.refs_2_), channel_id=1, source_target_pairs={{0,2},{1,3},{2,0},{3,1},{4,6},{5,7},{6,4},{7,5},{8,10},{9,11},{10,... | collective-permute-start | bytes 786440 | tf_op jit(solution)/shard_map/ppermute | solution.py:295
  13.3 6.7 %collective-permute-start.14 = (bf16[2,128,512]{2,1,0:T(8,128)(2,1)S(1)}, bf16[2,128,512]{2,1,0:T(8,128)(2,1)S(1)}, u32[]{:S(2)}, u32[]{:S(2)}) collective-permute-start(bf16[2,128,512]{2,1,0:T(8,128)(2,1)S(1)} %shard_map.66.refs_2_), channel_id=1, source_target_pairs={{0,1},{1,0},{2,3},{3,2},{4,5},{5,4},{6,7},{7,6},{8,9},{9,8},{10,11... | collective-permute-start | bytes 786440 | tf_op jit(solution)/shard_map/ppermute | solution.py:295
  13.3 6.7 %collective-permute-start.29 = (bf16[2,128,512]{2,1,0:T(8,128)(2,1)S(1)}, bf16[2,128,512]{2,1,0:T(8,128)(2,1)S(1)}, u32[]{:S(2)}, u32[]{:S(2)}) collective-permute-start(bf16[2,128,512]{2,1,0:T(8,128)(2,1)S(1)} %collective-permute-done.18.refs_6_), channel_id=1, source_target_pairs={{0,1},{1,0},{2,3},{3,2},{4,5},{5,4},{6,7},{7,6},{8,9},{9,8},{10,11... | collective-permute-start | bytes 786440 | tf_op jit(solution)/shard_map/ppermute | solution.py:295
  13.8 6.7 %collective-permute-start.28 = (bf16[2,128,512]{2,1,0:T(8,128)(2,1)S(1)}, bf16[2,128,512]{2,1,0:T(8,128)(2,1)S(1)}, u32[]{:S(2)}, u32[]{:S(2)}) collective-permute-start(bf16[2,128,512]{2,1,0:T(8,128)(2,1)S(1)} %collective-permute-done.5.refs_4_), channel_id=1, source_target_pairs={{0,1},{1,0},{2,3},{3,2},{4,5},{5,4},{6,7},{7,6},{8,9},{9,8},{10,11... | collective-permute-start | bytes 786440 | tf_op jit(solution)/shard_map/ppermute | solution.py:295
  18.5 11.0 %collective-permute-start.19 = (bf16[2,128,512]{2,1,0:T(8,128)(2,1)S(1)}, bf16[2,128,512]{2,1,0:T(8,128)(2,1)S(1)}, u32[]{:S(2)}, u32[]{:S(2)}) collective-permute-start(bf16[2,128,512]{2,1,0:T(8,128)(2,1)S(1)} %collective-permute-done.18.refs_6_), channel_id=1, source_target_pairs={{0,4},{1,5},{2,6},{3,7},{4,8},{5,9},{6,10},{7,11},{8,12},{9,13},{1... | collective-permute-start | bytes 786440 | tf_op jit(solution)/shard_map/ppermute | solution.py:295
  18.5 12.5 %collective-permute-start.24 = (bf16[2,128,512]{2,1,0:T(8,128)(2,1)S(1)}, bf16[2,128,512]{2,1,0:T(8,128)(2,1)S(1)}, u32[]{:S(2)}, u32[]{:S(2)}) collective-permute-start(bf16[2,128,512]{2,1,0:T(8,128)(2,1)S(1)} %collective-permute-done.18.refs_6_), channel_id=1, source_target_pairs={{0,2},{1,3},{2,0},{3,1},{4,6},{5,7},{6,4},{7,5},{8,10},{9,11},{10,... | collective-permute-start | bytes 786440 | tf_op jit(solution)/shard_map/ppermute | solution.py:295
  20.0 11.0 %collective-permute-start.17 = (bf16[2,128,512]{2,1,0:T(8,128)(2,1)S(1)}, bf16[2,128,512]{2,1,0:T(8,128)(2,1)S(1)}, u32[]{:S(2)}, u32[]{:S(2)}) collective-permute-start(bf16[2,128,512]{2,1,0:T(8,128)(2,1)S(1)} %collective-permute-done.refs_6_), channel_id=1, source_target_pairs={{0,1},{1,0},{2,3},{3,2},{4,5},{5,4},{6,7},{7,6},{8,9},{9,8},{10,11... | collective-permute-start | bytes 786440 | tf_op jit(solution)/shard_map/ppermute | solution.py:295
  20.0 11.5 %collective-permute-start.16 = (bf16[2,128,512]{2,1,0:T(8,128)(2,1)S(1)}, bf16[2,128,512]{2,1,0:T(8,128)(2,1)S(1)}, u32[]{:S(2)}, u32[]{:S(2)}) collective-permute-start(bf16[2,128,512]{2,1,0:T(8,128)(2,1)S(1)} %collective-permute-done.15.refs_4_), channel_id=1, source_target_pairs={{0,1},{1,0},{2,3},{3,2},{4,5},{5,4},{6,7},{7,6},{8,9},{9,8},{10,11... | collective-permute-start | bytes 786440 | tf_op jit(solution)/shard_map/ppermute | solution.py:295
  20.5 13.3 %collective-permute-start.1 = (bf16[2,128,512]{2,1,0:T(8,128)(2,1)S(1)}, bf16[2,128,512]{2,1,0:T(8,128)(2,1)S(1)}, u32[]{:S(2)}, u32[]{:S(2)}) collective-permute-start(bf16[2,128,512]{2,1,0:T(8,128)(2,1)S(1)} %collective-permute-done.refs_6_), channel_id=1, source_target_pairs={{0,4},{1,5},{2,6},{3,7},{4,8},{5,9},{6,10},{7,11},{8,12},{9,13},{1... | collective-permute-start | bytes 786440 | tf_op jit(solution)/shard_map/ppermute | solution.py:295
  29.5 8.1 %collective-permute-start.11 = (bf16[2,128,512]{2,1,0:T(8,128)(2,1)S(1)}, bf16[2,128,512]{2,1,0:T(8,128)(2,1)S(1)}, u32[]{:S(2)}, u32[]{:S(2)}) collective-permute-start(bf16[2,128,512]{2,1,0:T(8,128)(2,1)S(1)} %collective-permute-done.refs_6_), channel_id=1, source_target_pairs={{0,2},{1,3},{2,0},{3,1},{4,6},{5,7},{6,4},{7,5},{8,10},{9,11},{10,... | collective-permute-start | bytes 786440 | tf_op jit(solution)/shard_map/ppermute | solution.py:295
  31.0 6.6 %collective-permute-start.26 = (bf16[2,128,512]{2,1,0:T(8,128)(2,1)S(1)}, bf16[2,128,512]{2,1,0:T(8,128)(2,1)S(1)}, u32[]{:S(2)}, u32[]{:S(2)}) collective-permute-start(bf16[2,128,512]{2,1,0:T(8,128)(2,1)S(1)} %collective-permute-done.19.refs_4_), channel_id=1, source_target_pairs={{0,1},{1,0},{2,3},{3,2},{4,5},{5,4},{6,7},{7,6},{8,9},{9,8},{10,11... | collective-permute-start | bytes 786440 | tf_op jit(solution)/shard_map/ppermute | solution.py:295
  31.0 6.6 %collective-permute-start.25 = (bf16[2,128,512]{2,1,0:T(8,128)(2,1)S(1)}, bf16[2,128,512]{2,1,0:T(8,128)(2,1)S(1)}, u32[]{:S(2)}, u32[]{:S(2)}) collective-permute-start(bf16[2,128,512]{2,1,0:T(8,128)(2,1)S(1)} %collective-permute-done.24.refs_2_), channel_id=1, source_target_pairs={{0,1},{1,0},{2,3},{3,2},{4,5},{5,4},{6,7},{7,6},{8,9},{9,8},{10,11... | collective-permute-start | bytes 786440 | tf_op jit(solution)/shard_map/ppermute | solution.py:295
  31.5 12.4 %collective-permute-start.20 = (bf16[2,128,512]{2,1,0:T(8,128)(2,1)S(1)}, bf16[2,128,512]{2,1,0:T(8,128)(2,1)S(1)}, u32[]{:S(2)}, u32[]{:S(2)}) collective-permute-start(bf16[2,128,512]{2,1,0:T(8,128)(2,1)S(1)} %collective-permute-done.19.refs_4_), channel_id=1, source_target_pairs={{0,2},{1,3},{2,0},{3,1},{4,6},{5,7},{6,4},{7,5},{8,10},{9,11},{10,... | collective-permute-start | bytes 786440 | tf_op jit(solution)/shard_map/ppermute | solution.py:295
  33.8 12.6 %collective-permute-start.2 = (bf16[2,128,512]{2,1,0:T(8,128)(2,1)S(1)}, bf16[2,128,512]{2,1,0:T(8,128)(2,1)S(1)}, u32[]{:S(2)}, u32[]{:S(2)}) collective-permute-start(bf16[2,128,512]{2,1,0:T(8,128)(2,1)S(1)} %collective-permute-done.1.refs_4_), channel_id=1, source_target_pairs={{0,4},{1,5},{2,6},{3,7},{4,8},{5,9},{6,10},{7,11},{8,12},{9,13},{1... | collective-permute-start | bytes 786440 | tf_op jit(solution)/shard_map/ppermute | solution.py:295
  37.5 10.7 %collective-permute-start.22 = (bf16[2,128,512]{2,1,0:T(8,128)(2,1)S(1)}, bf16[2,128,512]{2,1,0:T(8,128)(2,1)S(1)}, u32[]{:S(2)}, u32[]{:S(2)}) collective-permute-start(bf16[2,128,512]{2,1,0:T(8,128)(2,1)S(1)} %collective-permute-done.19.refs_4_), channel_id=1, source_target_pairs={{0,4},{1,5},{2,6},{3,7},{4,8},{5,9},{6,10},{7,11},{8,12},{9,13},{1... | collective-permute-start | bytes 786440 | tf_op jit(solution)/shard_map/ppermute | solution.py:295
  37.6 14.7 %collective-permute-start.13 = (bf16[2,128,512]{2,1,0:T(8,128)(2,1)S(1)}, bf16[2,128,512]{2,1,0:T(8,128)(2,1)S(1)}, u32[]{:S(2)}, u32[]{:S(2)}) collective-permute-start(bf16[2,128,512]{2,1,0:T(8,128)(2,1)S(1)} %collective-permute-done.1.refs_4_), channel_id=1, source_target_pairs={{0,1},{1,0},{2,3},{3,2},{4,5},{5,4},{6,7},{7,6},{8,9},{9,8},{10,11... | collective-permute-start | bytes 786440 | tf_op jit(solution)/shard_map/ppermute | solution.py:295
  37.6 14.8 %collective-permute-start.12 = (bf16[2,128,512]{2,1,0:T(8,128)(2,1)S(1)}, bf16[2,128,512]{2,1,0:T(8,128)(2,1)S(1)}, u32[]{:S(2)}, u32[]{:S(2)}) collective-permute-start(bf16[2,128,512]{2,1,0:T(8,128)(2,1)S(1)} %collective-permute-done.11.refs_2_), channel_id=1, source_target_pairs={{0,1},{1,0},{2,3},{3,2},{4,5},{5,4},{6,7},{7,6},{8,9},{9,8},{10,11... | collective-permute-start | bytes 786440 | tf_op jit(solution)/shard_map/ppermute | solution.py:295
  43.9 10.4 %collective-permute-start.8 = (bf16[2,128,512]{2,1,0:T(8,128)(2,1)S(1)}, bf16[2,128,512]{2,1,0:T(8,128)(2,1)S(1)}, u32[]{:S(2)}, u32[]{:S(2)}) collective-permute-start(bf16[2,128,512]{2,1,0:T(8,128)(2,1)S(1)} %collective-permute-done.1.refs_4_), channel_id=1, source_target_pairs={{0,2},{1,3},{2,0},{3,1},{4,6},{5,7},{6,4},{7,5},{8,10},{9,11},{10,... | collective-permute-start | bytes 786440 | tf_op jit(solution)/shard_map/ppermute | solution.py:295
  46.4 8.3 %collective-permute-start.21 = (bf16[2,128,512]{2,1,0:T(8,128)(2,1)S(1)}, bf16[2,128,512]{2,1,0:T(8,128)(2,1)S(1)}, u32[]{:S(2)}, u32[]{:S(2)}) collective-permute-start(bf16[2,128,512]{2,1,0:T(8,128)(2,1)S(1)} %collective-permute-done.20.refs_2_), channel_id=1, source_target_pairs={{0,1},{1,0},{2,3},{3,2},{4,5},{5,4},{6,7},{7,6},{8,9},{9,8},{10,11... | collective-permute-start | bytes 786440 | tf_op jit(solution)/shard_map/ppermute | solution.py:295
  48.3 10.2 %collective-permute-start.6 = (bf16[2,128,512]{2,1,0:T(8,128)(2,1)S(1)}, bf16[2,128,512]{2,1,0:T(8,128)(2,1)S(1)}, u32[]{:S(2)}, u32[]{:S(2)}) collective-permute-start(bf16[2,128,512]{2,1,0:T(8,128)(2,1)S(1)} %collective-permute-done.5.refs_4_), channel_id=1, source_target_pairs={{0,12},{1,13},{2,14},{3,15},{4,0},{5,1},{6,2},{7,3},{8,4},{9,5},{1... | collective-permute-start | bytes 786440 | tf_op jit(solution)/shard_map/ppermute | solution.py:295
  52.2 8.4 %collective-permute-start.3 = (bf16[2,128,512]{2,1,0:T(8,128)(2,1)S(1)}, bf16[2,128,512]{2,1,0:T(8,128)(2,1)S(1)}, u32[]{:S(2)}, u32[]{:S(2)}) collective-permute-start(bf16[2,128,512]{2,1,0:T(8,128)(2,1)S(1)} %collective-permute-done.2.refs_4_), channel_id=1, source_target_pairs={{0,2},{1,3},{2,0},{3,1},{4,6},{5,7},{6,4},{7,5},{8,10},{9,11},{10,... | collective-permute-start | bytes 786440 | tf_op jit(solution)/shard_map/ppermute | solution.py:295
  52.4 9.7 %collective-permute-start.23 = (bf16[2,128,512]{2,1,0:T(8,128)(2,1)S(1)}, bf16[2,128,512]{2,1,0:T(8,128)(2,1)S(1)}, u32[]{:S(2)}, u32[]{:S(2)}) collective-permute-start(bf16[2,128,512]{2,1,0:T(8,128)(2,1)S(1)} %collective-permute-done.22.refs_4_), channel_id=1, source_target_pairs={{0,1},{1,0},{2,3},{3,2},{4,5},{5,4},{6,7},{7,6},{8,9},{9,8},{10,11... | collective-permute-start | bytes 786440 | tf_op jit(solution)/shard_map/ppermute | solution.py:295
  54.3 9.2 %collective-permute-start.10 = (bf16[2,128,512]{2,1,0:T(8,128)(2,1)S(1)}, bf16[2,128,512]{2,1,0:T(8,128)(2,1)S(1)}, u32[]{:S(2)}, u32[]{:S(2)}) collective-permute-start(bf16[2,128,512]{2,1,0:T(8,128)(2,1)S(1)} %collective-permute-done.2.refs_4_), channel_id=1, source_target_pairs={{0,1},{1,0},{2,3},{3,2},{4,5},{5,4},{6,7},{7,6},{8,9},{9,8},{10,11... | collective-permute-start | bytes 786440 | tf_op jit(solution)/shard_map/ppermute | solution.py:295
  54.7 8.8 %collective-permute-start.9 = (bf16[2,128,512]{2,1,0:T(8,128)(2,1)S(1)}, bf16[2,128,512]{2,1,0:T(8,128)(2,1)S(1)}, u32[]{:S(2)}, u32[]{:S(2)}) collective-permute-start(bf16[2,128,512]{2,1,0:T(8,128)(2,1)S(1)} %collective-permute-done.8.refs_2_), channel_id=1, source_target_pairs={{0,1},{1,0},{2,3},{3,2},{4,5},{5,4},{6,7},{7,6},{8,9},{9,8},{10,11... | collective-permute-start | bytes 786440 | tf_op jit(solution)/shard_map/ppermute | solution.py:295
  58.5 6.5 %collective-permute-start.7 = (bf16[2,128,512]{2,1,0:T(8,128)(2,1)S(1)}, bf16[2,128,512]{2,1,0:T(8,128)(2,1)S(1)}, u32[]{:S(2)}, u32[]{:S(2)}) collective-permute-start(bf16[2,128,512]{2,1,0:T(8,128)(2,1)S(1)} %collective-permute-done.6.refs_7_), channel_id=1, source_target_pairs={{0,1},{1,0},{2,3},{3,2},{4,5},{5,4},{6,7},{7,6},{8,9},{9,8},{10,11... | collective-permute-start | bytes 786440 | tf_op jit(solution)/shard_map/ppermute | solution.py:295
  60.7 4.3 %collective-permute-start.4 = (bf16[2,128,512]{2,1,0:T(8,128)(2,1)S(1)}, bf16[2,128,512]{2,1,0:T(8,128)(2,1)S(1)}, u32[]{:S(2)}, u32[]{:S(2)}) collective-permute-start(bf16[2,128,512]{2,1,0:T(8,128)(2,1)S(1)} %collective-permute-done.3.refs_5_), channel_id=1, source_target_pairs={{0,1},{1,0},{2,3},{3,2},{4,5},{5,4},{6,7},{7,6},{8,9},{9,8},{10,11... | collective-permute-start | bytes 786440 | tf_op jit(solution)/shard_map/ppermute | solution.py:295

commit v9 on v8

--- a/solution.py
+++ b/solution.py
@@ -145,132 +145,160 @@
 
 
 def stage_kernel(cfg, *refs):
-    (outer, inner), groups, last, rows = cfg["shape"], cfg["groups"], cfg["last"], cfg["rows"]
+    shape, where, rows = cfg["shape"], cfg["where"], cfg["rows"]
     refs = list(refs)
 
     def take(n):
         return [refs.pop(0) for _ in range(n)]
 
-    x_refs = [take(2) for _ in groups]
-    live_ref = take(1)[0] if last else None
-    pieces = [[take(2) for _ in g["where"]] for g in groups]
-    starts = [take(3) if g["carry"] else None for g in groups]
-    outs = take(1) if last else None
-    product = take(1)[0] if last else None
-    totals = [take(3) for _ in groups]
+    x_refs = take(2)
+    pieces = [take(2) for _ in where]
+    start = take(3) if cfg["carry"] else None
+    total = take(3)
     w = take(1)[0]
+    tiles = w.shape[2] // TILE
+    spans = []
+    for slot, (key, pair) in enumerate(zip(where, pieces)):
+        spans.append(lay_out(shape, key, pair, rows, w, slot * 2 * rows))
+    for slot, x_span in enumerate(spans):
+        span = slice(slot * 2 * rows, (slot + 1) * 2 * rows)
+        came = start if slot == 0 else total
+        for s in range(2):
+            part = jnp.dot(x_refs[s][:, x_span], w[s, span, :], preferred_element_type=jnp.float32)
+            total[s][...] = part if came is None else came[s][...] + part
+        for s in range(2):
+            for t in range(tiles):
+                one = w[s, span, t * TILE : (t + 1) * TILE]
+                part = lax.dot_general(one, one, (((0,), (0,)), ((), ())), preferred_element_type=jnp.float32)
+                i = s * tiles + t
+                total[2][i] = part if came is None else came[2][i] + part
+
+
+def lay_out(shape, key, pair, rows, w, base):
+    outer, inner = shape
+    da, db = key
     me = lax.axis_index("tok")
     a, b, c = me // (2 * inner), (me // 2) % inner, me % 2
-    spans, slot = [], 0
-    for g, arrays in zip(groups, pieces):
-        for (da, db), pair in zip(g["where"], arrays):
-            owner = ((a + outer - da) % outer) * inner + (b + inner - db) % inner
-            start = pl.multiple_of(owner * 2 * rows, LANES)
-            for dc, array in enumerate(pair):
-                spot = pl.multiple_of(slot * 2 * rows + ((c + dc) % 2) * rows, LANES)
-                w[:, pl.ds(spot, rows), :] = array[...]
-            spans.append(pl.ds(start, 2 * rows))
-            slot += 1
-    tiles = w.shape[2] // TILE
-    slot = 0
-    for n, (g, start, total) in enumerate(zip(groups, starts, totals)):
-        for first in range(len(g["where"])):
-            span = slice(slot * 2 * rows, (slot + 1) * 2 * rows)
-            came = start if first == 0 else total
-            for s in range(2):
-                x = x_refs[n][s][:, spans[slot]]
-                part = jnp.dot(x, w[s, span, :], preferred_element_type=jnp.float32)
-                if came is not None:
-                    part = came[s][...] + part
-                if last and s == 1:
-                    part = total[0][...] * part
-                    product[...] = part if g is groups[0] else product[...] + part
-                else:
-                    total[s][...] = part
-            for s in range(2):
-                for t in range(tiles):
-                    one = w[s, span, t * TILE : (t + 1) * TILE]
-                    part = lax.dot_general(one, one, (((0,), (0,)), ((), ())), preferred_element_type=jnp.float32)
-                    i = s * tiles + t
-                    total[2][i] = part if came is None else came[2][i] + part
-            slot += 1
-    if last:
-        columns = w.shape[2]
-        row = lax.broadcasted_iota(jnp.int32, (TILE, TILE), 0)
-        col = lax.broadcasted_iota(jnp.int32, (TILE, TILE), 1)
-        same = row // RANK == col // RANK
-        norm = []
-        for t in range(tiles):
-            both = sum(total[2][t] * total[2][tiles + t] for total in totals)
-            norm.append(jnp.sum(jnp.where(same, both, 0.0), axis=0, keepdims=True))
-        norm = jnp.broadcast_to(jnp.concatenate(norm, axis=1), (8, columns))
-        chooser = group_sums(columns)
-        scale = 1.0 / jnp.sqrt(split_dot(norm, chooser)[:1] + 1e-06)
-        tokens = product.shape[0]
-        for low in range(0, tokens, LANES):
-            span = slice(low, low + LANES)
-            rest, terms = product[span], []
-            for _ in range(TERMS):
-                terms.append(rest.astype(jnp.bfloat16))
-                rest = rest - terms[-1].astype(jnp.float32)
-            raw = jnp.dot(jnp.concatenate(terms, axis=0), chooser, preferred_element_type=jnp.float32)
-            raw = sum(raw[i * LANES : (i + 1) * LANES] for i in range(TERMS))
-            token = low + lax.broadcasted_iota(jnp.int32, raw.shape, 0)
-            scaled = jnp.where(token < live_ref[:1], raw * scale, 0.0)
-            outs[0][:, span] = scaled.T[: columns // RANK]
-
-
-def stage(shape, groups, live=None):
-    last = live is not None
-    rows, columns = groups[0]["arrays"][0][0].shape[1:]
-    tokens = groups[0]["tokens"][0].shape[0]
-    slots = sum(len(g["where"]) for g in groups)
+    owner = ((a + outer - da) % outer) * inner + (b + inner - db) % inner
+    for dc, array in enumerate(pair):
+        spot = pl.multiple_of(base + ((c + dc) % 2) * rows, LANES)
+        w[:, pl.ds(spot, rows), :] = array[...]
+    return pl.ds(pl.multiple_of(owner * 2 * rows, LANES), 2 * rows)
+
+
+def stage(shape, where, arrays, tokens, carry):
+    rows, columns = arrays[0][0].shape[1:]
+    count = tokens[0].shape[0]
+    slots = len(where)
     tiles = 2 * (columns // TILE)
+    args = list(tokens) + [piece for pair in arrays for piece in pair]
+    aliases = {}
+    if carry is not None:
+        aliases = {len(args) + i: i for i in range(3)}
+        args += list(carry)
     vmem = pl.BlockSpec(memory_space=pltpu.VMEM)
-    args, specs = [], []
-    for g in groups:
-        args += g["tokens"]
-        specs += [vmem] * 2
-    if last:
-        args.append(live)
-        specs.append(vmem)
-    for g in groups:
-        for pair in g["arrays"]:
-            args += pair
-            specs += [vmem] * 2
-    aliases = {}
-    for n, g in enumerate(groups):
-        if g["carry"] is not None:
-            if not last:
-                aliases.update({len(args) + i: 3 * n + i for i in range(3)})
-            args += list(g["carry"])
-            specs += [vmem] * 3
-    sums = [((tokens, columns), jnp.float32)] * 2 + [((tiles, TILE, TILE), jnp.float32)]
-    scratch = []
-    if last:
-        out_shape = jax.ShapeDtypeStruct((columns // RANK, tokens), jnp.float32)
-        out_specs = vmem
-        scratch = [pltpu.VMEM(*sums[0])] + [pltpu.VMEM(*one) for one in sums] * len(groups)
-    else:
-        out_shape = tuple(jax.ShapeDtypeStruct(*one) for one in sums) * len(groups)
-        out_specs = (vmem,) * len(out_shape)
-    cfg = dict(
-        shape=shape,
-        rows=rows,
-        last=last,
-        groups=[dict(layer=g["layer"], where=g["where"], carry=g["carry"] is not None) for g in groups],
-    )
-    flops = 4 * slots * rows * columns * (2 * tokens + tiles * TILE)
+    proj = jax.ShapeDtypeStruct((count, columns), jnp.float32)
+    cfg = dict(shape=shape, rows=rows, where=where, carry=carry is not None)
     return pl.pallas_call(
         functools.partial(stage_kernel, cfg),
-        out_shape=out_shape,
-        in_specs=specs,
-        out_specs=out_specs,
-        scratch_shapes=scratch + [pltpu.VMEM((2, slots * 2 * rows, columns), jnp.bfloat16)],
+        out_shape=(proj, proj, jax.ShapeDtypeStruct((tiles, TILE, TILE), jnp.float32)),
+        in_specs=[vmem] * len(args),
+        out_specs=(vmem,) * 3,
+        scratch_shapes=[pltpu.VMEM((2, slots * 2 * rows, columns), jnp.bfloat16)],
         input_output_aliases=aliases,
         compiler_params=pltpu.CompilerParams(vmem_limit_bytes=GRANT),
         cost_estimate=pl.CostEstimate(
-            flops=flops, bytes_accessed=8 * slots * rows * (tokens + columns), transcendentals=0
+            flops=4 * slots * rows * columns * (2 * count + tiles * TILE),
+            bytes_accessed=8 * slots * rows * (count + columns),
+            transcendentals=0,
+        ),
+    )(*args)
+
+
+def finish_kernel(cfg, *refs):
+    shape, layers, tile, rows, key = cfg["shape"], cfg["layers"], cfg["tile"], cfg["rows"], cfg["key"]
+    refs = list(refs)
+
+    def take(n):
+        return [refs.pop(0) for _ in range(n)]
+
+    live_ref = take(1)[0]
+    x_refs = [take(2) for _ in range(layers)]
+    pieces = [take(2) for _ in range(layers)]
+    carries = [take(3) for _ in range(layers)]
+    if tile:
+        take(1)
+    out_ref, w, held, product, made, sem = take(6)
+    cols = slice(tile * TILE, (tile + 1) * TILE)
+    tiles = carries[0][2].shape[0] // 2
+    spans = [lay_out(shape, key, pieces[n], rows, w.at[n], 0) for n in range(layers)]
+    row = lax.broadcasted_iota(jnp.int32, (TILE, TILE), 0)
+    col = lax.broadcasted_iota(jnp.int32, (TILE, TILE), 1)
+    norm = None
+    for n, carry in enumerate(carries):
+        for s in range(2):
+            part = jnp.dot(x_refs[n][s][:, spans[n]], w[n, s], preferred_element_type=jnp.float32)
+            part = carry[s][:, cols] + part
+            if s == 0:
+                held[...] = part
+            else:
+                part = held[...] * part
+                product[...] = part if n == 0 else product[...] + part
+        grams = []
+        for s in range(2):
+            one = w[n, s]
+            part = lax.dot_general(one, one, (((0,), (0,)), ((), ())), preferred_element_type=jnp.float32)
+            grams.append(carry[2][s * tiles + tile] + part)
+        both = grams[0] * grams[1]
+        norm = both if norm is None else norm + both
+    norm = jnp.sum(jnp.where(row // RANK == col // RANK, norm, 0.0), axis=0, keepdims=True)
+    chooser = group_sums(TILE)
+    norm = split_dot(jnp.broadcast_to(norm, (8, TILE)), chooser)[:1]
+    scale = 1.0 / jnp.sqrt(norm + 1e-06)
+    for low in range(0, product.shape[0], LANES):
+        span = slice(low, low + LANES)
+        rest, terms = product[span], []
+        for _ in range(TERMS):
+            terms.append(rest.astype(jnp.bfloat16))
+            rest = rest - terms[-1].astype(jnp.float32)
+        raw = jnp.dot(jnp.concatenate(terms, axis=0), chooser, preferred_element_type=jnp.float32)
+        raw = sum(raw[i * LANES : (i + 1) * LANES] for i in range(TERMS))
+        token = low + lax.broadcasted_iota(jnp.int32, raw.shape, 0)
+        scaled = jnp.where(token < live_ref[:1], raw * scale, 0.0)
+        made[:, span] = scaled.T[: TILE // RANK]
+    out = pltpu.make_async_copy(made, out_ref.at[pl.ds(tile * (TILE // RANK), TILE // RANK), :], sem)
+    out.start()
+    out.wait()
+
+
+def finish(shape, key, tile, arrays, tokens, carries, live, before):
+    layers, rows = len(arrays), arrays[0][0].shape[1]
+    count, columns = carries[0][0].shape
+    args = [live] + [one for pair in tokens for one in pair] + [one for pair in arrays for one in pair]
+    args += [one for carry in carries for one in carry]
+    vmem, hbm = pl.BlockSpec(memory_space=pltpu.VMEM), pl.BlockSpec(memory_space=pltpu.HBM)
+    specs, aliases = [vmem] * len(args), {}
+    if tile:
+        aliases = {len(args): 0}
+        args.append(before)
+        specs.append(hbm)
+    cfg = dict(shape=shape, layers=layers, tile=tile, rows=rows, key=key)
+    return pl.pallas_call(
+        functools.partial(finish_kernel, cfg),
+        out_shape=jax.ShapeDtypeStruct((columns // RANK, count), jnp.float32),
+        in_specs=specs,
+        out_specs=hbm,
+        scratch_shapes=[
+            pltpu.VMEM((layers, 2, 2 * rows, TILE), jnp.bfloat16),
+            pltpu.VMEM((count, TILE), jnp.float32),
+            pltpu.VMEM((count, TILE), jnp.float32),
+            pltpu.VMEM((TILE // RANK, count), jnp.float32),
+            pltpu.SemaphoreType.DMA,
+        ],
+        input_output_aliases=aliases,
+        compiler_params=pltpu.CompilerParams(vmem_limit_bytes=GRANT),
+        cost_estimate=pl.CostEstimate(
+            flops=8 * layers * rows * TILE * count, bytes_accessed=8 * rows * count, transcendentals=0
         ),
     )(*args)
 
@@ -303,28 +331,33 @@
             if da < outer - 1:
                 fed = h[(da, 0)]
                 h[(da + 1, 0)] = move(fed, 1, 0, 0)
-            if da == outer - 1 and layer == 1:
-                fed = after(h[(0, 1)], have[0][(da, 0)])
-                h[(da, 1)] = move(fed, -1, 0, 0)
-            else:
+            if da < outer - 1:
                 h[(da, 1)] = move(h[(da, 0)], 0, 1, 0)
+    end = (outer - 1, 1)
+    tiles = have[0][(0, 0)].shape[2] // TILE
+    ends = [[], []]
+    for t in range(tiles):
+        cut = slice(t * TILE, (t + 1) * TILE)
+        across = have[0][(outer - 1, 0)]
+        ends[1].append(move(after(have[1][(0, 1)][:, :, cut], across), -1, 0, 0))
+        ends[0].append(move(across[:, :, cut], 0, 1, 0))
     for layer in range(2):
         for key, piece in have[layer].items():
             pairs[layer][key] = [piece, move(piece, 0, 0, 1)]
 
     live, *first = load(0, counts, gradients, activations)
     tokens = [first, load(1, counts, gradients, activations)]
-
-    def group(layer, keys, carry):
-        return dict(layer=layer, where=keys, arrays=[pairs[layer][key] for key in keys], carry=carry, tokens=tokens[layer])
 
     parts = [[(0, 0), (0, 1), (1, 0)]] + [[(da, 1), (da + 1, 0)] for da in range(1, outer - 1)]
     carry = [None, None]
     for keys in parts:
         for layer in range(2):
-            carry[layer] = stage(
-                shape, [group(layer, keys, carry[layer])])
-    scores = stage(shape, [group(layer, [(outer - 1, 1)], carry[layer]) for layer in range(2)], live=live)
+            arrays = [pairs[layer][one] for one in keys]
+            carry[layer] = stage(shape, keys, arrays, tokens[layer], carry[layer])
+    scores = None
+    for t in range(tiles):
+        arrays = [[ends[layer][t], move(ends[layer][t], 0, 0, 1)] for layer in range(2)]
+        scores = finish(shape, end, t, arrays, tokens, carry, live, scores)
     return scores.T
 
 

time: 68.1 us -> 71.2 us (1.046)
  waiting for transfers between devices: 25.9 us -> 27.9 us
  Pallas kernels: 20.2 us -> 21 us
    ppermute x30 -> x34, waiting for transfers between devices: 25.9 us -> 27.9 us  [move(): return lax.ppermute(value, 'tok', steps)]
    pallas_call x7 -> x8, Pallas kernels: 12.2 us -> 13 us  [the longest x6 9.23 us: stage(): pl.pallas_call(functools.partial(stage_kernel, cfg), out_shape=(proj, pro...]
    ppermute x30 -> x34, starting transfers between devices: 21 us -> 21 us  [move(): return lax.ppermute(value, 'tok', steps)]
  transfers between devices with their start and end apart: 30 -> 34, of which waited for: 8 -> 9; matrix products, arithmetic and copies ran while one was open for 0% -> 0% of each run, Pallas kernels for 23% -> 25%
where the time goes in v9:
time: 71.2 us; the launch traced here: 71 us
  waiting for transfers between devices  27.9 us (39%)
  Pallas kernels  21 us (29%)
  starting transfers between devices  21 us (29%)
  between operations  1.06 us (1%)
    ppermute x34, waiting for transfers between devices, move(): return lax.ppermute(value, 'tok', steps)  27.9 us
    ppermute x34, starting transfers between devices, move(): return lax.ppermute(value, 'tok', steps)  21 us
    pallas_call x6, Pallas kernels, stage(): pl.pallas_call(functools.partial(stage_kernel, cfg), out_shape=(proj, pro...  9.23 us
    pallas_call x2, Pallas kernels, load(): pl.pallas_call(functools.partial(load_kernel, layer), out_shape=tuple(out...  5.1 us
    pallas_call x2, Pallas kernels, finish(): pl.pallas_call(functools.partial(finish_kernel, cfg), out_shape=jax.Shape...  3.77 us
    pallas_call x2, Pallas kernels, pick(): pl.pallas_call(functools.partial(pick_kernel, layer), out_shape=jax.Shape...  2.88 us
  transfers between devices with their start and end apart: 34, of which 9 were waited for; matrix products, arithmetic and copies ran while one was open for 0% of the time, Pallas kernels for 25%

profile of v9, /device:TPU:0, one launch (start us, length us, event | category | flops | bytes accessed | tf_op | source)
XLA Modules:
  0.0 71.0 jit_solution(11178150870756959145)
XLA Ops:
  0.0 1.4 %shard_map.67.refs_2_ = bf16[2,128,512]{2,1,0:T(8,128)(2,1)S(1)} custom-call(s32[2,16]{1,0:T(2,128)} %ids_hbm.3, bf16[2,128,1024]{2,1,0:T(8,128)(2,1)} %u_ref.3, bf16[2,128,1024]{2,1,0:T(8,128)(2,1)} %v_ref.3), custom_call_target="tpu_custom_call" | custom-call | flops 262144 | bytes 786432 | tf_op jit(solution)/shard_map/pallas_call | solution.py:84
  1.4 3.1 %collective-permute-start.18 = (bf16[2,128,512]{2,1,0:T(8,128)(2,1)S(1)}, bf16[2,128,512]{2,1,0:T(8,128)(2,1)S(1)}, u32[]{:S(2)}, u32[]{:S(2)}) collective-permute-start(bf16[2,128,512]{2,1,0:T(8,128)(2,1)S(1)} %shard_map.67.refs_2_), channel_id=1, source_target_pairs={{0,4},{1,5},{2,6},{3,7},{4,8},{5,9},{6,10},{7,11},{8,12},{9,13},{1... | collective-permute-start | bytes 786440 | tf_op jit(solution)/shard_map/ppermute | solution.py:323
  4.6 1.5 %collective-permute-start.5 = (bf16[2,128,512]{2,1,0:T(8,128)(2,1)S(1)}, bf16[2,128,512]{2,1,0:T(8,128)(2,1)S(1)}, u32[]{:S(2)}, u32[]{:S(2)}) collective-permute-start(bf16[2,128,512]{2,1,0:T(8,128)(2,1)S(1)} %shard_map.67.refs_2_), channel_id=1, source_target_pairs={{0,2},{1,3},{2,0},{3,1},{4,6},{5,7},{6,4},{7,5},{8,10},{9,11},{10,... | collective-permute-start | bytes 786440 | tf_op jit(solution)/shard_map/ppermute | solution.py:323
  6.0 0.0 collective-permute-start.27
  6.0 1.4 %shard_map.66.refs_2_ = bf16[2,128,512]{2,1,0:T(8,128)(2,1)S(1)} custom-call(s32[2,16]{1,0:T(2,128)} %ids_hbm.3, bf16[2,128,1024]{2,1,0:T(8,128)(2,1)} %u_ref.3, bf16[2,128,1024]{2,1,0:T(8,128)(2,1)} %v_ref.3), custom_call_target="tpu_custom_call" | custom-call | flops 262144 | bytes 786432 | tf_op jit(solution)/shard_map/pallas_call | solution.py:84
  7.5 1.6 %collective-permute-start = (bf16[2,128,512]{2,1,0:T(8,128)(2,1)S(1)}, bf16[2,128,512]{2,1,0:T(8,128)(2,1)S(1)}, u32[]{:S(2)}, u32[]{:S(2)}) collective-permute-start(bf16[2,128,512]{2,1,0:T(8,128)(2,1)S(1)} %shard_map.66.refs_2_), channel_id=1, source_target_pairs={{0,4},{1,5},{2,6},{3,7},{4,8},{5,9},{6,10},{7,11},{8,12},{9,13},{1... | collective-permute-start | bytes 786440 | tf_op jit(solution)/shard_map/ppermute | solution.py:323
  9.1 0.5 collective-permute-start.15
  9.7 3.7 %collective-permute-done.18.refs_6_ = bf16[2,128,512]{2,1,0:T(8,128)(2,1)S(1)} collective-permute-done((bf16[2,128,512]{2,1,0:T(8,128)(2,1)S(1)}, bf16[2,128,512]{2,1,0:T(8,128)(2,1)S(1)}, u32[]{:S(2)}, u32[]{:S(2)}) %collective-permute-start.18) | collective-permute-done | bytes 262176 | tf_op jit(solution)/shard_map/ppermute | solution.py:323
  13.3 0.0 collective-permute-start.14
  13.3 0.0 collective-permute-done.5.refs_4_
  13.3 0.5 collective-permute-start.29
  13.8 0.1 collective-permute-start.28
  13.9 4.6 %collective-permute-done.refs_6_ = bf16[2,128,512]{2,1,0:T(8,128)(2,1)S(1)} collective-permute-done((bf16[2,128,512]{2,1,0:T(8,128)(2,1)S(1)}, bf16[2,128,512]{2,1,0:T(8,128)(2,1)S(1)}, u32[]{:S(2)}, u32[]{:S(2)}) %collective-permute-start) | collective-permute-done | bytes 262176 | tf_op jit(solution)/shard_map/ppermute | solution.py:323
  18.5 0.0 collective-permute-done.15.refs_4_
  18.5 1.5 %collective-permute-start.24 = (bf16[2,128,512]{2,1,0:T(8,128)(2,1)S(1)}, bf16[2,128,512]{2,1,0:T(8,128)(2,1)S(1)}, u32[]{:S(2)}, u32[]{:S(2)}) collective-permute-start(bf16[2,128,512]{2,1,0:T(8,128)(2,1)S(1)} %collective-permute-done.18.refs_6_), channel_id=1, source_target_pairs={{0,2},{1,3},{2,0},{3,1},{4,6},{5,7},{6,4},{7,5},{8,10},{9,11},{10,... | collective-permute-start | bytes 786440 | tf_op jit(solution)/shard_map/ppermute | solution.py:323
  20.0 1.3 %collective-permute-start.1 = (bf16[2,128,512]{2,1,0:T(8,128)(2,1)S(1)}, bf16[2,128,512]{2,1,0:T(8,128)(2,1)S(1)}, u32[]{:S(2)}, u32[]{:S(2)}) collective-permute-start(bf16[2,128,512]{2,1,0:T(8,128)(2,1)S(1)} %collective-permute-done.refs_6_), channel_id=1, source_target_pairs={{0,4},{1,5},{2,6},{3,7},{4,8},{5,9},{6,10},{7,11},{8,12},{9,13},{1... | collective-permute-start | bytes 786440 | tf_op jit(solution)/shard_map/ppermute | solution.py:323
  21.4 0.2 collective-permute-start.16
  21.5 7.9 %collective-permute-done.19.refs_4_ = bf16[2,128,512]{2,1,0:T(8,128)(2,1)S(1)} collective-permute-done((bf16[2,128,512]{2,1,0:T(8,128)(2,1)S(1)}, bf16[2,128,512]{2,1,0:T(8,128)(2,1)S(1)}, u32[]{:S(2)}, u32[]{:S(2)}) %collective-permute-start.19) | collective-permute-done | bytes 262176 | tf_op jit(solution)/shard_map/ppermute | solution.py:323
  29.5 1.5 %collective-permute-start.11 = (bf16[2,128,512]{2,1,0:T(8,128)(2,1)S(1)}, bf16[2,128,512]{2,1,0:T(8,128)(2,1)S(1)}, u32[]{:S(2)}, u32[]{:S(2)}) collective-permute-start(bf16[2,128,512]{2,1,0:T(8,128)(2,1)S(1)} %collective-permute-done.refs_6_), channel_id=1, source_target_pairs={{0,2},{1,3},{2,0},{3,1},{4,6},{5,7},{6,4},{7,5},{8,10},{9,11},{10,... | collective-permute-start | bytes 786440 | tf_op jit(solution)/shard_map/ppermute | solution.py:323
  31.0 0.5 collective-permute-start.25
  31.5 2.3 %collective-permute-done.1.refs_4_ = bf16[2,128,512]{2,1,0:T(8,128)(2,1)S(1)} collective-permute-done((bf16[2,128,512]{2,1,0:T(8,128)(2,1)S(1)}, bf16[2,128,512]{2,1,0:T(8,128)(2,1)S(1)}, u32[]{:S(2)}, u32[]{:S(2)}) %collective-permute-start.1) | collective-permute-done | bytes 262176 | tf_op jit(solution)/shard_map/ppermute | solution.py:323
  34.5 2.6 %shard_map.65 = (bf16[640,2048]{1,0:T(8,128)(2,1)S(1)}, bf16[640,2048]{1,0:T(8,128)(2,1)S(1)}) custom-call(bf16[2,640,2048]{2,1,0:T(8,128)(2,1)} %refs_0_.2, bf16[2,640,2048]{2,1,0:T(8,128)(2,1)} %refs_1_.3), custom_call_target="tpu_custom_call" | custom-call | tf_op jit(solution)/shard_map/pallas_call | solution.py:120
  37.0 2.6 %shard_map.64 = (s32[8,128]{1,0:T(8,128)S(1)}, bf16[640,2048]{1,0:T(8,128)(2,1)S(1)}, bf16[640,2048]{1,0:T(8,128)(2,1)S(1)}) custom-call(s32[1]{0:T(128)S(6)} %copy.33.refs_0_, bf16[2,640,2048]{2,1,0:T(8,128)(2,1)} %refs_0_.2, bf16[2,640,2048]{2,1,0:T(8,128)(2,1)} %refs_1_.3), custom_call_target="tpu_custom_call" | custom-call | tf_op jit(solution)/shard_map/pallas_call | solution.py:120
  39.6 0.9 %collective-permute-start.20 = (bf16[2,128,512]{2,1,0:T(8,128)(2,1)S(1)}, bf16[2,128,512]{2,1,0:T(8,128)(2,1)S(1)}, u32[]{:S(2)}, u32[]{:S(2)}) collective-permute-start(bf16[2,128,512]{2,1,0:T(8,128)(2,1)S(1)} %collective-permute-done.19.refs_4_), channel_id=1, source_target_pairs={{0,2},{1,3},{2,0},{3,1},{4,6},{5,7},{6,4},{7,5},{8,10},{9,11},{10,... | collective-permute-start | bytes 786440 | tf_op jit(solution)/shard_map/ppermute | solution.py:323
  40.6 0.1 collective-permute-start.13
  40.6 1.2 %collective-permute-start.8 = (bf16[2,128,512]{2,1,0:T(8,128)(2,1)S(1)}, bf16[2,128,512]{2,1,0:T(8,128)(2,1)S(1)}, u32[]{:S(2)}, u32[]{:S(2)}) collective-permute-start(bf16[2,128,512]{2,1,0:T(8,128)(2,1)S(1)} %collective-permute-done.1.refs_4_), channel_id=1, source_target_pairs={{0,2},{1,3},{2,0},{3,1},{4,6},{5,7},{6,4},{7,5},{8,10},{9,11},{10,... | collective-permute-start | bytes 786440 | tf_op jit(solution)/shard_map/ppermute | solution.py:323
  41.9 0.8 %collective-permute-done.2.refs_4_ = bf16[2,128,512]{2,1,0:T(8,128)(2,1)S(1)} collective-permute-done((bf16[2,128,512]{2,1,0:T(8,128)(2,1)S(1)}, bf16[2,128,512]{2,1,0:T(8,128)(2,1)S(1)}, u32[]{:S(2)}, u32[]{:S(2)}) %collective-permute-start.2) | collective-permute-done | bytes 262176 | tf_op jit(solution)/shard_map/ppermute | solution.py:323
  42.6 1.8 %shard_map.71 = (f32[640,512]{1,0:T(8,128)S(1)}, f32[640,512]{1,0:T(8,128)S(1)}, f32[4,256,256]{2,1,0:T(8,128)S(1)}) custom-call(bf16[640,2048]{1,0:T(8,128)(2,1)S(1)} %get-tuple-element.33.refs_0_.refs_3_, bf16[640,2048]{1,0:T(8,128)(2,1)S(1)} %get-tuple-element.34.refs_1_.refs_4_, bf16[2,128,512]{2,1,0:T(8,128)(2,1)S(1)} %shard_map.67.refs_2_, ...), custom_call_target="tpu_custom_call" | custom-call | flops 1811939328 | bytes 3538944 | tf_op jit(solution)/shard_map/pallas_call | solution.py:202
  44.5 4.4 %collective-permute-done.20.refs_2_ = bf16[2,128,512]{2,1,0:T(8,128)(2,1)S(1)} collective-permute-done((bf16[2,128,512]{2,1,0:T(8,128)(2,1)S(1)}, bf16[2,128,512]{2,1,0:T(8,128)(2,1)S(1)}, u32[]{:S(2)}, u32[]{:S(2)}) %collective-permute-start.20) | collective-permute-done | bytes 262176 | tf_op jit(solution)/shard_map/ppermute | solution.py:323
  48.9 3.8 %collective-permute-start.32 = (bf16[2,128,256]{2,1,0:T(8,128)(2,1)S(1)}, bf16[2,128,256]{2,1,0:T(8,128)(2,1)S(1)}, u32[]{:S(2)}, u32[]{:S(2)}) collective-permute-start(bf16[2,128,256]{2,1,0:T(8,128)(2,1)S(1)} %get-tuple-element.54), channel_id=1, source_target_pairs={{0,12},{1,13},{2,14},{3,15},{4,0},{5,1},{6,2},{7,3},{8,4},{9,5},{1... | collective-permute-start | bytes 393224 | tf_op jit(solution)/shard_map/ppermute | solution.py:323
  52.7 0.1 collective-permute-start.30
  52.8 0.2 collective-permute-start.6
  53.0 0.1 collective-permute-start.21
  53.0 0.7 collective-permute-done.8.refs_2_
  53.7 1.8 %shard_map.68 = (f32[640,512]{1,0:T(8,128)S(1)}, f32[640,512]{1,0:T(8,128)S(1)}, f32[4,256,256]{2,1,0:T(8,128)S(1)}) custom-call(bf16[640,2048]{1,0:T(8,128)(2,1)S(1)} %get-tuple-element.31.refs_0_.refs_1_, bf16[640,2048]{1,0:T(8,128)(2,1)S(1)} %get-tuple-element.32.refs_1_.refs_2_, bf16[2,128,512]{2,1,0:T(8,128)(2,1)S(1)} %shard_map.66.refs_2_, ...), custom_call_target="tpu_custom_call" | custom-call | flops 1811939328 | bytes 3538944 | tf_op jit(solution)/shard_map/pallas_call | solution.py:202
  55.5 0.6 collective-permute-start.10
  56.1 1.6 %collective-permute-done.30.refs_5_ = bf16[2,128,256]{2,1,0:T(8,128)(2,1)S(1)} collective-permute-done((bf16[2,128,256]{2,1,0:T(8,128)(2,1)S(1)}, bf16[2,128,256]{2,1,0:T(8,128)(2,1)S(1)}, u32[]{:S(2)}, u32[]{:S(2)}) %collective-permute-start.30) | collective-permute-done | bytes 131104 | tf_op jit(solution)/shard_map/ppermute | solution.py:323
  57.7 1.4 %shard_map.72 = (f32[640,512]{1,0:T(8,128)S(1)}, f32[640,512]{1,0:T(8,128)S(1)}, f32[4,256,256]{2,1,0:T(8,128)S(1)}) custom-call(bf16[640,2048]{1,0:T(8,128)(2,1)S(1)} %get-tuple-element.33.refs_0_.refs_3_, bf16[640,2048]{1,0:T(8,128)(2,1)S(1)} %get-tuple-element.34.refs_1_.refs_4_, ...), custom_call_target="tpu_custom_call", output_to_operand_aliasing={{0}: (6, {}), {1}: (7, {}), {2}: (8, {})} | custom-call | flops 1207959552 | bytes 2359296 | tf_op jit(solution)/shard_map/pallas_call | solution.py:202
  59.1 0.6 collective-permute-start.3
  59.7 1.4 %shard_map.69 = (f32[640,512]{1,0:T(8,128)S(1)}, f32[640,512]{1,0:T(8,128)S(1)}, f32[4,256,256]{2,1,0:T(8,128)S(1)}) custom-call(bf16[640,2048]{1,0:T(8,128)(2,1)S(1)} %get-tuple-element.31.refs_0_.refs_1_, bf16[640,2048]{1,0:T(8,128)(2,1)S(1)} %get-tuple-element.32.refs_1_.refs_2_, ...), custom_call_target="tpu_custom_call", output_to_operand_aliasing={{0}: (6, {}), {1}: (7, {}), {2}: (8, {})} | custom-call | flops 1207959552 | bytes 2359296 | tf_op jit(solution)/shard_map/pallas_call | solution.py:202
  61.1 0.1 collective-permute-start.33
  61.2 0.5 collective-permute-start.31
  61.7 1.4 %shard_map.73 = (f32[640,512]{1,0:T(8,128)S(1)}, f32[640,512]{1,0:T(8,128)S(1)}, f32[4,256,256]{2,1,0:T(8,128)S(1)}) custom-call(bf16[640,2048]{1,0:T(8,128)(2,1)S(1)} %get-tuple-element.33.refs_0_.refs_3_, bf16[640,2048]{1,0:T(8,128)(2,1)S(1)} %get-tuple-element.34.refs_1_.refs_4_, ...), custom_call_target="tpu_custom_call", output_to_operand_aliasing={{0}: (6, {}), {1}: (7, {}), {2}: (8, {})} | custom-call | flops 1207959552 | bytes 2359296 | tf_op jit(solution)/shard_map/pallas_call | solution.py:202
  63.1 1.9 %collective-permute-done.3.refs_5_ = bf16[2,128,256]{2,1,0:T(8,128)(2,1)S(1)} collective-permute-done((bf16[2,128,256]{2,1,0:T(8,128)(2,1)S(1)}, bf16[2,128,256]{2,1,0:T(8,128)(2,1)S(1)}, u32[]{:S(2)}, u32[]{:S(2)}) %collective-permute-start.3) | collective-permute-done | bytes 131104 | tf_op jit(solution)/shard_map/ppermute | solution.py:323
  65.1 0.5 collective-permute-start.4
  65.6 1.4 %shard_map.70 = (f32[640,512]{1,0:T(8,128)S(1)}, f32[640,512]{1,0:T(8,128)S(1)}, f32[4,256,256]{2,1,0:T(8,128)S(1)}) custom-call(bf16[640,2048]{1,0:T(8,128)(2,1)S(1)} %get-tuple-element.31.refs_0_.refs_1_, bf16[640,2048]{1,0:T(8,128)(2,1)S(1)} %get-tuple-element.32.refs_1_.refs_2_, ...), custom_call_target="tpu_custom_call", output_to_operand_aliasing={{0}: (6, {}), {1}: (7, {}), {2}: (8, {})} | custom-call | flops 1207959552 | bytes 2359296 | tf_op jit(solution)/shard_map/pallas_call | solution.py:202
  67.0 1.9 %shard_map.74.refs_15_ = f32[64,640]{1,0:T(8,128)} custom-call(s32[8,128]{1,0:T(8,128)S(1)} %get-tuple-element.30.refs_0_, bf16[640,2048]{1,0:T(8,128)(2,1)S(1)} %get-tuple-element.31.refs_0_.refs_1_, bf16[640,2048]{1,0:T(8,128)(2,1)S(1)} %get-tuple-element.32.refs_1_.refs_2_, bf16[640,2048]{1,0:T(8,128)(2,1)S(1)} %get-tuple-element.33.refs_0_.refs_3_, ...), custom_call_target="tpu_custom_call" | custom-call | flops 335544320 | bytes 655360 | tf_op jit(solution)/shard_map/pallas_call | solution.py:286
  68.9 1.9 %shard_map.75 = f32[64,640]{1,0:T(8,128)} custom-call(s32[8,128]{1,0:T(8,128)S(1)} %get-tuple-element.30.refs_0_, bf16[640,2048]{1,0:T(8,128)(2,1)S(1)} %get-tuple-element.31.refs_0_.refs_1_, bf16[640,2048]{1,0:T(8,128)(2,1)S(1)} %get-tuple-element.32.refs_1_.refs_2_, ...), custom_call_target="tpu_custom_call", output_to_operand_aliasing={{}: (15, {})} | custom-call | flops 335544320 | bytes 655360 | tf_op jit(solution)/shard_map/pallas_call | solution.py:286
  (34 shorter events, 0.1 us)
Async XLA Ops:
  1.4 11.9 %collective-permute-start.18 = (bf16[2,128,512]{2,1,0:T(8,128)(2,1)S(1)}, bf16[2,128,512]{2,1,0:T(8,128)(2,1)S(1)}, u32[]{:S(2)}, u32[]{:S(2)}) collective-permute-start(bf16[2,128,512]{2,1,0:T(8,128)(2,1)S(1)} %shard_map.67.refs_2_), channel_id=1, source_target_pairs={{0,4},{1,5},{2,6},{3,7},{4,8},{5,9},{6,10},{7,11},{8,12},{9,13},{1... | collective-permute-start | bytes 786440 | tf_op jit(solution)/shard_map/ppermute | solution.py:323
  4.6 8.8 %collective-permute-start.5 = (bf16[2,128,512]{2,1,0:T(8,128)(2,1)S(1)}, bf16[2,128,512]{2,1,0:T(8,128)(2,1)S(1)}, u32[]{:S(2)}, u32[]{:S(2)}) collective-permute-start(bf16[2,128,512]{2,1,0:T(8,128)(2,1)S(1)} %shard_map.67.refs_2_), channel_id=1, source_target_pairs={{0,2},{1,3},{2,0},{3,1},{4,6},{5,7},{6,4},{7,5},{8,10},{9,11},{10,... | collective-permute-start | bytes 786440 | tf_op jit(solution)/shard_map/ppermute | solution.py:323
  6.0 7.8 %collective-permute-start.27 = (bf16[2,128,512]{2,1,0:T(8,128)(2,1)S(1)}, bf16[2,128,512]{2,1,0:T(8,128)(2,1)S(1)}, u32[]{:S(2)}, u32[]{:S(2)}) collective-permute-start(bf16[2,128,512]{2,1,0:T(8,128)(2,1)S(1)} %shard_map.67.refs_2_), channel_id=1, source_target_pairs={{0,1},{1,0},{2,3},{3,2},{4,5},{5,4},{6,7},{7,6},{8,9},{9,8},{10,11... | collective-permute-start | bytes 786440 | tf_op jit(solution)/shard_map/ppermute | solution.py:323
  7.5 11.0 %collective-permute-start = (bf16[2,128,512]{2,1,0:T(8,128)(2,1)S(1)}, bf16[2,128,512]{2,1,0:T(8,128)(2,1)S(1)}, u32[]{:S(2)}, u32[]{:S(2)}) collective-permute-start(bf16[2,128,512]{2,1,0:T(8,128)(2,1)S(1)} %shard_map.66.refs_2_), channel_id=1, source_target_pairs={{0,4},{1,5},{2,6},{3,7},{4,8},{5,9},{6,10},{7,11},{8,12},{9,13},{1... | collective-permute-start | bytes 786440 | tf_op jit(solution)/shard_map/ppermute | solution.py:323
  9.1 9.4 %collective-permute-start.15 = (bf16[2,128,512]{2,1,0:T(8,128)(2,1)S(1)}, bf16[2,128,512]{2,1,0:T(8,128)(2,1)S(1)}, u32[]{:S(2)}, u32[]{:S(2)}) collective-permute-start(bf16[2,128,512]{2,1,0:T(8,128)(2,1)S(1)} %shard_map.66.refs_2_), channel_id=1, source_target_pairs={{0,2},{1,3},{2,0},{3,1},{4,6},{5,7},{6,4},{7,5},{8,10},{9,11},{10,... | collective-permute-start | bytes 786440 | tf_op jit(solution)/shard_map/ppermute | solution.py:323
  13.3 6.7 %collective-permute-start.14 = (bf16[2,128,512]{2,1,0:T(8,128)(2,1)S(1)}, bf16[2,128,512]{2,1,0:T(8,128)(2,1)S(1)}, u32[]{:S(2)}, u32[]{:S(2)}) collective-permute-start(bf16[2,128,512]{2,1,0:T(8,128)(2,1)S(1)} %shard_map.66.refs_2_), channel_id=1, source_target_pairs={{0,1},{1,0},{2,3},{3,2},{4,5},{5,4},{6,7},{7,6},{8,9},{9,8},{10,11... | collective-permute-start | bytes 786440 | tf_op jit(solution)/shard_map/ppermute | solution.py:323
  13.3 6.7 %collective-permute-start.29 = (bf16[2,128,512]{2,1,0:T(8,128)(2,1)S(1)}, bf16[2,128,512]{2,1,0:T(8,128)(2,1)S(1)}, u32[]{:S(2)}, u32[]{:S(2)}) collective-permute-start(bf16[2,128,512]{2,1,0:T(8,128)(2,1)S(1)} %collective-permute-done.18.refs_6_), channel_id=1, source_target_pairs={{0,1},{1,0},{2,3},{3,2},{4,5},{5,4},{6,7},{7,6},{8,9},{9,8},{10,11... | collective-permute-start | bytes 786440 | tf_op jit(solution)/shard_map/ppermute | solution.py:323
  13.8 7.5 %collective-permute-start.28 = (bf16[2,128,512]{2,1,0:T(8,128)(2,1)S(1)}, bf16[2,128,512]{2,1,0:T(8,128)(2,1)S(1)}, u32[]{:S(2)}, u32[]{:S(2)}) collective-permute-start(bf16[2,128,512]{2,1,0:T(8,128)(2,1)S(1)} %collective-permute-done.5.refs_4_), channel_id=1, source_target_pairs={{0,1},{1,0},{2,3},{3,2},{4,5},{5,4},{6,7},{7,6},{8,9},{9,8},{10,11... | collective-permute-start | bytes 786440 | tf_op jit(solution)/shard_map/ppermute | solution.py:323
  18.5 11.0 %collective-permute-start.19 = (bf16[2,128,512]{2,1,0:T(8,128)(2,1)S(1)}, bf16[2,128,512]{2,1,0:T(8,128)(2,1)S(1)}, u32[]{:S(2)}, u32[]{:S(2)}) collective-permute-start(bf16[2,128,512]{2,1,0:T(8,128)(2,1)S(1)} %collective-permute-done.18.refs_6_), channel_id=1, source_target_pairs={{0,4},{1,5},{2,6},{3,7},{4,8},{5,9},{6,10},{7,11},{8,12},{9,13},{1... | collective-permute-start | bytes 786440 | tf_op jit(solution)/shard_map/ppermute | solution.py:323
  18.5 12.5 %collective-permute-start.24 = (bf16[2,128,512]{2,1,0:T(8,128)(2,1)S(1)}, bf16[2,128,512]{2,1,0:T(8,128)(2,1)S(1)}, u32[]{:S(2)}, u32[]{:S(2)}) collective-permute-start(bf16[2,128,512]{2,1,0:T(8,128)(2,1)S(1)} %collective-permute-done.18.refs_6_), channel_id=1, source_target_pairs={{0,2},{1,3},{2,0},{3,1},{4,6},{5,7},{6,4},{7,5},{8,10},{9,11},{10,... | collective-permute-start | bytes 786440 | tf_op jit(solution)/shard_map/ppermute | solution.py:323
  20.0 11.0 %collective-permute-start.17 = (bf16[2,128,512]{2,1,0:T(8,128)(2,1)S(1)}, bf16[2,128,512]{2,1,0:T(8,128)(2,1)S(1)}, u32[]{:S(2)}, u32[]{:S(2)}) collective-permute-start(bf16[2,128,512]{2,1,0:T(8,128)(2,1)S(1)} %collective-permute-done.refs_6_), channel_id=1, source_target_pairs={{0,1},{1,0},{2,3},{3,2},{4,5},{5,4},{6,7},{7,6},{8,9},{9,8},{10,11... | collective-permute-start | bytes 786440 | tf_op jit(solution)/shard_map/ppermute | solution.py:323
  20.0 13.8 %collective-permute-start.1 = (bf16[2,128,512]{2,1,0:T(8,128)(2,1)S(1)}, bf16[2,128,512]{2,1,0:T(8,128)(2,1)S(1)}, u32[]{:S(2)}, u32[]{:S(2)}) collective-permute-start(bf16[2,128,512]{2,1,0:T(8,128)(2,1)S(1)} %collective-permute-done.refs_6_), channel_id=1, source_target_pairs={{0,4},{1,5},{2,6},{3,7},{4,8},{5,9},{6,10},{7,11},{8,12},{9,13},{1... | collective-permute-start | bytes 786440 | tf_op jit(solution)/shard_map/ppermute | solution.py:323
  21.4 18.3 %collective-permute-start.16 = (bf16[2,128,512]{2,1,0:T(8,128)(2,1)S(1)}, bf16[2,128,512]{2,1,0:T(8,128)(2,1)S(1)}, u32[]{:S(2)}, u32[]{:S(2)}) collective-permute-start(bf16[2,128,512]{2,1,0:T(8,128)(2,1)S(1)} %collective-permute-done.15.refs_4_), channel_id=1, source_target_pairs={{0,1},{1,0},{2,3},{3,2},{4,5},{5,4},{6,7},{7,6},{8,9},{9,8},{10,11... | collective-permute-start | bytes 786440 | tf_op jit(solution)/shard_map/ppermute | solution.py:323
  29.5 11.1 %collective-permute-start.11 = (bf16[2,128,512]{2,1,0:T(8,128)(2,1)S(1)}, bf16[2,128,512]{2,1,0:T(8,128)(2,1)S(1)}, u32[]{:S(2)}, u32[]{:S(2)}) collective-permute-start(bf16[2,128,512]{2,1,0:T(8,128)(2,1)S(1)} %collective-permute-done.refs_6_), channel_id=1, source_target_pairs={{0,2},{1,3},{2,0},{3,1},{4,6},{5,7},{6,4},{7,5},{8,10},{9,11},{10,... | collective-permute-start | bytes 786440 | tf_op jit(solution)/shard_map/ppermute | solution.py:323
  31.0 9.6 %collective-permute-start.26 = (bf16[2,128,512]{2,1,0:T(8,128)(2,1)S(1)}, bf16[2,128,512]{2,1,0:T(8,128)(2,1)S(1)}, u32[]{:S(2)}, u32[]{:S(2)}) collective-permute-start(bf16[2,128,512]{2,1,0:T(8,128)(2,1)S(1)} %collective-permute-done.19.refs_4_), channel_id=1, source_target_pairs={{0,1},{1,0},{2,3},{3,2},{4,5},{5,4},{6,7},{7,6},{8,9},{9,8},{10,11... | collective-permute-start | bytes 786440 | tf_op jit(solution)/shard_map/ppermute | solution.py:323
  31.0 9.7 %collective-permute-start.25 = (bf16[2,128,512]{2,1,0:T(8,128)(2,1)S(1)}, bf16[2,128,512]{2,1,0:T(8,128)(2,1)S(1)}, u32[]{:S(2)}, u32[]{:S(2)}) collective-permute-start(bf16[2,128,512]{2,1,0:T(8,128)(2,1)S(1)} %collective-permute-done.24.refs_2_), channel_id=1, source_target_pairs={{0,1},{1,0},{2,3},{3,2},{4,5},{5,4},{6,7},{7,6},{8,9},{9,8},{10,11... | collective-permute-start | bytes 786440 | tf_op jit(solution)/shard_map/ppermute | solution.py:323
  33.8 8.8 %collective-permute-start.2 = (bf16[2,128,512]{2,1,0:T(8,128)(2,1)S(1)}, bf16[2,128,512]{2,1,0:T(8,128)(2,1)S(1)}, u32[]{:S(2)}, u32[]{:S(2)}) collective-permute-start(bf16[2,128,512]{2,1,0:T(8,128)(2,1)S(1)} %collective-permute-done.1.refs_4_), channel_id=1, source_target_pairs={{0,4},{1,5},{2,6},{3,7},{4,8},{5,9},{6,10},{7,11},{8,12},{9,13},{1... | collective-permute-start | bytes 786440 | tf_op jit(solution)/shard_map/ppermute | solution.py:323
  39.6 9.2 %collective-permute-start.20 = (bf16[2,128,512]{2,1,0:T(8,128)(2,1)S(1)}, bf16[2,128,512]{2,1,0:T(8,128)(2,1)S(1)}, u32[]{:S(2)}, u32[]{:S(2)}) collective-permute-start(bf16[2,128,512]{2,1,0:T(8,128)(2,1)S(1)} %collective-permute-done.19.refs_4_), channel_id=1, source_target_pairs={{0,2},{1,3},{2,0},{3,1},{4,6},{5,7},{6,4},{7,5},{8,10},{9,11},{10,... | collective-permute-start | bytes 786440 | tf_op jit(solution)/shard_map/ppermute | solution.py:323
  40.5 12.1 %collective-permute-start.22 = (bf16[2,128,512]{2,1,0:T(8,128)(2,1)S(1)}, bf16[2,128,512]{2,1,0:T(8,128)(2,1)S(1)}, u32[]{:S(2)}, u32[]{:S(2)}) collective-permute-start(bf16[2,128,512]{2,1,0:T(8,128)(2,1)S(1)} %collective-permute-done.19.refs_4_), channel_id=1, source_target_pairs={{0,4},{1,5},{2,6},{3,7},{4,8},{5,9},{6,10},{7,11},{8,12},{9,13},{1... | collective-permute-start | bytes 786440 | tf_op jit(solution)/shard_map/ppermute | solution.py:323
  40.6 12.2 %collective-permute-start.13 = (bf16[2,128,512]{2,1,0:T(8,128)(2,1)S(1)}, bf16[2,128,512]{2,1,0:T(8,128)(2,1)S(1)}, u32[]{:S(2)}, u32[]{:S(2)}) collective-permute-start(bf16[2,128,512]{2,1,0:T(8,128)(2,1)S(1)} %collective-permute-done.1.refs_4_), channel_id=1, source_target_pairs={{0,1},{1,0},{2,3},{3,2},{4,5},{5,4},{6,7},{7,6},{8,9},{9,8},{10,11... | collective-permute-start | bytes 786440 | tf_op jit(solution)/shard_map/ppermute | solution.py:323
  40.6 13.1 %collective-permute-start.8 = (bf16[2,128,512]{2,1,0:T(8,128)(2,1)S(1)}, bf16[2,128,512]{2,1,0:T(8,128)(2,1)S(1)}, u32[]{:S(2)}, u32[]{:S(2)}) collective-permute-start(bf16[2,128,512]{2,1,0:T(8,128)(2,1)S(1)} %collective-permute-done.1.refs_4_), channel_id=1, source_target_pairs={{0,2},{1,3},{2,0},{3,1},{4,6},{5,7},{6,4},{7,5},{8,10},{9,11},{10,... | collective-permute-start | bytes 786440 | tf_op jit(solution)/shard_map/ppermute | solution.py:323
  42.6 10.3 %collective-permute-start.12 = (bf16[2,128,512]{2,1,0:T(8,128)(2,1)S(1)}, bf16[2,128,512]{2,1,0:T(8,128)(2,1)S(1)}, u32[]{:S(2)}, u32[]{:S(2)}) collective-permute-start(bf16[2,128,512]{2,1,0:T(8,128)(2,1)S(1)} %collective-permute-done.11.refs_2_), channel_id=1, source_target_pairs={{0,1},{1,0},{2,3},{3,2},{4,5},{5,4},{6,7},{7,6},{8,9},{9,8},{10,11... | collective-permute-start | bytes 786440 | tf_op jit(solution)/shard_map/ppermute | solution.py:323
  48.9 6.6 %collective-permute-start.32 = (bf16[2,128,256]{2,1,0:T(8,128)(2,1)S(1)}, bf16[2,128,256]{2,1,0:T(8,128)(2,1)S(1)}, u32[]{:S(2)}, u32[]{:S(2)}) collective-permute-start(bf16[2,128,256]{2,1,0:T(8,128)(2,1)S(1)} %get-tuple-element.54), channel_id=1, source_target_pairs={{0,12},{1,13},{2,14},{3,15},{4,0},{5,1},{6,2},{7,3},{8,4},{9,5},{1... | collective-permute-start | bytes 393224 | tf_op jit(solution)/shard_map/ppermute | solution.py:323
  52.7 5.0 %collective-permute-start.30 = (bf16[2,128,256]{2,1,0:T(8,128)(2,1)S(1)}, bf16[2,128,256]{2,1,0:T(8,128)(2,1)S(1)}, u32[]{:S(2)}, u32[]{:S(2)}) collective-permute-start(bf16[2,128,256]{2,1,0:T(8,128)(2,1)S(1)} %get-tuple-element.57), channel_id=1, source_target_pairs={{0,2},{1,3},{2,0},{3,1},{4,6},{5,7},{6,4},{7,5},{8,10},{9,11},{10,... | collective-permute-start | bytes 393224 | tf_op jit(solution)/shard_map/ppermute | solution.py:323
  52.8 6.3 %collective-permute-start.6 = (bf16[2,128,256]{2,1,0:T(8,128)(2,1)S(1)}, bf16[2,128,256]{2,1,0:T(8,128)(2,1)S(1)}, u32[]{:S(2)}, u32[]{:S(2)}) collective-permute-start(bf16[2,128,256]{2,1,0:T(8,128)(2,1)S(1)} %get-tuple-element.35), channel_id=1, source_target_pairs={{0,12},{1,13},{2,14},{3,15},{4,0},{5,1},{6,2},{7,3},{8,4},{9,5},{1... | collective-permute-start | bytes 393224 | tf_op jit(solution)/shard_map/ppermute | solution.py:323
  53.0 8.2 %collective-permute-start.21 = (bf16[2,128,512]{2,1,0:T(8,128)(2,1)S(1)}, bf16[2,128,512]{2,1,0:T(8,128)(2,1)S(1)}, u32[]{:S(2)}, u32[]{:S(2)}) collective-permute-start(bf16[2,128,512]{2,1,0:T(8,128)(2,1)S(1)} %collective-permute-done.20.refs_2_), channel_id=1, source_target_pairs={{0,1},{1,0},{2,3},{3,2},{4,5},{5,4},{6,7},{7,6},{8,9},{9,8},{10,11... | collective-permute-start | bytes 786440 | tf_op jit(solution)/shard_map/ppermute | solution.py:323
  53.7 7.5 %collective-permute-start.23 = (bf16[2,128,512]{2,1,0:T(8,128)(2,1)S(1)}, bf16[2,128,512]{2,1,0:T(8,128)(2,1)S(1)}, u32[]{:S(2)}, u32[]{:S(2)}) collective-permute-start(bf16[2,128,512]{2,1,0:T(8,128)(2,1)S(1)} %collective-permute-done.22.refs_4_), channel_id=1, source_target_pairs={{0,1},{1,0},{2,3},{3,2},{4,5},{5,4},{6,7},{7,6},{8,9},{9,8},{10,11... | collective-permute-start | bytes 786440 | tf_op jit(solution)/shard_map/ppermute | solution.py:323
  55.5 9.6 %collective-permute-start.10 = (bf16[2,128,512]{2,1,0:T(8,128)(2,1)S(1)}, bf16[2,128,512]{2,1,0:T(8,128)(2,1)S(1)}, u32[]{:S(2)}, u32[]{:S(2)}) collective-permute-start(bf16[2,128,512]{2,1,0:T(8,128)(2,1)S(1)} %collective-permute-done.2.refs_4_), channel_id=1, source_target_pairs={{0,1},{1,0},{2,3},{3,2},{4,5},{5,4},{6,7},{7,6},{8,9},{9,8},{10,11... | collective-permute-start | bytes 786440 | tf_op jit(solution)/shard_map/ppermute | solution.py:323
  57.7 7.9 %collective-permute-start.9 = (bf16[2,128,512]{2,1,0:T(8,128)(2,1)S(1)}, bf16[2,128,512]{2,1,0:T(8,128)(2,1)S(1)}, u32[]{:S(2)}, u32[]{:S(2)}) collective-permute-start(bf16[2,128,512]{2,1,0:T(8,128)(2,1)S(1)} %collective-permute-done.8.refs_2_), channel_id=1, source_target_pairs={{0,1},{1,0},{2,3},{3,2},{4,5},{5,4},{6,7},{7,6},{8,9},{9,8},{10,11... | collective-permute-start | bytes 786440 | tf_op jit(solution)/shard_map/ppermute | solution.py:323
  59.1 6.0 %collective-permute-start.3 = (bf16[2,128,256]{2,1,0:T(8,128)(2,1)S(1)}, bf16[2,128,256]{2,1,0:T(8,128)(2,1)S(1)}, u32[]{:S(2)}, u32[]{:S(2)}) collective-permute-start(bf16[2,128,256]{2,1,0:T(8,128)(2,1)S(1)} %get-tuple-element.58), channel_id=1, source_target_pairs={{0,2},{1,3},{2,0},{3,1},{4,6},{5,7},{6,4},{7,5},{8,10},{9,11},{10,... | collective-permute-start | bytes 393224 | tf_op jit(solution)/shard_map/ppermute | solution.py:323
  61.1 5.9 %collective-permute-start.33 = (bf16[2,128,256]{2,1,0:T(8,128)(2,1)S(1)}, bf16[2,128,256]{2,1,0:T(8,128)(2,1)S(1)}, u32[]{:S(2)}, u32[]{:S(2)}) collective-permute-start(bf16[2,128,256]{2,1,0:T(8,128)(2,1)S(1)} %collective-permute-done.32.refs_7_), channel_id=1, source_target_pairs={{0,1},{1,0},{2,3},{3,2},{4,5},{5,4},{6,7},{7,6},{8,9},{9,8},{10,11... | collective-permute-start | bytes 393224 | tf_op jit(solution)/shard_map/ppermute | solution.py:323
  61.2 5.8 %collective-permute-start.31 = (bf16[2,128,256]{2,1,0:T(8,128)(2,1)S(1)}, bf16[2,128,256]{2,1,0:T(8,128)(2,1)S(1)}, u32[]{:S(2)}, u32[]{:S(2)}) collective-permute-start(bf16[2,128,256]{2,1,0:T(8,128)(2,1)S(1)} %collective-permute-done.30.refs_5_), channel_id=1, source_target_pairs={{0,1},{1,0},{2,3},{3,2},{4,5},{5,4},{6,7},{7,6},{8,9},{9,8},{10,11... | collective-permute-start | bytes 393224 | tf_op jit(solution)/shard_map/ppermute | solution.py:323
  65.1 3.8 %collective-permute-start.7 = (bf16[2,128,256]{2,1,0:T(8,128)(2,1)S(1)}, bf16[2,128,256]{2,1,0:T(8,128)(2,1)S(1)}, u32[]{:S(2)}, u32[]{:S(2)}) collective-permute-start(bf16[2,128,256]{2,1,0:T(8,128)(2,1)S(1)} %collective-permute-done.6.refs_7_), channel_id=1, source_target_pairs={{0,1},{1,0},{2,3},{3,2},{4,5},{5,4},{6,7},{7,6},{8,9},{9,8},{10,11... | collective-permute-start | bytes 393224 | tf_op jit(solution)/shard_map/ppermute | solution.py:323
  65.1 3.9 %collective-permute-start.4 = (bf16[2,128,256]{2,1,0:T(8,128)(2,1)S(1)}, bf16[2,128,256]{2,1,0:T(8,128)(2,1)S(1)}, u32[]{:S(2)}, u32[]{:S(2)}) collective-permute-start(bf16[2,128,256]{2,1,0:T(8,128)(2,1)S(1)} %collective-permute-done.3.refs_5_), channel_id=1, source_target_pairs={{0,1},{1,0},{2,3},{3,2},{4,5},{5,4},{6,7},{7,6},{8,9},{9,8},{10,11... | collective-permute-start | bytes 393224 | tf_op jit(solution)/shard_map/ppermute | solution.py:323

commit v10 on v8

--- a/solution.py
+++ b/solution.py
@@ -60,17 +60,18 @@
         copy.start()
     named.wait()
     lane = lax.broadcasted_iota(jnp.int32, (rows, LANES), 1) // width
+    for copy in copies:
+        copy.wait()
     for s in range(2):
-        copies[s].wait()
         for chunk in range(columns // LANES):
             total = None
             for k in range(per):
                 stored = ids_ref[layer, chunk * per + k]
                 start = pl.multiple_of((stored // per) * LANES, LANES)
-                part = held[s, :, pl.ds(start, LANES)].astype(jnp.float32)
+                part = held[s, :, pl.ds(start, LANES)]
                 part = pltpu.roll(part, lax.rem(k - stored % per + per, per) * width, 1)
                 total = part if total is None else jnp.where(lane == k, part, total)
-            out_ref[s, :, chunk * LANES : (chunk + 1) * LANES] = total.astype(jnp.bfloat16)
+            out_ref[s, :, chunk * LANES : (chunk + 1) * LANES] = total
 
 
 def in_hbm(*arrays):

time: 68.1 us -> 68.1 us (level)
  no operation moved by 1% of the time
where the time goes in v10:
time: 68.1 us; the launch traced here: 67.9 us
  waiting for transfers between devices  25.9 us (38%)
  starting transfers between devices  21 us (31%)
  Pallas kernels  20.2 us (30%)
  between operations  0.83 us (1%)
    ppermute x30, waiting for transfers between devices, move(): return lax.ppermute(value, 'tok', steps)  25.9 us
    ppermute x30, starting transfers between devices, move(): return lax.ppermute(value, 'tok', steps)  21 us
    pallas_call x7, Pallas kernels, stage(): pl.pallas_call(functools.partial(stage_kernel, cfg), out_shape=out_shape,...  12.2 us
    pallas_call x2, Pallas kernels, load(): pl.pallas_call(functools.partial(load_kernel, layer), out_shape=tuple(out...  5.1 us
    pallas_call x2, Pallas kernels, pick(): pl.pallas_call(functools.partial(pick_kernel, layer), out_shape=jax.Shape...  2.87 us
  transfers between devices with their start and end apart: 30, of which 8 were waited for; matrix products, arithmetic and copies ran while one was open for 0% of the time, Pallas kernels for 23%

profile of v10, /device:TPU:0, one launch (start us, length us, event | category | flops | bytes accessed | tf_op | source)
XLA Modules:
  0.0 67.9 jit_solution(3327757502908672841)
XLA Ops:
  0.0 1.4 %shard_map.67.refs_2_ = bf16[2,128,512]{2,1,0:T(8,128)(2,1)S(1)} custom-call(s32[2,16]{1,0:T(2,128)} %ids_hbm.3, bf16[2,128,1024]{2,1,0:T(8,128)(2,1)} %u_ref.3, bf16[2,128,1024]{2,1,0:T(8,128)(2,1)} %v_ref.3), custom_call_target="tpu_custom_call" | custom-call | flops 262144 | bytes 786432 | tf_op jit(solution)/shard_map/pallas_call | solution.py:85
  1.4 3.1 %collective-permute-start.18 = (bf16[2,128,512]{2,1,0:T(8,128)(2,1)S(1)}, bf16[2,128,512]{2,1,0:T(8,128)(2,1)S(1)}, u32[]{:S(2)}, u32[]{:S(2)}) collective-permute-start(bf16[2,128,512]{2,1,0:T(8,128)(2,1)S(1)} %shard_map.67.refs_2_), channel_id=1, source_target_pairs={{0,4},{1,5},{2,6},{3,7},{4,8},{5,9},{6,10},{7,11},{8,12},{9,13},{1... | collective-permute-start | bytes 786440 | tf_op jit(solution)/shard_map/ppermute | solution.py:296
  4.5 1.5 %collective-permute-start.5 = (bf16[2,128,512]{2,1,0:T(8,128)(2,1)S(1)}, bf16[2,128,512]{2,1,0:T(8,128)(2,1)S(1)}, u32[]{:S(2)}, u32[]{:S(2)}) collective-permute-start(bf16[2,128,512]{2,1,0:T(8,128)(2,1)S(1)} %shard_map.67.refs_2_), channel_id=1, source_target_pairs={{0,2},{1,3},{2,0},{3,1},{4,6},{5,7},{6,4},{7,5},{8,10},{9,11},{10,... | collective-permute-start | bytes 786440 | tf_op jit(solution)/shard_map/ppermute | solution.py:296
  6.0 0.0 collective-permute-start.27
  6.0 1.4 %shard_map.66.refs_2_ = bf16[2,128,512]{2,1,0:T(8,128)(2,1)S(1)} custom-call(s32[2,16]{1,0:T(2,128)} %ids_hbm.3, bf16[2,128,1024]{2,1,0:T(8,128)(2,1)} %u_ref.3, bf16[2,128,1024]{2,1,0:T(8,128)(2,1)} %v_ref.3), custom_call_target="tpu_custom_call" | custom-call | flops 262144 | bytes 786432 | tf_op jit(solution)/shard_map/pallas_call | solution.py:85
  7.5 1.6 %collective-permute-start = (bf16[2,128,512]{2,1,0:T(8,128)(2,1)S(1)}, bf16[2,128,512]{2,1,0:T(8,128)(2,1)S(1)}, u32[]{:S(2)}, u32[]{:S(2)}) collective-permute-start(bf16[2,128,512]{2,1,0:T(8,128)(2,1)S(1)} %shard_map.66.refs_2_), channel_id=1, source_target_pairs={{0,4},{1,5},{2,6},{3,7},{4,8},{5,9},{6,10},{7,11},{8,12},{9,13},{1... | collective-permute-start | bytes 786440 | tf_op jit(solution)/shard_map/ppermute | solution.py:296
  9.1 0.5 collective-permute-start.15
  9.6 3.7 %collective-permute-done.18.refs_6_ = bf16[2,128,512]{2,1,0:T(8,128)(2,1)S(1)} collective-permute-done((bf16[2,128,512]{2,1,0:T(8,128)(2,1)S(1)}, bf16[2,128,512]{2,1,0:T(8,128)(2,1)S(1)}, u32[]{:S(2)}, u32[]{:S(2)}) %collective-permute-start.18) | collective-permute-done | bytes 262176 | tf_op jit(solution)/shard_map/ppermute | solution.py:296
  13.3 0.0 collective-permute-start.14
  13.3 0.0 collective-permute-done.5.refs_4_
  13.3 0.5 collective-permute-start.29
  13.8 0.0 collective-permute-done.27.refs_3_
  13.8 0.1 collective-permute-start.28
  13.9 4.6 %collective-permute-done.refs_6_ = bf16[2,128,512]{2,1,0:T(8,128)(2,1)S(1)} collective-permute-done((bf16[2,128,512]{2,1,0:T(8,128)(2,1)S(1)}, bf16[2,128,512]{2,1,0:T(8,128)(2,1)S(1)}, u32[]{:S(2)}, u32[]{:S(2)}) %collective-permute-start) | collective-permute-done | bytes 262176 | tf_op jit(solution)/shard_map/ppermute | solution.py:296
  18.5 1.5 %collective-permute-start.24 = (bf16[2,128,512]{2,1,0:T(8,128)(2,1)S(1)}, bf16[2,128,512]{2,1,0:T(8,128)(2,1)S(1)}, u32[]{:S(2)}, u32[]{:S(2)}) collective-permute-start(bf16[2,128,512]{2,1,0:T(8,128)(2,1)S(1)} %collective-permute-done.18.refs_6_), channel_id=1, source_target_pairs={{0,2},{1,3},{2,0},{3,1},{4,6},{5,7},{6,4},{7,5},{8,10},{9,11},{10,... | collective-permute-start | bytes 786440 | tf_op jit(solution)/shard_map/ppermute | solution.py:296
  20.0 0.0 collective-permute-start.17
  20.0 0.0 collective-permute-done.29.refs_7_
  20.0 0.5 collective-permute-start.16
  20.5 1.3 %collective-permute-start.1 = (bf16[2,128,512]{2,1,0:T(8,128)(2,1)S(1)}, bf16[2,128,512]{2,1,0:T(8,128)(2,1)S(1)}, u32[]{:S(2)}, u32[]{:S(2)}) collective-permute-start(bf16[2,128,512]{2,1,0:T(8,128)(2,1)S(1)} %collective-permute-done.refs_6_), channel_id=1, source_target_pairs={{0,4},{1,5},{2,6},{3,7},{4,8},{5,9},{6,10},{7,11},{8,12},{9,13},{1... | collective-permute-start | bytes 786440 | tf_op jit(solution)/shard_map/ppermute | solution.py:296
  21.8 7.7 %collective-permute-done.19.refs_4_ = bf16[2,128,512]{2,1,0:T(8,128)(2,1)S(1)} collective-permute-done((bf16[2,128,512]{2,1,0:T(8,128)(2,1)S(1)}, bf16[2,128,512]{2,1,0:T(8,128)(2,1)S(1)}, u32[]{:S(2)}, u32[]{:S(2)}) %collective-permute-start.19) | collective-permute-done | bytes 262176 | tf_op jit(solution)/shard_map/ppermute | solution.py:296
  29.5 1.5 %collective-permute-start.11 = (bf16[2,128,512]{2,1,0:T(8,128)(2,1)S(1)}, bf16[2,128,512]{2,1,0:T(8,128)(2,1)S(1)}, u32[]{:S(2)}, u32[]{:S(2)}) collective-permute-start(bf16[2,128,512]{2,1,0:T(8,128)(2,1)S(1)} %collective-permute-done.refs_6_), channel_id=1, source_target_pairs={{0,2},{1,3},{2,0},{3,1},{4,6},{5,7},{6,4},{7,5},{8,10},{9,11},{10,... | collective-permute-start | bytes 786440 | tf_op jit(solution)/shard_map/ppermute | solution.py:296
  31.0 0.0 collective-permute-done.24.refs_2_
  31.0 0.5 collective-permute-start.25
  31.5 0.0 collective-permute-done.16.refs_5_
  31.5 0.5 collective-permute-start.20
  32.0 1.8 %collective-permute-done.1.refs_4_ = bf16[2,128,512]{2,1,0:T(8,128)(2,1)S(1)} collective-permute-done((bf16[2,128,512]{2,1,0:T(8,128)(2,1)S(1)}, bf16[2,128,512]{2,1,0:T(8,128)(2,1)S(1)}, u32[]{:S(2)}, u32[]{:S(2)}) %collective-permute-start.1) | collective-permute-done | bytes 262176 | tf_op jit(solution)/shard_map/ppermute | solution.py:296
  33.8 3.7 %collective-permute-done.11.refs_2_ = bf16[2,128,512]{2,1,0:T(8,128)(2,1)S(1)} collective-permute-done((bf16[2,128,512]{2,1,0:T(8,128)(2,1)S(1)}, bf16[2,128,512]{2,1,0:T(8,128)(2,1)S(1)}, u32[]{:S(2)}, u32[]{:S(2)}) %collective-permute-start.11) | collective-permute-done | bytes 262176 | tf_op jit(solution)/shard_map/ppermute | solution.py:296
  37.5 0.0 collective-permute-start.22
  37.5 0.0 collective-permute-done.26.refs_5_
  37.6 0.5 collective-permute-start.12
  38.7 2.6 %shard_map.65 = (bf16[640,2048]{1,0:T(8,128)(2,1)S(1)}, bf16[640,2048]{1,0:T(8,128)(2,1)S(1)}) custom-call(bf16[2,640,2048]{2,1,0:T(8,128)(2,1)} %refs_0_.2, bf16[2,640,2048]{2,1,0:T(8,128)(2,1)} %refs_1_.3), custom_call_target="tpu_custom_call" | custom-call | tf_op jit(solution)/shard_map/pallas_call | solution.py:121
  41.3 2.6 %shard_map.64 = (s32[8,128]{1,0:T(8,128)S(1)}, bf16[640,2048]{1,0:T(8,128)(2,1)S(1)}, bf16[640,2048]{1,0:T(8,128)(2,1)S(1)}) custom-call(s32[1]{0:T(128)S(6)} %copy.31.refs_0_, bf16[2,640,2048]{2,1,0:T(8,128)(2,1)} %refs_0_.2, bf16[2,640,2048]{2,1,0:T(8,128)(2,1)} %refs_1_.3), custom_call_target="tpu_custom_call" | custom-call | tf_op jit(solution)/shard_map/pallas_call | solution.py:121
  43.8 2.5 %collective-permute-start.8 = (bf16[2,128,512]{2,1,0:T(8,128)(2,1)S(1)}, bf16[2,128,512]{2,1,0:T(8,128)(2,1)S(1)}, u32[]{:S(2)}, u32[]{:S(2)}) collective-permute-start(bf16[2,128,512]{2,1,0:T(8,128)(2,1)S(1)} %collective-permute-done.1.refs_4_), channel_id=1, source_target_pairs={{0,2},{1,3},{2,0},{3,1},{4,6},{5,7},{6,4},{7,5},{8,10},{9,11},{10,... | collective-permute-start | bytes 786440 | tf_op jit(solution)/shard_map/ppermute | solution.py:296
  46.4 1.8 %shard_map.71 = (f32[640,512]{1,0:T(8,128)S(1)}, f32[640,512]{1,0:T(8,128)S(1)}, f32[4,256,256]{2,1,0:T(8,128)S(1)}) custom-call(bf16[640,2048]{1,0:T(8,128)(2,1)S(1)} %get-tuple-element.31.refs_0_.refs_2_, bf16[640,2048]{1,0:T(8,128)(2,1)S(1)} %get-tuple-element.32.refs_1_.refs_3_, bf16[2,128,512]{2,1,0:T(8,128)(2,1)S(1)} %shard_map.67.refs_2_, ...), custom_call_target="tpu_custom_call" | custom-call | flops 1811939328 | bytes 3538944 | tf_op jit(solution)/shard_map/pallas_call | solution.py:265
  48.2 0.1 collective-permute-done.22.refs_4_
  48.2 4.0 %collective-permute-start.6 = (bf16[2,128,512]{2,1,0:T(8,128)(2,1)S(1)}, bf16[2,128,512]{2,1,0:T(8,128)(2,1)S(1)}, u32[]{:S(2)}, u32[]{:S(2)}) collective-permute-start(bf16[2,128,512]{2,1,0:T(8,128)(2,1)S(1)} %collective-permute-done.5.refs_4_), channel_id=1, source_target_pairs={{0,12},{1,13},{2,14},{3,15},{4,0},{5,1},{6,2},{7,3},{8,4},{9,5},{1... | collective-permute-start | bytes 786440 | tf_op jit(solution)/shard_map/ppermute | solution.py:296
  52.2 0.2 collective-permute-start.3
  52.4 0.2 collective-permute-start.23
  52.5 1.8 %shard_map.68 = (f32[640,512]{1,0:T(8,128)S(1)}, f32[640,512]{1,0:T(8,128)S(1)}, f32[4,256,256]{2,1,0:T(8,128)S(1)}) custom-call(bf16[640,2048]{1,0:T(8,128)(2,1)S(1)} %get-tuple-element.29.refs_0_, bf16[640,2048]{1,0:T(8,128)(2,1)S(1)} %get-tuple-element.30.refs_1_, bf16[2,128,512]{2,1,0:T(8,128)(2,1)S(1)} %shard_map.66.refs_2_, ...), custom_call_target="tpu_custom_call" | custom-call | flops 1811939328 | bytes 3538944 | tf_op jit(solution)/shard_map/pallas_call | solution.py:265
  54.3 0.4 collective-permute-start.10
  54.7 0.2 collective-permute-start.9
  54.9 1.4 %shard_map.72 = (f32[640,512]{1,0:T(8,128)S(1)}, f32[640,512]{1,0:T(8,128)S(1)}, f32[4,256,256]{2,1,0:T(8,128)S(1)}) custom-call(bf16[640,2048]{1,0:T(8,128)(2,1)S(1)} %get-tuple-element.31.refs_0_.refs_2_, bf16[640,2048]{1,0:T(8,128)(2,1)S(1)} %get-tuple-element.32.refs_1_.refs_3_, ...), custom_call_target="tpu_custom_call", output_to_operand_aliasing={{0}: (6, {}), {1}: (7, {}), {2}: (8, {})} | custom-call | flops 1207959552 | bytes 2359296 | tf_op jit(solution)/shard_map/pallas_call | solution.py:265
  56.3 2.1 %collective-permute-done.6.refs_7_ = bf16[2,128,512]{2,1,0:T(8,128)(2,1)S(1)} collective-permute-done((bf16[2,128,512]{2,1,0:T(8,128)(2,1)S(1)}, bf16[2,128,512]{2,1,0:T(8,128)(2,1)S(1)}, u32[]{:S(2)}, u32[]{:S(2)}) %collective-permute-start.6) | collective-permute-done | bytes 262176 | tf_op jit(solution)/shard_map/ppermute | solution.py:296
  58.4 2.2 %collective-permute-done.3.refs_5_ = bf16[2,128,512]{2,1,0:T(8,128)(2,1)S(1)} collective-permute-done((bf16[2,128,512]{2,1,0:T(8,128)(2,1)S(1)}, bf16[2,128,512]{2,1,0:T(8,128)(2,1)S(1)}, u32[]{:S(2)}, u32[]{:S(2)}) %collective-permute-start.3) | collective-permute-done | bytes 262176 | tf_op jit(solution)/shard_map/ppermute | solution.py:296
  60.7 1.4 %shard_map.69 = (f32[640,512]{1,0:T(8,128)S(1)}, f32[640,512]{1,0:T(8,128)S(1)}, f32[4,256,256]{2,1,0:T(8,128)S(1)}) custom-call(bf16[640,2048]{1,0:T(8,128)(2,1)S(1)} %get-tuple-element.29.refs_0_, bf16[640,2048]{1,0:T(8,128)(2,1)S(1)} %get-tuple-element.30.refs_1_, ...), custom_call_target="tpu_custom_call", output_to_operand_aliasing={{0}: (6, {}), {1}: (7, {}), {2}: (8, {})} | custom-call | flops 1207959552 | bytes 2359296 | tf_op jit(solution)/shard_map/pallas_call | solution.py:265
  62.1 1.4 %shard_map.73 = (f32[640,512]{1,0:T(8,128)S(1)}, f32[640,512]{1,0:T(8,128)S(1)}, f32[4,256,256]{2,1,0:T(8,128)S(1)}) custom-call(bf16[640,2048]{1,0:T(8,128)(2,1)S(1)} %get-tuple-element.31.refs_0_.refs_2_, bf16[640,2048]{1,0:T(8,128)(2,1)S(1)} %get-tuple-element.32.refs_1_.refs_3_, ...), custom_call_target="tpu_custom_call", output_to_operand_aliasing={{0}: (6, {}), {1}: (7, {}), {2}: (8, {})} | custom-call | flops 1207959552 | bytes 2359296 | tf_op jit(solution)/shard_map/pallas_call | solution.py:265
  63.5 1.4 %shard_map.70 = (f32[640,512]{1,0:T(8,128)S(1)}, f32[640,512]{1,0:T(8,128)S(1)}, f32[4,256,256]{2,1,0:T(8,128)S(1)}) custom-call(bf16[640,2048]{1,0:T(8,128)(2,1)S(1)} %get-tuple-element.29.refs_0_, bf16[640,2048]{1,0:T(8,128)(2,1)S(1)} %get-tuple-element.30.refs_1_, ...), custom_call_target="tpu_custom_call", output_to_operand_aliasing={{0}: (6, {}), {1}: (7, {}), {2}: (8, {})} | custom-call | flops 1207959552 | bytes 2359296 | tf_op jit(solution)/shard_map/pallas_call | solution.py:265
  65.0 2.9 %shard_map.74 = f32[64,640]{1,0:T(8,128)} custom-call(bf16[640,2048]{1,0:T(8,128)(2,1)S(1)} %get-tuple-element.29.refs_0_, bf16[640,2048]{1,0:T(8,128)(2,1)S(1)} %get-tuple-element.30.refs_1_, bf16[640,2048]{1,0:T(8,128)(2,1)S(1)} %get-tuple-element.31.refs_0_.refs_2_, bf16[640,2048]{1,0:T(8,128)(2,1)S(1)} %get-tuple-element.32.refs_1_.refs_3_, ...), custom_call_target="tpu_custom_call" | custom-call | flops 1207959552 | bytes 2359296 | tf_op jit(solution)/shard_map/pallas_call | solution.py:265
  (23 shorter events, 0.1 us)
Async XLA Ops:
  1.4 11.9 %collective-permute-start.18 = (bf16[2,128,512]{2,1,0:T(8,128)(2,1)S(1)}, bf16[2,128,512]{2,1,0:T(8,128)(2,1)S(1)}, u32[]{:S(2)}, u32[]{:S(2)}) collective-permute-start(bf16[2,128,512]{2,1,0:T(8,128)(2,1)S(1)} %shard_map.67.refs_2_), channel_id=1, source_target_pairs={{0,4},{1,5},{2,6},{3,7},{4,8},{5,9},{6,10},{7,11},{8,12},{9,13},{1... | collective-permute-start | bytes 786440 | tf_op jit(solution)/shard_map/ppermute | solution.py:296
  4.5 8.8 %collective-permute-start.5 = (bf16[2,128,512]{2,1,0:T(8,128)(2,1)S(1)}, bf16[2,128,512]{2,1,0:T(8,128)(2,1)S(1)}, u32[]{:S(2)}, u32[]{:S(2)}) collective-permute-start(bf16[2,128,512]{2,1,0:T(8,128)(2,1)S(1)} %shard_map.67.refs_2_), channel_id=1, source_target_pairs={{0,2},{1,3},{2,0},{3,1},{4,6},{5,7},{6,4},{7,5},{8,10},{9,11},{10,... | collective-permute-start | bytes 786440 | tf_op jit(solution)/shard_map/ppermute | solution.py:296
  6.0 7.8 %collective-permute-start.27 = (bf16[2,128,512]{2,1,0:T(8,128)(2,1)S(1)}, bf16[2,128,512]{2,1,0:T(8,128)(2,1)S(1)}, u32[]{:S(2)}, u32[]{:S(2)}) collective-permute-start(bf16[2,128,512]{2,1,0:T(8,128)(2,1)S(1)} %shard_map.67.refs_2_), channel_id=1, source_target_pairs={{0,1},{1,0},{2,3},{3,2},{4,5},{5,4},{6,7},{7,6},{8,9},{9,8},{10,11... | collective-permute-start | bytes 786440 | tf_op jit(solution)/shard_map/ppermute | solution.py:296
  7.5 11.0 %collective-permute-start = (bf16[2,128,512]{2,1,0:T(8,128)(2,1)S(1)}, bf16[2,128,512]{2,1,0:T(8,128)(2,1)S(1)}, u32[]{:S(2)}, u32[]{:S(2)}) collective-permute-start(bf16[2,128,512]{2,1,0:T(8,128)(2,1)S(1)} %shard_map.66.refs_2_), channel_id=1, source_target_pairs={{0,4},{1,5},{2,6},{3,7},{4,8},{5,9},{6,10},{7,11},{8,12},{9,13},{1... | collective-permute-start | bytes 786440 | tf_op jit(solution)/shard_map/ppermute | solution.py:296
  9.1 9.4 %collective-permute-start.15 = (bf16[2,128,512]{2,1,0:T(8,128)(2,1)S(1)}, bf16[2,128,512]{2,1,0:T(8,128)(2,1)S(1)}, u32[]{:S(2)}, u32[]{:S(2)}) collective-permute-start(bf16[2,128,512]{2,1,0:T(8,128)(2,1)S(1)} %shard_map.66.refs_2_), channel_id=1, source_target_pairs={{0,2},{1,3},{2,0},{3,1},{4,6},{5,7},{6,4},{7,5},{8,10},{9,11},{10,... | collective-permute-start | bytes 786440 | tf_op jit(solution)/shard_map/ppermute | solution.py:296
  13.3 6.7 %collective-permute-start.14 = (bf16[2,128,512]{2,1,0:T(8,128)(2,1)S(1)}, bf16[2,128,512]{2,1,0:T(8,128)(2,1)S(1)}, u32[]{:S(2)}, u32[]{:S(2)}) collective-permute-start(bf16[2,128,512]{2,1,0:T(8,128)(2,1)S(1)} %shard_map.66.refs_2_), channel_id=1, source_target_pairs={{0,1},{1,0},{2,3},{3,2},{4,5},{5,4},{6,7},{7,6},{8,9},{9,8},{10,11... | collective-permute-start | bytes 786440 | tf_op jit(solution)/shard_map/ppermute | solution.py:296
  13.3 6.7 %collective-permute-start.29 = (bf16[2,128,512]{2,1,0:T(8,128)(2,1)S(1)}, bf16[2,128,512]{2,1,0:T(8,128)(2,1)S(1)}, u32[]{:S(2)}, u32[]{:S(2)}) collective-permute-start(bf16[2,128,512]{2,1,0:T(8,128)(2,1)S(1)} %collective-permute-done.18.refs_6_), channel_id=1, source_target_pairs={{0,1},{1,0},{2,3},{3,2},{4,5},{5,4},{6,7},{7,6},{8,9},{9,8},{10,11... | collective-permute-start | bytes 786440 | tf_op jit(solution)/shard_map/ppermute | solution.py:296
  13.8 6.7 %collective-permute-start.28 = (bf16[2,128,512]{2,1,0:T(8,128)(2,1)S(1)}, bf16[2,128,512]{2,1,0:T(8,128)(2,1)S(1)}, u32[]{:S(2)}, u32[]{:S(2)}) collective-permute-start(bf16[2,128,512]{2,1,0:T(8,128)(2,1)S(1)} %collective-permute-done.5.refs_4_), channel_id=1, source_target_pairs={{0,1},{1,0},{2,3},{3,2},{4,5},{5,4},{6,7},{7,6},{8,9},{9,8},{10,11... | collective-permute-start | bytes 786440 | tf_op jit(solution)/shard_map/ppermute | solution.py:296
  18.5 11.0 %collective-permute-start.19 = (bf16[2,128,512]{2,1,0:T(8,128)(2,1)S(1)}, bf16[2,128,512]{2,1,0:T(8,128)(2,1)S(1)}, u32[]{:S(2)}, u32[]{:S(2)}) collective-permute-start(bf16[2,128,512]{2,1,0:T(8,128)(2,1)S(1)} %collective-permute-done.18.refs_6_), channel_id=1, source_target_pairs={{0,4},{1,5},{2,6},{3,7},{4,8},{5,9},{6,10},{7,11},{8,12},{9,13},{1... | collective-permute-start | bytes 786440 | tf_op jit(solution)/shard_map/ppermute | solution.py:296
  18.5 12.5 %collective-permute-start.24 = (bf16[2,128,512]{2,1,0:T(8,128)(2,1)S(1)}, bf16[2,128,512]{2,1,0:T(8,128)(2,1)S(1)}, u32[]{:S(2)}, u32[]{:S(2)}) collective-permute-start(bf16[2,128,512]{2,1,0:T(8,128)(2,1)S(1)} %collective-permute-done.18.refs_6_), channel_id=1, source_target_pairs={{0,2},{1,3},{2,0},{3,1},{4,6},{5,7},{6,4},{7,5},{8,10},{9,11},{10,... | collective-permute-start | bytes 786440 | tf_op jit(solution)/shard_map/ppermute | solution.py:296
  20.0 11.0 %collective-permute-start.17 = (bf16[2,128,512]{2,1,0:T(8,128)(2,1)S(1)}, bf16[2,128,512]{2,1,0:T(8,128)(2,1)S(1)}, u32[]{:S(2)}, u32[]{:S(2)}) collective-permute-start(bf16[2,128,512]{2,1,0:T(8,128)(2,1)S(1)} %collective-permute-done.refs_6_), channel_id=1, source_target_pairs={{0,1},{1,0},{2,3},{3,2},{4,5},{5,4},{6,7},{7,6},{8,9},{9,8},{10,11... | collective-permute-start | bytes 786440 | tf_op jit(solution)/shard_map/ppermute | solution.py:296
  20.0 11.5 %collective-permute-start.16 = (bf16[2,128,512]{2,1,0:T(8,128)(2,1)S(1)}, bf16[2,128,512]{2,1,0:T(8,128)(2,1)S(1)}, u32[]{:S(2)}, u32[]{:S(2)}) collective-permute-start(bf16[2,128,512]{2,1,0:T(8,128)(2,1)S(1)} %collective-permute-done.15.refs_4_), channel_id=1, source_target_pairs={{0,1},{1,0},{2,3},{3,2},{4,5},{5,4},{6,7},{7,6},{8,9},{9,8},{10,11... | collective-permute-start | bytes 786440 | tf_op jit(solution)/shard_map/ppermute | solution.py:296
  20.5 13.3 %collective-permute-start.1 = (bf16[2,128,512]{2,1,0:T(8,128)(2,1)S(1)}, bf16[2,128,512]{2,1,0:T(8,128)(2,1)S(1)}, u32[]{:S(2)}, u32[]{:S(2)}) collective-permute-start(bf16[2,128,512]{2,1,0:T(8,128)(2,1)S(1)} %collective-permute-done.refs_6_), channel_id=1, source_target_pairs={{0,4},{1,5},{2,6},{3,7},{4,8},{5,9},{6,10},{7,11},{8,12},{9,13},{1... | collective-permute-start | bytes 786440 | tf_op jit(solution)/shard_map/ppermute | solution.py:296
  29.5 8.1 %collective-permute-start.11 = (bf16[2,128,512]{2,1,0:T(8,128)(2,1)S(1)}, bf16[2,128,512]{2,1,0:T(8,128)(2,1)S(1)}, u32[]{:S(2)}, u32[]{:S(2)}) collective-permute-start(bf16[2,128,512]{2,1,0:T(8,128)(2,1)S(1)} %collective-permute-done.refs_6_), channel_id=1, source_target_pairs={{0,2},{1,3},{2,0},{3,1},{4,6},{5,7},{6,4},{7,5},{8,10},{9,11},{10,... | collective-permute-start | bytes 786440 | tf_op jit(solution)/shard_map/ppermute | solution.py:296
  31.0 6.6 %collective-permute-start.26 = (bf16[2,128,512]{2,1,0:T(8,128)(2,1)S(1)}, bf16[2,128,512]{2,1,0:T(8,128)(2,1)S(1)}, u32[]{:S(2)}, u32[]{:S(2)}) collective-permute-start(bf16[2,128,512]{2,1,0:T(8,128)(2,1)S(1)} %collective-permute-done.19.refs_4_), channel_id=1, source_target_pairs={{0,1},{1,0},{2,3},{3,2},{4,5},{5,4},{6,7},{7,6},{8,9},{9,8},{10,11... | collective-permute-start | bytes 786440 | tf_op jit(solution)/shard_map/ppermute | solution.py:296
  31.0 6.6 %collective-permute-start.25 = (bf16[2,128,512]{2,1,0:T(8,128)(2,1)S(1)}, bf16[2,128,512]{2,1,0:T(8,128)(2,1)S(1)}, u32[]{:S(2)}, u32[]{:S(2)}) collective-permute-start(bf16[2,128,512]{2,1,0:T(8,128)(2,1)S(1)} %collective-permute-done.24.refs_2_), channel_id=1, source_target_pairs={{0,1},{1,0},{2,3},{3,2},{4,5},{5,4},{6,7},{7,6},{8,9},{9,8},{10,11... | collective-permute-start | bytes 786440 | tf_op jit(solution)/shard_map/ppermute | solution.py:296
  31.5 12.3 %collective-permute-start.20 = (bf16[2,128,512]{2,1,0:T(8,128)(2,1)S(1)}, bf16[2,128,512]{2,1,0:T(8,128)(2,1)S(1)}, u32[]{:S(2)}, u32[]{:S(2)}) collective-permute-start(bf16[2,128,512]{2,1,0:T(8,128)(2,1)S(1)} %collective-permute-done.19.refs_4_), channel_id=1, source_target_pairs={{0,2},{1,3},{2,0},{3,1},{4,6},{5,7},{6,4},{7,5},{8,10},{9,11},{10,... | collective-permute-start | bytes 786440 | tf_op jit(solution)/shard_map/ppermute | solution.py:296
  33.8 12.6 %collective-permute-start.2 = (bf16[2,128,512]{2,1,0:T(8,128)(2,1)S(1)}, bf16[2,128,512]{2,1,0:T(8,128)(2,1)S(1)}, u32[]{:S(2)}, u32[]{:S(2)}) collective-permute-start(bf16[2,128,512]{2,1,0:T(8,128)(2,1)S(1)} %collective-permute-done.1.refs_4_), channel_id=1, source_target_pairs={{0,4},{1,5},{2,6},{3,7},{4,8},{5,9},{6,10},{7,11},{8,12},{9,13},{1... | collective-permute-start | bytes 786440 | tf_op jit(solution)/shard_map/ppermute | solution.py:296
  37.5 10.7 %collective-permute-start.22 = (bf16[2,128,512]{2,1,0:T(8,128)(2,1)S(1)}, bf16[2,128,512]{2,1,0:T(8,128)(2,1)S(1)}, u32[]{:S(2)}, u32[]{:S(2)}) collective-permute-start(bf16[2,128,512]{2,1,0:T(8,128)(2,1)S(1)} %collective-permute-done.19.refs_4_), channel_id=1, source_target_pairs={{0,4},{1,5},{2,6},{3,7},{4,8},{5,9},{6,10},{7,11},{8,12},{9,13},{1... | collective-permute-start | bytes 786440 | tf_op jit(solution)/shard_map/ppermute | solution.py:296
  37.5 14.7 %collective-permute-start.13 = (bf16[2,128,512]{2,1,0:T(8,128)(2,1)S(1)}, bf16[2,128,512]{2,1,0:T(8,128)(2,1)S(1)}, u32[]{:S(2)}, u32[]{:S(2)}) collective-permute-start(bf16[2,128,512]{2,1,0:T(8,128)(2,1)S(1)} %collective-permute-done.1.refs_4_), channel_id=1, source_target_pairs={{0,1},{1,0},{2,3},{3,2},{4,5},{5,4},{6,7},{7,6},{8,9},{9,8},{10,11... | collective-permute-start | bytes 786440 | tf_op jit(solution)/shard_map/ppermute | solution.py:296
  37.6 14.8 %collective-permute-start.12 = (bf16[2,128,512]{2,1,0:T(8,128)(2,1)S(1)}, bf16[2,128,512]{2,1,0:T(8,128)(2,1)S(1)}, u32[]{:S(2)}, u32[]{:S(2)}) collective-permute-start(bf16[2,128,512]{2,1,0:T(8,128)(2,1)S(1)} %collective-permute-done.11.refs_2_), channel_id=1, source_target_pairs={{0,1},{1,0},{2,3},{3,2},{4,5},{5,4},{6,7},{7,6},{8,9},{9,8},{10,11... | collective-permute-start | bytes 786440 | tf_op jit(solution)/shard_map/ppermute | solution.py:296
  43.8 10.4 %collective-permute-start.8 = (bf16[2,128,512]{2,1,0:T(8,128)(2,1)S(1)}, bf16[2,128,512]{2,1,0:T(8,128)(2,1)S(1)}, u32[]{:S(2)}, u32[]{:S(2)}) collective-permute-start(bf16[2,128,512]{2,1,0:T(8,128)(2,1)S(1)} %collective-permute-done.1.refs_4_), channel_id=1, source_target_pairs={{0,2},{1,3},{2,0},{3,1},{4,6},{5,7},{6,4},{7,5},{8,10},{9,11},{10,... | collective-permute-start | bytes 786440 | tf_op jit(solution)/shard_map/ppermute | solution.py:296
  46.4 8.4 %collective-permute-start.21 = (bf16[2,128,512]{2,1,0:T(8,128)(2,1)S(1)}, bf16[2,128,512]{2,1,0:T(8,128)(2,1)S(1)}, u32[]{:S(2)}, u32[]{:S(2)}) collective-permute-start(bf16[2,128,512]{2,1,0:T(8,128)(2,1)S(1)} %collective-permute-done.20.refs_2_), channel_id=1, source_target_pairs={{0,1},{1,0},{2,3},{3,2},{4,5},{5,4},{6,7},{7,6},{8,9},{9,8},{10,11... | collective-permute-start | bytes 786440 | tf_op jit(solution)/shard_map/ppermute | solution.py:296
  48.2 10.2 %collective-permute-start.6 = (bf16[2,128,512]{2,1,0:T(8,128)(2,1)S(1)}, bf16[2,128,512]{2,1,0:T(8,128)(2,1)S(1)}, u32[]{:S(2)}, u32[]{:S(2)}) collective-permute-start(bf16[2,128,512]{2,1,0:T(8,128)(2,1)S(1)} %collective-permute-done.5.refs_4_), channel_id=1, source_target_pairs={{0,12},{1,13},{2,14},{3,15},{4,0},{5,1},{6,2},{7,3},{8,4},{9,5},{1... | collective-permute-start | bytes 786440 | tf_op jit(solution)/shard_map/ppermute | solution.py:296
  52.2 8.4 %collective-permute-start.3 = (bf16[2,128,512]{2,1,0:T(8,128)(2,1)S(1)}, bf16[2,128,512]{2,1,0:T(8,128)(2,1)S(1)}, u32[]{:S(2)}, u32[]{:S(2)}) collective-permute-start(bf16[2,128,512]{2,1,0:T(8,128)(2,1)S(1)} %collective-permute-done.2.refs_4_), channel_id=1, source_target_pairs={{0,2},{1,3},{2,0},{3,1},{4,6},{5,7},{6,4},{7,5},{8,10},{9,11},{10,... | collective-permute-start | bytes 786440 | tf_op jit(solution)/shard_map/ppermute | solution.py:296
  52.4 9.7 %collective-permute-start.23 = (bf16[2,128,512]{2,1,0:T(8,128)(2,1)S(1)}, bf16[2,128,512]{2,1,0:T(8,128)(2,1)S(1)}, u32[]{:S(2)}, u32[]{:S(2)}) collective-permute-start(bf16[2,128,512]{2,1,0:T(8,128)(2,1)S(1)} %collective-permute-done.22.refs_4_), channel_id=1, source_target_pairs={{0,1},{1,0},{2,3},{3,2},{4,5},{5,4},{6,7},{7,6},{8,9},{9,8},{10,11... | collective-permute-start | bytes 786440 | tf_op jit(solution)/shard_map/ppermute | solution.py:296
  54.3 9.2 %collective-permute-start.10 = (bf16[2,128,512]{2,1,0:T(8,128)(2,1)S(1)}, bf16[2,128,512]{2,1,0:T(8,128)(2,1)S(1)}, u32[]{:S(2)}, u32[]{:S(2)}) collective-permute-start(bf16[2,128,512]{2,1,0:T(8,128)(2,1)S(1)} %collective-permute-done.2.refs_4_), channel_id=1, source_target_pairs={{0,1},{1,0},{2,3},{3,2},{4,5},{5,4},{6,7},{7,6},{8,9},{9,8},{10,11... | collective-permute-start | bytes 786440 | tf_op jit(solution)/shard_map/ppermute | solution.py:296
  54.7 8.8 %collective-permute-start.9 = (bf16[2,128,512]{2,1,0:T(8,128)(2,1)S(1)}, bf16[2,128,512]{2,1,0:T(8,128)(2,1)S(1)}, u32[]{:S(2)}, u32[]{:S(2)}) collective-permute-start(bf16[2,128,512]{2,1,0:T(8,128)(2,1)S(1)} %collective-permute-done.8.refs_2_), channel_id=1, source_target_pairs={{0,1},{1,0},{2,3},{3,2},{4,5},{5,4},{6,7},{7,6},{8,9},{9,8},{10,11... | collective-permute-start | bytes 786440 | tf_op jit(solution)/shard_map/ppermute | solution.py:296
  58.4 6.5 %collective-permute-start.7 = (bf16[2,128,512]{2,1,0:T(8,128)(2,1)S(1)}, bf16[2,128,512]{2,1,0:T(8,128)(2,1)S(1)}, u32[]{:S(2)}, u32[]{:S(2)}) collective-permute-start(bf16[2,128,512]{2,1,0:T(8,128)(2,1)S(1)} %collective-permute-done.6.refs_7_), channel_id=1, source_target_pairs={{0,1},{1,0},{2,3},{3,2},{4,5},{5,4},{6,7},{7,6},{8,9},{9,8},{10,11... | collective-permute-start | bytes 786440 | tf_op jit(solution)/shard_map/ppermute | solution.py:296
  60.6 4.4 %collective-permute-start.4 = (bf16[2,128,512]{2,1,0:T(8,128)(2,1)S(1)}, bf16[2,128,512]{2,1,0:T(8,128)(2,1)S(1)}, u32[]{:S(2)}, u32[]{:S(2)}) collective-permute-start(bf16[2,128,512]{2,1,0:T(8,128)(2,1)S(1)} %collective-permute-done.3.refs_5_), channel_id=1, source_target_pairs={{0,1},{1,0},{2,3},{3,2},{4,5},{5,4},{6,7},{7,6},{8,9},{9,8},{10,11... | collective-permute-start | bytes 786440 | tf_op jit(solution)/shard_map/ppermute | solution.py:296
